TPU v7x, 512 devices: a whole 4x4x16 slice. The times are simulated.
512 devices in a mesh: branch: 8 (over y_lo, x), sky: 64 (over z, y_hi, core).
Axes of the slice: x: 4, y: 4 (y_hi: 2, y_lo: 2; y = y_hi * 2 + y_lo), z: 16, core: 2. Of those that a mesh axis runs over, the one named last changes fastest.
Arguments:
- sky_maps: bfloat16 [8, 64, 16384], P('branch', None, 'sky'), may hold values from -6 to 6
- footprint: int32 [8, 16384], P('branch', 'sky'), may hold values 0 or 1
- neighbours: int32 [9, 16384], P(None, 'sky'), may hold values from -1 to 16383, as said below
- enc_weight: bfloat16 [8, 6, 9, 64, 64], P('branch'), may hold values from -0.1875 to 0.1875
- join_weight: bfloat16 [256, 512], P(None, 'branch'), may hold values from -0.25 to 0.25
- dec_weight: bfloat16 [9, 256, 256], P(None, 'branch'), may hold values from -0.125 to 0.125
- cotangent: bfloat16 [256, 16384], P('branch', 'sky'), may hold values from -6 to 6
Outputs:
- map_grads: bfloat16 [8, 64, 16384], P('branch', None, 'sky')
- weight_grads: float32 [8, 6, 9, 64, 64], P('branch')
Inputs may be any that keep to these rules, and one draw needn't show every extreme that they name: `neighbours`: slot 4 of each row is the row itself; every other entry is -1 or a row index that differs from the row's own by at most 256.
All inputs are finite; a program needn't handle non-finite values. No bound on the sum of `footprint` on one device may be relied on, other than what follows from the above.
Results may differ from a plain program's by a relative error of at most 0.017.
Values may be sent and summed in bfloat16 or wider, within the bound.
No kernel may reach another device: no remote copies, remote signals or barrier semaphores. Data moves between devices by JAX's collectives and lax.ppermute only.
A program may use at most 64 MiB of HBM per device.

v0:
```python
import math

import jax
import jax.numpy as jnp
from jax import lax
from jax.sharding import PartitionSpec as P


def from_behind(value, axis, by):
    peers = lax.axis_size(axis)
    pairs = [(i, i + by) for i in range(peers) if 0 <= i + by < peers]
    return lax.ppermute(value, axis, pairs)


def with_halo(cells, sides, width):
    for axis, dim in sides:
        count = lax.axis_size(axis)
        ends = count - 1
        head = lax.slice_in_dim(cells, 0, width, axis=dim)
        tail = lax.slice_in_dim(cells, cells.shape[dim] - width, cells.shape[dim], axis=dim)
        cells = jnp.concatenate(
            [
                lax.ppermute(tail, axis, [(i, (i + 1) % count) for i in range(ends)]),
                cells,
                lax.ppermute(head, axis, [((i + 1) % count, i) for i in range(ends)]),
            ],
            axis=dim,
        )
    return cells


def silu_slope(value):
    sigmoid = jax.nn.sigmoid(value)
    return sigmoid * (1.0 + value * (1.0 - sigmoid))


def flat_taps(weight):
    return jnp.transpose(weight, (1, 2, 0)).reshape(weight.shape[1], -1)


def pick_columns(padded, position, present):
    channels = padded.shape[0]
    picked = jnp.take(padded, position.reshape(-1), axis=1).reshape(channels, 9, -1)
    return jnp.where(present[None], picked, jnp.zeros((), padded.dtype))


def spread_columns(contrib, position, present, channels, total_span):
    contrib = jnp.where(present[None], contrib.reshape(channels, 9, -1), 0.0)
    target = jnp.zeros((channels, total_span), jnp.float32)
    return target.at[:, position.reshape(-1)].add(contrib.reshape(channels, -1))


def fold_rims(padded, row_count):
    lower = from_behind(padded[:, :row_count].astype(jnp.bfloat16), "sky", -1).astype(jnp.float32)
    upper = from_behind(padded[:, 2 * row_count :].astype(jnp.bfloat16), "sky", 1).astype(
        jnp.float32
    )
    return padded[:, row_count : 2 * row_count] + lower + upper


def fold_unit_rims(padded, row_count):
    lower = from_behind(padded[:, :row_count].astype(jnp.bfloat16), "sky", -1).astype(jnp.float32)
    upper = from_behind(padded[:, 2 * row_count :].astype(jnp.bfloat16), "sky", 1).astype(
        jnp.float32
    )
    return padded[:, row_count : 2 * row_count] + lower + upper


def per_device(sky_maps, footprint, neighbours, enc_weight, join_weight, dec_weight, cotangent):
    row_count = sky_maps.shape[2]
    channels = sky_maps.shape[1]
    own_start = lax.axis_index("sky") * row_count
    first_row = own_start - row_count
    present = neighbours >= 0
    position = jnp.where(present, neighbours - first_row, 0)
    retained = footprint[0].astype(jnp.float32)[None, :]
    weights = enc_weight[0]
    depth = weights.shape[0]
    hidden = sky_maps[0]
    padded_list = []
    pre_list = []
    for layer_index in range(depth):
        padded = with_halo(hidden, (("sky", 1),), row_count)
        picked = pick_columns(padded, position, present)
        preact = jnp.dot(
            flat_taps(weights[layer_index]),
            picked.reshape(-1, row_count),
            preferred_element_type=jnp.float32,
        )
        hidden = (retained * (hidden.astype(jnp.float32) + jax.nn.silu(preact))).astype(
            jnp.bfloat16
        )
        padded_list.append(padded)
        pre_list.append(preact)
    partial_sum = jnp.dot(join_weight, hidden, preferred_element_type=jnp.float32)
    unit_share = lax.psum_scatter(
        partial_sum.astype(jnp.bfloat16), "branch", scatter_dimension=0, tiled=True
    ).astype(jnp.float32)
    slope_share = silu_slope(unit_share).astype(jnp.bfloat16)
    full_width = dec_weight.shape[2]
    dec_terms = lax.dot_general(
        flat_taps(dec_weight),
        cotangent,
        (((0,), (0,)), ((), ())),
        preferred_element_type=jnp.float32,
    )
    unit_pad = spread_columns(dec_terms, position, present, full_width, 3 * row_count)
    summed = lax.psum(fold_unit_rims(unit_pad, row_count), "branch")
    all_slopes = lax.all_gather(slope_share, "branch", axis=0, tiled=True)
    unit_grad = (summed * all_slopes.astype(jnp.float32)).astype(jnp.bfloat16)
    gradient = lax.dot_general(
        join_weight, unit_grad, (((0,), (0,)), ((), ())), preferred_element_type=jnp.float32
    )
    normalizer = 1.0 / math.sqrt(row_count * lax.axis_size("sky"))
    layer_grads = [None] * depth
    for layer_index in reversed(range(depth)):
        masked = retained * gradient
        act_grad = (masked * silu_slope(pre_list[layer_index])).astype(jnp.bfloat16)
        picked = pick_columns(padded_list[layer_index], position, present).reshape(-1, row_count)
        tap_grads = lax.dot_general(
            act_grad, picked, (((1,), (1,)), ((), ())), preferred_element_type=jnp.float32
        )
        layer_grads[layer_index] = jnp.transpose(
            tap_grads.reshape(channels, channels, 9), (2, 0, 1)
        )
        spread = lax.dot_general(
            flat_taps(weights[layer_index]),
            act_grad,
            (((0,), (0,)), ((), ())),
            preferred_element_type=jnp.float32,
        )
        gradient = masked + fold_rims(
            spread_columns(spread, position, present, channels, 3 * row_count), row_count
        )
    summed_weights = lax.psum(jnp.stack(layer_grads), "sky") * normalizer
    return (gradient.astype(jnp.bfloat16)[None], summed_weights[None])


def solution(mesh):
    in_specs = (
        P("branch", None, "sky"),
        P("branch", "sky"),
        P(None, "sky"),
        P("branch", None, None, None, None),
        P(None, "branch"),
        P(None, "branch", None),
        P("branch", "sky"),
    )
    out_specs = (P("branch", None, "sky"), P("branch", None, None, None, None))
    return jax.shard_map(
        per_device, mesh=mesh, in_specs=in_specs, out_specs=out_specs, check_vma=False
    )
```

profile of v0, /device:TPU:1, one launch (start us, length us, event | category | flops | bytes accessed | tf_op | source)
XLA Modules:
  0.0 955.7 jit_solution(9312221840940899464)
XLA Ops:
  7.2 6.2 collective-permute-start.2
  13.4 3.9 collective-permute-start.3
  21.3 4.7 gather_fusion
  34.3 3.1 collective-permute-done.5
  37.6 4.7 gather_fusion.1
  50.8 2.9 collective-permute-done.7
  53.8 4.7 gather_fusion.2
  65.2 5.2 collective-permute-done.9
  70.6 4.7 gather_fusion.3
  82.9 13.8 %scatter_custom_fusion = f32[256,768]{0,1:T(8,128)S(1)} fusion(s32[2304]{0:T(1024)S(1)} %fusion.94, f32[2304,256]{1,0:T(8,128)} %bitcast.220, f32[]{:T(128)} %constant.17.clone.1), kind=kCustom, calls=%fused_computation.80 | custom fusion | flops 589824 | bytes 786944 | tf_op jit(solution)/shard_map/scatter-add | solution.py:50
  97.7 4.7 gather_fusion.4
  105.6 5.8 collective-permute-start.12
  116.0 5.1 collective-permute-start.1
  121.3 4.7 gather_fusion.5
  132.9 48.7 %reduce-scatter.4.cloned.1.call-done = bf16[32,256]{1,0:T(8,128)(2,1)} async-done(((bf16[256,256]{1,0:T(8,128)(2,1)}), bf16[32,256]{1,0:T(8,128)(2,1)}) %reduce-scatter.4.cloned.1.call-update) | async-done | bytes 16400 | tf_op jit(solution)/shard_map/reduce_scatter | solution.py:96
  182.3 21.8 %all_gather.3 = bf16[256,256]{1,0:T(8,128)(2,1)S(1)} all-gather(bf16[32,256]{1,0:T(8,128)(2,1)S(1)} %fusion.83), channel_id=1, replica_groups=mesh['branch'=8,'sky'=64] {'branch'}, dimensions={0}, use_global_device_ids=true | all-gather | bytes 147456 | tf_op jit(solution)/shard_map/all_gather | solution.py:109
  204.2 69.7 %all-reduce.3.cloned.1.call-done = f32[256,256]{0,1:T(8,128)} async-done(((f32[256,256]{0,1:T(8,128)}), f32[256,256]{0,1:T(8,128)}) %all-reduce.3.cloned.1.call-update) | async-done | bytes 262160 | tf_op jit(solution)/shard_map/psum | solution.py:108
  276.4 16.2 %scatter_custom_fusion.1 = f32[64,768]{0,1:T(8,128)S(1)} fusion(s32[2304]{0:T(1024)} %copy-done.40, f32[64,2304]{0,1:T(8,128)S(1)} %copy.134, f32[]{:T(128)} %constant.17.clone.1, pred[2304]{0:T(1024)(128)(4,1)S(1)} %broadcast_in_dim.154), kind=kCustom, calls=%fused_computation.31 | custom fusion | flops 294912 | bytes 789760 | tf_op jit(solution)/shard_map/scatter-add | solution.py:50
  292.8 7.5 collective-permute-start.14
  300.3 4.2 collective-permute-start.15
  307.3 16.0 %scatter_custom_fusion.2 = f32[64,768]{0,1:T(8,128)S(1)} fusion(s32[2304]{0:T(1024)} %copy-done.40, f32[64,2304]{0,1:T(8,128)S(1)} %copy.138, f32[]{:T(128)} %constant.17.clone.1, pred[2304]{0:T(1024)(128)(4,1)S(1)} %broadcast_in_dim.154), kind=kCustom, calls=%fused_computation.29 | custom fusion | flops 294912 | bytes 789760 | tf_op jit(solution)/shard_map/scatter-add | solution.py:50
  325.5 5.9 collective-permute-start.17
  334.0 16.2 %scatter_custom_fusion.3 = f32[64,768]{0,1:T(8,128)S(1)} fusion(s32[2304]{0:T(1024)} %copy-done.40, f32[64,2304]{0,1:T(8,128)S(1)} %copy.142, f32[]{:T(128)} %constant.17.clone.1, pred[2304]{0:T(1024)(128)(4,1)S(1)} %broadcast_in_dim.154), kind=kCustom, calls=%fused_computation.27 | custom fusion | flops 294912 | bytes 789760 | tf_op jit(solution)/shard_map/scatter-add | solution.py:50
  352.3 5.2 collective-permute-start.19
  360.4 16.0 %scatter_custom_fusion.4 = f32[64,768]{0,1:T(8,128)S(1)} fusion(s32[2304]{0:T(1024)} %copy-done.40, f32[64,2304]{0,1:T(8,128)S(1)} %copy.146, f32[]{:T(128)} %constant.17.clone.1, pred[2304]{0:T(1024)(128)(4,1)S(1)} %broadcast_in_dim.154), kind=kCustom, calls=%fused_computation.25 | custom fusion | flops 294912 | bytes 789760 | tf_op jit(solution)/shard_map/scatter-add | solution.py:50
  378.5 5.7 collective-permute-start.21
  387.4 16.0 %scatter_custom_fusion.5 = f32[64,768]{0,1:T(8,128)S(1)} fusion(s32[2304]{0:T(1024)} %copy-done.40, f32[64,2304]{0,1:T(8,128)S(1)} %copy.150, f32[]{:T(128)} %constant.17.clone.1, pred[2304]{0:T(1024)(128)(4,1)S(1)} %broadcast_in_dim.154), kind=kCustom, calls=%fused_computation.23 | custom fusion | flops 294912 | bytes 789760 | tf_op jit(solution)/shard_map/scatter-add | solution.py:50
  405.6 5.7 collective-permute-start.23
  417.9 16.0 %scatter_custom_fusion.6 = f32[64,768]{0,1:T(8,128)S(1)} fusion(s32[2304]{0:T(1024)} %copy-done.40, f32[64,2304]{0,1:T(8,128)S(1)} %copy.154, f32[]{:T(128)} %constant.17.clone.1, pred[2304]{0:T(1024)(128)(4,1)S(1)} %broadcast_in_dim.154), kind=kCustom, calls=%fused_computation.21 | custom fusion | flops 294912 | bytes 789760 | tf_op jit(solution)/shard_map/scatter-add | solution.py:50
  436.1 5.7 collective-permute-start.25
  443.4 502.4 %all-reduce.5.cloned.1.call-done = f32[6,9,64,64]{3,2,1,0:T(8,128)} async-done(((f32[6,9,64,64]{3,2,1,0:T(8,128)}), f32[6,9,64,64]{3,2,1,0:T(8,128)}) %all-reduce.5.cloned.1.call-update) | async-done | bytes 884752 | tf_op jit(solution)/shard_map/psum | solution.py:135
  945.8 2.9 multiply_bitcast_fusion
  (240 shorter events, 84.1 us)
Async XLA Ops:
  7.2 121.5 %copy-start = (bf16[256,64]{0,1:T(8,128)(2,1)S(1)}, bf16[256,64]{0,1:T(8,128)(2,1)}, u32[]{:S(2)}) copy-start(bf16[256,64]{0,1:T(8,128)(2,1)} %param.13) | copy-start | bytes 98308
  7.2 174.4 %reduce-scatter.4.cloned.1.call-start = ((), (), s32[]{:S(2)}) async-start(), calls=%async_computation.3 | async-start | bytes 147456 | tf_op jit(solution)/shard_map/reduce_scatter | solution.py:96
  7.2 12.3 %collective-permute-start.2 = (bf16[64,256]{1,0:T(8,128)(2,1)}, bf16[64,256]{1,0:T(8,128)(2,1)S(1)}, u32[]{:S(2)}, u32[]{:S(2)}) collective-permute-start(bf16[64,256]{1,0:T(8,128)(2,1)} %bitcast.241), channel_id=1, source_target_pairs={{0,1},{1,2},{2,3},{3,4},{4,5},{5,6},{6,7},{7,8},{8,9},{9,10},{10,1... | collective-permute-start | bytes 98312 | tf_op jit(solution)/shard_map/ppermute | solution.py:23
  13.4 7.0 collective-permute-start.3
  28.4 5.9 collective-permute-start.4
  30.7 6.7 collective-permute-start.5
  44.6 6.2 collective-permute-start.6
  46.6 7.1 collective-permute-start.7
  60.8 4.4 collective-permute-start.8
  63.0 7.4 collective-permute-start.9
  78.5 19.0 %collective-permute-start.10 = (bf16[64,256]{1,0:T(8,128)(2,1)S(1)}, bf16[64,256]{1,0:T(8,128)(2,1)S(1)}, u32[]{:S(2)}, u32[]{:S(2)}) collective-permute-start(bf16[64,256]{1,0:T(8,128)(2,1)S(1)} %get-tuple-element.35), channel_id=1, source_target_pairs={{0,1},{1,2},{2,3},{3,4},{4,5},{5,6},{6,7},{7,8},{8,9},{9,10},{10,1... | collective-permute-start | bytes 98312 | tf_op jit(solution)/shard_map/ppermute | solution.py:23
  80.4 17.1 %collective-permute-start.11 = (bf16[64,256]{1,0:T(8,128)(2,1)S(1)}, bf16[64,256]{1,0:T(8,128)(2,1)S(1)}, u32[]{:S(2)}, u32[]{:S(2)}) collective-permute-start(bf16[64,256]{1,0:T(8,128)(2,1)S(1)} %get-tuple-element.35), channel_id=1, source_target_pairs={{1,0},{2,1},{3,2},{4,3},{5,4},{6,5},{7,6},{8,7},{9,8},{10,9},{11,1... | collective-permute-start | bytes 98312 | tf_op jit(solution)/shard_map/ppermute | solution.py:25
  105.6 15.5 %collective-permute-start.12 = (bf16[64,256]{1,0:T(8,128)(2,1)S(1)}, bf16[64,256]{1,0:T(8,128)(2,1)S(1)}, u32[]{:S(2)}, u32[]{:S(2)}) collective-permute-start(bf16[64,256]{1,0:T(8,128)(2,1)S(1)} %get-tuple-element.37), channel_id=1, source_target_pairs={{0,1},{1,2},{2,3},{3,4},{4,5},{5,6},{6,7},{7,8},{8,9},{9,10},{10,1... | collective-permute-start | bytes 98312 | tf_op jit(solution)/shard_map/ppermute | solution.py:23
  111.4 9.7 %collective-permute-start.13 = (bf16[64,256]{1,0:T(8,128)(2,1)S(1)}, bf16[64,256]{1,0:T(8,128)(2,1)S(1)}, u32[]{:S(2)}, u32[]{:S(2)}) collective-permute-start(bf16[64,256]{1,0:T(8,128)(2,1)S(1)} %get-tuple-element.37), channel_id=1, source_target_pairs={{1,0},{2,1},{3,2},{4,3},{5,4},{6,5},{7,6},{8,7},{9,8},{10,9},{11,1... | collective-permute-start | bytes 98312 | tf_op jit(solution)/shard_map/ppermute | solution.py:25
  114.1 17.0 %collective-permute-start = (bf16[256,256]{0,1:T(8,128)(2,1)}, bf16[256,256]{0,1:T(8,128)(2,1)}, u32[]{:S(2)}, u32[]{:S(2)}) collective-permute-start(bf16[256,256]{0,1:T(8,128)(2,1)} %get-tuple-element.15), channel_id=1, source_target_pairs={{1,0},{2,1},{3,2},{4,3},{5,4},{6,5},{7,6},{8,7},{9,8},{10,9},{11,1... | collective-permute-start | bytes 393224 | tf_op jit(solution)/shard_map/ppermute | solution.py:12
  116.0 15.1 %collective-permute-start.1 = (bf16[256,256]{0,1:T(8,128)(2,1)}, bf16[256,256]{0,1:T(8,128)(2,1)}, u32[]{:S(2)}, u32[]{:S(2)}) collective-permute-start(bf16[256,256]{0,1:T(8,128)(2,1)} %get-tuple-element.16), channel_id=1, source_target_pairs={{0,1},{1,2},{2,3},{3,4},{4,5},{5,6},{6,7},{7,8},{8,9},{9,10},{10,1... | collective-permute-start | bytes 393224 | tf_op jit(solution)/shard_map/ppermute | solution.py:12
  129.7 144.1 %all-reduce.3.cloned.1.call-start = ((), (), s32[]{:S(2)}) async-start(), calls=%async_computation.1 | async-start | bytes 524288 | tf_op jit(solution)/shard_map/psum | solution.py:108
  132.8 813.0 %all-reduce.5.cloned.1.call-start = ((), (), s32[]{:S(2)}) async-start(), calls=%async_computation.2 | async-start | bytes 3538944 | tf_op jit(solution)/shard_map/psum | solution.py:135
  275.0 30.5 %copy-start.8 = (f32[64,256]{1,0:T(8,128)}, f32[64,256]{1,0:T(8,128)S(1)}, u32[]{:S(2)}) copy-start(f32[64,256]{1,0:T(8,128)S(1)} %get-tuple-element.40) | copy-start | bytes 196612
  276.4 28.1 %copy-start.7 = (bf16[64,64,9]{1,0,2:T(8,128)(2,1)S(1)}, bf16[64,64,9]{1,0,2:T(8,128)(2,1)}, u32[]{:S(2)}) copy-start(bf16[64,64,9]{1,0,2:T(8,128)(2,1)} %get-tuple-element.14) | copy-start | bytes 221188
  292.8 12.1 %collective-permute-start.14 = (bf16[64,256]{1,0:T(8,128)(2,1)S(1)}, bf16[64,256]{1,0:T(8,128)(2,1)S(1)}, u32[]{:S(2)}, u32[]{:S(2)}) collective-permute-start(bf16[64,256]{1,0:T(8,128)(2,1)S(1)} %get-tuple-element.27), channel_id=1, source_target_pairs={{1,0},{2,1},{3,2},{4,3},{5,4},{6,5},{7,6},{8,7},{9,8},{10,9},{11,1... | collective-permute-start | bytes 98312 | tf_op jit(solution)/shard_map/ppermute | solution.py:12
  300.3 5.3 collective-permute-start.15
  323.6 9.1 collective-permute-start.16
  325.5 7.2 collective-permute-start.17
  350.4 7.5 collective-permute-start.18
  352.3 6.2 collective-permute-start.19
  376.6 8.9 collective-permute-start.20
  378.5 7.0 collective-permute-start.21
  403.7 7.6 collective-permute-start.22
  405.6 6.4 collective-permute-start.23
  434.1 7.7 collective-permute-start.24
  436.1 6.7 collective-permute-start.25
  (38 other events, 236.1 us)
Sparse Core Ops, SparseCore 0:
  129.9 51.6 reduce-scatter.3
  185.3 88.5 all-reduce.2
  416.9 528.8 all-reduce.4
where the time goes:
time: 965 us; the launch traced here: 956 us
  waiting for transfers between devices  636 us (66%)
  other arithmetic  129 us (13%)
  starting transfers between devices  91.9 us (10%)
  local copies, waits for them, and re-layouts  47.1 us (5%)
  blocking collectives  21.8 us (2%)
  between operations  15.7 us (2%)
  matrix products  14.2 us (1%)
    psum x1, waiting for transfers between devices, per_device(): summed_weights = lax.psum(jnp.stack(layer_grads), 'sky') * normalizer  502 us
    scatter-add x7, other arithmetic, spread_columns(): return target.at[:, position.reshape(-1)].add(contrib.reshape(channels, -1))  110 us
    psum x1, waiting for transfers between devices, per_device(): summed = lax.psum(fold_unit_rims(unit_pad, row_count), 'branch')  69.7 us
    ppermute x14, starting transfers between devices, from_behind(): return lax.ppermute(value, axis, pairs)  56.7 us
    reduce_scatter x1, waiting for transfers between devices, per_device(): lax.psum_scatter(partial_sum.astype(jnp.bfloat16), 'branch', scatter_dime...  48.7 us
    gather x6, local copies, waits for them, and re-layouts, pick_columns(): jnp.take(padded, position.reshape(-1), axis=1).reshape(channels, 9, -1)  28 us
    all_gather x1, blocking collectives, per_device(): all_slopes = lax.all_gather(slope_share, 'branch', axis=0, tiled=True)  21.8 us
    ppermute x6, starting transfers between devices, with_halo(): lax.ppermute(tail, axis, [(i, (i + 1) % count) for i in range(ends)])  20.3 us
  transfers between devices with their start and end apart: 29, of which 11 were waited for; matrix products, arithmetic and copies ran while one was open for 6% of the time, Pallas kernels for 0%

commit v1 on v0

v1 whole, which is shorter than its diff:
```python
import functools
import math

import jax
import jax.numpy as jnp
from jax import lax
from jax.experimental import pallas as pl
from jax.experimental.pallas import tpu as pltpu
from jax.sharding import Mesh, PartitionSpec as P

SKY = ("z", "yh", "core")
QUAD = ("yh", "core")
C = 64
R = 256
TAPS = 9
F32 = jnp.float32
BF16 = jnp.bfloat16
VMEM = pl.BlockSpec(memory_space=pltpu.VMEM)
SMEM = pl.BlockSpec(memory_space=pltpu.SMEM)


def shift(value, by):
    peers = lax.axis_size(SKY)
    return lax.ppermute(value, SKY, [(i, i + by) for i in range(peers) if 0 <= i + by < peers])


def widen(value):
    below = shift(value, 2)
    above = shift(value, -2)
    other = lax.ppermute(jnp.concatenate([value, below, above], axis=0), "core", [(0, 1), (1, 0)])
    return below, above, other


def inner(other, first, even, start, size):
    own = other[start : start + size]
    below = other[first + start : first + start + size]
    above = other[2 * first + start : 2 * first + start + size]
    return jnp.where(even, below, own), jnp.where(even, own, above)


def slope_of(value, sigmoid):
    return sigmoid * (1.0 + value * (1.0 - sigmoid))


def low_onehot(low):
    return (lax.broadcasted_iota(jnp.int32, (R, R), 0) == low).astype(BF16)


def conv(blocks, pos, weight, picked_ref):
    stack = jnp.concatenate(blocks, axis=0)
    for k in range(TAPS):
        if k == 4:
            column = blocks[1]
        else:
            at = pos[k : k + 1]
            block = at >> 8
            found = jnp.dot(stack, low_onehot(at & 255), preferred_element_type=F32)
            column = jnp.where(
                block == 0,
                found[:C],
                jnp.where(block == 1, found[C : 2 * C], jnp.where(block == 2, found[2 * C :], 0.0)),
            ).astype(BF16)
        picked_ref[k * C : (k + 1) * C, :] = column
    return jnp.dot(weight, picked_ref[...], preferred_element_type=F32)


def spread(act, pos, weight, parts):
    terms = lax.dot_general(weight, act, (((0,), (0,)), ((), ())), preferred_element_type=F32)
    total = None
    for k in range(TAPS):
        if k == 4:
            continue
        at = pos[k : k + 1]
        block = at >> 8
        term = terms[k * C : (k + 1) * C].astype(BF16)
        zero = jnp.zeros_like(term)
        sent = jnp.concatenate([jnp.where(block == part, term, zero) for part in parts], axis=0)
        added = lax.dot_general(
            sent, low_onehot(at & 255), (((1,), (1,)), ((), ())), preferred_element_type=F32
        )
        total = added if total is None else total + added
    out = {part: total[i * C : (i + 1) * C] for i, part in enumerate(parts)}
    if 1 in out:
        out[1] = out[1] + terms[4 * C : 5 * C]
    return out


def two_layers(blocks, pos, kept, w_ref, h_ref, picked_ref, slopes_ref, last_ref, scratch):
    middle = []
    for b in (1, 2, 3):
        target = picked_ref.at[0] if b == 2 else scratch.at[b // 2]
        pre = conv(blocks[b - 1 : b + 2], pos[b], w_ref[0], target)
        sigmoid = jax.nn.sigmoid(pre)
        slopes_ref[b - 1] = slope_of(pre, sigmoid)
        middle.append((kept[b] * (blocks[b].astype(F32) + pre * sigmoid)).astype(BF16))
    pre = conv(middle, pos[2], w_ref[1], picked_ref.at[1])
    sigmoid = jax.nn.sigmoid(pre)
    last_ref[...] = slope_of(pre, sigmoid)
    hidden = (kept[2] * (middle[1].astype(F32) + pre * sigmoid)).astype(BF16)
    if h_ref is not None:
        h_ref[...] = hidden
    return hidden


def first_kernel(
    par_ref, x_ref, below_ref, above_ref, other_ref, w_ref,
    h_ref, picked_ref, slopes_ref, last_ref, pos_ref, kept_ref, scratch,
):
    even = par_ref[0] == 0
    size = x_ref.shape[0]
    other = other_ref[...]
    meta_at = size - 16
    meta1, meta3 = inner(other, size, even, meta_at, 16)
    metas = [below_ref[meta_at:, :], meta1, x_ref[meta_at:, :], meta3, above_ref[meta_at:, :]]
    column = lax.broadcasted_iota(jnp.int32, (16, R), 1)
    pos, kept = [], []
    for b, meta in enumerate(metas):
        offset = meta.astype(F32)
        at = jnp.where(offset > 400.0, 768, offset.astype(jnp.int32) + column + R)
        pos_ref[16 * b : 16 * (b + 1), :] = at
        keep = offset[TAPS : TAPS + 1]
        kept_ref[b : b + 1, :] = keep
        pos.append(at)
        kept.append(keep)
    kept_ref[5:8, :] = jnp.zeros((3, R), F32)
    map1, map3 = inner(other, size, even, 0, C)
    blocks = [below_ref[:C, :], map1, x_ref[:C, :], map3, above_ref[:C, :]]
    two_layers(blocks, pos, kept, w_ref, h_ref, picked_ref, slopes_ref, last_ref, scratch)


def read_tables(pos_ref, kept_ref):
    pos = [pos_ref[16 * b : 16 * b + 16, :] for b in range(5)]
    kept = [kept_ref[b : b + 1, :] for b in range(5)]
    return pos, kept


def layers_kernel(
    par_ref, x_ref, below_ref, above_ref, other_ref, w_ref, pos_ref, kept_ref,
    h_ref, picked_ref, slopes_ref, last_ref, scratch,
):
    even = par_ref[0] == 0
    pos, kept = read_tables(pos_ref, kept_ref)
    one, three = inner(other_ref[...], C, even, 0, C)
    blocks = [below_ref[...], one, x_ref[...], three, above_ref[...]]
    two_layers(blocks, pos, kept, w_ref, h_ref, picked_ref, slopes_ref, last_ref, scratch)


def join_kernel(
    par_ref, x_ref, below_ref, above_ref, other_ref, w_ref, pos_ref, kept_ref, joinw_ref, unit_ref,
    share_ref, picked_ref, slopes_ref, last_ref, scratch,
):
    even = par_ref[0] == 0
    pos, kept = read_tables(pos_ref, kept_ref)
    one, three = inner(other_ref[...], C, even, 0, C)
    blocks = [below_ref[...], one, x_ref[...], three, above_ref[...]]
    hidden = two_layers(blocks, pos, kept, w_ref, None, picked_ref, slopes_ref, last_ref, scratch)
    partial = lax.dot_general(
        joinw_ref[...], hidden, (((0,), (0,)), ((), ())), preferred_element_type=F32
    ).astype(BF16)
    count = share_ref.shape[0]
    each = partial.shape[0] // count
    for c in range(count):
        share_ref[c, :each, :] = partial[c * each : (c + 1) * each]
        share_ref[c, each:, :] = unit_ref[c * each : (c + 1) * each, :]


def unit_kernel(par_ref, x_ref, other_ref, pos_ref, dec_ref, unit_ref, scratch):
    even = par_ref[0] == 0
    size = x_ref.shape[0]
    each = size - 16 - C
    one, three = inner(other_ref[...], size, even, C, each)
    sources = [one, x_ref[C : C + each, :], three]
    pos = [pos_ref[16 * b : 16 * b + 16, :] for b in (1, 2, 3)]
    for k in range(TAPS):
        if k == 4:
            scratch[k * each : (k + 1) * each, :] = sources[1]
            continue
        total = None
        for i in range(3):
            at = pos[i][k : k + 1]
            sent = jnp.where((at >> 8) == 2 - i, sources[i], jnp.zeros_like(sources[i]))
            added = lax.dot_general(
                sent, low_onehot(at & 255), (((1,), (1,)), ((), ())), preferred_element_type=F32
            )
            total = added if total is None else total + added
        scratch[k * each : (k + 1) * each, :] = total.astype(BF16)
    unit_ref[...] = jnp.dot(dec_ref[...], scratch[...], preferred_element_type=F32).astype(BF16)


def slope_kernel(parts_ref, out_ref):
    total = parts_ref[0].astype(F32)
    for i in range(1, parts_ref.shape[0]):
        total = total + parts_ref[i].astype(F32)
    each = total.shape[0] // 2
    joined = total[:each]
    slope = slope_of(joined, jax.nn.sigmoid(joined)).astype(BF16).astype(F32)
    grad = (total[each:] * slope).astype(BF16)
    for i in range(out_ref.shape[0]):
        out_ref[i] = grad


def head_kernel(unit_ref, joinw_ref, kept_ref, last_ref, pack_ref, masked_ref):
    gradient = jnp.dot(joinw_ref[...], unit_ref[...], preferred_element_type=F32)
    masked = kept_ref[2:3, :] * gradient
    masked_ref[...] = masked
    pack_ref[:C, :] = (masked * last_ref[...]).astype(BF16)
    pack_ref[C:, :] = masked.astype(BF16)


def weight_grad(act, picked):
    return lax.dot_general(
        act, picked, (((1,), (1,)), ((), ())), preferred_element_type=F32
    ).astype(BF16)


def back_kernel(final, *refs):
    if final:
        (par_ref, x_ref, below_ref, above_ref, other_ref, masked_ref, w_ref, pos_ref, kept_ref,
         picked_ref, slopes_ref, map_ref, grad_ref) = refs
    else:
        (par_ref, x_ref, below_ref, above_ref, other_ref, masked_ref, w_ref, pos_ref, kept_ref,
         picked_ref, slopes_ref, next_ref, pack_ref, out_ref, grad_ref) = refs
    even = par_ref[0] == 0
    pos, kept = read_tables(pos_ref, kept_ref)
    other = other_ref[...]
    act1, act3 = inner(other, 2 * C, even, 0, C)
    mask1, mask3 = inner(other, 2 * C, even, C, C)
    acts = [below_ref[:C, :], act1, x_ref[:C, :], act3, above_ref[:C, :]]
    masked = [mask1.astype(F32), masked_ref[...], mask3.astype(F32)]
    upper = w_ref[1]
    needed = [(2,), (1, 2), (0, 1, 2), (0, 1), (0,)]
    gradient = list(masked)
    for b in range(5):
        for part, value in spread(acts[b], pos[b], upper, needed[b]).items():
            gradient[b + part - 2] = gradient[b + part - 2] + value
    lower = [kept[i + 1] * gradient[i] for i in range(3)]
    low_acts = [(lower[i] * slopes_ref[i]).astype(BF16) for i in range(3)]
    grad_ref[1] = weight_grad(acts[2], picked_ref[1])
    grad_ref[0] = weight_grad(low_acts[1], picked_ref[0])
    result = lower[1]
    for i, part in ((0, 2), (1, 1), (2, 0)):
        result = result + spread(low_acts[i], pos[i + 1], w_ref[0], (part,))[part]
    if final:
        map_ref[...] = result.astype(BF16)
    else:
        out = kept[2] * result
        out_ref[...] = out
        pack_ref[:C, :] = (out * next_ref[...]).astype(BF16)
        pack_ref[C:, :] = out.astype(BF16)


def final_kernel(scale, sum_ref, out_ref):
    for layer in range(out_ref.shape[0]):
        for k in range(TAPS):
            out_ref[layer, k] = sum_ref[layer, :, k * C : (k + 1) * C].astype(F32) * scale


def sds(shape, dtype):
    return jax.ShapeDtypeStruct(shape, dtype)


def call(body, name, ins, outs, scratch=()):
    specs = [spec for spec, _ in ins]
    return pl.pallas_call(
        body,
        name=name,
        in_specs=specs,
        out_specs=[pl.BlockSpec(memory_space=pltpu.VMEM) for _ in outs],
        out_shape=outs,
        scratch_shapes=list(scratch),
    )(*[value for _, value in ins])


def v(value):
    return (VMEM, value)


def reduce_chunks(value, axes, parts):
    got = lax.all_to_all(value.reshape((parts, -1) + value.shape[1:]), axes, 0, 0, tiled=True)
    return jnp.sum(got.astype(F32), axis=0).astype(BF16)


def gather_chunks(value, axes, parts):
    got = lax.all_to_all(
        jnp.broadcast_to(value[None], (parts,) + value.shape), axes, 0, 0, tiled=True
    )
    return got.reshape((-1,) + value.shape[1:])


def per_device(sky_maps, footprint, neighbours, enc_weight, join_weight, dec_weight, cotangent):
    depth = enc_weight.shape[1]
    branches = lax.axis_size("branch")
    peers = lax.axis_size(SKY)
    par = lax.axis_index("core").astype(jnp.int32).reshape(1)
    rows = lax.axis_index(SKY) * R + lax.broadcasted_iota(jnp.int32, (TAPS, R), 1)
    offset = jnp.where(neighbours >= 0, neighbours - rows, 512).astype(BF16)
    pack = jnp.concatenate(
        [sky_maps[0], cotangent, offset, footprint.astype(BF16), jnp.zeros((6, R), BF16)], axis=0
    )
    weights = [
        jnp.transpose(enc_weight[0, i : i + 2], (0, 2, 1, 3)).reshape(2, C, TAPS * C)
        for i in range(0, depth, 2)
    ]
    joinw = join_weight.T
    dec = jnp.transpose(dec_weight, (2, 0, 1)).reshape(dec_weight.shape[2], -1)

    layer_outs = [
        sds((C, R), BF16), sds((2, TAPS * C, R), BF16), sds((3, C, R), F32), sds((C, R), F32),
    ]
    scratch = [pltpu.VMEM((2, TAPS * C, R), BF16)]
    below, above, other = widen(pack)
    hidden, picked, slopes, last, pos, kept = call(
        first_kernel, "layers01",
        [(SMEM, par), v(pack), v(below), v(above), v(other), v(weights[0])],
        layer_outs + [sds((80, R), jnp.int32), sds((8, R), F32)], scratch,
    )
    saved = [(picked, slopes, last)]
    unit = call(
        unit_kernel, "unit",
        [(SMEM, par), v(pack), v(other), v(pos), v(dec)],
        [sds((dec.shape[0], R), BF16)],
        [pltpu.VMEM((TAPS * cotangent.shape[0], R), BF16)],
    )[0]
    for group in range(1, depth // 2):
        below, above, other = widen(hidden)
        ins = [(SMEM, par), v(hidden), v(below), v(above), v(other), v(weights[group]), v(pos), v(kept)]
        if group < depth // 2 - 1:
            hidden, picked, slopes, last = call(layers_kernel, "layers", ins, layer_outs, scratch)
        else:
            share = sds((branches, 2 * (dec.shape[0] // branches), R), BF16)
            share, picked, slopes, last = call(
                join_kernel, "layersjoin", ins + [v(joinw), v(unit)],
                [share] + layer_outs[1:], scratch,
            )
        saved.append((picked, slopes, last))
    parts = lax.all_to_all(share, "branch", 0, 0, tiled=True)
    grads = call(
        slope_kernel, "slope", [v(parts)], [sds((branches, parts.shape[1] // 2, R), BF16)]
    )[0]
    unit_grad = lax.all_to_all(grads, "branch", 0, 0, tiled=True).reshape(-1, R)
    pack, masked = call(
        head_kernel, "head",
        [v(unit_grad), v(joinw), v(kept), v(saved[-1][2])],
        [sds((2 * C, R), BF16), sds((C, R), F32)],
    )
    weight_grads = [None] * (depth // 2)
    for group in reversed(range(depth // 2)):
        below, above, other = widen(pack)
        picked, slopes, _ = saved[group]
        ins = [
            (SMEM, par), v(pack), v(below), v(above), v(other), v(masked), v(weights[group]),
            v(pos), v(kept), v(picked), v(slopes),
        ]
        grad_out = sds((2, C, TAPS * C), BF16)
        if group:
            pack, masked, weight_grads[group] = call(
                functools.partial(back_kernel, False), "back", ins + [v(saved[group - 1][2])],
                [sds((2 * C, R), BF16), sds((C, R), F32), grad_out],
            )
        else:
            map_grads, weight_grads[group] = call(
                functools.partial(back_kernel, True), "backlast", ins, [sds((C, R), BF16), grad_out]
            )
    stacked = jnp.concatenate(weight_grads, axis=0).reshape(depth * C, TAPS * C)
    quads = lax.axis_size(QUAD)
    length = lax.axis_size("z")
    chunk = reduce_chunks(stacked, QUAD, quads)
    chunk = reduce_chunks(chunk, "z", length)
    chunk = gather_chunks(chunk, "z", length)
    total = gather_chunks(chunk, QUAD, quads).reshape(depth, C, TAPS * C)
    summed = call(
        functools.partial(final_kernel, 1.0 / math.sqrt(R * peers)), "final", [v(total)],
        [sds((depth, TAPS, C, C), F32)],
    )[0]
    return map_grads[None], summed[None]


def solution(mesh):
    branches, sky = mesh.devices.shape
    mesh = Mesh(mesh.devices.reshape(branches, sky // 4, 2, 2), ("branch",) + SKY)
    in_specs = (
        P("branch", None, SKY),
        P("branch", SKY),
        P(None, SKY),
        P("branch", None, None, None, None),
        P(None, "branch"),
        P(None, "branch", None),
        P("branch", SKY),
    )
    out_specs = (P("branch", None, SKY), P("branch", None, None, None, None))
    return jax.shard_map(
        per_device, mesh=mesh, in_specs=in_specs, out_specs=out_specs, check_vma=False
    )
```

time: 965 us -> 252 us (0.26)
  waiting for transfers between devices: 636 us -> 15 us
  other arithmetic: 129 us -> 6.72 us
  blocking collectives: 21.8 us -> 103 us
  Pallas kernels: 0 us -> 41.2 us
  local copies, waits for them, and re-layouts: 47.1 us -> 12.3 us
  starting transfers between devices: 91.9 us -> 71.1 us
  between operations: 15.7 us -> 0.98 us
  matrix products: 14.2 us -> 0 us
    psum x2 -> x0, waiting for transfers between devices: 572 us -> none  [the longest x1 502 us: per_device(): summed_weights = lax.psum(jnp.stack(layer_grads), 'sky') * normalizer]
    scatter-add x7 -> x0, other arithmetic: 110 us -> none  [spread_columns(): return target.at[:, position.reshape(-1)].add(contrib.reshape(channels, -1))]
    all_to_all x0 -> x6, blocking collectives: none -> 103 us  [the longest x2 46.1 us: reduce_chunks(): lax.all_to_all(value.reshape((parts, -1) + value.shape[1:]), axes, 0, 0,...]
    reduce_scatter x1 -> x0, waiting for transfers between devices: 48.7 us -> none  [per_device(): lax.psum_scatter(partial_sum.astype(jnp.bfloat16), 'branch', scatter_dime...]
    pallas_call x0 -> x10, Pallas kernels: none -> 41.2 us  [call(): pl.pallas_call(body, name=name, in_specs=specs, out_specs=[pl.BlockSpec(m...]
    gather x6 -> x0, local copies, waits for them, and re-layouts: 28 us -> none  [pick_columns(): jnp.take(padded, position.reshape(-1), axis=1).reshape(channels, 9, -1)]
    all_gather x1 -> x0, blocking collectives: 21.8 us -> none  [per_device(): all_slopes = lax.all_gather(slope_share, 'branch', axis=0, tiled=True)]
    ppermute x26 -> x18, starting transfers between devices: 91.7 us -> 71.1 us  [the longest x12 47.2 us: shift(): lax.ppermute(value, SKY, [(i, i + by) for i in range(peers) if 0 <= i + b...]
  transfers between devices with their start and end apart: 29 -> 18, of which waited for: 11 -> 11; matrix products, arithmetic and copies ran while one was open for 6% -> 2% of each run, Pallas kernels for 0% -> 1%
where the time goes in v1:
time: 252 us; the launch traced here: 250 us
  blocking collectives  103 us (41%)
  starting transfers between devices  71.1 us (28%)
  Pallas kernels  41.2 us (16%)
  waiting for transfers between devices  15 us (6%)
  local copies, waits for them, and re-layouts  12.3 us (5%)
  other arithmetic  6.72 us (3%)
    ppermute x12, starting transfers between devices, shift(): lax.ppermute(value, SKY, [(i, i + by) for i in range(peers) if 0 <= i + b...  47.2 us
    all_to_all x2, blocking collectives, reduce_chunks(): lax.all_to_all(value.reshape((parts, -1) + value.shape[1:]), axes, 0, 0,...  46.1 us
    pallas_call x10, Pallas kernels, call(): pl.pallas_call(body, name=name, in_specs=specs, out_specs=[pl.BlockSpec(m...  41.2 us
    all_to_all x2, blocking collectives, gather_chunks(): lax.all_to_all(jnp.broadcast_to(value[None], (parts,) + value.shape), axe...  36 us
    ppermute x6, starting transfers between devices, widen(): lax.ppermute(jnp.concatenate([value, below, above], axis=0), 'core', [(0,...  23.8 us
    ppermute x12, waiting for transfers between devices, shift(): lax.ppermute(value, SKY, [(i, i + by) for i in range(peers) if 0 <= i + b...  11.9 us
    all_to_all x1, blocking collectives, per_device(): parts = lax.all_to_all(share, 'branch', 0, 0, tiled=True)  11.6 us
    all_to_all x1, blocking collectives, per_device(): unit_grad = lax.all_to_all(grads, 'branch', 0, 0, tiled=True).reshape(-1, R)  9.42 us
  transfers between devices with their start and end apart: 18, of which 11 were waited for; matrix products, arithmetic and copies ran while one was open for 2% of the time, Pallas kernels for 1%

profile of v1, /device:TPU:1, one launch (start us, length us, event | category | flops | bytes accessed | tf_op | source)
XLA Modules:
  0.0 250.5 jit_solution(14049945998861272506)
XLA Ops:
  4.9 6.3 %collective-permute-start = (bf16[112,256]{1,0:T(8,128)(2,1)S(1)}, bf16[112,256]{1,0:T(8,128)(2,1)S(1)}, u32[]{:S(2)}, u32[]{:S(2)}) collective-permute-start(bf16[112,256]{1,0:T(8,128)(2,1)S(1)} %concatenate.25.x_ref), channel_id=1, source_target_pairs={{0,2},{1,3},{2,4},{3,5},{4,6},{5,7},{6,8},{7,9},{8,10},{9,11},{10,... | collective-permute-start | bytes 172040 | tf_op jit(solution)/shard_map/ppermute | solution.py:24
  11.2 1.7 collective-permute-done.below_ref
  14.4 8.6 %collective-permute-start.2 = (bf16[336,256]{1,0:T(8,128)(2,1)S(1)}, bf16[336,256]{1,0:T(8,128)(2,1)S(1)}, u32[]{:S(2)}, u32[]{:S(2)}) collective-permute-start(bf16[336,256]{1,0:T(8,128)(2,1)S(1)} %concatenate.26), channel_id=1, source_target_pairs={{0,1},{1,0},{2,3},{3,2},{4,5},{5,4},{6,7},{7,6},{8,9},{9,8},{10,11... | collective-permute-start | bytes 516104 | tf_op jit(solution)/shard_map/ppermute | solution.py:30
  26.0 3.7 %layers01.1 = (bf16[64,256]{1,0:T(8,128)(2,1)}, bf16[2,576,256]{2,1,0:T(8,128)(2,1)}, f32[3,64,256]{2,1,0:T(8,128)}, f32[64,256]{1,0:T(8,128)}, s32[80,256]{1,0:T(8,128)}, /*index=5*/f32[8,256]{1,0:T(8,128)}) custom-call(s32[1]{0:T(128)} %bitcast.par_ref.refs_0_, bf16[112,256]{1,0:T(8,128)(2,1)} %copy-done.1, bf16[112,256]{1,0:T(8,128)(2,1)} %copy-done.9, ...), custom_call_target="tpu_custom_call" | custom-call | tf_op jit(solution)/shard_map/layers01/pallas_call | solution.py:264
  31.0 6.1 %collective-permute-start.3 = (bf16[64,256]{1,0:T(8,128)(2,1)}, bf16[64,256]{1,0:T(8,128)(2,1)S(1)}, u32[]{:S(2)}, u32[]{:S(2)}) collective-permute-start(bf16[64,256]{1,0:T(8,128)(2,1)} %get-tuple-element.26.x_ref), channel_id=1, source_target_pairs={{0,2},{1,3},{2,4},{3,5},{4,6},{5,7},{6,8},{7,9},{8,10},{9,11},{10,... | collective-permute-start | bytes 98312 | tf_op jit(solution)/shard_map/ppermute | solution.py:24
  39.2 2.8 %collective-permute-start.5 = (bf16[192,256]{1,0:T(8,128)(2,1)S(1)}, bf16[192,256]{1,0:T(8,128)(2,1)S(1)}, u32[]{:S(2)}, u32[]{:S(2)}) collective-permute-start(bf16[192,256]{1,0:T(8,128)(2,1)S(1)} %pad_maximum_fusion.4), channel_id=1, source_target_pairs={{0,1},{1,0},{2,3},{3,2},{4,5},{5,4},{6,7},{7,6},{8,9},{9,8},{10,11... | collective-permute-start | bytes 294920 | tf_op jit(solution)/shard_map/ppermute | solution.py:30
  43.7 3.7 %layers.1 = (bf16[64,256]{1,0:T(8,128)(2,1)}, bf16[2,576,256]{2,1,0:T(8,128)(2,1)}, f32[3,64,256]{2,1,0:T(8,128)}, f32[64,256]{1,0:T(8,128)}) custom-call(s32[1]{0:T(128)} %bitcast.par_ref.refs_0_, bf16[64,256]{1,0:T(8,128)(2,1)} %get-tuple-element.26.x_ref, bf16[64,256]{1,0:T(8,128)(2,1)} %copy-done.19, bf16[64,256]{1,0:T(8,128)(2,1)} %copy-done.18, ...), custom_call_target="tpu_custom_call" | custom-call | tf_op jit(solution)/shard_map/layers/pallas_call | solution.py:264
  48.7 6.7 %collective-permute-start.6 = (bf16[64,256]{1,0:T(8,128)(2,1)}, bf16[64,256]{1,0:T(8,128)(2,1)S(1)}, u32[]{:S(2)}, u32[]{:S(2)}) collective-permute-start(bf16[64,256]{1,0:T(8,128)(2,1)} %get-tuple-element.29.x_ref), channel_id=1, source_target_pairs={{0,2},{1,3},{2,4},{3,5},{4,6},{5,7},{6,8},{7,9},{8,10},{9,11},{10,... | collective-permute-start | bytes 98312 | tf_op jit(solution)/shard_map/ppermute | solution.py:24
  57.5 2.9 %collective-permute-start.8 = (bf16[192,256]{1,0:T(8,128)(2,1)S(1)}, bf16[192,256]{1,0:T(8,128)(2,1)S(1)}, u32[]{:S(2)}, u32[]{:S(2)}) collective-permute-start(bf16[192,256]{1,0:T(8,128)(2,1)S(1)} %pad_maximum_fusion.5), channel_id=1, source_target_pairs={{0,1},{1,0},{2,3},{3,2},{4,5},{5,4},{6,7},{7,6},{8,9},{9,8},{10,11... | collective-permute-start | bytes 294920 | tf_op jit(solution)/shard_map/ppermute | solution.py:30
  62.3 3.0 %unit.1.unit_ref = bf16[256,256]{1,0:T(8,128)(2,1)} custom-call(s32[1]{0:T(128)} %bitcast.par_ref.refs_0_, bf16[112,256]{1,0:T(8,128)(2,1)} %copy-done.1, bf16[336,256]{1,0:T(8,128)(2,1)} %copy-done, s32[80,256]{1,0:T(8,128)} %get-tuple-element.27.pos_ref.refs_7_, bf16[256,288]{1,0:T(8,128)(2,1)} %copy.18.dec_ref), custom_call_target="tpu_custom_call" | custom-call | tf_op jit(solution)/shard_map/unit/pallas_call | solution.py:264
  66.0 3.9 %layersjoin.1 = (bf16[8,64,256]{2,1,0:T(8,128)(2,1)}, bf16[2,576,256]{2,1,0:T(8,128)(2,1)}, f32[3,64,256]{2,1,0:T(8,128)}, f32[64,256]{1,0:T(8,128)}) custom-call(s32[1]{0:T(128)} %bitcast.par_ref.refs_0_, bf16[64,256]{1,0:T(8,128)(2,1)} %get-tuple-element.29.x_ref, bf16[64,256]{1,0:T(8,128)(2,1)} %copy-done.17, bf16[64,256]{1,0:T(8,128)(2,1)} %copy-done.16, ...), custom_call_target="tpu_custom_call" | custom-call | tf_op jit(solution)/shard_map/layersjoin/pallas_call | solution.py:264
  69.9 11.6 %all_to_all.30.parts_ref = bf16[8,64,256]{2,1,0:T(8,128)(2,1)} all-to-all(bf16[8,64,256]{2,1,0:T(8,128)(2,1)} %get-tuple-element.30), channel_id=1, replica_groups=mesh['branch'=8,'z'=16,'yh'=2,'core'=2] {'branch'}, dimensions={0} | all-to-all | bytes 524288 | tf_op jit(solution)/shard_map/all_to_all | solution.py:336
  81.5 1.6 slope.1
  83.1 9.4 %all_to_all.31 = bf16[8,32,256]{2,1,0:T(8,128)(2,1)} all-to-all(bf16[8,32,256]{2,1,0:T(8,128)(2,1)} %slope.1), channel_id=1, replica_groups=mesh['branch'=8,'z'=16,'yh'=2,'core'=2] {'branch'}, dimensions={0} | all-to-all | bytes 262144 | tf_op jit(solution)/shard_map/all_to_all | solution.py:340
  92.5 1.8 head.1
  95.6 6.9 %collective-permute-start.9 = (bf16[128,256]{1,0:T(8,128)(2,1)}, bf16[128,256]{1,0:T(8,128)(2,1)S(1)}, u32[]{:S(2)}, u32[]{:S(2)}) collective-permute-start(bf16[128,256]{1,0:T(8,128)(2,1)} %get-tuple-element.32.refs_1_), channel_id=1, source_target_pairs={{0,2},{1,3},{2,4},{3,5},{4,6},{5,7},{6,8},{7,9},{8,10},{9,11},{10,... | collective-permute-start | bytes 196616 | tf_op jit(solution)/shard_map/ppermute | solution.py:24
  102.5 1.6 collective-permute-done.9.refs_2_
  105.0 4.6 %collective-permute-start.11 = (bf16[384,256]{1,0:T(8,128)(2,1)S(1)}, bf16[384,256]{1,0:T(8,128)(2,1)S(1)}, u32[]{:S(2)}, u32[]{:S(2)}) collective-permute-start(bf16[384,256]{1,0:T(8,128)(2,1)S(1)} %pad_maximum_fusion.1), channel_id=1, source_target_pairs={{0,1},{1,0},{2,3},{3,2},{4,5},{5,4},{6,7},{7,6},{8,9},{9,8},{10,11... | collective-permute-start | bytes 589832 | tf_op jit(solution)/shard_map/ppermute | solution.py:30
  111.3 7.0 %back.2 = (bf16[128,256]{1,0:T(8,128)(2,1)}, f32[64,256]{1,0:T(8,128)}, bf16[2,64,576]{2,1,0:T(8,128)(2,1)}) custom-call(s32[1]{0:T(128)} %bitcast.par_ref.refs_0_, bf16[128,256]{1,0:T(8,128)(2,1)} %get-tuple-element.32.refs_1_, bf16[128,256]{1,0:T(8,128)(2,1)} %copy-done.5, bf16[128,256]{1,0:T(8,128)(2,1)} %copy-done.2, bf16[384,256]{1,0:T(8,128)(2,1)} %copy-done.10, ...), custom_call_target="tpu_custom_call" | custom-call | tf_op jit(solution)/shard_map/back/pallas_call | solution.py:264
  119.6 7.1 %collective-permute-start.12 = (bf16[128,256]{1,0:T(8,128)(2,1)}, bf16[128,256]{1,0:T(8,128)(2,1)S(1)}, u32[]{:S(2)}, u32[]{:S(2)}) collective-permute-start(bf16[128,256]{1,0:T(8,128)(2,1)} %get-tuple-element.37.refs_1_), channel_id=1, source_target_pairs={{0,2},{1,3},{2,4},{3,5},{4,6},{5,7},{6,8},{7,9},{8,10},{9,11},{10,... | collective-permute-start | bytes 196616 | tf_op jit(solution)/shard_map/ppermute | solution.py:24
  126.9 2.6 %collective-permute-done.12.refs_2_ = bf16[128,256]{1,0:T(8,128)(2,1)S(1)} collective-permute-done((bf16[128,256]{1,0:T(8,128)(2,1)}, bf16[128,256]{1,0:T(8,128)(2,1)S(1)}, u32[]{:S(2)}, u32[]{:S(2)}) %collective-permute-start.12) | collective-permute-done | bytes 65568 | tf_op jit(solution)/shard_map/ppermute | solution.py:24
  130.4 2.5 %collective-permute-start.14 = (bf16[384,256]{1,0:T(8,128)(2,1)S(1)}, bf16[384,256]{1,0:T(8,128)(2,1)S(1)}, u32[]{:S(2)}, u32[]{:S(2)}) collective-permute-start(bf16[384,256]{1,0:T(8,128)(2,1)S(1)} %pad_maximum_fusion.2), channel_id=1, source_target_pairs={{0,1},{1,0},{2,3},{3,2},{4,5},{5,4},{6,7},{7,6},{8,9},{9,8},{10,11... | collective-permute-start | bytes 589832 | tf_op jit(solution)/shard_map/ppermute | solution.py:30
  134.7 7.0 %back.3 = (bf16[128,256]{1,0:T(8,128)(2,1)}, f32[64,256]{1,0:T(8,128)}, bf16[2,64,576]{2,1,0:T(8,128)(2,1)}) custom-call(s32[1]{0:T(128)} %bitcast.par_ref.refs_0_, bf16[128,256]{1,0:T(8,128)(2,1)} %get-tuple-element.37.refs_1_, bf16[128,256]{1,0:T(8,128)(2,1)} %copy-done.7, bf16[128,256]{1,0:T(8,128)(2,1)} %copy-done.4, bf16[384,256]{1,0:T(8,128)(2,1)} %copy-done.12, ...), custom_call_target="tpu_custom_call" | custom-call | tf_op jit(solution)/shard_map/back/pallas_call | solution.py:264
  143.1 6.4 %collective-permute-start.15 = (bf16[128,256]{1,0:T(8,128)(2,1)}, bf16[128,256]{1,0:T(8,128)(2,1)S(1)}, u32[]{:S(2)}, u32[]{:S(2)}) collective-permute-start(bf16[128,256]{1,0:T(8,128)(2,1)} %get-tuple-element.42.refs_1_), channel_id=1, source_target_pairs={{0,2},{1,3},{2,4},{3,5},{4,6},{5,7},{6,8},{7,9},{8,10},{9,11},{10,... | collective-permute-start | bytes 196616 | tf_op jit(solution)/shard_map/ppermute | solution.py:24
  150.0 2.6 %collective-permute-done.15.refs_2_ = bf16[128,256]{1,0:T(8,128)(2,1)S(1)} collective-permute-done((bf16[128,256]{1,0:T(8,128)(2,1)}, bf16[128,256]{1,0:T(8,128)(2,1)S(1)}, u32[]{:S(2)}, u32[]{:S(2)}) %collective-permute-start.15) | collective-permute-done | bytes 65568 | tf_op jit(solution)/shard_map/ppermute | solution.py:24
  153.5 2.4 collective-permute-start.17
  157.6 6.9 %backlast.1 = (bf16[64,256]{1,0:T(8,128)(2,1)}, bf16[2,64,576]{2,1,0:T(8,128)(2,1)}) custom-call(s32[1]{0:T(128)} %bitcast.par_ref.refs_0_, bf16[128,256]{1,0:T(8,128)(2,1)} %get-tuple-element.42.refs_1_, bf16[128,256]{1,0:T(8,128)(2,1)} %copy-done.6, bf16[128,256]{1,0:T(8,128)(2,1)} %copy-done.3, bf16[384,256]{1,0:T(8,128)(2,1)} %copy-done.11, ...), custom_call_target="tpu_custom_call" | custom-call | tf_op jit(solution)/shard_map/backlast/pallas_call | solution.py:264
  165.4 14.5 %all_to_all.32 = bf16[4,96,576]{2,1,0:T(8,128)(2,1)S(1)} all-to-all(bf16[4,96,576]{2,1,0:T(8,128)(2,1)S(1)} %bitcast.26), channel_id=1, replica_groups=mesh['branch'=8,'z'=16,'yh'=2,'core'=2] {'yh','core'}, dimensions={0} | all-to-all | bytes 884736 | tf_op jit(solution)/shard_map/all_to_all | solution.py:279
  180.1 31.6 %all_to_all.33 = bf16[16,6,576]{2,1,0:T(8,128)(2,1)S(1)} all-to-all(bf16[16,6,576]{2,1,0:T(8,128)(2,1)S(1)} %reshape.33), channel_id=1, replica_groups=mesh['branch'=8,'z'=16,'yh'=2,'core'=2] {'z'}, dimensions={0} | all-to-all | bytes 221184 | tf_op jit(solution)/shard_map/all_to_all | solution.py:279
  211.8 19.5 %all_to_all.34 = bf16[16,6,576]{2,1,0:T(8,128)(2,1)S(1)} all-to-all(bf16[16,6,576]{2,1,0:T(8,128)(2,1)S(1)} %broadcast_in_dim.29), channel_id=1, replica_groups=mesh['branch'=8,'z'=16,'yh'=2,'core'=2] {'z'}, dimensions={0} | all-to-all | bytes 221184 | tf_op jit(solution)/shard_map/all_to_all | solution.py:284
  231.4 16.5 %all_to_all.35 = bf16[4,96,576]{2,1,0:T(8,128)(2,1)} all-to-all(bf16[4,96,576]{2,1,0:T(8,128)(2,1)S(1)} %broadcast_in_dim.31), channel_id=1, replica_groups=mesh['branch'=8,'z'=16,'yh'=2,'core'=2] {'yh','core'}, dimensions={0} | all-to-all | bytes 884736 | tf_op jit(solution)/shard_map/all_to_all | solution.py:284
  248.0 2.5 %final.1 = f32[6,9,64,64]{3,2,1,0:T(8,128)} custom-call(bf16[6,64,576]{2,1,0:T(8,128)(2,1)} %bitcast.27), custom_call_target="tpu_custom_call" | custom-call | tf_op jit(solution)/shard_map/final/pallas_call | solution.py:264
  (90 shorter events, 33.4 us)
Async XLA Ops:
  3.6 21.8 %copy-start.1 = (bf16[112,256]{1,0:T(8,128)(2,1)}, bf16[112,256]{1,0:T(8,128)(2,1)S(1)}, u32[]{:S(2)}) copy-start(bf16[112,256]{1,0:T(8,128)(2,1)S(1)} %concatenate.25.x_ref) | copy-start | bytes 172036
  3.6 7.6 %collective-permute-start.1 = (bf16[112,256]{1,0:T(8,128)(2,1)S(1)}, bf16[112,256]{1,0:T(8,128)(2,1)S(1)}, u32[]{:S(2)}, u32[]{:S(2)}) collective-permute-start(bf16[112,256]{1,0:T(8,128)(2,1)S(1)} %concatenate.25.x_ref), channel_id=1, source_target_pairs={{2,0},{3,1},{4,2},{5,3},{6,4},{7,5},{8,6},{9,7},{10,8},{11,9},{12,... | collective-permute-start | bytes 172040 | tf_op jit(solution)/shard_map/ppermute | solution.py:24
  4.9 8.0 %collective-permute-start = (bf16[112,256]{1,0:T(8,128)(2,1)S(1)}, bf16[112,256]{1,0:T(8,128)(2,1)S(1)}, u32[]{:S(2)}, u32[]{:S(2)}) collective-permute-start(bf16[112,256]{1,0:T(8,128)(2,1)S(1)} %concatenate.25.x_ref), channel_id=1, source_target_pairs={{0,2},{1,3},{2,4},{3,5},{4,6},{5,7},{6,8},{7,9},{8,10},{9,11},{10,... | collective-permute-start | bytes 172040 | tf_op jit(solution)/shard_map/ppermute | solution.py:24
  11.2 14.2 %copy-start.8 = (bf16[112,256]{1,0:T(8,128)(2,1)}, bf16[112,256]{1,0:T(8,128)(2,1)S(1)}, u32[]{:S(2)}) copy-start(bf16[112,256]{1,0:T(8,128)(2,1)S(1)} %collective-permute-done.1.above_ref) | copy-start | bytes 172036
  12.9 12.5 %copy-start.9 = (bf16[112,256]{1,0:T(8,128)(2,1)}, bf16[112,256]{1,0:T(8,128)(2,1)S(1)}, u32[]{:S(2)}) copy-start(bf16[112,256]{1,0:T(8,128)(2,1)S(1)} %collective-permute-done.below_ref) | copy-start | bytes 172036
  14.4 10.9 %collective-permute-start.2 = (bf16[336,256]{1,0:T(8,128)(2,1)S(1)}, bf16[336,256]{1,0:T(8,128)(2,1)S(1)}, u32[]{:S(2)}, u32[]{:S(2)}) collective-permute-start(bf16[336,256]{1,0:T(8,128)(2,1)S(1)} %concatenate.26), channel_id=1, source_target_pairs={{0,1},{1,0},{2,3},{3,2},{4,5},{5,4},{6,7},{7,6},{8,9},{9,8},{10,11... | collective-permute-start | bytes 516104 | tf_op jit(solution)/shard_map/ppermute | solution.py:30
  24.2 36.2 %copy-start.15 = (bf16[9,32,256]{2,1,0:T(8,128)(2,1)S(1)}, bf16[9,32,256]{2,1,0:T(8,128)(2,1)}, u32[]{:S(2)}) copy-start(bf16[9,32,256]{2,1,0:T(8,128)(2,1)} %param.12) | copy-start | bytes 442372
  29.7 7.4 %collective-permute-start.4 = (bf16[64,256]{1,0:T(8,128)(2,1)}, bf16[64,256]{1,0:T(8,128)(2,1)S(1)}, u32[]{:S(2)}, u32[]{:S(2)}) collective-permute-start(bf16[64,256]{1,0:T(8,128)(2,1)} %get-tuple-element.26.x_ref), channel_id=1, source_target_pairs={{2,0},{3,1},{4,2},{5,3},{6,4},{7,5},{8,6},{9,7},{10,8},{11,9},{12,... | collective-permute-start | bytes 98312 | tf_op jit(solution)/shard_map/ppermute | solution.py:24
  31.0 7.4 %collective-permute-start.3 = (bf16[64,256]{1,0:T(8,128)(2,1)}, bf16[64,256]{1,0:T(8,128)(2,1)S(1)}, u32[]{:S(2)}, u32[]{:S(2)}) collective-permute-start(bf16[64,256]{1,0:T(8,128)(2,1)} %get-tuple-element.26.x_ref), channel_id=1, source_target_pairs={{0,2},{1,3},{2,4},{3,5},{4,6},{5,7},{6,8},{7,9},{8,10},{9,11},{10,... | collective-permute-start | bytes 98312 | tf_op jit(solution)/shard_map/ppermute | solution.py:24
  37.1 5.9 %copy-start.18 = (bf16[64,256]{1,0:T(8,128)(2,1)}, bf16[64,256]{1,0:T(8,128)(2,1)S(1)}, u32[]{:S(2)}) copy-start(bf16[64,256]{1,0:T(8,128)(2,1)S(1)} %collective-permute-done.4.above_ref) | copy-start | bytes 98308
  38.4 4.6 %copy-start.19 = (bf16[64,256]{1,0:T(8,128)(2,1)}, bf16[64,256]{1,0:T(8,128)(2,1)S(1)}, u32[]{:S(2)}) copy-start(bf16[64,256]{1,0:T(8,128)(2,1)S(1)} %collective-permute-done.3.below_ref) | copy-start | bytes 98308
  39.2 3.8 %collective-permute-start.5 = (bf16[192,256]{1,0:T(8,128)(2,1)S(1)}, bf16[192,256]{1,0:T(8,128)(2,1)S(1)}, u32[]{:S(2)}, u32[]{:S(2)}) collective-permute-start(bf16[192,256]{1,0:T(8,128)(2,1)S(1)} %pad_maximum_fusion.4), channel_id=1, source_target_pairs={{0,1},{1,0},{2,3},{3,2},{4,5},{5,4},{6,7},{7,6},{8,9},{9,8},{10,11... | collective-permute-start | bytes 294920 | tf_op jit(solution)/shard_map/ppermute | solution.py:30
  47.4 8.0 %collective-permute-start.7 = (bf16[64,256]{1,0:T(8,128)(2,1)}, bf16[64,256]{1,0:T(8,128)(2,1)S(1)}, u32[]{:S(2)}, u32[]{:S(2)}) collective-permute-start(bf16[64,256]{1,0:T(8,128)(2,1)} %get-tuple-element.29.x_ref), channel_id=1, source_target_pairs={{2,0},{3,1},{4,2},{5,3},{6,4},{7,5},{8,6},{9,7},{10,8},{11,9},{12,... | collective-permute-start | bytes 98312 | tf_op jit(solution)/shard_map/ppermute | solution.py:24
  48.7 8.1 %collective-permute-start.6 = (bf16[64,256]{1,0:T(8,128)(2,1)}, bf16[64,256]{1,0:T(8,128)(2,1)S(1)}, u32[]{:S(2)}, u32[]{:S(2)}) collective-permute-start(bf16[64,256]{1,0:T(8,128)(2,1)} %get-tuple-element.29.x_ref), channel_id=1, source_target_pairs={{0,2},{1,3},{2,4},{3,5},{4,6},{5,7},{6,8},{7,9},{8,10},{9,11},{10,... | collective-permute-start | bytes 98312 | tf_op jit(solution)/shard_map/ppermute | solution.py:24
  55.3 10.0 %copy-start.16 = (bf16[64,256]{1,0:T(8,128)(2,1)}, bf16[64,256]{1,0:T(8,128)(2,1)S(1)}, u32[]{:S(2)}) copy-start(bf16[64,256]{1,0:T(8,128)(2,1)S(1)} %collective-permute-done.7.above_ref) | copy-start | bytes 98308
  56.8 8.6 %copy-start.17 = (bf16[64,256]{1,0:T(8,128)(2,1)}, bf16[64,256]{1,0:T(8,128)(2,1)S(1)}, u32[]{:S(2)}) copy-start(bf16[64,256]{1,0:T(8,128)(2,1)S(1)} %collective-permute-done.6.below_ref) | copy-start | bytes 98308
  57.5 7.8 %collective-permute-start.8 = (bf16[192,256]{1,0:T(8,128)(2,1)S(1)}, bf16[192,256]{1,0:T(8,128)(2,1)S(1)}, u32[]{:S(2)}, u32[]{:S(2)}) collective-permute-start(bf16[192,256]{1,0:T(8,128)(2,1)S(1)} %pad_maximum_fusion.5), channel_id=1, source_target_pairs={{0,1},{1,0},{2,3},{3,2},{4,5},{5,4},{6,7},{7,6},{8,9},{9,8},{10,11... | collective-permute-start | bytes 294920 | tf_op jit(solution)/shard_map/ppermute | solution.py:30
  94.3 8.2 %collective-permute-start.10 = (bf16[128,256]{1,0:T(8,128)(2,1)}, bf16[128,256]{1,0:T(8,128)(2,1)S(1)}, u32[]{:S(2)}, u32[]{:S(2)}) collective-permute-start(bf16[128,256]{1,0:T(8,128)(2,1)} %get-tuple-element.32.refs_1_), channel_id=1, source_target_pairs={{2,0},{3,1},{4,2},{5,3},{6,4},{7,5},{8,6},{9,7},{10,8},{11,9},{12,... | collective-permute-start | bytes 196616 | tf_op jit(solution)/shard_map/ppermute | solution.py:24
  95.6 8.5 %collective-permute-start.9 = (bf16[128,256]{1,0:T(8,128)(2,1)}, bf16[128,256]{1,0:T(8,128)(2,1)S(1)}, u32[]{:S(2)}, u32[]{:S(2)}) collective-permute-start(bf16[128,256]{1,0:T(8,128)(2,1)} %get-tuple-element.32.refs_1_), channel_id=1, source_target_pairs={{0,2},{1,3},{2,4},{3,5},{4,6},{5,7},{6,8},{7,9},{8,10},{9,11},{10,... | collective-permute-start | bytes 196616 | tf_op jit(solution)/shard_map/ppermute | solution.py:24
  102.5 8.2 %copy-start.2 = (bf16[128,256]{1,0:T(8,128)(2,1)}, bf16[128,256]{1,0:T(8,128)(2,1)S(1)}, u32[]{:S(2)}) copy-start(bf16[128,256]{1,0:T(8,128)(2,1)S(1)} %collective-permute-done.10.refs_3_) | copy-start | bytes 196612
  104.1 6.5 %copy-start.5 = (bf16[128,256]{1,0:T(8,128)(2,1)}, bf16[128,256]{1,0:T(8,128)(2,1)S(1)}, u32[]{:S(2)}) copy-start(bf16[128,256]{1,0:T(8,128)(2,1)S(1)} %collective-permute-done.9.refs_2_) | copy-start | bytes 196612
  105.0 5.6 %collective-permute-start.11 = (bf16[384,256]{1,0:T(8,128)(2,1)S(1)}, bf16[384,256]{1,0:T(8,128)(2,1)S(1)}, u32[]{:S(2)}, u32[]{:S(2)}) collective-permute-start(bf16[384,256]{1,0:T(8,128)(2,1)S(1)} %pad_maximum_fusion.1), channel_id=1, source_target_pairs={{0,1},{1,0},{2,3},{3,2},{4,5},{5,4},{6,7},{7,6},{8,9},{9,8},{10,11... | collective-permute-start | bytes 589832 | tf_op jit(solution)/shard_map/ppermute | solution.py:30
  118.3 8.6 %collective-permute-start.13 = (bf16[128,256]{1,0:T(8,128)(2,1)}, bf16[128,256]{1,0:T(8,128)(2,1)S(1)}, u32[]{:S(2)}, u32[]{:S(2)}) collective-permute-start(bf16[128,256]{1,0:T(8,128)(2,1)} %get-tuple-element.37.refs_1_), channel_id=1, source_target_pairs={{2,0},{3,1},{4,2},{5,3},{6,4},{7,5},{8,6},{9,7},{10,8},{11,9},{12,... | collective-permute-start | bytes 196616 | tf_op jit(solution)/shard_map/ppermute | solution.py:24
  119.6 9.9 %collective-permute-start.12 = (bf16[128,256]{1,0:T(8,128)(2,1)}, bf16[128,256]{1,0:T(8,128)(2,1)S(1)}, u32[]{:S(2)}, u32[]{:S(2)}) collective-permute-start(bf16[128,256]{1,0:T(8,128)(2,1)} %get-tuple-element.37.refs_1_), channel_id=1, source_target_pairs={{0,2},{1,3},{2,4},{3,5},{4,6},{5,7},{6,8},{7,9},{8,10},{9,11},{10,... | collective-permute-start | bytes 196616 | tf_op jit(solution)/shard_map/ppermute | solution.py:24
  126.9 7.1 %copy-start.4 = (bf16[128,256]{1,0:T(8,128)(2,1)}, bf16[128,256]{1,0:T(8,128)(2,1)S(1)}, u32[]{:S(2)}) copy-start(bf16[128,256]{1,0:T(8,128)(2,1)S(1)} %collective-permute-done.13.refs_3_) | copy-start | bytes 196612
  130.4 34.1 %copy-start.13 = (bf16[2,64,576]{2,1,0:T(8,128)(2,1)S(1)}, bf16[2,64,576]{2,1,0:T(8,128)(2,1)}, u32[]{:S(2)}) copy-start(bf16[2,64,576]{2,1,0:T(8,128)(2,1)} %get-tuple-element.49) | copy-start | bytes 442372
  130.4 3.6 %collective-permute-start.14 = (bf16[384,256]{1,0:T(8,128)(2,1)S(1)}, bf16[384,256]{1,0:T(8,128)(2,1)S(1)}, u32[]{:S(2)}, u32[]{:S(2)}) collective-permute-start(bf16[384,256]{1,0:T(8,128)(2,1)S(1)} %pad_maximum_fusion.2), channel_id=1, source_target_pairs={{0,1},{1,0},{2,3},{3,2},{4,5},{5,4},{6,7},{7,6},{8,9},{9,8},{10,11... | collective-permute-start | bytes 589832 | tf_op jit(solution)/shard_map/ppermute | solution.py:30
  141.7 22.8 %copy-start.14 = (bf16[2,64,576]{2,1,0:T(8,128)(2,1)S(1)}, bf16[2,64,576]{2,1,0:T(8,128)(2,1)}, u32[]{:S(2)}) copy-start(bf16[2,64,576]{2,1,0:T(8,128)(2,1)} %get-tuple-element.48) | copy-start | bytes 442372
  141.7 8.3 %collective-permute-start.16 = (bf16[128,256]{1,0:T(8,128)(2,1)}, bf16[128,256]{1,0:T(8,128)(2,1)S(1)}, u32[]{:S(2)}, u32[]{:S(2)}) collective-permute-start(bf16[128,256]{1,0:T(8,128)(2,1)} %get-tuple-element.42.refs_1_), channel_id=1, source_target_pairs={{2,0},{3,1},{4,2},{5,3},{6,4},{7,5},{8,6},{9,7},{10,8},{11,9},{12,... | collective-permute-start | bytes 196616 | tf_op jit(solution)/shard_map/ppermute | solution.py:24
  143.1 9.5 %collective-permute-start.15 = (bf16[128,256]{1,0:T(8,128)(2,1)}, bf16[128,256]{1,0:T(8,128)(2,1)S(1)}, u32[]{:S(2)}, u32[]{:S(2)}) collective-permute-start(bf16[128,256]{1,0:T(8,128)(2,1)} %get-tuple-element.42.refs_1_), channel_id=1, source_target_pairs={{0,2},{1,3},{2,4},{3,5},{4,6},{5,7},{6,8},{7,9},{8,10},{9,11},{10,... | collective-permute-start | bytes 196616 | tf_op jit(solution)/shard_map/ppermute | solution.py:24
  150.0 6.9 %copy-start.3 = (bf16[128,256]{1,0:T(8,128)(2,1)}, bf16[128,256]{1,0:T(8,128)(2,1)S(1)}, u32[]{:S(2)}) copy-start(bf16[128,256]{1,0:T(8,128)(2,1)S(1)} %collective-permute-done.16.refs_3_) | copy-start | bytes 196612
  153.5 3.4 %collective-permute-start.17 = (bf16[384,256]{1,0:T(8,128)(2,1)S(1)}, bf16[384,256]{1,0:T(8,128)(2,1)S(1)}, u32[]{:S(2)}, u32[]{:S(2)}) collective-permute-start(bf16[384,256]{1,0:T(8,128)(2,1)S(1)} %pad_maximum_fusion.3), channel_id=1, source_target_pairs={{0,1},{1,0},{2,3},{3,2},{4,5},{5,4},{6,7},{7,6},{8,9},{9,8},{10,11... | collective-permute-start | bytes 589832 | tf_op jit(solution)/shard_map/ppermute | solution.py:30
  (8 other events, 12.8 us)

commit v2 on v1

v2 whole, which is shorter than its diff:
```python
import functools
import math

import jax
import jax.numpy as jnp
from jax import lax
from jax.experimental import pallas as pl
from jax.experimental.pallas import tpu as pltpu
from jax.sharding import Mesh, PartitionSpec as P

SKY = ("z", "yh", "core")
QUAD = ("yh", "core")
C = 64
R = 256
TAPS = 9
F32 = jnp.float32
BF16 = jnp.bfloat16
VMEM = pl.BlockSpec(memory_space=pltpu.VMEM)
SMEM = pl.BlockSpec(memory_space=pltpu.SMEM)


def shift(value, by):
    peers = lax.axis_size(SKY)
    return lax.ppermute(value, SKY, [(i, i + by) for i in range(peers) if 0 <= i + by < peers])


def widen(value):
    below = shift(value, 2)
    above = shift(value, -2)
    other = lax.ppermute(jnp.concatenate([value, below, above], axis=0), "core", [(0, 1), (1, 0)])
    return below, above, other


def inner(other, first, even, start, size):
    own = other[start : start + size]
    below = other[first + start : first + start + size]
    above = other[2 * first + start : 2 * first + start + size]
    return jnp.where(even, below, own), jnp.where(even, own, above)


def slope_of(value, sigmoid):
    return sigmoid * (1.0 + value * (1.0 - sigmoid))


def low_onehot(low):
    return (lax.broadcasted_iota(jnp.int32, (R, R), 0) == low).astype(BF16)


def conv(blocks, pos, weight, picked_ref):
    stack = jnp.concatenate(blocks, axis=0)
    for k in range(TAPS):
        if k == 4:
            column = blocks[1]
        else:
            at = pos[k : k + 1]
            block = at >> 8
            found = jnp.dot(stack, low_onehot(at & 255), preferred_element_type=F32)
            column = jnp.where(
                block == 0,
                found[:C],
                jnp.where(block == 1, found[C : 2 * C], jnp.where(block == 2, found[2 * C :], 0.0)),
            ).astype(BF16)
        picked_ref[k * C : (k + 1) * C, :] = column
    return jnp.dot(weight, picked_ref[...], preferred_element_type=F32)


def spread(act, pos, weight, parts):
    terms = lax.dot_general(weight, act, (((0,), (0,)), ((), ())), preferred_element_type=F32)
    total = None
    for k in range(TAPS):
        if k == 4:
            continue
        at = pos[k : k + 1]
        block = at >> 8
        term = terms[k * C : (k + 1) * C].astype(BF16)
        zero = jnp.zeros_like(term)
        sent = jnp.concatenate([jnp.where(block == part, term, zero) for part in parts], axis=0)
        added = lax.dot_general(
            sent, low_onehot(at & 255), (((1,), (1,)), ((), ())), preferred_element_type=F32
        )
        total = added if total is None else total + added
    out = {part: total[i * C : (i + 1) * C] for i, part in enumerate(parts)}
    if 1 in out:
        out[1] = out[1] + terms[4 * C : 5 * C]
    return out


def two_layers(blocks, pos, kept, w_ref, h_ref, picked_ref, slopes_ref, last_ref, scratch):
    middle = []
    for b in (1, 2, 3):
        target = picked_ref.at[0] if b == 2 else scratch.at[b // 2]
        pre = conv(blocks[b - 1 : b + 2], pos[b], w_ref[0], target)
        sigmoid = jax.nn.sigmoid(pre)
        slopes_ref[b - 1] = slope_of(pre, sigmoid)
        middle.append((kept[b] * (blocks[b].astype(F32) + pre * sigmoid)).astype(BF16))
    pre = conv(middle, pos[2], w_ref[1], picked_ref.at[1])
    sigmoid = jax.nn.sigmoid(pre)
    last_ref[...] = slope_of(pre, sigmoid)
    hidden = (kept[2] * (middle[1].astype(F32) + pre * sigmoid)).astype(BF16)
    if h_ref is not None:
        h_ref[...] = hidden
    return hidden


def first_kernel(
    par_ref, x_ref, below_ref, above_ref, other_ref, w_ref,
    h_ref, picked_ref, slopes_ref, last_ref, pos_ref, kept_ref, scratch,
):
    even = par_ref[0] == 0
    size = x_ref.shape[0]
    other = other_ref[...]
    meta_at = size - 16
    meta1, meta3 = inner(other, size, even, meta_at, 16)
    metas = [below_ref[meta_at:, :], meta1, x_ref[meta_at:, :], meta3, above_ref[meta_at:, :]]
    column = lax.broadcasted_iota(jnp.int32, (16, R), 1)
    pos, kept = [], []
    for b, meta in enumerate(metas):
        offset = meta.astype(F32)
        at = jnp.where(offset > 400.0, 768, offset.astype(jnp.int32) + column + R)
        pos_ref[16 * b : 16 * (b + 1), :] = at
        keep = offset[TAPS : TAPS + 1]
        kept_ref[b : b + 1, :] = keep
        pos.append(at)
        kept.append(keep)
    kept_ref[5:8, :] = jnp.zeros((3, R), F32)
    map1, map3 = inner(other, size, even, 0, C)
    blocks = [below_ref[:C, :], map1, x_ref[:C, :], map3, above_ref[:C, :]]
    two_layers(blocks, pos, kept, w_ref, h_ref, picked_ref, slopes_ref, last_ref, scratch)


def read_tables(pos_ref, kept_ref):
    pos = [pos_ref[16 * b : 16 * b + 16, :] for b in range(5)]
    kept = [kept_ref[b : b + 1, :] for b in range(5)]
    return pos, kept


def layers_kernel(
    par_ref, x_ref, below_ref, above_ref, other_ref, w_ref, pos_ref, kept_ref,
    h_ref, picked_ref, slopes_ref, last_ref, scratch,
):
    even = par_ref[0] == 0
    pos, kept = read_tables(pos_ref, kept_ref)
    one, three = inner(other_ref[...], C, even, 0, C)
    blocks = [below_ref[...], one, x_ref[...], three, above_ref[...]]
    two_layers(blocks, pos, kept, w_ref, h_ref, picked_ref, slopes_ref, last_ref, scratch)


def last_layers_kernel(
    par_ref, x_ref, below_ref, above_ref, other_ref, w_ref, pos_ref, kept_ref,
    share_ref, picked_ref, slopes_ref, last_ref, scratch,
):
    even = par_ref[0] == 0
    pos, kept = read_tables(pos_ref, kept_ref)
    one, three = inner(other_ref[...], C, even, 0, C)
    blocks = [below_ref[...], one, x_ref[...], three, above_ref[...]]
    hidden = two_layers(blocks, pos, kept, w_ref, None, picked_ref, slopes_ref, last_ref, scratch)
    for i in range(share_ref.shape[0]):
        share_ref[i] = hidden


def pack_kernel(par_ref, maps_ref, cot_ref, near_ref, foot_ref, pack_ref):
    each = cot_ref.shape[0]
    row = par_ref[1] + lax.broadcasted_iota(jnp.int32, (TAPS, R), 1)
    near = near_ref[...]
    offset = jnp.where(near >= 0, near - row, 512).astype(F32)
    meta = jnp.concatenate(
        [offset, foot_ref[...].astype(F32), jnp.zeros((16 - TAPS - 1, R), F32)], axis=0
    )
    pack_ref[:C, :] = maps_ref[...]
    pack_ref[C : C + each, :] = cot_ref[...]
    pack_ref[C + each :, :] = meta.astype(BF16)


def bundle_kernel(par_ref, x_ref, other_ref, joinw_ref, dec_ref, out_ref):
    even = par_ref[0] == 0
    size = x_ref.shape[0]
    each = size - 16 - C
    one, three = inner(other_ref[...], size, even, C, each)
    for i in range(out_ref.shape[0]):
        out_ref[i, :each, :] = one
        out_ref[i, each : 2 * each, :] = x_ref[C : C + each, :]
        out_ref[i, 2 * each : 3 * each, :] = three
        out_ref[i, 3 * each : 3 * each + C, :] = joinw_ref[...]
        out_ref[i, 3 * each + C :, :] = dec_ref[...]


def unit_kernel(got_ref, pos_ref, unit_ref, join_ref):
    count, size, _ = got_ref.shape
    each = (size - C) // (3 + TAPS)
    pos = [pos_ref[16 * b : 16 * b + 16, :] for b in (1, 2, 3)]

    def rows(start, length):
        return jnp.concatenate([got_ref[d, start : start + length, :] for d in range(count)], axis=0)

    sources = [rows(each * i, each) for i in range(3)]
    unit = None
    for k in range(TAPS):
        if k == 4:
            total = sources[1]
        else:
            total = None
            for i in range(3):
                at = pos[i][k : k + 1]
                sent = jnp.where((at >> 8) == 2 - i, sources[i], jnp.zeros_like(sources[i]))
                added = lax.dot_general(
                    sent, low_onehot(at & 255), (((1,), (1,)), ((), ())), preferred_element_type=F32
                )
                total = added if total is None else total + added
            total = total.astype(BF16)
        dec = rows(3 * each + C + each * k, each)
        added = lax.dot_general(dec, total, (((0,), (0,)), ((), ())), preferred_element_type=F32)
        unit = added if unit is None else unit + added
    unit_ref[...] = unit
    join_ref[...] = jnp.transpose(rows(3 * each, C))


def head_kernel(
    hidden_ref, join_ref, unit_ref, joinw_ref, kept_ref, last_ref, pack_ref, masked_ref
):
    count = hidden_ref.shape[0]
    hidden = jnp.concatenate([hidden_ref[d] for d in range(count)], axis=0)
    joined = jnp.dot(join_ref[...], hidden, preferred_element_type=F32)
    slope = slope_of(joined, jax.nn.sigmoid(joined)).astype(BF16).astype(F32)
    unit_grad = (unit_ref[...] * slope).astype(BF16)
    gradient = jnp.dot(joinw_ref[...], unit_grad, preferred_element_type=F32)
    masked = kept_ref[2:3, :] * gradient
    masked_ref[...] = masked
    pack_ref[:C, :] = (masked * last_ref[...]).astype(BF16)
    pack_ref[C:, :] = masked.astype(BF16)


def weight_grad(act, picked):
    return lax.dot_general(
        act, picked, (((1,), (1,)), ((), ())), preferred_element_type=F32
    ).astype(BF16)


def beside_kernel(has_low, *refs):
    if has_low:
        x_ref, w_ref, pos_ref, picked_ref, low_ref, low_picked_ref, own_ref, grad_ref = refs
        grad_ref[...] = jnp.concatenate(
            [weight_grad(low_ref[C : 2 * C, :], low_picked_ref[0]),
             weight_grad(x_ref[:C, :], picked_ref[1])], axis=1,
        )
    else:
        x_ref, w_ref, pos_ref, picked_ref, own_ref, grad_ref = refs
        grad_ref[...] = weight_grad(x_ref[:C, :], picked_ref[1])
    for part, value in spread(x_ref[:C, :], pos_ref[32:48, :], w_ref[1], (0, 1, 2)).items():
        own_ref[part] = value


def upper_layer(
    par_ref, x_ref, below_ref, above_ref, other_ref, masked_ref, own_ref, w_ref, pos_ref, kept_ref,
    slopes_ref,
):
    even = par_ref[0] == 0
    pos, kept = read_tables(pos_ref, kept_ref)
    other = other_ref[...]
    act1, act3 = inner(other, 2 * C, even, 0, C)
    mask1, mask3 = inner(other, 2 * C, even, C, C)
    acts = [below_ref[:C, :], act1, None, act3, above_ref[:C, :]]
    gradient = [mask1.astype(F32), masked_ref[...], mask3.astype(F32)]
    gradient = [gradient[i] + own_ref[i] for i in range(3)]
    needed = [(2,), (1, 2), (), (0, 1), (0,)]
    for b in (0, 1, 3, 4):
        for part, value in spread(acts[b], pos[b], w_ref[1], needed[b]).items():
            gradient[b + part - 2] = gradient[b + part - 2] + value
    lower = [kept[i + 1] * gradient[i] for i in range(3)]
    low_acts = [(lower[i] * slopes_ref[i]).astype(BF16) for i in range(3)]
    return lower, low_acts


def lower_layer(own, low_acts, pos, weight):
    for i, part in ((0, 2), (1, 1), (2, 0)):
        own = own + spread(low_acts[i], pos[i + 1], weight, (part,))[part]
    return own


def back_kernel(
    par_ref, x_ref, below_ref, above_ref, other_ref, masked_ref, own_ref, w_ref, pos_ref, kept_ref,
    slopes_ref, next_ref, pack_ref, out_ref, low_ref,
):
    lower, low_acts = upper_layer(
        par_ref, x_ref, below_ref, above_ref, other_ref, masked_ref, own_ref, w_ref, pos_ref,
        kept_ref, slopes_ref,
    )
    pos, kept = read_tables(pos_ref, kept_ref)
    out = kept[2] * lower_layer(lower[1], low_acts, pos, w_ref[0])
    out_ref[...] = out
    pack_ref[:C, :] = (out * next_ref[...]).astype(BF16)
    pack_ref[C:, :] = out.astype(BF16)
    for i in range(3):
        low_ref[i * C : (i + 1) * C, :] = low_acts[i]


def last_back_kernel(
    par_ref, x_ref, below_ref, above_ref, other_ref, masked_ref, own_ref, w_ref, pos_ref, kept_ref,
    slopes_ref, picked_ref, grad5_ref, grad43_ref, grad21_ref, low_ref, out_ref, grads_ref,
):
    lower, low_acts = upper_layer(
        par_ref, x_ref, below_ref, above_ref, other_ref, masked_ref, own_ref, w_ref, pos_ref,
        kept_ref, slopes_ref,
    )
    out_ref[...] = lower[1]
    for i in range(3):
        low_ref[i * C : (i + 1) * C, :] = low_acts[i]
    grads_ref[:C, :] = grad43_ref[...]
    grads_ref[C : 2 * C, :] = grad21_ref[...]
    grads_ref[2 * C :, :] = jnp.concatenate(
        [weight_grad(low_acts[1], picked_ref[0]), grad5_ref[...]], axis=1
    )


def map_kernel(low_ref, own_ref, w_ref, pos_ref, map_ref):
    low_acts = [low_ref[i * C : (i + 1) * C, :] for i in range(3)]
    pos = [pos_ref[16 * b : 16 * b + 16, :] for b in range(5)]
    map_ref[...] = lower_layer(own_ref[...], low_acts, pos, w_ref[0]).astype(BF16)


def final_kernel(scale, sum_ref, out_ref):
    wide = TAPS * C
    for row, first, second in ((0, 4, 3), (1, 2, 1), (2, 0, 5)):
        for half, layer in ((0, first), (1, second)):
            for k in range(TAPS):
                at = half * wide + k * C
                out_ref[layer, k] = (
                    sum_ref[row * C : (row + 1) * C, at : at + C].astype(F32) * scale
                )


def sds(shape, dtype):
    return jax.ShapeDtypeStruct(shape, dtype)


def call(body, name, ins, outs, scratch=()):
    specs = [spec for spec, _ in ins]
    return pl.pallas_call(
        body,
        name=name,
        in_specs=specs,
        out_specs=[pl.BlockSpec(memory_space=pltpu.VMEM) for _ in outs],
        out_shape=outs,
        scratch_shapes=list(scratch),
    )(*[value for _, value in ins])


def v(value):
    return (VMEM, value)


def exchange(value, axes):
    return lax.all_to_all(value, axes, 0, 0, tiled=True)


def add_up(parts):
    return jnp.sum(parts.astype(F32), axis=0).astype(BF16)


def copies(value, count):
    return jnp.broadcast_to(value[None], (count,) + value.shape)


def sum_over_sky(value, quads, length):
    rows, lanes = value.shape
    chunk = add_up(exchange(value.reshape(quads, rows // quads, lanes), QUAD))
    tiles = (rows // quads // 8) * (lanes // 128)
    each = -(-tiles // length)
    chunk = chunk.reshape(rows // quads // 8, 8, lanes // 128, 128).transpose(0, 2, 1, 3)
    chunk = jnp.pad(chunk.reshape(tiles, 8, 128), ((0, each * length - tiles), (0, 0), (0, 0)))
    chunk = add_up(exchange(chunk.reshape(length, each, 8, 128), "z"))
    chunk = exchange(copies(chunk, length), "z").reshape(each * length, 8, 128)[:tiles]
    chunk = chunk.reshape(rows // quads // 8, lanes // 128, 8, 128).transpose(0, 2, 1, 3)
    return exchange(copies(chunk.reshape(rows // quads, lanes), quads), QUAD).reshape(rows, lanes)


def per_device(sky_maps, footprint, neighbours, enc_weight, join_weight, dec_weight, cotangent):
    depth = enc_weight.shape[1]
    branches = lax.axis_size("branch")
    peers = lax.axis_size(SKY)
    par = jnp.stack([lax.axis_index("core"), lax.axis_index(SKY) * R]).astype(jnp.int32)
    here = (SMEM, par)
    weights = [
        jnp.transpose(enc_weight[0, i : i + 2], (0, 2, 1, 3)).reshape(2, C, TAPS * C)
        for i in range(0, depth, 2)
    ]
    joinw = join_weight.T
    dec = dec_weight.reshape(-1, dec_weight.shape[2])
    each = cotangent.shape[0]
    full = dec.shape[1]
    half = sds((C, R), BF16)
    whole = sds((C, R), F32)
    pack = call(
        pack_kernel, "pack",
        [here, v(sky_maps[0]), v(cotangent), v(neighbours), v(footprint)],
        [sds((C + each + 16, R), BF16)],
    )[0]
    layer_outs = [half, sds((2, TAPS * C, R), BF16), sds((3, C, R), F32), whole]
    scratch = [pltpu.VMEM((2, TAPS * C, R), BF16)]
    below, above, other = widen(pack)
    hidden, picked, slopes, last, pos, kept = call(
        first_kernel, "layers01",
        [here, v(pack), v(below), v(above), v(other), v(weights[0])],
        layer_outs + [sds((80, R), jnp.int32), sds((8, R), F32)], scratch,
    )
    saved = [(picked, slopes, last)]
    bundle = call(
        bundle_kernel, "bundle", [here, v(pack), v(other), v(joinw), v(dec)],
        [sds((branches, 3 * each + C + dec.shape[0], R), BF16)],
    )[0]
    bundle = exchange(bundle, "branch")
    for group in range(1, depth // 2):
        below, above, other = widen(hidden)
        ins = [here, v(hidden), v(below), v(above), v(other), v(weights[group]), v(pos), v(kept)]
        if group < depth // 2 - 1:
            hidden, picked, slopes, last = call(layers_kernel, "layers", ins, layer_outs, scratch)
        else:
            share, picked, slopes, last = call(
                last_layers_kernel, "lastlayers", ins,
                [sds((branches, C, R), BF16)] + layer_outs[1:], scratch,
            )
        saved.append((picked, slopes, last))
    unit, join = call(
        unit_kernel, "unit", [v(bundle), v(pos)],
        [sds((full, R), F32), sds((full, branches * C), BF16)],
    )
    hiddens = exchange(share, "branch")
    pack, masked = call(
        head_kernel, "head",
        [v(hiddens), v(join), v(unit), v(joinw), v(kept), v(saved[-1][2])],
        [sds((2 * C, R), BF16), whole],
    )
    wide = TAPS * C
    grads = []
    low = None
    for group in reversed(range(depth // 2)):
        below, above, other = widen(pack)
        picked, slopes, _ = saved[group]
        beside = [v(pack), v(weights[group]), v(pos), v(picked)]
        if low is not None:
            beside = beside + [v(low), v(saved[group + 1][0])]
        own, grad = call(
            functools.partial(beside_kernel, low is not None), "beside", beside,
            [sds((3, C, R), F32), sds((C, wide if low is None else 2 * wide), BF16)],
        )
        grads.append(grad)
        ins = [
            here, v(pack), v(below), v(above), v(other), v(masked), v(own), v(weights[group]),
            v(pos), v(kept), v(slopes),
        ]
        if group:
            pack, masked, low = call(
                back_kernel, "back", ins + [v(saved[group - 1][2])],
                [sds((2 * C, R), BF16), whole, sds((3 * C, R), BF16)],
            )
        else:
            low, own, stacked = call(
                last_back_kernel, "lastback", ins + [v(picked)] + [v(g) for g in grads],
                [sds((3 * C, R), BF16), whole, sds((3 * C, 2 * wide), BF16)],
            )
    map_grads = call(
        map_kernel, "mapgrad", [v(low), v(own), v(weights[0]), v(pos)], [half]
    )[0]
    total = sum_over_sky(stacked, lax.axis_size(QUAD), lax.axis_size("z"))
    summed = call(
        functools.partial(final_kernel, 1.0 / math.sqrt(R * peers)), "final", [v(total)],
        [sds((depth, TAPS, C, C), F32)],
    )[0]
    return map_grads[None], summed[None]


def solution(mesh):
    branches, sky = mesh.devices.shape
    mesh = Mesh(mesh.devices.reshape(branches, sky // 4, 2, 2), ("branch",) + SKY)
    in_specs = (
        P("branch", None, SKY),
        P("branch", SKY),
        P(None, SKY),
        P("branch", None, None, None, None),
        P(None, "branch"),
        P(None, "branch", None),
        P("branch", SKY),
    )
    out_specs = (P("branch", None, SKY), P("branch", None, None, None, None))
    return jax.shard_map(
        per_device, mesh=mesh, in_specs=in_specs, out_specs=out_specs, check_vma=False
    )
```

time: 252 us -> 249 us (0.988)
  blocking collectives: 103 us -> 62.6 us
  starting transfers between devices: 71.1 us -> 85.8 us
  waiting for transfers between devices: 15 us -> 29.2 us
  Pallas kernels: 41.2 us -> 52.5 us
    all_to_all x6 -> x3, blocking collectives: 103 us -> 62.6 us  [exchange(): return lax.all_to_all(value, axes, 0, 0, tiled=True)]
    all_to_all x0 -> x3, starting transfers between devices: none -> 17 us  [exchange(): return lax.all_to_all(value, axes, 0, 0, tiled=True)]
    pallas_call x10 -> x15, Pallas kernels: 41.2 us -> 52.5 us  [call(): pl.pallas_call(body, name=name, in_specs=specs, out_specs=[pl.BlockSpec(m...]
    all_to_all x0 -> x3, waiting for transfers between devices: none -> 8.39 us  [exchange(): return lax.all_to_all(value, axes, 0, 0, tiled=True)]
    ppermute x12, waiting for transfers between devices: 11.9 us -> 19.8 us  [shift(): lax.ppermute(value, SKY, [(i, i + by) for i in range(peers) if 0 <= i + b...]
    concatenate x2 -> x0, local copies, waits for them, and re-layouts: 3 us -> none  [the longest x1 1.5 us: widen(): jnp.concatenate([value, below, above], axis=0)]
    unnamed x44 -> x42, local copies, waits for them, and re-layouts: 3.98 us -> 5.4 us
    concatenate x5 -> x6, other arithmetic: 4.18 us -> 5.04 us  [widen(): jnp.concatenate([value, below, above], axis=0)]
  transfers between devices with their start and end apart: 18 -> 21, of which waited for: 11 -> 11; matrix products, arithmetic and copies ran while one was open for 2% -> 2% of each run, Pallas kernels for 1% -> 11%
where the time goes in v2:
time: 249 us; the launch traced here: 247 us
  starting transfers between devices  85.8 us (34%)
  blocking collectives  62.6 us (25%)
  Pallas kernels  52.5 us (21%)
  waiting for transfers between devices  29.2 us (12%)
  local copies, waits for them, and re-layouts  10.5 us (4%)
  other arithmetic  5.73 us (2%)
    all_to_all x3, blocking collectives, exchange(): return lax.all_to_all(value, axes, 0, 0, tiled=True)  62.6 us
    pallas_call x15, Pallas kernels, call(): pl.pallas_call(body, name=name, in_specs=specs, out_specs=[pl.BlockSpec(m...  52.5 us
    ppermute x12, starting transfers between devices, shift(): lax.ppermute(value, SKY, [(i, i + by) for i in range(peers) if 0 <= i + b...  47 us
    ppermute x6, starting transfers between devices, widen(): lax.ppermute(jnp.concatenate([value, below, above], axis=0), 'core', [(0,...  21.8 us
    ppermute x12, waiting for transfers between devices, shift(): lax.ppermute(value, SKY, [(i, i + by) for i in range(peers) if 0 <= i + b...  19.8 us
    all_to_all x3, starting transfers between devices, exchange(): return lax.all_to_all(value, axes, 0, 0, tiled=True)  17 us
    all_to_all x3, waiting for transfers between devices, exchange(): return lax.all_to_all(value, axes, 0, 0, tiled=True)  8.39 us
    unnamed x42, local copies, waits for them, and re-layouts  5.4 us
  transfers between devices with their start and end apart: 21, of which 11 were waited for; matrix products, arithmetic and copies ran while one was open for 2% of the time, Pallas kernels for 11%

profile of v2, /device:TPU:1, one launch (start us, length us, event | category | flops | bytes accessed | tf_op | source)
XLA Modules:
  0.0 247.4 jit_solution(6334425994867124073)
XLA Ops:
  3.9 6.3 %collective-permute-start = (bf16[112,256]{1,0:T(8,128)(2,1)}, bf16[112,256]{1,0:T(8,128)(2,1)S(1)}, u32[]{:S(2)}, u32[]{:S(2)}) collective-permute-start(bf16[112,256]{1,0:T(8,128)(2,1)} %pack.1.x_ref), channel_id=1, source_target_pairs={{0,2},{1,3},{2,4},{3,5},{4,6},{5,7},{6,8},{7,9},{8,10},{9,11},{10,... | collective-permute-start | bytes 172040 | tf_op jit(solution)/shard_map/ppermute | solution.py:24
  13.2 8.6 %collective-permute-start.2 = (bf16[336,256]{1,0:T(8,128)(2,1)S(1)}, bf16[336,256]{1,0:T(8,128)(2,1)S(1)}, u32[]{:S(2)}, u32[]{:S(2)}) collective-permute-start(bf16[336,256]{1,0:T(8,128)(2,1)S(1)} %pad_maximum_fusion.3), channel_id=1, source_target_pairs={{0,1},{1,0},{2,3},{3,2},{4,5},{5,4},{6,7},{7,6},{8,9},{9,8},{10,11... | collective-permute-start | bytes 516104 | tf_op jit(solution)/shard_map/ppermute | solution.py:30
  23.5 2.4 bundle.1
  25.9 3.6 %all-to-all-start.1 = ((bf16[8,448,256]{2,1,0:T(8,128)(2,1)}), bf16[8,448,256]{2,1,0:T(8,128)(2,1)S(1)}, u32[]{:S(2)}, u32[]{:S(2)}) async-start(bf16[8,448,256]{2,1,0:T(8,128)(2,1)} %bundle.1), calls=%async_computation.1 | async-start | bytes 3670016 | tf_op jit(solution)/shard_map/all_to_all | solution.py:352
  31.7 3.8 %layers01.1 = (bf16[64,256]{1,0:T(8,128)(2,1)}, bf16[2,576,256]{2,1,0:T(8,128)(2,1)}, f32[3,64,256]{2,1,0:T(8,128)}, f32[64,256]{1,0:T(8,128)}, s32[80,256]{1,0:T(8,128)}, /*index=5*/f32[8,256]{1,0:T(8,128)}) custom-call(s32[2]{0:T(128)} %pad_add_fusion.par_ref, bf16[112,256]{1,0:T(8,128)(2,1)} %pack.1.x_ref, bf16[112,256]{1,0:T(8,128)(2,1)} %copy-done.11, ...), custom_call_target="tpu_custom_call" | custom-call | tf_op jit(solution)/shard_map/layers01/pallas_call | solution.py:337
  36.8 6.0 %collective-permute-start.3 = (bf16[64,256]{1,0:T(8,128)(2,1)}, bf16[64,256]{1,0:T(8,128)(2,1)S(1)}, u32[]{:S(2)}, u32[]{:S(2)}) collective-permute-start(bf16[64,256]{1,0:T(8,128)(2,1)} %get-tuple-element.35.x_ref), channel_id=1, source_target_pairs={{0,2},{1,3},{2,4},{3,5},{4,6},{5,7},{6,8},{7,9},{8,10},{9,11},{10,... | collective-permute-start | bytes 98312 | tf_op jit(solution)/shard_map/ppermute | solution.py:24
  42.8 8.1 %collective-permute-done.4.above_ref = bf16[64,256]{1,0:T(8,128)(2,1)S(1)} collective-permute-done((bf16[64,256]{1,0:T(8,128)(2,1)}, bf16[64,256]{1,0:T(8,128)(2,1)S(1)}, u32[]{:S(2)}, u32[]{:S(2)}) %collective-permute-start.4) | collective-permute-done | bytes 32800 | tf_op jit(solution)/shard_map/ppermute | solution.py:24
  55.7 3.8 %layers.1 = (bf16[64,256]{1,0:T(8,128)(2,1)}, bf16[2,576,256]{2,1,0:T(8,128)(2,1)}, f32[3,64,256]{2,1,0:T(8,128)}, f32[64,256]{1,0:T(8,128)}) custom-call(s32[2]{0:T(128)} %pad_add_fusion.par_ref, bf16[64,256]{1,0:T(8,128)(2,1)} %get-tuple-element.35.x_ref, bf16[64,256]{1,0:T(8,128)(2,1)} %copy-done.18, bf16[64,256]{1,0:T(8,128)(2,1)} %copy-done.16, ...), custom_call_target="tpu_custom_call" | custom-call | tf_op jit(solution)/shard_map/layers/pallas_call | solution.py:337
  60.8 7.6 %collective-permute-start.6 = (bf16[64,256]{1,0:T(8,128)(2,1)}, bf16[64,256]{1,0:T(8,128)(2,1)S(1)}, u32[]{:S(2)}, u32[]{:S(2)}) collective-permute-start(bf16[64,256]{1,0:T(8,128)(2,1)} %get-tuple-element.38.x_ref), channel_id=1, source_target_pairs={{0,2},{1,3},{2,4},{3,5},{4,6},{5,7},{6,8},{7,9},{8,10},{9,11},{10,... | collective-permute-start | bytes 98312 | tf_op jit(solution)/shard_map/ppermute | solution.py:24
  70.5 3.0 %collective-permute-start.8 = (bf16[192,256]{1,0:T(8,128)(2,1)S(1)}, bf16[192,256]{1,0:T(8,128)(2,1)S(1)}, u32[]{:S(2)}, u32[]{:S(2)}) collective-permute-start(bf16[192,256]{1,0:T(8,128)(2,1)S(1)} %pad_maximum_fusion.5), channel_id=1, source_target_pairs={{0,1},{1,0},{2,3},{3,2},{4,5},{5,4},{6,7},{7,6},{8,9},{9,8},{10,11... | collective-permute-start | bytes 294920 | tf_op jit(solution)/shard_map/ppermute | solution.py:30
  75.2 3.8 %lastlayers.1 = (bf16[8,64,256]{2,1,0:T(8,128)(2,1)}, bf16[2,576,256]{2,1,0:T(8,128)(2,1)}, f32[3,64,256]{2,1,0:T(8,128)}, f32[64,256]{1,0:T(8,128)}) custom-call(s32[2]{0:T(128)} %pad_add_fusion.par_ref, bf16[64,256]{1,0:T(8,128)(2,1)} %get-tuple-element.38.x_ref, bf16[64,256]{1,0:T(8,128)(2,1)} %copy-done.17, bf16[64,256]{1,0:T(8,128)(2,1)} %copy-done.15, ...), custom_call_target="tpu_custom_call" | custom-call | tf_op jit(solution)/shard_map/lastlayers/pallas_call | solution.py:337
  79.1 6.4 %all-to-all-start = ((bf16[8,64,256]{2,1,0:T(8,128)(2,1)}), bf16[8,64,256]{2,1,0:T(8,128)(2,1)S(1)}, u32[]{:S(2)}, u32[]{:S(2)}) async-start(bf16[8,64,256]{2,1,0:T(8,128)(2,1)} %get-tuple-element.39), calls=%async_computation | async-start | bytes 524288 | tf_op jit(solution)/shard_map/all_to_all | solution.py:352
  85.5 4.1 %unit.1 = (f32[256,256]{1,0:T(8,128)}, bf16[256,512]{1,0:T(8,128)(2,1)}) custom-call(bf16[8,448,256]{2,1,0:T(8,128)(2,1)} %copy-done, s32[80,256]{1,0:T(8,128)} %get-tuple-element.36.pos_ref.refs_2_), custom_call_target="tpu_custom_call" | custom-call | tf_op jit(solution)/shard_map/unit/pallas_call | solution.py:337
  89.6 3.3 %all-to-all-done.hidden_ref = bf16[8,64,256]{2,1,0:T(8,128)(2,1)S(1)} async-done(((bf16[8,64,256]{2,1,0:T(8,128)(2,1)}), bf16[8,64,256]{2,1,0:T(8,128)(2,1)S(1)}, u32[]{:S(2)}, u32[]{:S(2)}) %all-to-all-start) | async-done | bytes 262176 | tf_op jit(solution)/shard_map/all_to_all | solution.py:352
  97.1 6.6 %collective-permute-start.9 = (bf16[128,256]{1,0:T(8,128)(2,1)}, bf16[128,256]{1,0:T(8,128)(2,1)S(1)}, u32[]{:S(2)}, u32[]{:S(2)}) collective-permute-start(bf16[128,256]{1,0:T(8,128)(2,1)} %get-tuple-element.43.refs_0_.x_ref), channel_id=1, source_target_pairs={{0,2},{1,3},{2,4},{3,5},{4,6},{5,7},{6,8},{7,9},{8,10},{9,11},{10,... | collective-permute-start | bytes 196616 | tf_op jit(solution)/shard_map/ppermute | solution.py:24
  106.8 3.2 %collective-permute-start.11 = (bf16[384,256]{1,0:T(8,128)(2,1)S(1)}, bf16[384,256]{1,0:T(8,128)(2,1)S(1)}, u32[]{:S(2)}, u32[]{:S(2)}) collective-permute-start(bf16[384,256]{1,0:T(8,128)(2,1)S(1)} %pad_maximum_fusion), channel_id=1, source_target_pairs={{0,1},{1,0},{2,3},{3,2},{4,5},{5,4},{6,7},{7,6},{8,9},{9,8},{10,11... | collective-permute-start | bytes 589832 | tf_op jit(solution)/shard_map/ppermute | solution.py:30
  110.0 2.8 %beside.3 = (f32[3,64,256]{2,1,0:T(8,128)}, bf16[64,576]{1,0:T(8,128)(2,1)}) custom-call(bf16[128,256]{1,0:T(8,128)(2,1)} %get-tuple-element.43.refs_0_.x_ref, bf16[2,64,576]{2,1,0:T(8,128)(2,1)} %copy.30.w_ref.refs_1_, s32[80,256]{1,0:T(8,128)} %get-tuple-element.36.pos_ref.refs_2_, bf16[2,576,256]{2,1,0:T(8,128)(2,1)} %get-tuple-element.45.refs_3_.refs_5_), custom_call_target="tpu_custom_call" | custom-call | tf_op jit(solution)/shard_map/beside/pallas_call | solution.py:337
  113.4 5.9 %back.2 = (bf16[128,256]{1,0:T(8,128)(2,1)}, f32[64,256]{1,0:T(8,128)}, bf16[192,256]{1,0:T(8,128)(2,1)}) custom-call(s32[2]{0:T(128)} %pad_add_fusion.par_ref, bf16[128,256]{1,0:T(8,128)(2,1)} %get-tuple-element.43.refs_0_.x_ref, bf16[128,256]{1,0:T(8,128)(2,1)} %copy-done.9, bf16[128,256]{1,0:T(8,128)(2,1)} %copy-done.7, bf16[384,256]{1,0:T(8,128)(2,1)} %copy-done.14, ...), custom_call_target="tpu_custom_call" | custom-call | tf_op jit(solution)/shard_map/back/pallas_call | solution.py:337
  120.6 6.7 %collective-permute-start.12 = (bf16[128,256]{1,0:T(8,128)(2,1)}, bf16[128,256]{1,0:T(8,128)(2,1)S(1)}, u32[]{:S(2)}, u32[]{:S(2)}) collective-permute-start(bf16[128,256]{1,0:T(8,128)(2,1)} %get-tuple-element.49.refs_0_.x_ref), channel_id=1, source_target_pairs={{0,2},{1,3},{2,4},{3,5},{4,6},{5,7},{6,8},{7,9},{8,10},{9,11},{10,... | collective-permute-start | bytes 196616 | tf_op jit(solution)/shard_map/ppermute | solution.py:24
  133.5 3.1 %beside.4 = (f32[3,64,256]{2,1,0:T(8,128)}, bf16[64,1152]{1,0:T(8,128)(2,1)}) custom-call(bf16[128,256]{1,0:T(8,128)(2,1)} %get-tuple-element.49.refs_0_.x_ref, bf16[2,64,576]{2,1,0:T(8,128)(2,1)} %copy.28.w_ref.refs_1_, s32[80,256]{1,0:T(8,128)} %get-tuple-element.36.pos_ref.refs_2_, bf16[2,576,256]{2,1,0:T(8,128)(2,1)} %get-tuple-element.51.refs_3_.refs_5_, ...), custom_call_target="tpu_custom_call" | custom-call | tf_op jit(solution)/shard_map/beside/pallas_call | solution.py:337
  137.3 5.9 %back.3 = (bf16[128,256]{1,0:T(8,128)(2,1)}, f32[64,256]{1,0:T(8,128)}, bf16[192,256]{1,0:T(8,128)(2,1)}) custom-call(s32[2]{0:T(128)} %pad_add_fusion.par_ref, bf16[128,256]{1,0:T(8,128)(2,1)} %get-tuple-element.49.refs_0_.x_ref, bf16[128,256]{1,0:T(8,128)(2,1)} %copy-done.8, bf16[128,256]{1,0:T(8,128)(2,1)} %copy-done.6, bf16[384,256]{1,0:T(8,128)(2,1)} %copy-done.13, ...), custom_call_target="tpu_custom_call" | custom-call | tf_op jit(solution)/shard_map/back/pallas_call | solution.py:337
  144.5 6.1 %collective-permute-start.15 = (bf16[128,256]{1,0:T(8,128)(2,1)}, bf16[128,256]{1,0:T(8,128)(2,1)S(1)}, u32[]{:S(2)}, u32[]{:S(2)}) collective-permute-start(bf16[128,256]{1,0:T(8,128)(2,1)} %get-tuple-element.56.refs_0_.x_ref), channel_id=1, source_target_pairs={{0,2},{1,3},{2,4},{3,5},{4,6},{5,7},{6,8},{7,9},{8,10},{9,11},{10,... | collective-permute-start | bytes 196616 | tf_op jit(solution)/shard_map/ppermute | solution.py:24
  151.4 2.4 collective-permute-done.15.below_ref
  157.0 3.1 %beside.5 = (f32[3,64,256]{2,1,0:T(8,128)}, bf16[64,1152]{1,0:T(8,128)(2,1)}) custom-call(bf16[128,256]{1,0:T(8,128)(2,1)} %get-tuple-element.56.refs_0_.x_ref, bf16[2,64,576]{2,1,0:T(8,128)(2,1)} %copy.26.w_ref.refs_1_, s32[80,256]{1,0:T(8,128)} %get-tuple-element.36.pos_ref.refs_2_, bf16[2,576,256]{2,1,0:T(8,128)(2,1)} %get-tuple-element.58.refs_3_.picked_ref, ...), custom_call_target="tpu_custom_call" | custom-call | tf_op jit(solution)/shard_map/beside/pallas_call | solution.py:337
  160.8 4.1 %lastback.1 = (bf16[192,256]{1,0:T(8,128)(2,1)}, f32[64,256]{1,0:T(8,128)}, bf16[192,1152]{1,0:T(8,128)(2,1)}) custom-call(s32[2]{0:T(128)} %pad_add_fusion.par_ref, bf16[128,256]{1,0:T(8,128)(2,1)} %get-tuple-element.56.refs_0_.x_ref, bf16[128,256]{1,0:T(8,128)(2,1)} %copy-done.5, bf16[128,256]{1,0:T(8,128)(2,1)} %copy-done.4, bf16[384,256]{1,0:T(8,128)(2,1)} %copy-done.12, ...), custom_call_target="tpu_custom_call" | custom-call | tf_op jit(solution)/shard_map/lastback/pallas_call | solution.py:337
  164.9 14.1 %all_to_all.30 = bf16[4,48,1152]{2,1,0:T(8,128)(2,1)S(1)} all-to-all(bf16[4,48,1152]{2,1,0:T(8,128)(2,1)} %bitcast.43), channel_id=1, replica_groups=mesh['branch'=8,'z'=16,'yh'=2,'core'=2] {'yh','core'}, dimensions={0} | all-to-all | bytes 884736 | tf_op jit(solution)/shard_map/all_to_all | solution.py:352
  179.1 30.8 %all_to_all.31 = bf16[16,4,8,128]{3,2,1,0:T(8,128)(2,1)S(1)} all-to-all(bf16[16,4,8,128]{3,2,1,0:T(8,128)(2,1)S(1)} %bitcast.41), channel_id=1, replica_groups=mesh['branch'=8,'z'=16,'yh'=2,'core'=2] {'z'}, dimensions={0} | all-to-all | bytes 262144 | tf_op jit(solution)/shard_map/all_to_all | solution.py:352
  209.9 17.7 %all_to_all.32 = bf16[16,4,8,128]{3,2,1,0:T(8,128)(2,1)S(1)} all-to-all(bf16[16,4,8,128]{3,2,1,0:T(8,128)(2,1)S(1)} %broadcast_in_dim.20), channel_id=1, replica_groups=mesh['branch'=8,'z'=16,'yh'=2,'core'=2] {'z'}, dimensions={0} | all-to-all | bytes 262144 | tf_op jit(solution)/shard_map/all_to_all | solution.py:352
  228.4 7.0 %all-to-all-start.5 = ((bf16[4,48,1152]{2,1,0:T(8,128)(2,1)}), bf16[4,48,1152]{2,1,0:T(8,128)(2,1)S(1)}, u32[]{:S(2)}, u32[]{:S(2)}) async-start(bf16[4,48,1152]{2,1,0:T(8,128)(2,1)} %broadcast_in_dim.22), calls=%async_computation.5 | async-start | bytes 884736 | tf_op jit(solution)/shard_map/all_to_all | solution.py:352
  235.5 3.5 %mapgrad.1 = bf16[64,256]{1,0:T(8,128)(2,1)} custom-call(bf16[192,256]{1,0:T(8,128)(2,1)} %get-tuple-element.65.low_ref, f32[64,256]{1,0:T(8,128)} %get-tuple-element.66.own_ref, bf16[2,64,576]{2,1,0:T(8,128)(2,1)} %copy.26.w_ref.refs_1_, s32[80,256]{1,0:T(8,128)} %get-tuple-element.36.pos_ref.refs_2_), custom_call_target="tpu_custom_call" | custom-call | tf_op jit(solution)/shard_map/mapgrad/pallas_call | solution.py:337
  239.0 5.1 %all-to-all-done.5 = bf16[4,48,1152]{2,1,0:T(8,128)(2,1)S(1)} async-done(((bf16[4,48,1152]{2,1,0:T(8,128)(2,1)}), bf16[4,48,1152]{2,1,0:T(8,128)(2,1)S(1)}, u32[]{:S(2)}, u32[]{:S(2)}) %all-to-all-start.5) | async-done | bytes 442400 | tf_op jit(solution)/shard_map/all_to_all | solution.py:352
  244.9 2.5 %final.1 = f32[6,9,64,64]{3,2,1,0:T(8,128)} custom-call(bf16[192,1152]{1,0:T(8,128)(2,1)} %bitcast.37), custom_call_target="tpu_custom_call" | custom-call | tf_op jit(solution)/shard_map/final/pallas_call | solution.py:337
  (90 shorter events, 44.9 us)
Async XLA Ops:
  2.7 7.6 %collective-permute-start.1 = (bf16[112,256]{1,0:T(8,128)(2,1)}, bf16[112,256]{1,0:T(8,128)(2,1)S(1)}, u32[]{:S(2)}, u32[]{:S(2)}) collective-permute-start(bf16[112,256]{1,0:T(8,128)(2,1)} %pack.1.x_ref), channel_id=1, source_target_pairs={{2,0},{3,1},{4,2},{5,3},{6,4},{7,5},{8,6},{9,7},{10,8},{11,9},{12,... | collective-permute-start | bytes 172040 | tf_op jit(solution)/shard_map/ppermute | solution.py:24
  3.9 8.4 %collective-permute-start = (bf16[112,256]{1,0:T(8,128)(2,1)}, bf16[112,256]{1,0:T(8,128)(2,1)S(1)}, u32[]{:S(2)}, u32[]{:S(2)}) collective-permute-start(bf16[112,256]{1,0:T(8,128)(2,1)} %pack.1.x_ref), channel_id=1, source_target_pairs={{0,2},{1,3},{2,4},{3,5},{4,6},{5,7},{6,8},{7,9},{8,10},{9,11},{10,... | collective-permute-start | bytes 172040 | tf_op jit(solution)/shard_map/ppermute | solution.py:24
  10.2 15.7 %copy-start.10 = (bf16[112,256]{1,0:T(8,128)(2,1)}, bf16[112,256]{1,0:T(8,128)(2,1)S(1)}, u32[]{:S(2)}) copy-start(bf16[112,256]{1,0:T(8,128)(2,1)S(1)} %collective-permute-done.1.above_ref) | copy-start | bytes 172036
  12.3 13.6 %copy-start.11 = (bf16[112,256]{1,0:T(8,128)(2,1)}, bf16[112,256]{1,0:T(8,128)(2,1)S(1)}, u32[]{:S(2)}) copy-start(bf16[112,256]{1,0:T(8,128)(2,1)S(1)} %collective-permute-done.below_ref) | copy-start | bytes 172036
  13.2 9.6 %collective-permute-start.2 = (bf16[336,256]{1,0:T(8,128)(2,1)S(1)}, bf16[336,256]{1,0:T(8,128)(2,1)S(1)}, u32[]{:S(2)}, u32[]{:S(2)}) collective-permute-start(bf16[336,256]{1,0:T(8,128)(2,1)S(1)} %pad_maximum_fusion.3), channel_id=1, source_target_pairs={{0,1},{1,0},{2,3},{3,2},{4,5},{5,4},{6,7},{7,6},{8,9},{9,8},{10,11... | collective-permute-start | bytes 516104 | tf_op jit(solution)/shard_map/ppermute | solution.py:30
  25.9 53.1 %all-to-all-start.1 = ((bf16[8,448,256]{2,1,0:T(8,128)(2,1)}), bf16[8,448,256]{2,1,0:T(8,128)(2,1)S(1)}, u32[]{:S(2)}, u32[]{:S(2)}) async-start(bf16[8,448,256]{2,1,0:T(8,128)(2,1)} %bundle.1), calls=%async_computation.1 | async-start | bytes 3670016 | tf_op jit(solution)/shard_map/all_to_all | solution.py:352
  35.5 15.4 %collective-permute-start.4 = (bf16[64,256]{1,0:T(8,128)(2,1)}, bf16[64,256]{1,0:T(8,128)(2,1)S(1)}, u32[]{:S(2)}, u32[]{:S(2)}) collective-permute-start(bf16[64,256]{1,0:T(8,128)(2,1)} %get-tuple-element.35.x_ref), channel_id=1, source_target_pairs={{2,0},{3,1},{4,2},{5,3},{6,4},{7,5},{8,6},{9,7},{10,8},{11,9},{12,... | collective-permute-start | bytes 98312 | tf_op jit(solution)/shard_map/ppermute | solution.py:24
  36.8 14.1 %collective-permute-start.3 = (bf16[64,256]{1,0:T(8,128)(2,1)}, bf16[64,256]{1,0:T(8,128)(2,1)S(1)}, u32[]{:S(2)}, u32[]{:S(2)}) collective-permute-start(bf16[64,256]{1,0:T(8,128)(2,1)} %get-tuple-element.35.x_ref), channel_id=1, source_target_pairs={{0,2},{1,3},{2,4},{3,5},{4,6},{5,7},{6,8},{7,9},{8,10},{9,11},{10,... | collective-permute-start | bytes 98312 | tf_op jit(solution)/shard_map/ppermute | solution.py:24
  51.7 3.4 %collective-permute-start.5 = (bf16[192,256]{1,0:T(8,128)(2,1)S(1)}, bf16[192,256]{1,0:T(8,128)(2,1)S(1)}, u32[]{:S(2)}, u32[]{:S(2)}) collective-permute-start(bf16[192,256]{1,0:T(8,128)(2,1)S(1)} %pad_maximum_fusion.4), channel_id=1, source_target_pairs={{0,1},{1,0},{2,3},{3,2},{4,5},{5,4},{6,7},{7,6},{8,9},{9,8},{10,11... | collective-permute-start | bytes 294920 | tf_op jit(solution)/shard_map/ppermute | solution.py:30
  59.5 8.9 %collective-permute-start.7 = (bf16[64,256]{1,0:T(8,128)(2,1)}, bf16[64,256]{1,0:T(8,128)(2,1)S(1)}, u32[]{:S(2)}, u32[]{:S(2)}) collective-permute-start(bf16[64,256]{1,0:T(8,128)(2,1)} %get-tuple-element.38.x_ref), channel_id=1, source_target_pairs={{2,0},{3,1},{4,2},{5,3},{6,4},{7,5},{8,6},{9,7},{10,8},{11,9},{12,... | collective-permute-start | bytes 98312 | tf_op jit(solution)/shard_map/ppermute | solution.py:24
  60.8 9.0 %collective-permute-start.6 = (bf16[64,256]{1,0:T(8,128)(2,1)}, bf16[64,256]{1,0:T(8,128)(2,1)S(1)}, u32[]{:S(2)}, u32[]{:S(2)}) collective-permute-start(bf16[64,256]{1,0:T(8,128)(2,1)} %get-tuple-element.38.x_ref), channel_id=1, source_target_pairs={{0,2},{1,3},{2,4},{3,5},{4,6},{5,7},{6,8},{7,9},{8,10},{9,11},{10,... | collective-permute-start | bytes 98312 | tf_op jit(solution)/shard_map/ppermute | solution.py:24
  68.4 6.2 %copy-start.15 = (bf16[64,256]{1,0:T(8,128)(2,1)}, bf16[64,256]{1,0:T(8,128)(2,1)S(1)}, u32[]{:S(2)}) copy-start(bf16[64,256]{1,0:T(8,128)(2,1)S(1)} %collective-permute-done.7.above_ref) | copy-start | bytes 98308
  69.7 4.9 %copy-start.17 = (bf16[64,256]{1,0:T(8,128)(2,1)}, bf16[64,256]{1,0:T(8,128)(2,1)S(1)}, u32[]{:S(2)}) copy-start(bf16[64,256]{1,0:T(8,128)(2,1)S(1)} %collective-permute-done.6.below_ref) | copy-start | bytes 98308
  70.5 4.1 %collective-permute-start.8 = (bf16[192,256]{1,0:T(8,128)(2,1)S(1)}, bf16[192,256]{1,0:T(8,128)(2,1)S(1)}, u32[]{:S(2)}, u32[]{:S(2)}) collective-permute-start(bf16[192,256]{1,0:T(8,128)(2,1)S(1)} %pad_maximum_fusion.5), channel_id=1, source_target_pairs={{0,1},{1,0},{2,3},{3,2},{4,5},{5,4},{6,7},{7,6},{8,9},{9,8},{10,11... | collective-permute-start | bytes 294920 | tf_op jit(solution)/shard_map/ppermute | solution.py:30
  79.1 6.4 %copy-start = (bf16[8,448,256]{2,1,0:T(8,128)(2,1)}, bf16[8,448,256]{2,1,0:T(8,128)(2,1)S(1)}, u32[]{:S(2)}) copy-start(bf16[8,448,256]{2,1,0:T(8,128)(2,1)S(1)} %all-to-all-done.1.got_ref) | copy-start | bytes 5505028
  79.1 13.8 %all-to-all-start = ((bf16[8,64,256]{2,1,0:T(8,128)(2,1)}), bf16[8,64,256]{2,1,0:T(8,128)(2,1)S(1)}, u32[]{:S(2)}, u32[]{:S(2)}) async-start(bf16[8,64,256]{2,1,0:T(8,128)(2,1)} %get-tuple-element.39), calls=%async_computation | async-start | bytes 524288 | tf_op jit(solution)/shard_map/all_to_all | solution.py:352
  95.8 7.9 %collective-permute-start.10 = (bf16[128,256]{1,0:T(8,128)(2,1)}, bf16[128,256]{1,0:T(8,128)(2,1)S(1)}, u32[]{:S(2)}, u32[]{:S(2)}) collective-permute-start(bf16[128,256]{1,0:T(8,128)(2,1)} %get-tuple-element.43.refs_0_.x_ref), channel_id=1, source_target_pairs={{2,0},{3,1},{4,2},{5,3},{6,4},{7,5},{8,6},{9,7},{10,8},{11,9},{12,... | collective-permute-start | bytes 196616 | tf_op jit(solution)/shard_map/ppermute | solution.py:24
  97.1 8.8 %collective-permute-start.9 = (bf16[128,256]{1,0:T(8,128)(2,1)}, bf16[128,256]{1,0:T(8,128)(2,1)S(1)}, u32[]{:S(2)}, u32[]{:S(2)}) collective-permute-start(bf16[128,256]{1,0:T(8,128)(2,1)} %get-tuple-element.43.refs_0_.x_ref), channel_id=1, source_target_pairs={{0,2},{1,3},{2,4},{3,5},{4,6},{5,7},{6,8},{7,9},{8,10},{9,11},{10,... | collective-permute-start | bytes 196616 | tf_op jit(solution)/shard_map/ppermute | solution.py:24
  103.7 9.0 %copy-start.7 = (bf16[128,256]{1,0:T(8,128)(2,1)}, bf16[128,256]{1,0:T(8,128)(2,1)S(1)}, u32[]{:S(2)}) copy-start(bf16[128,256]{1,0:T(8,128)(2,1)S(1)} %collective-permute-done.10.above_ref) | copy-start | bytes 196612
  105.9 6.8 %copy-start.9 = (bf16[128,256]{1,0:T(8,128)(2,1)}, bf16[128,256]{1,0:T(8,128)(2,1)S(1)}, u32[]{:S(2)}) copy-start(bf16[128,256]{1,0:T(8,128)(2,1)S(1)} %collective-permute-done.9.below_ref) | copy-start | bytes 196612
  106.8 5.9 %collective-permute-start.11 = (bf16[384,256]{1,0:T(8,128)(2,1)S(1)}, bf16[384,256]{1,0:T(8,128)(2,1)S(1)}, u32[]{:S(2)}, u32[]{:S(2)}) collective-permute-start(bf16[384,256]{1,0:T(8,128)(2,1)S(1)} %pad_maximum_fusion), channel_id=1, source_target_pairs={{0,1},{1,0},{2,3},{3,2},{4,5},{5,4},{6,7},{7,6},{8,9},{9,8},{10,11... | collective-permute-start | bytes 589832 | tf_op jit(solution)/shard_map/ppermute | solution.py:30
  119.3 8.7 %collective-permute-start.13 = (bf16[128,256]{1,0:T(8,128)(2,1)}, bf16[128,256]{1,0:T(8,128)(2,1)S(1)}, u32[]{:S(2)}, u32[]{:S(2)}) collective-permute-start(bf16[128,256]{1,0:T(8,128)(2,1)} %get-tuple-element.49.refs_0_.x_ref), channel_id=1, source_target_pairs={{2,0},{3,1},{4,2},{5,3},{6,4},{7,5},{8,6},{9,7},{10,8},{11,9},{12,... | collective-permute-start | bytes 196616 | tf_op jit(solution)/shard_map/ppermute | solution.py:24
  120.6 9.7 %collective-permute-start.12 = (bf16[128,256]{1,0:T(8,128)(2,1)}, bf16[128,256]{1,0:T(8,128)(2,1)S(1)}, u32[]{:S(2)}, u32[]{:S(2)}) collective-permute-start(bf16[128,256]{1,0:T(8,128)(2,1)} %get-tuple-element.49.refs_0_.x_ref), channel_id=1, source_target_pairs={{0,2},{1,3},{2,4},{3,5},{4,6},{5,7},{6,8},{7,9},{8,10},{9,11},{10,... | collective-permute-start | bytes 196616 | tf_op jit(solution)/shard_map/ppermute | solution.py:24
  128.0 8.7 %copy-start.6 = (bf16[128,256]{1,0:T(8,128)(2,1)}, bf16[128,256]{1,0:T(8,128)(2,1)S(1)}, u32[]{:S(2)}) copy-start(bf16[128,256]{1,0:T(8,128)(2,1)S(1)} %collective-permute-done.13.above_ref) | copy-start | bytes 196612
  130.3 6.4 %copy-start.8 = (bf16[128,256]{1,0:T(8,128)(2,1)}, bf16[128,256]{1,0:T(8,128)(2,1)S(1)}, u32[]{:S(2)}) copy-start(bf16[128,256]{1,0:T(8,128)(2,1)S(1)} %collective-permute-done.12.below_ref) | copy-start | bytes 196612
  131.2 5.5 %collective-permute-start.14 = (bf16[384,256]{1,0:T(8,128)(2,1)S(1)}, bf16[384,256]{1,0:T(8,128)(2,1)S(1)}, u32[]{:S(2)}, u32[]{:S(2)}) collective-permute-start(bf16[384,256]{1,0:T(8,128)(2,1)S(1)} %pad_maximum_fusion.1), channel_id=1, source_target_pairs={{0,1},{1,0},{2,3},{3,2},{4,5},{5,4},{6,7},{7,6},{8,9},{9,8},{10,11... | collective-permute-start | bytes 589832 | tf_op jit(solution)/shard_map/ppermute | solution.py:30
  143.3 8.1 %collective-permute-start.16 = (bf16[128,256]{1,0:T(8,128)(2,1)}, bf16[128,256]{1,0:T(8,128)(2,1)S(1)}, u32[]{:S(2)}, u32[]{:S(2)}) collective-permute-start(bf16[128,256]{1,0:T(8,128)(2,1)} %get-tuple-element.56.refs_0_.x_ref), channel_id=1, source_target_pairs={{2,0},{3,1},{4,2},{5,3},{6,4},{7,5},{8,6},{9,7},{10,8},{11,9},{12,... | collective-permute-start | bytes 196616 | tf_op jit(solution)/shard_map/ppermute | solution.py:24
  144.5 9.2 %collective-permute-start.15 = (bf16[128,256]{1,0:T(8,128)(2,1)}, bf16[128,256]{1,0:T(8,128)(2,1)S(1)}, u32[]{:S(2)}, u32[]{:S(2)}) collective-permute-start(bf16[128,256]{1,0:T(8,128)(2,1)} %get-tuple-element.56.refs_0_.x_ref), channel_id=1, source_target_pairs={{0,2},{1,3},{2,4},{3,5},{4,6},{5,7},{6,8},{7,9},{8,10},{9,11},{10,... | collective-permute-start | bytes 196616 | tf_op jit(solution)/shard_map/ppermute | solution.py:24
  151.3 8.8 %copy-start.4 = (bf16[128,256]{1,0:T(8,128)(2,1)}, bf16[128,256]{1,0:T(8,128)(2,1)S(1)}, u32[]{:S(2)}) copy-start(bf16[128,256]{1,0:T(8,128)(2,1)S(1)} %collective-permute-done.16.above_ref) | copy-start | bytes 196612
  153.7 6.4 %copy-start.5 = (bf16[128,256]{1,0:T(8,128)(2,1)}, bf16[128,256]{1,0:T(8,128)(2,1)S(1)}, u32[]{:S(2)}) copy-start(bf16[128,256]{1,0:T(8,128)(2,1)S(1)} %collective-permute-done.15.below_ref) | copy-start | bytes 196612
  154.6 5.5 %collective-permute-start.17 = (bf16[384,256]{1,0:T(8,128)(2,1)S(1)}, bf16[384,256]{1,0:T(8,128)(2,1)S(1)}, u32[]{:S(2)}, u32[]{:S(2)}) collective-permute-start(bf16[384,256]{1,0:T(8,128)(2,1)S(1)} %pad_maximum_fusion.2), channel_id=1, source_target_pairs={{0,1},{1,0},{2,3},{3,2},{4,5},{5,4},{6,7},{7,6},{8,9},{9,8},{10,11... | collective-permute-start | bytes 589832 | tf_op jit(solution)/shard_map/ppermute | solution.py:30
  228.4 15.6 %all-to-all-start.5 = ((bf16[4,48,1152]{2,1,0:T(8,128)(2,1)}), bf16[4,48,1152]{2,1,0:T(8,128)(2,1)S(1)}, u32[]{:S(2)}, u32[]{:S(2)}) async-start(bf16[4,48,1152]{2,1,0:T(8,128)(2,1)} %broadcast_in_dim.22), calls=%async_computation.5 | async-start | bytes 884736 | tf_op jit(solution)/shard_map/all_to_all | solution.py:352
  (10 other events, 13.8 us)

commit v3 on v2

--- a/solution.py
+++ b/solution.py
@@ -13,10 +13,12 @@
 C = 64
 R = 256
 TAPS = 9
+LIMIT = 16 * 1024 * 1024
 F32 = jnp.float32
 BF16 = jnp.bfloat16
 VMEM = pl.BlockSpec(memory_space=pltpu.VMEM)
 SMEM = pl.BlockSpec(memory_space=pltpu.SMEM)
+HBM = pl.BlockSpec(memory_space=pltpu.HBM)
 
 
 def shift(value, by):
@@ -24,11 +26,32 @@
     return lax.ppermute(value, SKY, [(i, i + by) for i in range(peers) if 0 <= i + by < peers])
 
 
-def widen(value):
+def widen(value, after=()):
     below = shift(value, 2)
     above = shift(value, -2)
-    other = lax.ppermute(jnp.concatenate([value, below, above], axis=0), "core", [(0, 1), (1, 0)])
+    rows = value.shape[0]
+    stacked = call(
+        stack_kernel, "stack",
+        [v(value), v(below), v(above)] + [(pl.BlockSpec(memory_space=pl.ANY), x) for x in after],
+        [sds((3 * rows, R), BF16)],
+    )[0]
+    other = lax.ppermute(stacked, "core", [(0, 1), (1, 0)])
     return below, above, other
+
+
+def stack_kernel(*refs):
+    out_ref = refs[-1]
+    rows = refs[0].shape[0]
+    for i in range(3):
+        out_ref[i * rows : (i + 1) * rows, :] = refs[i][...]
+
+
+def fetch(pairs, sems):
+    copies = [pltpu.make_async_copy(src, dst, sems.at[i]) for i, (src, dst) in enumerate(pairs)]
+    for copy in copies:
+        copy.start()
+    for copy in copies:
+        copy.wait()
 
 
 def inner(other, first, even, start, size):
@@ -158,20 +181,36 @@
         share_ref[i] = hidden
 
 
-def pack_kernel(par_ref, maps_ref, cot_ref, near_ref, foot_ref, pack_ref):
-    each = cot_ref.shape[0]
+def pack_kernel(
+    par_ref, maps_hbm, cot_hbm, near_hbm, foot_hbm, pack_ref, near_ref, foot_ref, sems
+):
+    each = cot_hbm.shape[0]
+    fetch(
+        [(near_hbm, near_ref), (foot_hbm, foot_ref), (maps_hbm, pack_ref.at[pl.ds(0, C)]),
+         (cot_hbm, pack_ref.at[pl.ds(C, each)])], sems,
+    )
     row = par_ref[1] + lax.broadcasted_iota(jnp.int32, (TAPS, R), 1)
     near = near_ref[...]
     offset = jnp.where(near >= 0, near - row, 512).astype(F32)
     meta = jnp.concatenate(
         [offset, foot_ref[...].astype(F32), jnp.zeros((16 - TAPS - 1, R), F32)], axis=0
     )
-    pack_ref[:C, :] = maps_ref[...]
-    pack_ref[C : C + each, :] = cot_ref[...]
     pack_ref[C + each :, :] = meta.astype(BF16)
 
 
-def bundle_kernel(par_ref, x_ref, other_ref, joinw_ref, dec_ref, out_ref):
+def weights_kernel(w_hbm, *refs):
+    outs, w_ref, sems = refs[:-2], refs[-2], refs[-1]
+    fetch([(w_hbm, w_ref)], sems)
+    for group, out_ref in enumerate(outs):
+        for i in range(2):
+            layer = 2 * group + i
+            out_ref[i] = jnp.concatenate([w_ref[layer, k] for k in range(TAPS)], axis=1)
+
+
+def bundle_kernel(
+    par_ref, x_ref, other_ref, joinw_hbm, dec_hbm, _, out_ref, joinw_ref, dec_ref, sems
+):
+    fetch([(joinw_hbm, joinw_ref), (dec_hbm, dec_ref)], sems)
     even = par_ref[0] == 0
     size = x_ref.shape[0]
     each = size - 16 - C
@@ -332,7 +371,7 @@
     return jax.ShapeDtypeStruct(shape, dtype)
 
 
-def call(body, name, ins, outs, scratch=()):
+def call(body, name, ins, outs, scratch=(), limit=LIMIT):
     specs = [spec for spec, _ in ins]
     return pl.pallas_call(
         body,
@@ -341,6 +380,7 @@
         out_specs=[pl.BlockSpec(memory_space=pltpu.VMEM) for _ in outs],
         out_shape=outs,
         scratch_shapes=list(scratch),
+        compiler_params=pltpu.CompilerParams(vmem_limit_bytes=limit),
     )(*[value for _, value in ins])
 
 
@@ -379,10 +419,12 @@
     peers = lax.axis_size(SKY)
     par = jnp.stack([lax.axis_index("core"), lax.axis_index(SKY) * R]).astype(jnp.int32)
     here = (SMEM, par)
-    weights = [
-        jnp.transpose(enc_weight[0, i : i + 2], (0, 2, 1, 3)).reshape(2, C, TAPS * C)
-        for i in range(0, depth, 2)
-    ]
+    dma = pltpu.SemaphoreType.DMA
+    weights = call(
+        weights_kernel, "weights", [(HBM, enc_weight[0])],
+        [sds((2, C, TAPS * C), BF16)] * (depth // 2),
+        [pltpu.VMEM(enc_weight.shape[1:], BF16), dma((1,))], None,
+    )
     joinw = join_weight.T
     dec = dec_weight.reshape(-1, dec_weight.shape[2])
     each = cotangent.shape[0]
@@ -391,12 +433,13 @@
     whole = sds((C, R), F32)
     pack = call(
         pack_kernel, "pack",
-        [here, v(sky_maps[0]), v(cotangent), v(neighbours), v(footprint)],
+        [here, (HBM, sky_maps[0]), (HBM, cotangent), (HBM, neighbours), (HBM, footprint)],
         [sds((C + each + 16, R), BF16)],
+        [pltpu.VMEM((TAPS, R), jnp.int32), pltpu.VMEM((1, R), jnp.int32), dma((4,))], None,
     )[0]
     layer_outs = [half, sds((2, TAPS * C, R), BF16), sds((3, C, R), F32), whole]
     scratch = [pltpu.VMEM((2, TAPS * C, R), BF16)]
-    below, above, other = widen(pack)
+    below, above, other = widen(pack, [weights[0]])
     hidden, picked, slopes, last, pos, kept = call(
         first_kernel, "layers01",
         [here, v(pack), v(below), v(above), v(other), v(weights[0])],
@@ -404,8 +447,10 @@
     )
     saved = [(picked, slopes, last)]
     bundle = call(
-        bundle_kernel, "bundle", [here, v(pack), v(other), v(joinw), v(dec)],
+        bundle_kernel, "bundle",
+        [here, v(pack), v(other), (HBM, joinw), (HBM, dec), v(kept)],
         [sds((branches, 3 * each + C + dec.shape[0], R), BF16)],
+        [pltpu.VMEM(joinw.shape, BF16), pltpu.VMEM(dec.shape, BF16), dma((2,))],
     )[0]
     bundle = exchange(bundle, "branch")
     for group in range(1, depth // 2):
@@ -421,19 +466,18 @@
         saved.append((picked, slopes, last))
     unit, join = call(
         unit_kernel, "unit", [v(bundle), v(pos)],
-        [sds((full, R), F32), sds((full, branches * C), BF16)],
+        [sds((full, R), F32), sds((full, branches * C), BF16)], (), None,
     )
     hiddens = exchange(share, "branch")
     pack, masked = call(
         head_kernel, "head",
         [v(hiddens), v(join), v(unit), v(joinw), v(kept), v(saved[-1][2])],
-        [sds((2 * C, R), BF16), whole],
+        [sds((2 * C, R), BF16), whole], (), None,
     )
     wide = TAPS * C
     grads = []
     low = None
     for group in reversed(range(depth // 2)):
-        below, above, other = widen(pack)
         picked, slopes, _ = saved[group]
         beside = [v(pack), v(weights[group]), v(pos), v(picked)]
         if low is not None:
@@ -443,6 +487,7 @@
             [sds((3, C, R), F32), sds((C, wide if low is None else 2 * wide), BF16)],
         )
         grads.append(grad)
+        below, above, other = widen(pack, [own])
         ins = [
             here, v(pack), v(below), v(above), v(other), v(masked), v(own), v(weights[group]),
             v(pos), v(kept), v(slopes),

time: 249 us -> 241 us (0.968)
  waiting for transfers between devices: 29.2 us -> 49 us
  Pallas kernels: 52.5 us -> 38.9 us
  other arithmetic: 5.73 us -> 0.64 us
  starting transfers between devices: 85.8 us -> 81.7 us
  blocking collectives: 62.6 us -> 59.4 us
    ppermute x12, waiting for transfers between devices: 19.8 us -> 34.1 us  [shift(): lax.ppermute(value, SKY, [(i, i + by) for i in range(peers) if 0 <= i + b...]
    pallas_call x15 -> x22, Pallas kernels: 52.5 us -> 38.9 us  [call(): pl.pallas_call(body, name=name, in_specs=specs, out_specs=[pl.BlockSpec(m...]
    ppermute x12, starting transfers between devices: 47 us -> 38 us  [shift(): lax.ppermute(value, SKY, [(i, i + by) for i in range(peers) if 0 <= i + b...]
    concatenate x6 -> x0, other arithmetic: 5.04 us -> none  [widen(): jnp.concatenate([value, below, above], axis=0)]
    ppermute x6, waiting for transfers between devices: 1.03 us -> 6.01 us  [widen(): other = lax.ppermute(stacked, 'core', [(0, 1), (1, 0)])]
    all_to_all x3, starting transfers between devices: 17 us -> 21.3 us  [exchange(): return lax.all_to_all(value, axes, 0, 0, tiled=True)]
    all_to_all x3, blocking collectives: 62.6 us -> 59.4 us  [exchange(): return lax.all_to_all(value, axes, 0, 0, tiled=True)]
    unnamed x42 -> x40, local copies, waits for them, and re-layouts: 5.4 us -> 7.93 us
  transfers between devices with their start and end apart: 21 -> 21, of which waited for: 11 -> 14; matrix products, arithmetic and copies ran while one was open for 2% -> 0% of each run, Pallas kernels for 11% -> 7%
where the time goes in v3:
time: 241 us; the launch traced here: 239 us
  starting transfers between devices  81.7 us (34%)
  blocking collectives  59.4 us (25%)
  waiting for transfers between devices  49 us (20%)
  Pallas kernels  38.9 us (16%)
  local copies, waits for them, and re-layouts  8.77 us (4%)
    all_to_all x3, blocking collectives, exchange(): return lax.all_to_all(value, axes, 0, 0, tiled=True)  59.4 us
    pallas_call x22, Pallas kernels, call(): pl.pallas_call(body, name=name, in_specs=specs, out_specs=[pl.BlockSpec(m...  38.9 us
    ppermute x12, starting transfers between devices, shift(): lax.ppermute(value, SKY, [(i, i + by) for i in range(peers) if 0 <= i + b...  38 us
    ppermute x12, waiting for transfers between devices, shift(): lax.ppermute(value, SKY, [(i, i + by) for i in range(peers) if 0 <= i + b...  34.1 us
    ppermute x6, starting transfers between devices, widen(): other = lax.ppermute(stacked, 'core', [(0, 1), (1, 0)])  22.4 us
    all_to_all x3, starting transfers between devices, exchange(): return lax.all_to_all(value, axes, 0, 0, tiled=True)  21.3 us
    all_to_all x3, waiting for transfers between devices, exchange(): return lax.all_to_all(value, axes, 0, 0, tiled=True)  8.97 us
    unnamed x40, local copies, waits for them, and re-layouts  7.93 us
  transfers between devices with their start and end apart: 21, of which 14 were waited for; matrix products, arithmetic and copies ran while one was open for 0% of the time, Pallas kernels for 7%

profile of v3, /device:TPU:1, one launch (start us, length us, event | category | flops | bytes accessed | tf_op | source)
XLA Modules:
  0.0 239.5 jit_solution(15621405357490393144)
XLA Ops:
  3.4 5.7 %collective-permute-start = (bf16[112,256]{1,0:T(8,128)(2,1)}, bf16[112,256]{1,0:T(8,128)(2,1)S(1)}, u32[]{:S(2)}, u32[]{:S(2)}) collective-permute-start(bf16[112,256]{1,0:T(8,128)(2,1)} %pack.1.refs_0_.x_ref), channel_id=1, source_target_pairs={{0,2},{1,3},{2,4},{3,5},{4,6},{5,7},{6,8},{7,9},{8,10},{9,11},{10,... | collective-permute-start | bytes 172040 | tf_op jit(solution)/shard_map/ppermute | solution.py:26
  12.4 3.3 %collective-permute-done.1.refs_2_.above_ref = bf16[112,256]{1,0:T(8,128)(2,1)S(1)} collective-permute-done((bf16[112,256]{1,0:T(8,128)(2,1)}, bf16[112,256]{1,0:T(8,128)(2,1)S(1)}, u32[]{:S(2)}, u32[]{:S(2)}) %collective-permute-start.1) | collective-permute-done | bytes 57376 | tf_op jit(solution)/shard_map/ppermute | solution.py:26
  17.4 5.6 %collective-permute-start.2 = (bf16[336,256]{1,0:T(8,128)(2,1)S(1)}, bf16[336,256]{1,0:T(8,128)(2,1)S(1)}, u32[]{:S(2)}, u32[]{:S(2)}) collective-permute-start(bf16[336,256]{1,0:T(8,128)(2,1)S(1)} %stack.18), channel_id=1, source_target_pairs={{0,1},{1,0},{2,3},{3,2},{4,5},{5,4},{6,7},{7,6},{8,9},{9,8},{10,11... | collective-permute-start | bytes 516104 | tf_op jit(solution)/shard_map/ppermute | solution.py:38
  26.3 2.4 %layers01.1 = (bf16[64,256]{1,0:T(8,128)(2,1)S(1)}, bf16[2,576,256]{2,1,0:T(8,128)(2,1)S(1)}, f32[3,64,256]{2,1,0:T(8,128)S(1)}, f32[64,256]{1,0:T(8,128)S(1)}, ...) custom-call(s32[2]{0:T(128)S(1)} %copy-done.17, bf16[112,256]{1,0:T(8,128)(2,1)S(1)} %copy-done.8, ...), custom_call_target="tpu_custom_call" | custom-call | tf_op jit(solution)/shard_map/layers01/pallas_call | solution.py:376
  31.0 4.5 %all-to-all-start.1 = ((bf16[8,448,256]{2,1,0:T(8,128)(2,1)}), bf16[8,448,256]{2,1,0:T(8,128)(2,1)}, u32[]{:S(2)}, u32[]{:S(2)}) async-start(bf16[8,448,256]{2,1,0:T(8,128)(2,1)} %bundle.1), calls=%async_computation.1 | async-start | bytes 3670016 | tf_op jit(solution)/shard_map/all_to_all | solution.py:392
  35.5 3.9 %collective-permute-start.3 = (bf16[64,256]{1,0:T(8,128)(2,1)S(1)}, bf16[64,256]{1,0:T(8,128)(2,1)S(1)}, u32[]{:S(2)}, u32[]{:S(2)}) collective-permute-start(bf16[64,256]{1,0:T(8,128)(2,1)S(1)} %get-tuple-element.39.refs_0_.x_ref), channel_id=1, source_target_pairs={{0,2},{1,3},{2,4},{3,5},{4,6},{5,7},{6,8},{7,9},{8,10},{9,11},{10,... | collective-permute-start | bytes 98312 | tf_op jit(solution)/shard_map/ppermute | solution.py:26
  41.3 13.8 %collective-permute-done.4.refs_2_.above_ref = bf16[64,256]{1,0:T(8,128)(2,1)S(1)} collective-permute-done((bf16[64,256]{1,0:T(8,128)(2,1)S(1)}, bf16[64,256]{1,0:T(8,128)(2,1)S(1)}, u32[]{:S(2)}, u32[]{:S(2)}) %collective-permute-start.4) | collective-permute-done | bytes 32800 | tf_op jit(solution)/shard_map/ppermute | solution.py:26
  55.2 2.4 %collective-permute-start.5 = (bf16[192,256]{1,0:T(8,128)(2,1)S(1)}, bf16[192,256]{1,0:T(8,128)(2,1)S(1)}, u32[]{:S(2)}, u32[]{:S(2)}) collective-permute-start(bf16[192,256]{1,0:T(8,128)(2,1)S(1)} %stack.19), channel_id=1, source_target_pairs={{0,1},{1,0},{2,3},{3,2},{4,5},{5,4},{6,7},{7,6},{8,9},{9,8},{10,11... | collective-permute-start | bytes 294920 | tf_op jit(solution)/shard_map/ppermute | solution.py:38
  58.5 2.4 %layers.1 = (bf16[64,256]{1,0:T(8,128)(2,1)S(1)}, bf16[2,576,256]{2,1,0:T(8,128)(2,1)S(1)}, f32[3,64,256]{2,1,0:T(8,128)S(1)}, f32[64,256]{1,0:T(8,128)S(1)}) custom-call(s32[2]{0:T(128)S(1)} %copy-done.18, bf16[64,256]{1,0:T(8,128)(2,1)S(1)} %get-tuple-element.39.refs_0_.x_ref, bf16[64,256]{1,0:T(8,128)(2,1)S(1)} %collective-permute-done.3.refs_1_.below_ref, ...), custom_call_target="tpu_custom_call" | custom-call | tf_op jit(solution)/shard_map/layers/pallas_call | solution.py:376
  63.6 6.8 %collective-permute-done.7.refs_2_.above_ref = bf16[64,256]{1,0:T(8,128)(2,1)S(1)} collective-permute-done((bf16[64,256]{1,0:T(8,128)(2,1)S(1)}, bf16[64,256]{1,0:T(8,128)(2,1)S(1)}, u32[]{:S(2)}, u32[]{:S(2)}) %collective-permute-start.7) | collective-permute-done | bytes 32800 | tf_op jit(solution)/shard_map/ppermute | solution.py:26
  70.4 3.4 %collective-permute-start.8 = (bf16[192,256]{1,0:T(8,128)(2,1)S(1)}, bf16[192,256]{1,0:T(8,128)(2,1)S(1)}, u32[]{:S(2)}, u32[]{:S(2)}) collective-permute-start(bf16[192,256]{1,0:T(8,128)(2,1)S(1)} %stack.20), channel_id=1, source_target_pairs={{0,1},{1,0},{2,3},{3,2},{4,5},{5,4},{6,7},{7,6},{8,9},{9,8},{10,11... | collective-permute-start | bytes 294920 | tf_op jit(solution)/shard_map/ppermute | solution.py:38
  74.8 3.2 %lastlayers.1 = (bf16[8,64,256]{2,1,0:T(8,128)(2,1)}, bf16[2,576,256]{2,1,0:T(8,128)(2,1)S(1)}, f32[3,64,256]{2,1,0:T(8,128)S(1)}, f32[64,256]{1,0:T(8,128)S(1)}) custom-call(s32[2]{0:T(128)S(1)} %copy-done.18, bf16[64,256]{1,0:T(8,128)(2,1)S(1)} %get-tuple-element.43.refs_0_.x_ref, bf16[64,256]{1,0:T(8,128)(2,1)S(1)} %collective-permute-done.6.refs_1_.below_ref, ...), custom_call_target="tpu_custom_call" | custom-call | tf_op jit(solution)/shard_map/lastlayers/pallas_call | solution.py:376
  78.6 9.8 %all-to-all-start = ((bf16[8,64,256]{2,1,0:T(8,128)(2,1)}), bf16[8,64,256]{2,1,0:T(8,128)(2,1)S(1)}, u32[]{:S(2)}, u32[]{:S(2)}) async-start(bf16[8,64,256]{2,1,0:T(8,128)(2,1)} %get-tuple-element.45), calls=%async_computation | async-start | bytes 524288 | tf_op jit(solution)/shard_map/all_to_all | solution.py:392
  88.4 4.2 %unit.1 = (f32[256,256]{1,0:T(8,128)}, bf16[256,512]{1,0:T(8,128)(2,1)}) custom-call(bf16[8,448,256]{2,1,0:T(8,128)(2,1)} %all-to-all-done.1.got_ref, s32[80,256]{1,0:T(8,128)} %copy-done), custom_call_target="tpu_custom_call" | custom-call | tf_op jit(solution)/shard_map/unit/pallas_call | solution.py:376
  92.5 2.8 %all-to-all-done.hidden_ref = bf16[8,64,256]{2,1,0:T(8,128)(2,1)S(1)} async-done(((bf16[8,64,256]{2,1,0:T(8,128)(2,1)}), bf16[8,64,256]{2,1,0:T(8,128)(2,1)S(1)}, u32[]{:S(2)}, u32[]{:S(2)}) %all-to-all-start) | async-done | bytes 262176 | tf_op jit(solution)/shard_map/all_to_all | solution.py:392
  99.6 6.9 %collective-permute-start.9 = (bf16[128,256]{1,0:T(8,128)(2,1)}, bf16[128,256]{1,0:T(8,128)(2,1)S(1)}, u32[]{:S(2)}, u32[]{:S(2)}) collective-permute-start(bf16[128,256]{1,0:T(8,128)(2,1)} %get-tuple-element.49.refs_0_.x_ref), channel_id=1, source_target_pairs={{0,2},{1,3},{2,4},{3,5},{4,6},{5,7},{6,8},{7,9},{8,10},{9,11},{10,... | collective-permute-start | bytes 196616 | tf_op jit(solution)/shard_map/ppermute | solution.py:26
  108.3 3.9 %collective-permute-start.11 = (bf16[384,256]{1,0:T(8,128)(2,1)S(1)}, bf16[384,256]{1,0:T(8,128)(2,1)S(1)}, u32[]{:S(2)}, u32[]{:S(2)}) collective-permute-start(bf16[384,256]{1,0:T(8,128)(2,1)S(1)} %stack.21), channel_id=1, source_target_pairs={{0,1},{1,0},{2,3},{3,2},{4,5},{5,4},{6,7},{7,6},{8,9},{9,8},{10,11... | collective-permute-start | bytes 589832 | tf_op jit(solution)/shard_map/ppermute | solution.py:38
  114.9 4.4 %back.2 = (bf16[128,256]{1,0:T(8,128)(2,1)S(1)}, f32[64,256]{1,0:T(8,128)S(1)}, bf16[192,256]{1,0:T(8,128)(2,1)S(1)}) custom-call(s32[2]{0:T(128)S(1)} %copy-done.18, bf16[128,256]{1,0:T(8,128)(2,1)S(1)} %copy-done.10, bf16[128,256]{1,0:T(8,128)(2,1)S(1)} %collective-permute-done.9.refs_1_.below_ref, ...), custom_call_target="tpu_custom_call" | custom-call | tf_op jit(solution)/shard_map/back/pallas_call | solution.py:376
  119.3 6.2 %collective-permute-start.12 = (bf16[128,256]{1,0:T(8,128)(2,1)S(1)}, bf16[128,256]{1,0:T(8,128)(2,1)S(1)}, u32[]{:S(2)}, u32[]{:S(2)}) collective-permute-start(bf16[128,256]{1,0:T(8,128)(2,1)S(1)} %get-tuple-element.55.refs_0_.x_ref), channel_id=1, source_target_pairs={{0,2},{1,3},{2,4},{3,5},{4,6},{5,7},{6,8},{7,9},{8,10},{9,11},{10,... | collective-permute-start | bytes 196616 | tf_op jit(solution)/shard_map/ppermute | solution.py:26
  128.0 5.4 %collective-permute-done.13.refs_2_.above_ref = bf16[128,256]{1,0:T(8,128)(2,1)S(1)} collective-permute-done((bf16[128,256]{1,0:T(8,128)(2,1)S(1)}, bf16[128,256]{1,0:T(8,128)(2,1)S(1)}, u32[]{:S(2)}, u32[]{:S(2)}) %collective-permute-start.13) | collective-permute-done | bytes 65568 | tf_op jit(solution)/shard_map/ppermute | solution.py:26
  133.5 3.4 %collective-permute-start.14 = (bf16[384,256]{1,0:T(8,128)(2,1)S(1)}, bf16[384,256]{1,0:T(8,128)(2,1)S(1)}, u32[]{:S(2)}, u32[]{:S(2)}) collective-permute-start(bf16[384,256]{1,0:T(8,128)(2,1)S(1)} %stack.22), channel_id=1, source_target_pairs={{0,1},{1,0},{2,3},{3,2},{4,5},{5,4},{6,7},{7,6},{8,9},{9,8},{10,11... | collective-permute-start | bytes 589832 | tf_op jit(solution)/shard_map/ppermute | solution.py:38
  137.9 4.4 %back.3 = (bf16[128,256]{1,0:T(8,128)(2,1)S(1)}, f32[64,256]{1,0:T(8,128)S(1)}, bf16[192,256]{1,0:T(8,128)(2,1)S(1)}) custom-call(s32[2]{0:T(128)S(1)} %copy-done.18, bf16[128,256]{1,0:T(8,128)(2,1)S(1)} %get-tuple-element.55.refs_0_.x_ref, bf16[128,256]{1,0:T(8,128)(2,1)S(1)} %collective-permute-done.12.refs_1_.below_ref, ...), custom_call_target="tpu_custom_call" | custom-call | tf_op jit(solution)/shard_map/back/pallas_call | solution.py:376
  142.4 6.0 %collective-permute-start.15 = (bf16[128,256]{1,0:T(8,128)(2,1)S(1)}, bf16[128,256]{1,0:T(8,128)(2,1)S(1)}, u32[]{:S(2)}, u32[]{:S(2)}) collective-permute-start(bf16[128,256]{1,0:T(8,128)(2,1)S(1)} %get-tuple-element.62.refs_0_.x_ref), channel_id=1, source_target_pairs={{0,2},{1,3},{2,4},{3,5},{4,6},{5,7},{6,8},{7,9},{8,10},{9,11},{10,... | collective-permute-start | bytes 196616 | tf_op jit(solution)/shard_map/ppermute | solution.py:26
  150.8 4.1 %collective-permute-done.16.refs_2_.above_ref = bf16[128,256]{1,0:T(8,128)(2,1)S(1)} collective-permute-done((bf16[128,256]{1,0:T(8,128)(2,1)S(1)}, bf16[128,256]{1,0:T(8,128)(2,1)S(1)}, u32[]{:S(2)}, u32[]{:S(2)}) %collective-permute-start.16) | collective-permute-done | bytes 65568 | tf_op jit(solution)/shard_map/ppermute | solution.py:26
  155.0 3.7 %collective-permute-start.17 = (bf16[384,256]{1,0:T(8,128)(2,1)S(1)}, bf16[384,256]{1,0:T(8,128)(2,1)S(1)}, u32[]{:S(2)}, u32[]{:S(2)}) collective-permute-start(bf16[384,256]{1,0:T(8,128)(2,1)S(1)} %stack.23), channel_id=1, source_target_pairs={{0,1},{1,0},{2,3},{3,2},{4,5},{5,4},{6,7},{7,6},{8,9},{9,8},{10,11... | collective-permute-start | bytes 589832 | tf_op jit(solution)/shard_map/ppermute | solution.py:38
  159.7 2.3 lastback.1
  162.0 11.6 %all_to_all.30 = bf16[4,48,1152]{2,1,0:T(8,128)(2,1)S(1)} all-to-all(bf16[4,48,1152]{2,1,0:T(8,128)(2,1)S(1)} %bitcast.23), channel_id=1, replica_groups=mesh['branch'=8,'z'=16,'yh'=2,'core'=2] {'yh','core'}, dimensions={0} | all-to-all | bytes 884736 | tf_op jit(solution)/shard_map/all_to_all | solution.py:392
  173.7 30.1 %all_to_all.31 = bf16[16,4,8,128]{3,2,1,0:T(8,128)(2,1)S(1)} all-to-all(bf16[16,4,8,128]{3,2,1,0:T(8,128)(2,1)S(1)} %bitcast.29), channel_id=1, replica_groups=mesh['branch'=8,'z'=16,'yh'=2,'core'=2] {'z'}, dimensions={0} | all-to-all | bytes 262144 | tf_op jit(solution)/shard_map/all_to_all | solution.py:392
  203.8 17.7 %all_to_all.32 = bf16[16,4,8,128]{3,2,1,0:T(8,128)(2,1)S(1)} all-to-all(bf16[16,4,8,128]{3,2,1,0:T(8,128)(2,1)S(1)} %broadcast_in_dim.20), channel_id=1, replica_groups=mesh['branch'=8,'z'=16,'yh'=2,'core'=2] {'z'}, dimensions={0} | all-to-all | bytes 262144 | tf_op jit(solution)/shard_map/all_to_all | solution.py:392
  222.4 7.0 %all-to-all-start.5 = ((bf16[4,48,1152]{2,1,0:T(8,128)(2,1)}), bf16[4,48,1152]{2,1,0:T(8,128)(2,1)S(1)}, u32[]{:S(2)}, u32[]{:S(2)}) async-start(bf16[4,48,1152]{2,1,0:T(8,128)(2,1)} %broadcast_in_dim.22), calls=%async_computation.5 | async-start | bytes 884736 | tf_op jit(solution)/shard_map/all_to_all | solution.py:392
  229.4 2.5 %mapgrad.1 = bf16[64,256]{1,0:T(8,128)(2,1)} custom-call(bf16[192,256]{1,0:T(8,128)(2,1)S(1)} %get-tuple-element.71.low_ref, f32[64,256]{1,0:T(8,128)S(1)} %get-tuple-element.72.own_ref, bf16[2,64,576]{2,1,0:T(8,128)(2,1)S(1)} %copy-done.4, s32[80,256]{1,0:T(8,128)S(1)} %copy-done.1), custom_call_target="tpu_custom_call" | custom-call | tf_op jit(solution)/shard_map/mapgrad/pallas_call | solution.py:376
  231.9 6.1 %all-to-all-done.5 = bf16[4,48,1152]{2,1,0:T(8,128)(2,1)S(1)} async-done(((bf16[4,48,1152]{2,1,0:T(8,128)(2,1)}), bf16[4,48,1152]{2,1,0:T(8,128)(2,1)S(1)}, u32[]{:S(2)}, u32[]{:S(2)}) %all-to-all-start.5) | async-done | bytes 442400 | tf_op jit(solution)/shard_map/all_to_all | solution.py:392
  (82 shorter events, 38.3 us)
Async XLA Ops:
  0.6 28.2 %copy-start.14 = (bf16[256,64]{0,1:T(8,128)(2,1)S(1)}, bf16[256,64]{0,1:T(8,128)(2,1)}, u32[]{:S(2)}) copy-start(bf16[256,64]{0,1:T(8,128)(2,1)} %param.11) | copy-start | bytes 98308
  0.6 28.2 %copy-start.13 = (bf16[9,32,256]{2,1,0:T(8,128)(2,1)S(1)}, bf16[9,32,256]{2,1,0:T(8,128)(2,1)}, u32[]{:S(2)}) copy-start(bf16[9,32,256]{2,1,0:T(8,128)(2,1)} %param.12) | copy-start | bytes 442372
  3.4 9.0 %collective-permute-start = (bf16[112,256]{1,0:T(8,128)(2,1)}, bf16[112,256]{1,0:T(8,128)(2,1)S(1)}, u32[]{:S(2)}, u32[]{:S(2)}) collective-permute-start(bf16[112,256]{1,0:T(8,128)(2,1)} %pack.1.refs_0_.x_ref), channel_id=1, source_target_pairs={{0,2},{1,3},{2,4},{3,5},{4,6},{5,7},{6,8},{7,9},{8,10},{9,11},{10,... | collective-permute-start | bytes 172040 | tf_op jit(solution)/shard_map/ppermute | solution.py:26
  9.0 6.6 %collective-permute-start.1 = (bf16[112,256]{1,0:T(8,128)(2,1)}, bf16[112,256]{1,0:T(8,128)(2,1)S(1)}, u32[]{:S(2)}, u32[]{:S(2)}) collective-permute-start(bf16[112,256]{1,0:T(8,128)(2,1)} %pack.1.refs_0_.x_ref), channel_id=1, source_target_pairs={{2,0},{3,1},{4,2},{5,3},{6,4},{7,5},{8,6},{9,7},{10,8},{11,9},{12,... | collective-permute-start | bytes 172040 | tf_op jit(solution)/shard_map/ppermute | solution.py:26
  15.6 0.9 copy-start.2
  17.4 6.6 %collective-permute-start.2 = (bf16[336,256]{1,0:T(8,128)(2,1)S(1)}, bf16[336,256]{1,0:T(8,128)(2,1)S(1)}, u32[]{:S(2)}, u32[]{:S(2)}) collective-permute-start(bf16[336,256]{1,0:T(8,128)(2,1)S(1)} %stack.18), channel_id=1, source_target_pairs={{0,1},{1,0},{2,3},{3,2},{4,5},{5,4},{6,7},{7,6},{8,9},{9,8},{10,11... | collective-permute-start | bytes 516104 | tf_op jit(solution)/shard_map/ppermute | solution.py:38
  28.8 46.0 %copy-start = (s32[80,256]{1,0:T(8,128)}, s32[80,256]{1,0:T(8,128)S(1)}, u32[]{:S(2)}) copy-start(s32[80,256]{1,0:T(8,128)S(1)} %get-tuple-element.41.pos_ref.refs_2_) | copy-start | bytes 245764
  28.8 46.0 %copy-start.11 = (f32[8,256]{1,0:T(8,128)}, f32[8,256]{1,0:T(8,128)S(1)}, u32[]{:S(2)}) copy-start(f32[8,256]{1,0:T(8,128)S(1)} %get-tuple-element.42.kept_ref._) | copy-start | bytes 24580
  31.0 27.6 %copy-start.5 = (bf16[2,64,576]{2,1,0:T(8,128)(2,1)S(1)}, bf16[2,64,576]{2,1,0:T(8,128)(2,1)}, u32[]{:S(2)}) copy-start(bf16[2,64,576]{2,1,0:T(8,128)(2,1)} %get-tuple-element.40.w_ref.refs_1_) | copy-start | bytes 442372
  31.0 27.6 %copy-start.18 = (s32[2]{0:T(128)S(1)}, s32[2]{0:T(128)}, u32[]{:S(2)}) copy-start(s32[2]{0:T(128)} %pad_add_fusion.par_ref) | copy-start | bytes 28
  31.0 43.8 %copy-start.6 = (bf16[2,64,576]{2,1,0:T(8,128)(2,1)S(1)}, bf16[2,64,576]{2,1,0:T(8,128)(2,1)}, u32[]{:S(2)}) copy-start(bf16[2,64,576]{2,1,0:T(8,128)(2,1)} %get-tuple-element.44.w_ref.refs_1_) | copy-start | bytes 442372
  31.0 47.6 %all-to-all-start.1 = ((bf16[8,448,256]{2,1,0:T(8,128)(2,1)}), bf16[8,448,256]{2,1,0:T(8,128)(2,1)}, u32[]{:S(2)}, u32[]{:S(2)}) async-start(bf16[8,448,256]{2,1,0:T(8,128)(2,1)} %bundle.1), calls=%async_computation.1 | async-start | bytes 3670016 | tf_op jit(solution)/shard_map/all_to_all | solution.py:392
  35.5 5.8 %collective-permute-start.3 = (bf16[64,256]{1,0:T(8,128)(2,1)S(1)}, bf16[64,256]{1,0:T(8,128)(2,1)S(1)}, u32[]{:S(2)}, u32[]{:S(2)}) collective-permute-start(bf16[64,256]{1,0:T(8,128)(2,1)S(1)} %get-tuple-element.39.refs_0_.x_ref), channel_id=1, source_target_pairs={{0,2},{1,3},{2,4},{3,5},{4,6},{5,7},{6,8},{7,9},{8,10},{9,11},{10,... | collective-permute-start | bytes 98312 | tf_op jit(solution)/shard_map/ppermute | solution.py:26
  39.4 15.7 %collective-permute-start.4 = (bf16[64,256]{1,0:T(8,128)(2,1)S(1)}, bf16[64,256]{1,0:T(8,128)(2,1)S(1)}, u32[]{:S(2)}, u32[]{:S(2)}) collective-permute-start(bf16[64,256]{1,0:T(8,128)(2,1)S(1)} %get-tuple-element.39.refs_0_.x_ref), channel_id=1, source_target_pairs={{2,0},{3,1},{4,2},{5,3},{6,4},{7,5},{8,6},{9,7},{10,8},{11,9},{12,... | collective-permute-start | bytes 98312 | tf_op jit(solution)/shard_map/ppermute | solution.py:26
  55.2 3.4 %collective-permute-start.5 = (bf16[192,256]{1,0:T(8,128)(2,1)S(1)}, bf16[192,256]{1,0:T(8,128)(2,1)S(1)}, u32[]{:S(2)}, u32[]{:S(2)}) collective-permute-start(bf16[192,256]{1,0:T(8,128)(2,1)S(1)} %stack.19), channel_id=1, source_target_pairs={{0,1},{1,0},{2,3},{3,2},{4,5},{5,4},{6,7},{7,6},{8,9},{9,8},{10,11... | collective-permute-start | bytes 294920 | tf_op jit(solution)/shard_map/ppermute | solution.py:38
  61.0 2.6 %collective-permute-start.6 = (bf16[64,256]{1,0:T(8,128)(2,1)S(1)}, bf16[64,256]{1,0:T(8,128)(2,1)S(1)}, u32[]{:S(2)}, u32[]{:S(2)}) collective-permute-start(bf16[64,256]{1,0:T(8,128)(2,1)S(1)} %get-tuple-element.43.refs_0_.x_ref), channel_id=1, source_target_pairs={{0,2},{1,3},{2,4},{3,5},{4,6},{5,7},{6,8},{7,9},{8,10},{9,11},{10,... | collective-permute-start | bytes 98312 | tf_op jit(solution)/shard_map/ppermute | solution.py:26
  62.3 8.2 %collective-permute-start.7 = (bf16[64,256]{1,0:T(8,128)(2,1)S(1)}, bf16[64,256]{1,0:T(8,128)(2,1)S(1)}, u32[]{:S(2)}, u32[]{:S(2)}) collective-permute-start(bf16[64,256]{1,0:T(8,128)(2,1)S(1)} %get-tuple-element.43.refs_0_.x_ref), channel_id=1, source_target_pairs={{2,0},{3,1},{4,2},{5,3},{6,4},{7,5},{8,6},{9,7},{10,8},{11,9},{12,... | collective-permute-start | bytes 98312 | tf_op jit(solution)/shard_map/ppermute | solution.py:26
  70.4 4.3 %collective-permute-start.8 = (bf16[192,256]{1,0:T(8,128)(2,1)S(1)}, bf16[192,256]{1,0:T(8,128)(2,1)S(1)}, u32[]{:S(2)}, u32[]{:S(2)}) collective-permute-start(bf16[192,256]{1,0:T(8,128)(2,1)S(1)} %stack.20), channel_id=1, source_target_pairs={{0,1},{1,0},{2,3},{3,2},{4,5},{5,4},{6,7},{7,6},{8,9},{9,8},{10,11... | collective-permute-start | bytes 294920 | tf_op jit(solution)/shard_map/ppermute | solution.py:38
  78.6 28.0 %copy-start.1 = (s32[80,256]{1,0:T(8,128)S(1)}, s32[80,256]{1,0:T(8,128)}, u32[]{:S(2)}) copy-start(s32[80,256]{1,0:T(8,128)} %copy-done) | copy-start | bytes 245764
  78.6 16.8 %all-to-all-start = ((bf16[8,64,256]{2,1,0:T(8,128)(2,1)}), bf16[8,64,256]{2,1,0:T(8,128)(2,1)S(1)}, u32[]{:S(2)}, u32[]{:S(2)}) async-start(bf16[8,64,256]{2,1,0:T(8,128)(2,1)} %get-tuple-element.45), calls=%async_computation | async-start | bytes 524288 | tf_op jit(solution)/shard_map/all_to_all | solution.py:392
  88.4 24.9 %copy-start.12 = (f32[8,256]{1,0:T(8,128)S(1)}, f32[8,256]{1,0:T(8,128)}, u32[]{:S(2)}) copy-start(f32[8,256]{1,0:T(8,128)} %copy-done.11) | copy-start | bytes 24580
  98.3 9.9 %collective-permute-start.10 = (bf16[128,256]{1,0:T(8,128)(2,1)}, bf16[128,256]{1,0:T(8,128)(2,1)S(1)}, u32[]{:S(2)}, u32[]{:S(2)}) collective-permute-start(bf16[128,256]{1,0:T(8,128)(2,1)} %get-tuple-element.49.refs_0_.x_ref), channel_id=1, source_target_pairs={{2,0},{3,1},{4,2},{5,3},{6,4},{7,5},{8,6},{9,7},{10,8},{11,9},{12,... | collective-permute-start | bytes 196616 | tf_op jit(solution)/shard_map/ppermute | solution.py:26
  99.6 8.7 %collective-permute-start.9 = (bf16[128,256]{1,0:T(8,128)(2,1)}, bf16[128,256]{1,0:T(8,128)(2,1)S(1)}, u32[]{:S(2)}, u32[]{:S(2)}) collective-permute-start(bf16[128,256]{1,0:T(8,128)(2,1)} %get-tuple-element.49.refs_0_.x_ref), channel_id=1, source_target_pairs={{0,2},{1,3},{2,4},{3,5},{4,6},{5,7},{6,8},{7,9},{8,10},{9,11},{10,... | collective-permute-start | bytes 196616 | tf_op jit(solution)/shard_map/ppermute | solution.py:26
  108.3 4.9 %collective-permute-start.11 = (bf16[384,256]{1,0:T(8,128)(2,1)S(1)}, bf16[384,256]{1,0:T(8,128)(2,1)S(1)}, u32[]{:S(2)}, u32[]{:S(2)}) collective-permute-start(bf16[384,256]{1,0:T(8,128)(2,1)S(1)} %stack.21), channel_id=1, source_target_pairs={{0,1},{1,0},{2,3},{3,2},{4,5},{5,4},{6,7},{7,6},{8,9},{9,8},{10,11... | collective-permute-start | bytes 589832 | tf_op jit(solution)/shard_map/ppermute | solution.py:38
  119.3 30.4 %copy-start.4 = (bf16[2,64,576]{2,1,0:T(8,128)(2,1)S(1)}, bf16[2,64,576]{2,1,0:T(8,128)(2,1)}, u32[]{:S(2)}) copy-start(bf16[2,64,576]{2,1,0:T(8,128)(2,1)} %get-tuple-element.38.refs_3_.w_ref.refs_1_) | copy-start | bytes 442372
  119.3 8.7 %collective-permute-start.12 = (bf16[128,256]{1,0:T(8,128)(2,1)S(1)}, bf16[128,256]{1,0:T(8,128)(2,1)S(1)}, u32[]{:S(2)}, u32[]{:S(2)}) collective-permute-start(bf16[128,256]{1,0:T(8,128)(2,1)S(1)} %get-tuple-element.55.refs_0_.x_ref), channel_id=1, source_target_pairs={{0,2},{1,3},{2,4},{3,5},{4,6},{5,7},{6,8},{7,9},{8,10},{9,11},{10,... | collective-permute-start | bytes 196616 | tf_op jit(solution)/shard_map/ppermute | solution.py:26
  125.5 7.9 %collective-permute-start.13 = (bf16[128,256]{1,0:T(8,128)(2,1)S(1)}, bf16[128,256]{1,0:T(8,128)(2,1)S(1)}, u32[]{:S(2)}, u32[]{:S(2)}) collective-permute-start(bf16[128,256]{1,0:T(8,128)(2,1)S(1)} %get-tuple-element.55.refs_0_.x_ref), channel_id=1, source_target_pairs={{2,0},{3,1},{4,2},{5,3},{6,4},{7,5},{8,6},{9,7},{10,8},{11,9},{12,... | collective-permute-start | bytes 196616 | tf_op jit(solution)/shard_map/ppermute | solution.py:26
  133.5 4.5 %collective-permute-start.14 = (bf16[384,256]{1,0:T(8,128)(2,1)S(1)}, bf16[384,256]{1,0:T(8,128)(2,1)S(1)}, u32[]{:S(2)}, u32[]{:S(2)}) collective-permute-start(bf16[384,256]{1,0:T(8,128)(2,1)S(1)} %stack.22), channel_id=1, source_target_pairs={{0,1},{1,0},{2,3},{3,2},{4,5},{5,4},{6,7},{7,6},{8,9},{9,8},{10,11... | collective-permute-start | bytes 589832 | tf_op jit(solution)/shard_map/ppermute | solution.py:38
  142.4 8.4 %collective-permute-start.15 = (bf16[128,256]{1,0:T(8,128)(2,1)S(1)}, bf16[128,256]{1,0:T(8,128)(2,1)S(1)}, u32[]{:S(2)}, u32[]{:S(2)}) collective-permute-start(bf16[128,256]{1,0:T(8,128)(2,1)S(1)} %get-tuple-element.62.refs_0_.x_ref), channel_id=1, source_target_pairs={{0,2},{1,3},{2,4},{3,5},{4,6},{5,7},{6,8},{7,9},{8,10},{9,11},{10,... | collective-permute-start | bytes 196616 | tf_op jit(solution)/shard_map/ppermute | solution.py:26
  148.4 6.5 %collective-permute-start.16 = (bf16[128,256]{1,0:T(8,128)(2,1)S(1)}, bf16[128,256]{1,0:T(8,128)(2,1)S(1)}, u32[]{:S(2)}, u32[]{:S(2)}) collective-permute-start(bf16[128,256]{1,0:T(8,128)(2,1)S(1)} %get-tuple-element.62.refs_0_.x_ref), channel_id=1, source_target_pairs={{2,0},{3,1},{4,2},{5,3},{6,4},{7,5},{8,6},{9,7},{10,8},{11,9},{12,... | collective-permute-start | bytes 196616 | tf_op jit(solution)/shard_map/ppermute | solution.py:26
  155.0 4.8 %collective-permute-start.17 = (bf16[384,256]{1,0:T(8,128)(2,1)S(1)}, bf16[384,256]{1,0:T(8,128)(2,1)S(1)}, u32[]{:S(2)}, u32[]{:S(2)}) collective-permute-start(bf16[384,256]{1,0:T(8,128)(2,1)S(1)} %stack.23), channel_id=1, source_target_pairs={{0,1},{1,0},{2,3},{3,2},{4,5},{5,4},{6,7},{7,6},{8,9},{9,8},{10,11... | collective-permute-start | bytes 589832 | tf_op jit(solution)/shard_map/ppermute | solution.py:38
  222.4 15.6 %all-to-all-start.5 = ((bf16[4,48,1152]{2,1,0:T(8,128)(2,1)}), bf16[4,48,1152]{2,1,0:T(8,128)(2,1)S(1)}, u32[]{:S(2)}, u32[]{:S(2)}) async-start(bf16[4,48,1152]{2,1,0:T(8,128)(2,1)} %broadcast_in_dim.22), calls=%async_computation.5 | async-start | bytes 884736 | tf_op jit(solution)/shard_map/all_to_all | solution.py:392
  (9 other events, 7.0 us)

commit v4 on v3

--- a/solution.py
+++ b/solution.py
@@ -17,7 +17,6 @@
 F32 = jnp.float32
 BF16 = jnp.bfloat16
 VMEM = pl.BlockSpec(memory_space=pltpu.VMEM)
-SMEM = pl.BlockSpec(memory_space=pltpu.SMEM)
 HBM = pl.BlockSpec(memory_space=pltpu.HBM)
 
 
@@ -126,10 +125,10 @@
 
 
 def first_kernel(
-    par_ref, x_ref, below_ref, above_ref, other_ref, w_ref,
+    x_ref, below_ref, above_ref, other_ref, w_ref,
     h_ref, picked_ref, slopes_ref, last_ref, pos_ref, kept_ref, scratch,
 ):
-    even = par_ref[0] == 0
+    even = lax.axis_index("core") == 0
     size = x_ref.shape[0]
     other = other_ref[...]
     meta_at = size - 16
@@ -158,10 +157,10 @@
 
 
 def layers_kernel(
-    par_ref, x_ref, below_ref, above_ref, other_ref, w_ref, pos_ref, kept_ref,
+    x_ref, below_ref, above_ref, other_ref, w_ref, pos_ref, kept_ref,
     h_ref, picked_ref, slopes_ref, last_ref, scratch,
 ):
-    even = par_ref[0] == 0
+    even = lax.axis_index("core") == 0
     pos, kept = read_tables(pos_ref, kept_ref)
     one, three = inner(other_ref[...], C, even, 0, C)
     blocks = [below_ref[...], one, x_ref[...], three, above_ref[...]]
@@ -169,27 +168,33 @@
 
 
 def last_layers_kernel(
-    par_ref, x_ref, below_ref, above_ref, other_ref, w_ref, pos_ref, kept_ref,
+    x_ref, below_ref, above_ref, other_ref, w_ref, pos_ref, kept_ref, joinw_ref, unit_ref,
     share_ref, picked_ref, slopes_ref, last_ref, scratch,
 ):
-    even = par_ref[0] == 0
+    even = lax.axis_index("core") == 0
     pos, kept = read_tables(pos_ref, kept_ref)
     one, three = inner(other_ref[...], C, even, 0, C)
     blocks = [below_ref[...], one, x_ref[...], three, above_ref[...]]
     hidden = two_layers(blocks, pos, kept, w_ref, None, picked_ref, slopes_ref, last_ref, scratch)
-    for i in range(share_ref.shape[0]):
-        share_ref[i] = hidden
+    partial = lax.dot_general(
+        joinw_ref[...], hidden, (((0,), (0,)), ((), ())), preferred_element_type=F32
+    ).astype(BF16)
+    count = share_ref.shape[0]
+    each = partial.shape[0] // count
+    for c in range(count):
+        share_ref[c, :each, :] = partial[c * each : (c + 1) * each]
+        share_ref[c, each:, :] = unit_ref[c * each : (c + 1) * each, :]
 
 
 def pack_kernel(
-    par_ref, maps_hbm, cot_hbm, near_hbm, foot_hbm, pack_ref, near_ref, foot_ref, sems
+    maps_hbm, cot_hbm, near_hbm, foot_hbm, pack_ref, near_ref, foot_ref, sems
 ):
     each = cot_hbm.shape[0]
     fetch(
         [(near_hbm, near_ref), (foot_hbm, foot_ref), (maps_hbm, pack_ref.at[pl.ds(0, C)]),
          (cot_hbm, pack_ref.at[pl.ds(C, each)])], sems,
     )
-    row = par_ref[1] + lax.broadcasted_iota(jnp.int32, (TAPS, R), 1)
+    row = lax.axis_index(SKY) * R + lax.broadcasted_iota(jnp.int32, (TAPS, R), 1)
     near = near_ref[...]
     offset = jnp.where(near >= 0, near - row, 512).astype(F32)
     meta = jnp.concatenate(
@@ -207,60 +212,45 @@
             out_ref[i] = jnp.concatenate([w_ref[layer, k] for k in range(TAPS)], axis=1)
 
 
-def bundle_kernel(
-    par_ref, x_ref, other_ref, joinw_hbm, dec_hbm, _, out_ref, joinw_ref, dec_ref, sems
-):
-    fetch([(joinw_hbm, joinw_ref), (dec_hbm, dec_ref)], sems)
-    even = par_ref[0] == 0
+def unit_kernel(x_ref, other_ref, pos_ref, dec_ref, unit_ref, scratch):
+    even = lax.axis_index("core") == 0
     size = x_ref.shape[0]
     each = size - 16 - C
     one, three = inner(other_ref[...], size, even, C, each)
-    for i in range(out_ref.shape[0]):
-        out_ref[i, :each, :] = one
-        out_ref[i, each : 2 * each, :] = x_ref[C : C + each, :]
-        out_ref[i, 2 * each : 3 * each, :] = three
-        out_ref[i, 3 * each : 3 * each + C, :] = joinw_ref[...]
-        out_ref[i, 3 * each + C :, :] = dec_ref[...]
-
-
-def unit_kernel(got_ref, pos_ref, unit_ref, join_ref):
-    count, size, _ = got_ref.shape
-    each = (size - C) // (3 + TAPS)
+    sources = [one, x_ref[C : C + each, :], three]
     pos = [pos_ref[16 * b : 16 * b + 16, :] for b in (1, 2, 3)]
-
-    def rows(start, length):
-        return jnp.concatenate([got_ref[d, start : start + length, :] for d in range(count)], axis=0)
-
-    sources = [rows(each * i, each) for i in range(3)]
-    unit = None
     for k in range(TAPS):
         if k == 4:
-            total = sources[1]
-        else:
-            total = None
-            for i in range(3):
-                at = pos[i][k : k + 1]
-                sent = jnp.where((at >> 8) == 2 - i, sources[i], jnp.zeros_like(sources[i]))
-                added = lax.dot_general(
-                    sent, low_onehot(at & 255), (((1,), (1,)), ((), ())), preferred_element_type=F32
-                )
-                total = added if total is None else total + added
-            total = total.astype(BF16)
-        dec = rows(3 * each + C + each * k, each)
-        added = lax.dot_general(dec, total, (((0,), (0,)), ((), ())), preferred_element_type=F32)
-        unit = added if unit is None else unit + added
-    unit_ref[...] = unit
-    join_ref[...] = jnp.transpose(rows(3 * each, C))
-
-
-def head_kernel(
-    hidden_ref, join_ref, unit_ref, joinw_ref, kept_ref, last_ref, pack_ref, masked_ref
-):
-    count = hidden_ref.shape[0]
-    hidden = jnp.concatenate([hidden_ref[d] for d in range(count)], axis=0)
-    joined = jnp.dot(join_ref[...], hidden, preferred_element_type=F32)
+            scratch[k * each : (k + 1) * each, :] = sources[1]
+            continue
+        total = None
+        for i in range(3):
+            at = pos[i][k : k + 1]
+            sent = jnp.where((at >> 8) == 2 - i, sources[i], jnp.zeros_like(sources[i]))
+            added = lax.dot_general(
+                sent, low_onehot(at & 255), (((1,), (1,)), ((), ())), preferred_element_type=F32
+            )
+            total = added if total is None else total + added
+        scratch[k * each : (k + 1) * each, :] = total.astype(BF16)
+    unit_ref[...] = lax.dot_general(
+        dec_ref[...], scratch[...], (((0,), (0,)), ((), ())), preferred_element_type=F32
+    ).astype(BF16)
+
+
+def slope_kernel(parts_ref, out_ref):
+    total = parts_ref[0].astype(F32)
+    for i in range(1, parts_ref.shape[0]):
+        total = total + parts_ref[i].astype(F32)
+    each = total.shape[0] // 2
+    joined = total[:each]
     slope = slope_of(joined, jax.nn.sigmoid(joined)).astype(BF16).astype(F32)
-    unit_grad = (unit_ref[...] * slope).astype(BF16)
+    grad = (total[each:] * slope).astype(BF16)
+    for i in range(out_ref.shape[0]):
+        out_ref[i] = grad
+
+
+def head_kernel(unit_ref, joinw_ref, kept_ref, last_ref, pack_ref, masked_ref):
+    unit_grad = jnp.concatenate([unit_ref[d] for d in range(unit_ref.shape[0])], axis=0)
     gradient = jnp.dot(joinw_ref[...], unit_grad, preferred_element_type=F32)
     masked = kept_ref[2:3, :] * gradient
     masked_ref[...] = masked
@@ -289,10 +279,10 @@
 
 
 def upper_layer(
-    par_ref, x_ref, below_ref, above_ref, other_ref, masked_ref, own_ref, w_ref, pos_ref, kept_ref,
+    x_ref, below_ref, above_ref, other_ref, masked_ref, own_ref, w_ref, pos_ref, kept_ref,
     slopes_ref,
 ):
-    even = par_ref[0] == 0
+    even = lax.axis_index("core") == 0
     pos, kept = read_tables(pos_ref, kept_ref)
     other = other_ref[...]
     act1, act3 = inner(other, 2 * C, even, 0, C)
@@ -316,11 +306,11 @@
 
 
 def back_kernel(
-    par_ref, x_ref, below_ref, above_ref, other_ref, masked_ref, own_ref, w_ref, pos_ref, kept_ref,
+    x_ref, below_ref, above_ref, other_ref, masked_ref, own_ref, w_ref, pos_ref, kept_ref,
     slopes_ref, next_ref, pack_ref, out_ref, low_ref,
 ):
     lower, low_acts = upper_layer(
-        par_ref, x_ref, below_ref, above_ref, other_ref, masked_ref, own_ref, w_ref, pos_ref,
+        x_ref, below_ref, above_ref, other_ref, masked_ref, own_ref, w_ref, pos_ref,
         kept_ref, slopes_ref,
     )
     pos, kept = read_tables(pos_ref, kept_ref)
@@ -333,11 +323,11 @@
 
 
 def last_back_kernel(
-    par_ref, x_ref, below_ref, above_ref, other_ref, masked_ref, own_ref, w_ref, pos_ref, kept_ref,
+    x_ref, below_ref, above_ref, other_ref, masked_ref, own_ref, w_ref, pos_ref, kept_ref,
     slopes_ref, picked_ref, grad5_ref, grad43_ref, grad21_ref, low_ref, out_ref, grads_ref,
 ):
     lower, low_acts = upper_layer(
-        par_ref, x_ref, below_ref, above_ref, other_ref, masked_ref, own_ref, w_ref, pos_ref,
+        x_ref, below_ref, above_ref, other_ref, masked_ref, own_ref, w_ref, pos_ref,
         kept_ref, slopes_ref,
     )
     out_ref[...] = lower[1]
@@ -417,13 +407,11 @@
     depth = enc_weight.shape[1]
     branches = lax.axis_size("branch")
     peers = lax.axis_size(SKY)
-    par = jnp.stack([lax.axis_index("core"), lax.axis_index(SKY) * R]).astype(jnp.int32)
-    here = (SMEM, par)
     dma = pltpu.SemaphoreType.DMA
     weights = call(
         weights_kernel, "weights", [(HBM, enc_weight[0])],
         [sds((2, C, TAPS * C), BF16)] * (depth // 2),
-        [pltpu.VMEM(enc_weight.shape[1:], BF16), dma((1,))], None,
+        [pltpu.VMEM(enc_weight.shape[1:], BF16), dma((1,))],
     )
     joinw = join_weight.T
     dec = dec_weight.reshape(-1, dec_weight.shape[2])
@@ -433,7 +421,7 @@
     whole = sds((C, R), F32)
     pack = call(
         pack_kernel, "pack",
-        [here, (HBM, sky_maps[0]), (HBM, cotangent), (HBM, neighbours), (HBM, footprint)],
+        [(HBM, sky_maps[0]), (HBM, cotangent), (HBM, neighbours), (HBM, footprint)],
         [sds((C + each + 16, R), BF16)],
         [pltpu.VMEM((TAPS, R), jnp.int32), pltpu.VMEM((1, R), jnp.int32), dma((4,))], None,
     )[0]
@@ -442,37 +430,31 @@
     below, above, other = widen(pack, [weights[0]])
     hidden, picked, slopes, last, pos, kept = call(
         first_kernel, "layers01",
-        [here, v(pack), v(below), v(above), v(other), v(weights[0])],
+        [v(pack), v(below), v(above), v(other), v(weights[0])],
         layer_outs + [sds((80, R), jnp.int32), sds((8, R), F32)], scratch,
     )
     saved = [(picked, slopes, last)]
-    bundle = call(
-        bundle_kernel, "bundle",
-        [here, v(pack), v(other), (HBM, joinw), (HBM, dec), v(kept)],
-        [sds((branches, 3 * each + C + dec.shape[0], R), BF16)],
-        [pltpu.VMEM(joinw.shape, BF16), pltpu.VMEM(dec.shape, BF16), dma((2,))],
+    unit = call(
+        unit_kernel, "unit", [v(pack), v(other), v(pos), v(dec)],
+        [sds((full, R), BF16)], [pltpu.VMEM((TAPS * each, R), BF16)],
     )[0]
-    bundle = exchange(bundle, "branch")
     for group in range(1, depth // 2):
-        below, above, other = widen(hidden)
-        ins = [here, v(hidden), v(below), v(above), v(other), v(weights[group]), v(pos), v(kept)]
+        below, above, other = widen(hidden, [unit] if group == 1 else ())
+        ins = [v(hidden), v(below), v(above), v(other), v(weights[group]), v(pos), v(kept)]
         if group < depth // 2 - 1:
             hidden, picked, slopes, last = call(layers_kernel, "layers", ins, layer_outs, scratch)
         else:
             share, picked, slopes, last = call(
-                last_layers_kernel, "lastlayers", ins,
-                [sds((branches, C, R), BF16)] + layer_outs[1:], scratch,
+                last_layers_kernel, "lastlayers", ins + [v(joinw), v(unit)],
+                [sds((branches, 2 * each, R), BF16)] + layer_outs[1:], scratch,
             )
         saved.append((picked, slopes, last))
-    unit, join = call(
-        unit_kernel, "unit", [v(bundle), v(pos)],
-        [sds((full, R), F32), sds((full, branches * C), BF16)], (), None,
-    )
-    hiddens = exchange(share, "branch")
+    parts = exchange(share, "branch")
+    mine = call(slope_kernel, "slope", [v(parts)], [sds((branches, each, R), BF16)])[0]
     pack, masked = call(
         head_kernel, "head",
-        [v(hiddens), v(join), v(unit), v(joinw), v(kept), v(saved[-1][2])],
-        [sds((2 * C, R), BF16), whole], (), None,
+        [v(exchange(mine, "branch")), v(joinw), v(kept), v(saved[-1][2])],
+        [sds((2 * C, R), BF16), whole],
     )
     wide = TAPS * C
     grads = []
@@ -489,7 +471,7 @@
         grads.append(grad)
         below, above, other = widen(pack, [own])
         ins = [
-            here, v(pack), v(below), v(above), v(other), v(masked), v(own), v(weights[group]),
+            v(pack), v(below), v(above), v(other), v(masked), v(own), v(weights[group]),
             v(pos), v(kept), v(slopes),
         ]
         if group:

time: 241 us -> 210 us (0.87)
  waiting for transfers between devices: 49 us -> 17.6 us
  blocking collectives: 59.4 us -> 82.5 us
  Pallas kernels: 38.9 us -> 25.7 us
  local copies, waits for them, and re-layouts: 8.77 us -> 3.64 us
  starting transfers between devices: 81.7 us -> 78.1 us
    ppermute x12, waiting for transfers between devices: 34.1 us -> 5.6 us  [shift(): lax.ppermute(value, SKY, [(i, i + by) for i in range(peers) if 0 <= i + b...]
    all_to_all x3 -> x5, blocking collectives: 59.4 us -> 82.5 us  [exchange(): return lax.all_to_all(value, axes, 0, 0, tiled=True)]
    all_to_all x3 -> x1, starting transfers between devices: 21.3 us -> 7.03 us  [exchange(): return lax.all_to_all(value, axes, 0, 0, tiled=True)]
    pallas_call x22, Pallas kernels: 38.9 us -> 25.7 us  [call(): pl.pallas_call(body, name=name, in_specs=specs, out_specs=[pl.BlockSpec(m...]
    ppermute x12, starting transfers between devices: 38 us -> 46.9 us  [shift(): lax.ppermute(value, SKY, [(i, i + by) for i in range(peers) if 0 <= i + b...]
    unnamed x40 -> x10, local copies, waits for them, and re-layouts: 7.93 us -> 2.81 us
    all_to_all x3 -> x1, waiting for transfers between devices: 8.97 us -> 6.13 us  [exchange(): return lax.all_to_all(value, axes, 0, 0, tiled=True)]
  transfers between devices with their start and end apart: 21 -> 19, of which waited for: 14 -> 12; matrix products, arithmetic and copies ran while one was open for 0% -> 0% of each run, Pallas kernels for 7% -> 3%
where the time goes in v4:
time: 210 us; the launch traced here: 209 us
  blocking collectives  82.5 us (39%)
  starting transfers between devices  78.1 us (37%)
  Pallas kernels  25.7 us (12%)
  waiting for transfers between devices  17.6 us (8%)
  local copies, waits for them, and re-layouts  3.64 us (2%)
    all_to_all x5, blocking collectives, exchange(): return lax.all_to_all(value, axes, 0, 0, tiled=True)  82.5 us
    ppermute x12, starting transfers between devices, shift(): lax.ppermute(value, SKY, [(i, i + by) for i in range(peers) if 0 <= i + b...  46.9 us
    pallas_call x22, Pallas kernels, call(): pl.pallas_call(body, name=name, in_specs=specs, out_specs=[pl.BlockSpec(m...  25.7 us
    ppermute x6, starting transfers between devices, widen(): other = lax.ppermute(stacked, 'core', [(0, 1), (1, 0)])  24.2 us
    all_to_all x1, starting transfers between devices, exchange(): return lax.all_to_all(value, axes, 0, 0, tiled=True)  7.03 us
    all_to_all x1, waiting for transfers between devices, exchange(): return lax.all_to_all(value, axes, 0, 0, tiled=True)  6.13 us
    ppermute x6, waiting for transfers between devices, widen(): other = lax.ppermute(stacked, 'core', [(0, 1), (1, 0)])  5.83 us
    ppermute x12, waiting for transfers between devices, shift(): lax.ppermute(value, SKY, [(i, i + by) for i in range(peers) if 0 <= i + b...  5.6 us
  transfers between devices with their start and end apart: 19, of which 12 were waited for; matrix products, arithmetic and copies ran while one was open for 0% of the time, Pallas kernels for 3%

profile of v4, /device:TPU:1, one launch (start us, length us, event | category | flops | bytes accessed | tf_op | source)
XLA Modules:
  0.0 208.6 jit_solution(2474879745547764492)
XLA Ops:
  0.6 1.5 pack.1.refs_0_.x_ref
  3.4 6.3 %collective-permute-start = (bf16[112,256]{1,0:T(8,128)(2,1)}, bf16[112,256]{1,0:T(8,128)(2,1)S(1)}, u32[]{:S(2)}, u32[]{:S(2)}) collective-permute-start(bf16[112,256]{1,0:T(8,128)(2,1)} %pack.1.refs_0_.x_ref), channel_id=1, source_target_pairs={{0,2},{1,3},{2,4},{3,5},{4,6},{5,7},{6,8},{7,9},{8,10},{9,11},{10,... | collective-permute-start | bytes 172040 | tf_op jit(solution)/shard_map/ppermute | solution.py:25
  12.6 8.6 %collective-permute-start.2 = (bf16[336,256]{1,0:T(8,128)(2,1)S(1)}, bf16[336,256]{1,0:T(8,128)(2,1)S(1)}, u32[]{:S(2)}, u32[]{:S(2)}) collective-permute-start(bf16[336,256]{1,0:T(8,128)(2,1)S(1)} %stack.6), channel_id=1, source_target_pairs={{0,1},{1,0},{2,3},{3,2},{4,5},{5,4},{6,7},{7,6},{8,9},{9,8},{10,11... | collective-permute-start | bytes 516104 | tf_op jit(solution)/shard_map/ppermute | solution.py:37
  23.1 1.9 layers01.1
  25.0 1.3 collective-permute-start.4
  26.3 6.0 %collective-permute-start.3 = (bf16[64,256]{1,0:T(8,128)(2,1)S(1)}, bf16[64,256]{1,0:T(8,128)(2,1)S(1)}, u32[]{:S(2)}, u32[]{:S(2)}) collective-permute-start(bf16[64,256]{1,0:T(8,128)(2,1)S(1)} %get-tuple-element.37.refs_0_.x_ref), channel_id=1, source_target_pairs={{0,2},{1,3},{2,4},{3,5},{4,6},{5,7},{6,8},{7,9},{8,10},{9,11},{10,... | collective-permute-start | bytes 98312 | tf_op jit(solution)/shard_map/ppermute | solution.py:25
  33.7 2.8 %collective-permute-start.5 = (bf16[192,256]{1,0:T(8,128)(2,1)S(1)}, bf16[192,256]{1,0:T(8,128)(2,1)S(1)}, u32[]{:S(2)}, u32[]{:S(2)}) collective-permute-start(bf16[192,256]{1,0:T(8,128)(2,1)S(1)} %stack.7), channel_id=1, source_target_pairs={{0,1},{1,0},{2,3},{3,2},{4,5},{5,4},{6,7},{7,6},{8,9},{9,8},{10,11... | collective-permute-start | bytes 294920 | tf_op jit(solution)/shard_map/ppermute | solution.py:37
  37.4 1.9 layers.1
  40.6 6.7 %collective-permute-start.6 = (bf16[64,256]{1,0:T(8,128)(2,1)S(1)}, bf16[64,256]{1,0:T(8,128)(2,1)S(1)}, u32[]{:S(2)}, u32[]{:S(2)}) collective-permute-start(bf16[64,256]{1,0:T(8,128)(2,1)S(1)} %get-tuple-element.41.refs_0_.x_ref), channel_id=1, source_target_pairs={{0,2},{1,3},{2,4},{3,5},{4,6},{5,7},{6,8},{7,9},{8,10},{9,11},{10,... | collective-permute-start | bytes 98312 | tf_op jit(solution)/shard_map/ppermute | solution.py:25
  48.3 3.1 %collective-permute-start.8 = (bf16[192,256]{1,0:T(8,128)(2,1)S(1)}, bf16[192,256]{1,0:T(8,128)(2,1)S(1)}, u32[]{:S(2)}, u32[]{:S(2)}) collective-permute-start(bf16[192,256]{1,0:T(8,128)(2,1)S(1)} %stack.8), channel_id=1, source_target_pairs={{0,1},{1,0},{2,3},{3,2},{4,5},{5,4},{6,7},{7,6},{8,9},{9,8},{10,11... | collective-permute-start | bytes 294920 | tf_op jit(solution)/shard_map/ppermute | solution.py:37
  52.3 2.1 lastlayers.1
  54.4 9.8 %all_to_all.30.parts_ref = bf16[8,64,256]{2,1,0:T(8,128)(2,1)S(1)} all-to-all(bf16[8,64,256]{2,1,0:T(8,128)(2,1)S(1)} %get-tuple-element.43), channel_id=1, replica_groups=mesh['branch'=8,'z'=16,'yh'=2,'core'=2] {'branch'}, dimensions={0} | all-to-all | bytes 524288 | tf_op jit(solution)/shard_map/all_to_all | solution.py:382
  64.3 7.8 %all_to_all.31.unit_ref = bf16[8,32,256]{2,1,0:T(8,128)(2,1)S(1)} all-to-all(bf16[8,32,256]{2,1,0:T(8,128)(2,1)S(1)} %slope.1), channel_id=1, replica_groups=mesh['branch'=8,'z'=16,'yh'=2,'core'=2] {'branch'}, dimensions={0} | all-to-all | bytes 262144 | tf_op jit(solution)/shard_map/all_to_all | solution.py:382
  72.3 1.3 collective-permute-start.10
  73.6 7.0 %collective-permute-start.9 = (bf16[128,256]{1,0:T(8,128)(2,1)S(1)}, bf16[128,256]{1,0:T(8,128)(2,1)S(1)}, u32[]{:S(2)}, u32[]{:S(2)}) collective-permute-start(bf16[128,256]{1,0:T(8,128)(2,1)S(1)} %get-tuple-element.45.refs_0_.x_ref), channel_id=1, source_target_pairs={{0,2},{1,3},{2,4},{3,5},{4,6},{5,7},{6,8},{7,9},{8,10},{9,11},{10,... | collective-permute-start | bytes 196616 | tf_op jit(solution)/shard_map/ppermute | solution.py:25
  82.0 4.7 %collective-permute-start.11 = (bf16[384,256]{1,0:T(8,128)(2,1)S(1)}, bf16[384,256]{1,0:T(8,128)(2,1)S(1)}, u32[]{:S(2)}, u32[]{:S(2)}) collective-permute-start(bf16[384,256]{1,0:T(8,128)(2,1)S(1)} %stack.9), channel_id=1, source_target_pairs={{0,1},{1,0},{2,3},{3,2},{4,5},{5,4},{6,7},{7,6},{8,9},{9,8},{10,11... | collective-permute-start | bytes 589832 | tf_op jit(solution)/shard_map/ppermute | solution.py:37
  87.8 3.9 %back.2 = (bf16[128,256]{1,0:T(8,128)(2,1)S(1)}, f32[64,256]{1,0:T(8,128)S(1)}, bf16[192,256]{1,0:T(8,128)(2,1)S(1)}) custom-call(bf16[128,256]{1,0:T(8,128)(2,1)S(1)} %get-tuple-element.45.refs_0_.x_ref, bf16[128,256]{1,0:T(8,128)(2,1)S(1)} %collective-permute-done.9.refs_1_.below_ref, bf16[128,256]{1,0:T(8,128)(2,1)S(1)} %collective-permute-done.10.refs_2_.above_ref, ...), custom_call_target="tpu_custom_call" | custom-call | tf_op jit(solution)/shard_map/back/pallas_call | solution.py:366
  93.0 7.0 %collective-permute-start.12 = (bf16[128,256]{1,0:T(8,128)(2,1)S(1)}, bf16[128,256]{1,0:T(8,128)(2,1)S(1)}, u32[]{:S(2)}, u32[]{:S(2)}) collective-permute-start(bf16[128,256]{1,0:T(8,128)(2,1)S(1)} %get-tuple-element.51.refs_0_.x_ref), channel_id=1, source_target_pairs={{0,2},{1,3},{2,4},{3,5},{4,6},{5,7},{6,8},{7,9},{8,10},{9,11},{10,... | collective-permute-start | bytes 196616 | tf_op jit(solution)/shard_map/ppermute | solution.py:25
  101.0 1.8 collective-permute-done.12.refs_1_.below_ref
  102.8 2.6 %collective-permute-start.14 = (bf16[384,256]{1,0:T(8,128)(2,1)S(1)}, bf16[384,256]{1,0:T(8,128)(2,1)S(1)}, u32[]{:S(2)}, u32[]{:S(2)}) collective-permute-start(bf16[384,256]{1,0:T(8,128)(2,1)S(1)} %stack.10), channel_id=1, source_target_pairs={{0,1},{1,0},{2,3},{3,2},{4,5},{5,4},{6,7},{7,6},{8,9},{9,8},{10,11... | collective-permute-start | bytes 589832 | tf_op jit(solution)/shard_map/ppermute | solution.py:37
  106.2 3.9 %back.3 = (bf16[128,256]{1,0:T(8,128)(2,1)S(1)}, f32[64,256]{1,0:T(8,128)S(1)}, bf16[192,256]{1,0:T(8,128)(2,1)S(1)}) custom-call(bf16[128,256]{1,0:T(8,128)(2,1)S(1)} %get-tuple-element.51.refs_0_.x_ref, bf16[128,256]{1,0:T(8,128)(2,1)S(1)} %collective-permute-done.12.refs_1_.below_ref, bf16[128,256]{1,0:T(8,128)(2,1)S(1)} %collective-permute-done.13.refs_2_.above_ref, ...), custom_call_target="tpu_custom_call" | custom-call | tf_op jit(solution)/shard_map/back/pallas_call | solution.py:366
  111.4 6.3 %collective-permute-start.15 = (bf16[128,256]{1,0:T(8,128)(2,1)S(1)}, bf16[128,256]{1,0:T(8,128)(2,1)S(1)}, u32[]{:S(2)}, u32[]{:S(2)}) collective-permute-start(bf16[128,256]{1,0:T(8,128)(2,1)S(1)} %get-tuple-element.58.refs_0_.x_ref), channel_id=1, source_target_pairs={{0,2},{1,3},{2,4},{3,5},{4,6},{5,7},{6,8},{7,9},{8,10},{9,11},{10,... | collective-permute-start | bytes 196616 | tf_op jit(solution)/shard_map/ppermute | solution.py:25
  118.8 1.7 collective-permute-done.15.refs_1_.below_ref
  120.5 2.4 %collective-permute-start.17 = (bf16[384,256]{1,0:T(8,128)(2,1)S(1)}, bf16[384,256]{1,0:T(8,128)(2,1)S(1)}, u32[]{:S(2)}, u32[]{:S(2)}) collective-permute-start(bf16[384,256]{1,0:T(8,128)(2,1)S(1)} %stack.11), channel_id=1, source_target_pairs={{0,1},{1,0},{2,3},{3,2},{4,5},{5,4},{6,7},{7,6},{8,9},{9,8},{10,11... | collective-permute-start | bytes 589832 | tf_op jit(solution)/shard_map/ppermute | solution.py:37
  124.0 1.7 lastback.1
  125.7 14.3 %all_to_all.32 = bf16[4,48,1152]{2,1,0:T(8,128)(2,1)S(1)} all-to-all(bf16[4,48,1152]{2,1,0:T(8,128)(2,1)S(1)} %bitcast.22), channel_id=1, replica_groups=mesh['branch'=8,'z'=16,'yh'=2,'core'=2] {'yh','core'}, dimensions={0} | all-to-all | bytes 884736 | tf_op jit(solution)/shard_map/all_to_all | solution.py:382
  140.1 32.8 %all_to_all.33 = bf16[16,4,8,128]{3,2,1,0:T(8,128)(2,1)S(1)} all-to-all(bf16[16,4,8,128]{3,2,1,0:T(8,128)(2,1)S(1)} %bitcast.27), channel_id=1, replica_groups=mesh['branch'=8,'z'=16,'yh'=2,'core'=2] {'z'}, dimensions={0} | all-to-all | bytes 262144 | tf_op jit(solution)/shard_map/all_to_all | solution.py:382
  173.0 17.7 %all_to_all.34 = bf16[16,4,8,128]{3,2,1,0:T(8,128)(2,1)S(1)} all-to-all(bf16[16,4,8,128]{3,2,1,0:T(8,128)(2,1)S(1)} %broadcast_in_dim.20), channel_id=1, replica_groups=mesh['branch'=8,'z'=16,'yh'=2,'core'=2] {'z'}, dimensions={0} | all-to-all | bytes 262144 | tf_op jit(solution)/shard_map/all_to_all | solution.py:382
  191.5 7.0 %all-to-all-start.5 = ((bf16[4,48,1152]{2,1,0:T(8,128)(2,1)}), bf16[4,48,1152]{2,1,0:T(8,128)(2,1)S(1)}, u32[]{:S(2)}, u32[]{:S(2)}) async-start(bf16[4,48,1152]{2,1,0:T(8,128)(2,1)} %broadcast_in_dim.22), calls=%async_computation.5 | async-start | bytes 884736 | tf_op jit(solution)/shard_map/all_to_all | solution.py:382
  198.5 2.5 %mapgrad.1 = bf16[64,256]{1,0:T(8,128)(2,1)} custom-call(bf16[192,256]{1,0:T(8,128)(2,1)S(1)} %get-tuple-element.67.low_ref, f32[64,256]{1,0:T(8,128)S(1)} %get-tuple-element.68.own_ref, bf16[2,64,576]{2,1,0:T(8,128)(2,1)S(1)} %get-tuple-element.36.refs_3_.w_ref.refs_1_, s32[80,256]{1,0:T(8,128)S(1)} %get-tuple-element.38.pos_ref.refs_2_), custom_call_target="tpu_custom_call" | custom-call | tf_op jit(solution)/shard_map/mapgrad/pallas_call | solution.py:366
  201.0 6.1 %all-to-all-done.5 = bf16[4,48,1152]{2,1,0:T(8,128)(2,1)S(1)} async-done(((bf16[4,48,1152]{2,1,0:T(8,128)(2,1)}), bf16[4,48,1152]{2,1,0:T(8,128)(2,1)S(1)}, u32[]{:S(2)}, u32[]{:S(2)}) %all-to-all-start.5) | async-done | bytes 442400 | tf_op jit(solution)/shard_map/all_to_all | solution.py:382
  207.1 1.5 final.1
  (49 shorter events, 21.7 us)
Async XLA Ops:
  0.6 51.7 %copy-start.4 = (bf16[256,64]{0,1:T(8,128)(2,1)S(1)}, bf16[256,64]{0,1:T(8,128)(2,1)}, u32[]{:S(2)}) copy-start(bf16[256,64]{0,1:T(8,128)(2,1)} %param.11) | copy-start | bytes 98308
  2.1 9.1 %collective-permute-start.1 = (bf16[112,256]{1,0:T(8,128)(2,1)}, bf16[112,256]{1,0:T(8,128)(2,1)S(1)}, u32[]{:S(2)}, u32[]{:S(2)}) collective-permute-start(bf16[112,256]{1,0:T(8,128)(2,1)} %pack.1.refs_0_.x_ref), channel_id=1, source_target_pairs={{2,0},{3,1},{4,2},{5,3},{6,4},{7,5},{8,6},{9,7},{10,8},{11,9},{12,... | collective-permute-start | bytes 172040 | tf_op jit(solution)/shard_map/ppermute | solution.py:25
  3.4 8.4 %collective-permute-start = (bf16[112,256]{1,0:T(8,128)(2,1)}, bf16[112,256]{1,0:T(8,128)(2,1)S(1)}, u32[]{:S(2)}, u32[]{:S(2)}) collective-permute-start(bf16[112,256]{1,0:T(8,128)(2,1)} %pack.1.refs_0_.x_ref), channel_id=1, source_target_pairs={{0,2},{1,3},{2,4},{3,5},{4,6},{5,7},{6,8},{7,9},{8,10},{9,11},{10,... | collective-permute-start | bytes 172040 | tf_op jit(solution)/shard_map/ppermute | solution.py:25
  9.7 1.2 copy-start.2
  10.9 21.4 %copy-start.3 = (bf16[9,32,256]{2,1,0:T(8,128)(2,1)S(1)}, bf16[9,32,256]{2,1,0:T(8,128)(2,1)}, u32[]{:S(2)}) copy-start(bf16[9,32,256]{2,1,0:T(8,128)(2,1)} %param.12) | copy-start | bytes 442372
  11.8 0.8 copy-start
  12.6 9.6 %collective-permute-start.2 = (bf16[336,256]{1,0:T(8,128)(2,1)S(1)}, bf16[336,256]{1,0:T(8,128)(2,1)S(1)}, u32[]{:S(2)}, u32[]{:S(2)}) collective-permute-start(bf16[336,256]{1,0:T(8,128)(2,1)S(1)} %stack.6), channel_id=1, source_target_pairs={{0,1},{1,0},{2,3},{3,2},{4,5},{5,4},{6,7},{7,6},{8,9},{9,8},{10,11... | collective-permute-start | bytes 516104 | tf_op jit(solution)/shard_map/ppermute | solution.py:37
  22.2 0.8 copy-start.1
  25.0 8.6 %collective-permute-start.4 = (bf16[64,256]{1,0:T(8,128)(2,1)S(1)}, bf16[64,256]{1,0:T(8,128)(2,1)S(1)}, u32[]{:S(2)}, u32[]{:S(2)}) collective-permute-start(bf16[64,256]{1,0:T(8,128)(2,1)S(1)} %get-tuple-element.37.refs_0_.x_ref), channel_id=1, source_target_pairs={{2,0},{3,1},{4,2},{5,3},{6,4},{7,5},{8,6},{9,7},{10,8},{11,9},{12,... | collective-permute-start | bytes 98312 | tf_op jit(solution)/shard_map/ppermute | solution.py:25
  26.3 7.3 %collective-permute-start.3 = (bf16[64,256]{1,0:T(8,128)(2,1)S(1)}, bf16[64,256]{1,0:T(8,128)(2,1)S(1)}, u32[]{:S(2)}, u32[]{:S(2)}) collective-permute-start(bf16[64,256]{1,0:T(8,128)(2,1)S(1)} %get-tuple-element.37.refs_0_.x_ref), channel_id=1, source_target_pairs={{0,2},{1,3},{2,4},{3,5},{4,6},{5,7},{6,8},{7,9},{8,10},{9,11},{10,... | collective-permute-start | bytes 98312 | tf_op jit(solution)/shard_map/ppermute | solution.py:25
  33.7 3.7 %collective-permute-start.5 = (bf16[192,256]{1,0:T(8,128)(2,1)S(1)}, bf16[192,256]{1,0:T(8,128)(2,1)S(1)}, u32[]{:S(2)}, u32[]{:S(2)}) collective-permute-start(bf16[192,256]{1,0:T(8,128)(2,1)S(1)} %stack.7), channel_id=1, source_target_pairs={{0,1},{1,0},{2,3},{3,2},{4,5},{5,4},{6,7},{7,6},{8,9},{9,8},{10,11... | collective-permute-start | bytes 294920 | tf_op jit(solution)/shard_map/ppermute | solution.py:37
  39.3 8.0 %collective-permute-start.7 = (bf16[64,256]{1,0:T(8,128)(2,1)S(1)}, bf16[64,256]{1,0:T(8,128)(2,1)S(1)}, u32[]{:S(2)}, u32[]{:S(2)}) collective-permute-start(bf16[64,256]{1,0:T(8,128)(2,1)S(1)} %get-tuple-element.41.refs_0_.x_ref), channel_id=1, source_target_pairs={{2,0},{3,1},{4,2},{5,3},{6,4},{7,5},{8,6},{9,7},{10,8},{11,9},{12,... | collective-permute-start | bytes 98312 | tf_op jit(solution)/shard_map/ppermute | solution.py:25
  40.6 7.7 %collective-permute-start.6 = (bf16[64,256]{1,0:T(8,128)(2,1)S(1)}, bf16[64,256]{1,0:T(8,128)(2,1)S(1)}, u32[]{:S(2)}, u32[]{:S(2)}) collective-permute-start(bf16[64,256]{1,0:T(8,128)(2,1)S(1)} %get-tuple-element.41.refs_0_.x_ref), channel_id=1, source_target_pairs={{0,2},{1,3},{2,4},{3,5},{4,6},{5,7},{6,8},{7,9},{8,10},{9,11},{10,... | collective-permute-start | bytes 98312 | tf_op jit(solution)/shard_map/ppermute | solution.py:25
  48.3 4.0 %collective-permute-start.8 = (bf16[192,256]{1,0:T(8,128)(2,1)S(1)}, bf16[192,256]{1,0:T(8,128)(2,1)S(1)}, u32[]{:S(2)}, u32[]{:S(2)}) collective-permute-start(bf16[192,256]{1,0:T(8,128)(2,1)S(1)} %stack.8), channel_id=1, source_target_pairs={{0,1},{1,0},{2,3},{3,2},{4,5},{5,4},{6,7},{7,6},{8,9},{9,8},{10,11... | collective-permute-start | bytes 294920 | tf_op jit(solution)/shard_map/ppermute | solution.py:37
  72.3 9.2 %collective-permute-start.10 = (bf16[128,256]{1,0:T(8,128)(2,1)S(1)}, bf16[128,256]{1,0:T(8,128)(2,1)S(1)}, u32[]{:S(2)}, u32[]{:S(2)}) collective-permute-start(bf16[128,256]{1,0:T(8,128)(2,1)S(1)} %get-tuple-element.45.refs_0_.x_ref), channel_id=1, source_target_pairs={{2,0},{3,1},{4,2},{5,3},{6,4},{7,5},{8,6},{9,7},{10,8},{11,9},{12,... | collective-permute-start | bytes 196616 | tf_op jit(solution)/shard_map/ppermute | solution.py:25
  73.6 8.5 %collective-permute-start.9 = (bf16[128,256]{1,0:T(8,128)(2,1)S(1)}, bf16[128,256]{1,0:T(8,128)(2,1)S(1)}, u32[]{:S(2)}, u32[]{:S(2)}) collective-permute-start(bf16[128,256]{1,0:T(8,128)(2,1)S(1)} %get-tuple-element.45.refs_0_.x_ref), channel_id=1, source_target_pairs={{0,2},{1,3},{2,4},{3,5},{4,6},{5,7},{6,8},{7,9},{8,10},{9,11},{10,... | collective-permute-start | bytes 196616 | tf_op jit(solution)/shard_map/ppermute | solution.py:25
  82.0 5.8 %collective-permute-start.11 = (bf16[384,256]{1,0:T(8,128)(2,1)S(1)}, bf16[384,256]{1,0:T(8,128)(2,1)S(1)}, u32[]{:S(2)}, u32[]{:S(2)}) collective-permute-start(bf16[384,256]{1,0:T(8,128)(2,1)S(1)} %stack.9), channel_id=1, source_target_pairs={{0,1},{1,0},{2,3},{3,2},{4,5},{5,4},{6,7},{7,6},{8,9},{9,8},{10,11... | collective-permute-start | bytes 589832 | tf_op jit(solution)/shard_map/ppermute | solution.py:37
  91.7 9.3 %collective-permute-start.13 = (bf16[128,256]{1,0:T(8,128)(2,1)S(1)}, bf16[128,256]{1,0:T(8,128)(2,1)S(1)}, u32[]{:S(2)}, u32[]{:S(2)}) collective-permute-start(bf16[128,256]{1,0:T(8,128)(2,1)S(1)} %get-tuple-element.51.refs_0_.x_ref), channel_id=1, source_target_pairs={{2,0},{3,1},{4,2},{5,3},{6,4},{7,5},{8,6},{9,7},{10,8},{11,9},{12,... | collective-permute-start | bytes 196616 | tf_op jit(solution)/shard_map/ppermute | solution.py:25
  93.0 9.8 %collective-permute-start.12 = (bf16[128,256]{1,0:T(8,128)(2,1)S(1)}, bf16[128,256]{1,0:T(8,128)(2,1)S(1)}, u32[]{:S(2)}, u32[]{:S(2)}) collective-permute-start(bf16[128,256]{1,0:T(8,128)(2,1)S(1)} %get-tuple-element.51.refs_0_.x_ref), channel_id=1, source_target_pairs={{0,2},{1,3},{2,4},{3,5},{4,6},{5,7},{6,8},{7,9},{8,10},{9,11},{10,... | collective-permute-start | bytes 196616 | tf_op jit(solution)/shard_map/ppermute | solution.py:25
  102.8 3.4 %collective-permute-start.14 = (bf16[384,256]{1,0:T(8,128)(2,1)S(1)}, bf16[384,256]{1,0:T(8,128)(2,1)S(1)}, u32[]{:S(2)}, u32[]{:S(2)}) collective-permute-start(bf16[384,256]{1,0:T(8,128)(2,1)S(1)} %stack.10), channel_id=1, source_target_pairs={{0,1},{1,0},{2,3},{3,2},{4,5},{5,4},{6,7},{7,6},{8,9},{9,8},{10,11... | collective-permute-start | bytes 589832 | tf_op jit(solution)/shard_map/ppermute | solution.py:37
  110.1 8.6 %collective-permute-start.16 = (bf16[128,256]{1,0:T(8,128)(2,1)S(1)}, bf16[128,256]{1,0:T(8,128)(2,1)S(1)}, u32[]{:S(2)}, u32[]{:S(2)}) collective-permute-start(bf16[128,256]{1,0:T(8,128)(2,1)S(1)} %get-tuple-element.58.refs_0_.x_ref), channel_id=1, source_target_pairs={{2,0},{3,1},{4,2},{5,3},{6,4},{7,5},{8,6},{9,7},{10,8},{11,9},{12,... | collective-permute-start | bytes 196616 | tf_op jit(solution)/shard_map/ppermute | solution.py:25
  111.4 9.1 %collective-permute-start.15 = (bf16[128,256]{1,0:T(8,128)(2,1)S(1)}, bf16[128,256]{1,0:T(8,128)(2,1)S(1)}, u32[]{:S(2)}, u32[]{:S(2)}) collective-permute-start(bf16[128,256]{1,0:T(8,128)(2,1)S(1)} %get-tuple-element.58.refs_0_.x_ref), channel_id=1, source_target_pairs={{0,2},{1,3},{2,4},{3,5},{4,6},{5,7},{6,8},{7,9},{8,10},{9,11},{10,... | collective-permute-start | bytes 196616 | tf_op jit(solution)/shard_map/ppermute | solution.py:25
  120.5 3.4 %collective-permute-start.17 = (bf16[384,256]{1,0:T(8,128)(2,1)S(1)}, bf16[384,256]{1,0:T(8,128)(2,1)S(1)}, u32[]{:S(2)}, u32[]{:S(2)}) collective-permute-start(bf16[384,256]{1,0:T(8,128)(2,1)S(1)} %stack.11), channel_id=1, source_target_pairs={{0,1},{1,0},{2,3},{3,2},{4,5},{5,4},{6,7},{7,6},{8,9},{9,8},{10,11... | collective-permute-start | bytes 589832 | tf_op jit(solution)/shard_map/ppermute | solution.py:37
  191.5 15.6 %all-to-all-start.5 = ((bf16[4,48,1152]{2,1,0:T(8,128)(2,1)}), bf16[4,48,1152]{2,1,0:T(8,128)(2,1)S(1)}, u32[]{:S(2)}, u32[]{:S(2)}) async-start(bf16[4,48,1152]{2,1,0:T(8,128)(2,1)} %broadcast_in_dim.22), calls=%async_computation.5 | async-start | bytes 884736 | tf_op jit(solution)/shard_map/all_to_all | solution.py:382

commit v5 on v4

v5 whole, which is shorter than its diff:
```python
import functools
import math

import jax
import jax.numpy as jnp
from jax import lax
from jax.experimental import pallas as pl
from jax.experimental.pallas import tpu as pltpu
from jax.sharding import Mesh, PartitionSpec as P

SKY = ("z", "yh", "core")
QUAD = ("yh", "core")
C = 64
R = 256
TAPS = 9
LIMIT = 16 * 1024 * 1024
F32 = jnp.float32
BF16 = jnp.bfloat16
VMEM = pl.BlockSpec(memory_space=pltpu.VMEM)
HBM = pl.BlockSpec(memory_space=pltpu.HBM)


def swap_cores(value):
    return lax.ppermute(value, "core", [(0, 1), (1, 0)])


def widen(value, after=()):
    peers = lax.axis_size(SKY)
    pairs = [(i, i + 2) for i in range(0, peers - 2, 2)] + [(i, i - 2) for i in range(3, peers, 2)]
    got = lax.ppermute(value, SKY, pairs)
    if after:
        got = call(
            relay_kernel, "relay",
            [v(got)] + [(pl.BlockSpec(memory_space=pl.ANY), x) for x in after],
            [sds(value.shape, value.dtype)],
        )[0]
    return got, swap_cores(got)


def relay_kernel(*refs):
    refs[-1][...] = refs[0][...]


def ordered(got, other):
    even = lax.axis_index("core") == 0
    return jnp.where(even, got, other), jnp.where(even, other, got)


def own_of(first, second):
    return jnp.where(lax.axis_index("core") == 0, first, second)


def fetch(pairs, sems):
    copies = [pltpu.make_async_copy(src, dst, sems.at[i]) for i, (src, dst) in enumerate(pairs)]
    for copy in copies:
        copy.start()
    for copy in copies:
        copy.wait()


def inner(other, first, even, start, size):
    own = other[start : start + size]
    below = other[first + start : first + start + size]
    above = other[2 * first + start : 2 * first + start + size]
    return jnp.where(even, below, own), jnp.where(even, own, above)


def slope_of(value, sigmoid):
    return sigmoid * (1.0 + value * (1.0 - sigmoid))


def low_onehot(low):
    return (lax.broadcasted_iota(jnp.int32, (R, R), 0) == low).astype(BF16)


def conv(blocks, pos, weight, picked_ref):
    stack = jnp.concatenate(blocks, axis=0)
    for k in range(TAPS):
        if k == 4:
            column = blocks[1]
        else:
            at = pos[k : k + 1]
            block = at >> 8
            found = jnp.dot(stack, low_onehot(at & 255), preferred_element_type=F32)
            column = jnp.where(
                block == 0,
                found[:C],
                jnp.where(block == 1, found[C : 2 * C], jnp.where(block == 2, found[2 * C :], 0.0)),
            ).astype(BF16)
        picked_ref[k * C : (k + 1) * C, :] = column
    return jnp.dot(weight, picked_ref[...], preferred_element_type=F32)


def spread(act, pos, weight, parts):
    terms = lax.dot_general(weight, act, (((0,), (0,)), ((), ())), preferred_element_type=F32)
    total = None
    for k in range(TAPS):
        if k == 4:
            continue
        at = pos[k : k + 1]
        block = at >> 8
        term = terms[k * C : (k + 1) * C].astype(BF16)
        zero = jnp.zeros_like(term)
        sent = jnp.concatenate([jnp.where(block == part, term, zero) for part in parts], axis=0)
        added = lax.dot_general(
            sent, low_onehot(at & 255), (((1,), (1,)), ((), ())), preferred_element_type=F32
        )
        total = added if total is None else total + added
    out = {part: total[i * C : (i + 1) * C] for i, part in enumerate(parts)}
    if 1 in out:
        out[1] = out[1] + terms[4 * C : 5 * C]
    return out


def two_layers(blocks, pos, kept, w_ref, picked_ref, slopes_ref, last_ref, scratch):
    middle = []
    for b in (1, 2, 3, 4):
        target = picked_ref.at[0, b - 2] if b in (2, 3) else scratch.at[b // 4]
        pre = conv(blocks[b - 1 : b + 2], pos[b], w_ref[0], target)
        sigmoid = jax.nn.sigmoid(pre)
        slopes_ref[b - 1] = slope_of(pre, sigmoid)
        middle.append((kept[b] * (blocks[b].astype(F32) + pre * sigmoid)).astype(BF16))
    hidden = []
    for b in (2, 3):
        pre = conv(middle[b - 2 : b + 1], pos[b], w_ref[1], picked_ref.at[1, b - 2])
        sigmoid = jax.nn.sigmoid(pre)
        last_ref[b - 2] = slope_of(pre, sigmoid)
        hidden.append((kept[b] * (middle[b - 1].astype(F32) + pre * sigmoid)).astype(BF16))
    return hidden


def pair_kernel(own_ref, other_ref, out_ref):
    size = own_ref.shape[0]
    own, other = own_ref[...], other_ref[...]
    out_ref[:size, :] = own_of(own, other)
    out_ref[size:, :] = own_of(other, own)


def first_kernel(
    x_ref, got_ref, other_ref, w_ref,
    h_ref, picked_ref, slopes_ref, last_ref, pos_ref, kept_ref, near_pos_ref, near_cot_ref, scratch,
):
    size = x_ref.shape[0] // 2
    below, above = ordered(got_ref[...], other_ref[...])
    packs = [below[:size], below[size:], x_ref[:size, :], x_ref[size:, :], above[:size], above[size:]]
    column = lax.broadcasted_iota(jnp.int32, (16, R), 1)
    pos, kept = [], []
    for b, pack in enumerate(packs):
        offset = pack[size - 16 :].astype(F32)
        at = jnp.where(offset > 400.0, 768, offset.astype(jnp.int32) + column + R)
        pos_ref[16 * b : 16 * (b + 1), :] = at
        keep = offset[TAPS : TAPS + 1]
        kept_ref[b : b + 1, :] = keep
        pos.append(at)
        kept.append(keep)
    kept_ref[6:8, :] = jnp.zeros((2, R), F32)
    each = size - 16 - C
    for i in range(3):
        near_pos_ref[16 * i : 16 * (i + 1), :] = own_of(pos[i + 1], pos[i + 2])
        near_cot_ref[each * i : each * (i + 1), :] = own_of(
            packs[i + 1][C : C + each], packs[i + 2][C : C + each]
        )
    blocks = [pack[:C] for pack in packs]
    hidden = two_layers(blocks, pos, kept, w_ref, picked_ref, slopes_ref, last_ref, scratch)
    for i in range(2):
        h_ref[i * C : (i + 1) * C, :] = hidden[i]


def read_tables(pos_ref, kept_ref):
    pos = [pos_ref[16 * b : 16 * b + 16, :] for b in range(6)]
    kept = [kept_ref[b : b + 1, :] for b in range(6)]
    return pos, kept


def read_blocks(x_ref, got_ref, other_ref):
    below, above = ordered(got_ref[...], other_ref[...])
    return [below[:C], below[C:], x_ref[:C, :], x_ref[C:, :], above[:C], above[C:]]


def layers_kernel(
    x_ref, got_ref, other_ref, w_ref, pos_ref, kept_ref,
    h_ref, picked_ref, slopes_ref, last_ref, scratch,
):
    pos, kept = read_tables(pos_ref, kept_ref)
    blocks = read_blocks(x_ref, got_ref, other_ref)
    hidden = two_layers(blocks, pos, kept, w_ref, picked_ref, slopes_ref, last_ref, scratch)
    for i in range(2):
        h_ref[i * C : (i + 1) * C, :] = hidden[i]


def last_layers_kernel(
    x_ref, got_ref, other_ref, w_ref, pos_ref, kept_ref, joinw_ref, unit_ref,
    share_ref, picked_ref, slopes_ref, last_ref, scratch,
):
    pos, kept = read_tables(pos_ref, kept_ref)
    blocks = read_blocks(x_ref, got_ref, other_ref)
    hidden = two_layers(blocks, pos, kept, w_ref, picked_ref, slopes_ref, last_ref, scratch)
    partial = lax.dot_general(
        joinw_ref[...], own_of(*hidden), (((0,), (0,)), ((), ())), preferred_element_type=F32
    ).astype(BF16)
    count = share_ref.shape[0]
    each = partial.shape[0] // count
    for c in range(count):
        share_ref[c, :each, :] = partial[c * each : (c + 1) * each]
        share_ref[c, each:, :] = unit_ref[c * each : (c + 1) * each, :]


def pack_kernel(
    maps_hbm, cot_hbm, near_hbm, foot_hbm, pack_ref, near_ref, foot_ref, sems
):
    each = cot_hbm.shape[0]
    fetch(
        [(near_hbm, near_ref), (foot_hbm, foot_ref), (maps_hbm, pack_ref.at[pl.ds(0, C)]),
         (cot_hbm, pack_ref.at[pl.ds(C, each)])], sems,
    )
    row = lax.axis_index(SKY) * R + lax.broadcasted_iota(jnp.int32, (TAPS, R), 1)
    near = near_ref[...]
    offset = jnp.where(near >= 0, near - row, 512).astype(F32)
    meta = jnp.concatenate(
        [offset, foot_ref[...].astype(F32), jnp.zeros((16 - TAPS - 1, R), F32)], axis=0
    )
    pack_ref[C + each :, :] = meta.astype(BF16)


def weights_kernel(w_hbm, *refs):
    outs, w_ref, sems = refs[:-2], refs[-2], refs[-1]
    fetch([(w_hbm, w_ref)], sems)
    for group, out_ref in enumerate(outs):
        for i in range(2):
            layer = 2 * group + i
            out_ref[i] = jnp.concatenate([w_ref[layer, k] for k in range(TAPS)], axis=1)


def unit_kernel(cot_ref, pos_ref, dec_ref, unit_ref, scratch):
    each = cot_ref.shape[0] // 3
    sources = [cot_ref[each * i : each * (i + 1), :] for i in range(3)]
    pos = [pos_ref[16 * i : 16 * (i + 1), :] for i in range(3)]
    for k in range(TAPS):
        if k == 4:
            scratch[k * each : (k + 1) * each, :] = sources[1]
            continue
        total = None
        for i in range(3):
            at = pos[i][k : k + 1]
            sent = jnp.where((at >> 8) == 2 - i, sources[i], jnp.zeros_like(sources[i]))
            added = lax.dot_general(
                sent, low_onehot(at & 255), (((1,), (1,)), ((), ())), preferred_element_type=F32
            )
            total = added if total is None else total + added
        scratch[k * each : (k + 1) * each, :] = total.astype(BF16)
    unit_ref[...] = lax.dot_general(
        dec_ref[...], scratch[...], (((0,), (0,)), ((), ())), preferred_element_type=F32
    ).astype(BF16)


def slope_kernel(parts_ref, out_ref):
    total = parts_ref[0].astype(F32)
    for i in range(1, parts_ref.shape[0]):
        total = total + parts_ref[i].astype(F32)
    each = total.shape[0] // 2
    joined = total[:each]
    slope = slope_of(joined, jax.nn.sigmoid(joined)).astype(BF16).astype(F32)
    grad = (total[each:] * slope).astype(BF16)
    for i in range(out_ref.shape[0]):
        out_ref[i] = grad


def head_kernel(unit_ref, joinw_ref, kept_ref, last_ref, pack_ref):
    unit_grad = jnp.concatenate([unit_ref[d] for d in range(unit_ref.shape[0])], axis=0)
    gradient = jnp.dot(joinw_ref[...], unit_grad, preferred_element_type=F32)
    masked = own_of(kept_ref[2:3, :], kept_ref[3:4, :]) * gradient
    pack_ref[:C, :] = (masked * own_of(last_ref[0], last_ref[1])).astype(BF16)
    pack_ref[C:, :] = masked.astype(BF16)


def store_pack(pack_ref, masked_ref, acts, masked):
    for i in range(2):
        pack_ref[i * C : (i + 1) * C, :] = acts[i]
        masked_ref[i] = masked[i]
    pack_ref[2 * C :, :] = own_of(masked[1], masked[0]).astype(BF16)


def top_kernel(own_ref, other_ref, pack_ref, masked_ref):
    own, other = own_ref[...], other_ref[...]
    first, second = own_of(own, other), own_of(other, own)
    store_pack(
        pack_ref, masked_ref, [first[:C], second[:C]],
        [first[C:].astype(F32), second[C:].astype(F32)],
    )


def weight_grad(acts, picked):
    total = None
    for i in range(2):
        added = lax.dot_general(
            own_of(acts[i][: C // 2], acts[i][C // 2 :]), picked[i],
            (((1,), (1,)), ((), ())), preferred_element_type=F32,
        )
        total = added if total is None else total + added
    return total.astype(BF16)


def pair_of(ref):
    return [ref[:C, :], ref[C : 2 * C, :]]


def both(ref, layer):
    return [ref[layer, 0], ref[layer, 1]]


def beside_kernel(has_low, *refs):
    if has_low:
        x_ref, w_ref, pos_ref, picked_ref, low_ref, low_picked_ref, own_ref, grad_ref = refs
        grad_ref[...] = jnp.concatenate(
            [weight_grad(pair_of(low_ref), both(low_picked_ref, 0)),
             weight_grad(pair_of(x_ref), both(picked_ref, 1))], axis=1,
        )
    else:
        x_ref, w_ref, pos_ref, picked_ref, own_ref, grad_ref = refs
        grad_ref[...] = weight_grad(pair_of(x_ref), both(picked_ref, 1))
    first, second = [
        spread(act, pos_ref[16 * b : 16 * b + 16, :], w_ref[1], (0, 1, 2))
        for b, act in zip((2, 3), pair_of(x_ref))
    ]
    own_ref[0] = first[0]
    own_ref[1] = first[1] + second[0]
    own_ref[2] = first[2] + second[1]
    own_ref[3] = second[2]


def upper_layer(
    x_ref, got_ref, other_ref, masked_ref, own_ref, w_ref, pos_ref, kept_ref, slopes_ref
):
    pos, kept = read_tables(pos_ref, kept_ref)
    below, above = ordered(got_ref[...], other_ref[...])
    acts = {0: below[:C], 1: below[C : 2 * C], 4: above[:C], 5: above[C : 2 * C]}
    masked = [
        below[2 * C :].astype(F32), masked_ref[0], masked_ref[1], above[2 * C :].astype(F32)
    ]
    gradient = [masked[i] + own_ref[i] for i in range(4)]
    for b, parts in ((0, (2,)), (1, (1, 2)), (4, (0, 1)), (5, (0,))):
        for part, value in spread(acts[b], pos[b], w_ref[1], parts).items():
            gradient[b + part - 2] = gradient[b + part - 2] + value
    lower = [kept[i + 1] * gradient[i] for i in range(4)]
    low_acts = [(lower[i] * slopes_ref[i]).astype(BF16) for i in range(4)]
    return lower, low_acts


def back_kernel(
    x_ref, got_ref, other_ref, masked_ref, own_ref, w_ref, pos_ref, kept_ref, slopes_ref, next_ref,
    pack_ref, out_ref, low_ref,
):
    lower, low_acts = upper_layer(
        x_ref, got_ref, other_ref, masked_ref, own_ref, w_ref, pos_ref, kept_ref, slopes_ref
    )
    pos, kept = read_tables(pos_ref, kept_ref)
    result = [lower[1], lower[2]]
    for b, parts in ((1, (2,)), (2, (1, 2)), (3, (0, 1)), (4, (0,))):
        for part, value in spread(low_acts[b - 1], pos[b], w_ref[0], parts).items():
            result[b + part - 3] = result[b + part - 3] + value
    masked = [kept[2 + i] * result[i] for i in range(2)]
    acts = [(masked[i] * next_ref[i]).astype(BF16) for i in range(2)]
    store_pack(pack_ref, out_ref, acts, masked)
    for i in range(2):
        low_ref[i * C : (i + 1) * C, :] = low_acts[1 + i]


def last_back_kernel(
    x_ref, got_ref, other_ref, masked_ref, own_ref, w_ref, pos_ref, kept_ref, slopes_ref,
    picked_ref, grad5_ref, grad43_ref, grad21_ref, low_ref, out_ref, keep_ref, send_ref,
):
    lower, low_acts = upper_layer(
        x_ref, got_ref, other_ref, masked_ref, own_ref, w_ref, pos_ref, kept_ref, slopes_ref
    )
    out_ref[...] = own_of(lower[1], lower[2])
    for i in range(3):
        low_ref[i * C : (i + 1) * C, :] = own_of(low_acts[i], low_acts[i + 1])
    last = jnp.concatenate(
        [weight_grad(low_acts[1:3], both(picked_ref, 0)), grad5_ref[...]], axis=1
    )
    middle = grad21_ref[...]
    first = jnp.concatenate([grad43_ref[...], middle[: C // 4]], axis=0)
    second = jnp.concatenate([middle[C // 4 :], last], axis=0)
    low_half = lax.axis_index("yh") == 0
    keep_ref[...] = jnp.where(low_half, first, second)
    send_ref[...] = jnp.where(low_half, second, first)


def map_kernel(low_ref, own_ref, w_ref, pos_ref, map_ref):
    own = own_ref[...]
    for i, part in ((0, 2), (1, 1), (2, 0)):
        act = low_ref[i * C : (i + 1) * C, :]
        own = own + spread(act, pos_ref[16 * i : 16 * (i + 1), :], w_ref[0], (part,))[part]
    map_ref[...] = own.astype(BF16)


def final_kernel(scale, sum_ref, out_ref):
    wide = TAPS * C
    half_rows = C // 2
    for core in range(2):
        rows = jnp.concatenate([sum_ref[core], sum_ref[2 + core]], axis=0).astype(F32) * scale
        for slot, pair in enumerate(((4, 3), (2, 1), (0, 5))):
            for half, layer in enumerate(pair):
                for k in range(TAPS):
                    at = half * wide + k * C
                    out_ref[layer, k, core * half_rows : (core + 1) * half_rows, :] = rows[
                        slot * half_rows : (slot + 1) * half_rows, at : at + C
                    ]


def sds(shape, dtype):
    return jax.ShapeDtypeStruct(shape, dtype)


def call(body, name, ins, outs, scratch=(), limit=LIMIT):
    specs = [spec for spec, _ in ins]
    return pl.pallas_call(
        body,
        name=name,
        in_specs=specs,
        out_specs=[pl.BlockSpec(memory_space=pltpu.VMEM) for _ in outs],
        out_shape=outs,
        scratch_shapes=list(scratch),
        compiler_params=pltpu.CompilerParams(vmem_limit_bytes=limit),
    )(*[value for _, value in ins])


def v(value):
    return (VMEM, value)


def exchange(value, axes):
    return lax.all_to_all(value, axes, 0, 0, tiled=True)


def add_up(parts):
    return jnp.sum(parts.astype(F32), axis=0).astype(BF16)


def copies(value, count):
    return jnp.broadcast_to(value[None], (count,) + value.shape)


def sum_over_sky(keep, send, quads, length):
    rows, lanes = keep.shape
    got = lax.ppermute(send, "yh", [(0, 1), (1, 0)])
    chunk = (keep.astype(F32) + got.astype(F32)).astype(BF16)
    tiles = (rows // 8) * (lanes // 128)
    each = -(-tiles // length)
    chunk = chunk.reshape(rows // 8, 8, lanes // 128, 128).transpose(0, 2, 1, 3)
    chunk = jnp.pad(chunk.reshape(tiles, 8, 128), ((0, each * length - tiles), (0, 0), (0, 0)))
    chunk = add_up(exchange(chunk.reshape(length, each, 8, 128), "z"))
    chunk = exchange(copies(chunk, length), "z").reshape(each * length, 8, 128)[:tiles]
    chunk = chunk.reshape(rows // 8, lanes // 128, 8, 128).transpose(0, 2, 1, 3)
    return exchange(copies(chunk.reshape(rows, lanes), quads), QUAD)


def per_device(sky_maps, footprint, neighbours, enc_weight, join_weight, dec_weight, cotangent):
    depth = enc_weight.shape[1]
    branches = lax.axis_size("branch")
    peers = lax.axis_size(SKY)
    dma = pltpu.SemaphoreType.DMA
    weights = call(
        weights_kernel, "weights", [(HBM, enc_weight[0])],
        [sds((2, C, TAPS * C), BF16)] * (depth // 2),
        [pltpu.VMEM(enc_weight.shape[1:], BF16), dma((1,))],
    )
    joinw = join_weight.T
    dec = dec_weight.reshape(-1, dec_weight.shape[2])
    each = cotangent.shape[0]
    full = dec.shape[1]
    wide = TAPS * C
    size = C + each + 16
    pack = call(
        pack_kernel, "pack",
        [(HBM, sky_maps[0]), (HBM, cotangent), (HBM, neighbours), (HBM, footprint)],
        [sds((size, R), BF16)],
        [pltpu.VMEM((TAPS, R), jnp.int32), pltpu.VMEM((1, R), jnp.int32), dma((4,))], None,
    )[0]
    pack = call(
        pair_kernel, "pair", [v(pack), v(swap_cores(pack))], [sds((2 * size, R), BF16)]
    )[0]
    pair = sds((2, C, R), F32)
    layer_outs = [sds((2 * C, R), BF16), sds((2, 2, wide, R), BF16), sds((4, C, R), F32), pair]
    scratch = [pltpu.VMEM((2, wide, R), BF16)]
    got, other = widen(pack, [weights[0]])
    hidden, picked, slopes, last, pos, kept, near_pos, near_cot = call(
        first_kernel, "layers01", [v(pack), v(got), v(other), v(weights[0])],
        layer_outs
        + [sds((96, R), jnp.int32), sds((8, R), F32), sds((48, R), jnp.int32),
           sds((3 * each, R), BF16)],
        scratch,
    )
    saved = [(picked, slopes, last)]
    unit = call(
        unit_kernel, "unit", [v(near_cot), v(near_pos), v(dec)],
        [sds((full, R), BF16)], [pltpu.VMEM((TAPS * each, R), BF16)],
    )[0]
    for group in range(1, depth // 2):
        got, other = widen(hidden, [unit] if group == 1 else ())
        ins = [v(hidden), v(got), v(other), v(weights[group]), v(pos), v(kept)]
        if group < depth // 2 - 1:
            hidden, picked, slopes, last = call(layers_kernel, "layers", ins, layer_outs, scratch)
        else:
            share, picked, slopes, last = call(
                last_layers_kernel, "lastlayers", ins + [v(joinw), v(unit)],
                [sds((branches, 2 * each, R), BF16)] + layer_outs[1:], scratch,
            )
        saved.append((picked, slopes, last))
    parts = exchange(share, "branch")
    mine = call(slope_kernel, "slope", [v(parts)], [sds((branches, each, R), BF16)])[0]
    top = call(
        head_kernel, "head",
        [v(exchange(mine, "branch")), v(joinw), v(kept), v(saved[-1][2])], [sds((2 * C, R), BF16)],
    )[0]
    pack_outs = [sds((3 * C, R), BF16), pair]
    pack, masked = call(top_kernel, "top", [v(top), v(swap_cores(top))], pack_outs)
    grads = []
    low = None
    for group in reversed(range(depth // 2)):
        picked, slopes, _ = saved[group]
        beside = [v(pack), v(weights[group]), v(pos), v(picked)]
        if low is not None:
            beside = beside + [v(low), v(saved[group + 1][0])]
        own, grad = call(
            functools.partial(beside_kernel, low is not None), "beside", beside,
            [sds((4, C, R), F32), sds((C // 2, wide if low is None else 2 * wide), BF16)],
        )
        grads.append(grad)
        got, other = widen(pack, [own])
        ins = [
            v(pack), v(got), v(other), v(masked), v(own), v(weights[group]), v(pos), v(kept),
            v(slopes),
        ]
        if group:
            pack, masked, low = call(
                back_kernel, "back", ins + [v(saved[group - 1][2])],
                pack_outs + [sds((2 * C, R), BF16)],
            )
        else:
            half = sds((3 * C // 4, 2 * wide), BF16)
            low, own, keep, send = call(
                last_back_kernel, "lastback", ins + [v(picked)] + [v(g) for g in grads],
                [sds((3 * C, R), BF16), sds((C, R), F32), half, half],
            )
    map_grads = call(
        map_kernel, "mapgrad", [v(low), v(own), v(weights[0]), v(near_pos)], [sds((C, R), BF16)]
    )[0]
    total = sum_over_sky(keep, send, lax.axis_size(QUAD), lax.axis_size("z"))
    summed = call(
        functools.partial(final_kernel, 1.0 / math.sqrt(R * peers)), "final", [v(total)],
        [sds((depth, TAPS, C, C), F32)],
    )[0]
    return map_grads[None], summed[None]


def solution(mesh):
    branches, sky = mesh.devices.shape
    mesh = Mesh(mesh.devices.reshape(branches, sky // 4, 2, 2), ("branch",) + SKY)
    in_specs = (
        P("branch", None, SKY),
        P("branch", SKY),
        P(None, SKY),
        P("branch", None, None, None, None),
        P(None, "branch"),
        P(None, "branch", None),
        P("branch", SKY),
    )
    out_specs = (P("branch", None, SKY), P("branch", None, None, None, None))
    return jax.shard_map(
        per_device, mesh=mesh, in_specs=in_specs, out_specs=out_specs, check_vma=False
    )
```

time: 210 us -> 202 us (0.962)
  waiting for transfers between devices: 17.6 us -> 45 us
  starting transfers between devices: 78.1 us -> 51.6 us
  blocking collectives: 82.5 us -> 69.5 us
  Pallas kernels: 25.7 us -> 31.5 us
    ppermute x18 -> x15, waiting for transfers between devices: 11.4 us -> 38.8 us  [the longest x6 27.8 us: widen(): got = lax.ppermute(value, SKY, pairs)]
    ppermute x18 -> x15, starting transfers between devices: 71.1 us -> 44.4 us  [the longest x8 30.8 us: swap_cores(): return lax.ppermute(value, 'core', [(0, 1), (1, 0)])]
    all_to_all x5 -> x4, blocking collectives: 82.5 us -> 69.5 us  [exchange(): return lax.all_to_all(value, axes, 0, 0, tiled=True)]
    pallas_call x22 -> x23, Pallas kernels: 25.7 us -> 31.5 us  [call(): pl.pallas_call(body, name=name, in_specs=specs, out_specs=[pl.BlockSpec(m...]
  transfers between devices with their start and end apart: 19 -> 16, of which waited for: 12 -> 16; matrix products, arithmetic and copies ran while one was open for 0% -> 0% of each run, Pallas kernels for 3% -> 5%
where the time goes in v5:
time: 202 us; the launch traced here: 201 us
  blocking collectives  69.5 us (34%)
  starting transfers between devices  51.6 us (26%)
  waiting for transfers between devices  45 us (22%)
  Pallas kernels  31.5 us (16%)
  local copies, waits for them, and re-layouts  2.83 us (1%)
    all_to_all x4, blocking collectives, exchange(): return lax.all_to_all(value, axes, 0, 0, tiled=True)  69.5 us
    pallas_call x23, Pallas kernels, call(): pl.pallas_call(body, name=name, in_specs=specs, out_specs=[pl.BlockSpec(m...  31.5 us
    ppermute x8, starting transfers between devices, swap_cores(): return lax.ppermute(value, 'core', [(0, 1), (1, 0)])  30.8 us
    ppermute x6, waiting for transfers between devices, widen(): got = lax.ppermute(value, SKY, pairs)  27.8 us
    ppermute x8, waiting for transfers between devices, swap_cores(): return lax.ppermute(value, 'core', [(0, 1), (1, 0)])  7.94 us
    ppermute x6, starting transfers between devices, widen(): got = lax.ppermute(value, SKY, pairs)  7.88 us
    all_to_all x1, starting transfers between devices, exchange(): return lax.all_to_all(value, axes, 0, 0, tiled=True)  7.26 us
    all_to_all x1, waiting for transfers between devices, exchange(): return lax.all_to_all(value, axes, 0, 0, tiled=True)  6.13 us
  transfers between devices with their start and end apart: 16, of which 16 were waited for; matrix products, arithmetic and copies ran while one was open for 0% of the time, Pallas kernels for 5%

profile of v5, /device:TPU:1, one launch (start us, length us, event | category | flops | bytes accessed | tf_op | source)
XLA Modules:
  0.0 201.4 jit_solution(15157081111283852414)
XLA Ops:
  2.1 8.8 %collective-permute-start = (bf16[112,256]{1,0:T(8,128)(2,1)}, bf16[112,256]{1,0:T(8,128)(2,1)S(1)}, u32[]{:S(2)}, u32[]{:S(2)}) collective-permute-start(bf16[112,256]{1,0:T(8,128)(2,1)} %pack.1.own_ref), channel_id=1, source_target_pairs={{0,1},{1,0},{2,3},{3,2},{4,5},{5,4},{6,7},{7,6},{8,9},{9,8},{10,11... | collective-permute-start | bytes 172040 | tf_op jit(solution)/shard_map/ppermute | solution.py:24
  15.8 4.2 %collective-permute-done.1.refs_0_ = bf16[224,256]{1,0:T(8,128)(2,1)S(1)} collective-permute-done((bf16[224,256]{1,0:T(8,128)(2,1)S(1)}, bf16[224,256]{1,0:T(8,128)(2,1)S(1)}, u32[]{:S(2)}, u32[]{:S(2)}) %collective-permute-start.1) | collective-permute-done | bytes 114720 | tf_op jit(solution)/shard_map/ppermute | solution.py:30
  20.0 1.9 collective-permute-start.2
  23.2 2.6 %layers01.1 = (bf16[128,256]{1,0:T(8,128)(2,1)S(1)}, bf16[2,2,576,256]{3,2,1,0:T(8,128)(2,1)S(1)}, f32[4,64,256]{2,1,0:T(8,128)S(1)}, f32[2,64,256]{2,1,0:T(8,12...) custom-call(bf16[224,256]{1,0:T(8,128)(2,1)S(1)} %pair.1.x_ref, ...), custom_call_target="tpu_custom_call" | custom-call | tf_op jit(solution)/shard_map/layers01/pallas_call | solution.py:417
  28.4 3.9 %collective-permute-done.3.refs_0_ = bf16[128,256]{1,0:T(8,128)(2,1)S(1)} collective-permute-done((bf16[128,256]{1,0:T(8,128)(2,1)S(1)}, bf16[128,256]{1,0:T(8,128)(2,1)S(1)}, u32[]{:S(2)}, u32[]{:S(2)}) %collective-permute-start.3) | collective-permute-done | bytes 65568 | tf_op jit(solution)/shard_map/ppermute | solution.py:30
  32.3 1.9 collective-permute-start.4
  35.4 2.6 %layers.1 = (bf16[128,256]{1,0:T(8,128)(2,1)S(1)}, bf16[2,2,576,256]{3,2,1,0:T(8,128)(2,1)S(1)}, f32[4,64,256]{2,1,0:T(8,128)S(1)}, f32[2,64,256]{2,1,0:T(8,128)S(1)}) custom-call(bf16[128,256]{1,0:T(8,128)(2,1)S(1)} %get-tuple-element.40.x_ref, bf16[128,256]{1,0:T(8,128)(2,1)S(1)} %relay.6.got_ref, bf16[128,256]{1,0:T(8,128)(2,1)S(1)} %collective-permute-done.4.other_ref, ...), custom_call_target="tpu_custom_call" | custom-call | tf_op jit(solution)/shard_map/layers/pallas_call | solution.py:417
  39.3 5.2 %collective-permute-done.5.got_ref = bf16[128,256]{1,0:T(8,128)(2,1)S(1)} collective-permute-done((bf16[128,256]{1,0:T(8,128)(2,1)S(1)}, bf16[128,256]{1,0:T(8,128)(2,1)S(1)}, u32[]{:S(2)}, u32[]{:S(2)}) %collective-permute-start.5) | collective-permute-done | bytes 65568 | tf_op jit(solution)/shard_map/ppermute | solution.py:30
  44.5 2.5 %collective-permute-start.6 = (bf16[128,256]{1,0:T(8,128)(2,1)S(1)}, bf16[128,256]{1,0:T(8,128)(2,1)S(1)}, u32[]{:S(2)}, u32[]{:S(2)}) collective-permute-start(bf16[128,256]{1,0:T(8,128)(2,1)S(1)} %collective-permute-done.5.got_ref), channel_id=1, source_target_pairs={{0,1},{1,0},{2,3},{3,2},{4,5},{5,4},{6,7},{7,6},{8,9},{9,8},{10,11... | collective-permute-start | bytes 196616 | tf_op jit(solution)/shard_map/ppermute | solution.py:24
  48.0 2.7 %lastlayers.1 = (bf16[8,64,256]{2,1,0:T(8,128)(2,1)S(1)}, bf16[2,2,576,256]{3,2,1,0:T(8,128)(2,1)S(1)}, f32[4,64,256]{2,1,0:T(8,128)S(1)}, f32[2,64,256]{2,1,0:T(8,128)S(1)}) custom-call(bf16[128,256]{1,0:T(8,128)(2,1)S(1)} %get-tuple-element.46.x_ref, bf16[128,256]{1,0:T(8,128)(2,1)S(1)} %collective-permute-done.5.got_ref, ...), custom_call_target="tpu_custom_call" | custom-call | tf_op jit(solution)/shard_map/lastlayers/pallas_call | solution.py:417
  50.7 10.6 %all_to_all.25.parts_ref = bf16[8,64,256]{2,1,0:T(8,128)(2,1)S(1)} all-to-all(bf16[8,64,256]{2,1,0:T(8,128)(2,1)S(1)} %get-tuple-element.48), channel_id=1, replica_groups=mesh['branch'=8,'z'=16,'yh'=2,'core'=2] {'branch'}, dimensions={0} | all-to-all | bytes 524288 | tf_op jit(solution)/shard_map/all_to_all | solution.py:433
  61.4 7.8 %all_to_all.26.unit_ref = bf16[8,32,256]{2,1,0:T(8,128)(2,1)S(1)} all-to-all(bf16[8,32,256]{2,1,0:T(8,128)(2,1)S(1)} %slope.1), channel_id=1, replica_groups=mesh['branch'=8,'z'=16,'yh'=2,'core'=2] {'branch'}, dimensions={0} | all-to-all | bytes 262144 | tf_op jit(solution)/shard_map/all_to_all | solution.py:433
  69.4 4.4 %collective-permute-start.7 = (bf16[128,256]{1,0:T(8,128)(2,1)S(1)}, bf16[128,256]{1,0:T(8,128)(2,1)S(1)}, u32[]{:S(2)}, u32[]{:S(2)}) collective-permute-start(bf16[128,256]{1,0:T(8,128)(2,1)S(1)} %head.1.own_ref), channel_id=1, source_target_pairs={{0,1},{1,0},{2,3},{3,2},{4,5},{5,4},{6,7},{7,6},{8,9},{9,8},{10,11... | collective-permute-start | bytes 196616 | tf_op jit(solution)/shard_map/ppermute | solution.py:24
  77.4 5.5 %collective-permute-done.8.refs_0_ = bf16[192,256]{1,0:T(8,128)(2,1)S(1)} collective-permute-done((bf16[192,256]{1,0:T(8,128)(2,1)S(1)}, bf16[192,256]{1,0:T(8,128)(2,1)S(1)}, u32[]{:S(2)}, u32[]{:S(2)}) %collective-permute-start.8) | collective-permute-done | bytes 98336 | tf_op jit(solution)/shard_map/ppermute | solution.py:30
  82.9 3.9 %collective-permute-start.9 = (bf16[192,256]{1,0:T(8,128)(2,1)S(1)}, bf16[192,256]{1,0:T(8,128)(2,1)S(1)}, u32[]{:S(2)}, u32[]{:S(2)}) collective-permute-start(bf16[192,256]{1,0:T(8,128)(2,1)S(1)} %relay.7.got_ref), channel_id=1, source_target_pairs={{0,1},{1,0},{2,3},{3,2},{4,5},{5,4},{6,7},{7,6},{8,9},{9,8},{10,11... | collective-permute-start | bytes 294920 | tf_op jit(solution)/shard_map/ppermute | solution.py:24
  87.5 4.7 %back.2 = (bf16[192,256]{1,0:T(8,128)(2,1)S(1)}, f32[2,64,256]{2,1,0:T(8,128)S(1)}, bf16[128,256]{1,0:T(8,128)(2,1)S(1)}) custom-call(bf16[192,256]{1,0:T(8,128)(2,1)S(1)} %get-tuple-element.50.refs_0_.x_ref, bf16[192,256]{1,0:T(8,128)(2,1)S(1)} %relay.7.got_ref, bf16[192,256]{1,0:T(8,128)(2,1)S(1)} %collective-permute-done.9.other_ref, ...), custom_call_target="tpu_custom_call" | custom-call | tf_op jit(solution)/shard_map/back/pallas_call | solution.py:417
  93.5 1.8 beside.4
  95.3 4.5 %collective-permute-done.10.refs_0_ = bf16[192,256]{1,0:T(8,128)(2,1)S(1)} collective-permute-done((bf16[192,256]{1,0:T(8,128)(2,1)S(1)}, bf16[192,256]{1,0:T(8,128)(2,1)S(1)}, u32[]{:S(2)}, u32[]{:S(2)}) %collective-permute-start.10) | collective-permute-done | bytes 98336 | tf_op jit(solution)/shard_map/ppermute | solution.py:30
  99.8 3.7 %collective-permute-start.11 = (bf16[192,256]{1,0:T(8,128)(2,1)S(1)}, bf16[192,256]{1,0:T(8,128)(2,1)S(1)}, u32[]{:S(2)}, u32[]{:S(2)}) collective-permute-start(bf16[192,256]{1,0:T(8,128)(2,1)S(1)} %relay.8.got_ref), channel_id=1, source_target_pairs={{0,1},{1,0},{2,3},{3,2},{4,5},{5,4},{6,7},{7,6},{8,9},{9,8},{10,11... | collective-permute-start | bytes 294920 | tf_op jit(solution)/shard_map/ppermute | solution.py:24
  104.5 4.7 %back.3 = (bf16[192,256]{1,0:T(8,128)(2,1)S(1)}, f32[2,64,256]{2,1,0:T(8,128)S(1)}, bf16[128,256]{1,0:T(8,128)(2,1)S(1)}) custom-call(bf16[192,256]{1,0:T(8,128)(2,1)S(1)} %get-tuple-element.56.refs_0_.x_ref, bf16[192,256]{1,0:T(8,128)(2,1)S(1)} %relay.8.got_ref, bf16[192,256]{1,0:T(8,128)(2,1)S(1)} %collective-permute-done.11.other_ref, ...), custom_call_target="tpu_custom_call" | custom-call | tf_op jit(solution)/shard_map/back/pallas_call | solution.py:417
  110.4 1.8 beside.5
  112.3 4.5 %collective-permute-done.12.refs_0_ = bf16[192,256]{1,0:T(8,128)(2,1)S(1)} collective-permute-done((bf16[192,256]{1,0:T(8,128)(2,1)S(1)}, bf16[192,256]{1,0:T(8,128)(2,1)S(1)}, u32[]{:S(2)}, u32[]{:S(2)}) %collective-permute-start.12) | collective-permute-done | bytes 98336 | tf_op jit(solution)/shard_map/ppermute | solution.py:30
  116.8 3.7 %collective-permute-start.13 = (bf16[192,256]{1,0:T(8,128)(2,1)S(1)}, bf16[192,256]{1,0:T(8,128)(2,1)S(1)}, u32[]{:S(2)}, u32[]{:S(2)}) collective-permute-start(bf16[192,256]{1,0:T(8,128)(2,1)S(1)} %relay.9.got_ref), channel_id=1, source_target_pairs={{0,1},{1,0},{2,3},{3,2},{4,5},{5,4},{6,7},{7,6},{8,9},{9,8},{10,11... | collective-permute-start | bytes 294920 | tf_op jit(solution)/shard_map/ppermute | solution.py:24
  121.4 1.8 lastback.1
  123.3 5.6 %collective-permute-start.14 = (bf16[48,1152]{1,0:T(8,128)(2,1)S(1)}, bf16[48,1152]{1,0:T(8,128)(2,1)S(1)}, u32[]{:S(2)}, u32[]{:S(2)}) collective-permute-start(bf16[48,1152]{1,0:T(8,128)(2,1)S(1)} %get-tuple-element.75), channel_id=1, source_target_pairs={{0,2},{2,0},{1,3},{3,1},{4,6},{6,4},{5,7},{7,5},{8,10},{10,8},{9,1... | collective-permute-start | bytes 331784 | tf_op jit(solution)/shard_map/ppermute | solution.py:446
  128.9 3.1 %collective-permute-done.14 = bf16[48,1152]{1,0:T(8,128)(2,1)S(1)} collective-permute-done((bf16[48,1152]{1,0:T(8,128)(2,1)S(1)}, bf16[48,1152]{1,0:T(8,128)(2,1)S(1)}, u32[]{:S(2)}, u32[]{:S(2)}) %collective-permute-start.14) | collective-permute-done | bytes 110624 | tf_op jit(solution)/shard_map/ppermute | solution.py:446
  132.1 33.6 %all_to_all.27 = bf16[16,4,8,128]{3,2,1,0:T(8,128)(2,1)S(1)} all-to-all(bf16[16,4,8,128]{3,2,1,0:T(8,128)(2,1)S(1)} %bitcast.23), channel_id=1, replica_groups=mesh['branch'=8,'z'=16,'yh'=2,'core'=2] {'z'}, dimensions={0} | all-to-all | bytes 262144 | tf_op jit(solution)/shard_map/all_to_all | solution.py:433
  165.7 17.5 %all_to_all.28 = bf16[16,4,8,128]{3,2,1,0:T(8,128)(2,1)S(1)} all-to-all(bf16[16,4,8,128]{3,2,1,0:T(8,128)(2,1)S(1)} %broadcast_in_dim.20), channel_id=1, replica_groups=mesh['branch'=8,'z'=16,'yh'=2,'core'=2] {'z'}, dimensions={0} | all-to-all | bytes 262144 | tf_op jit(solution)/shard_map/all_to_all | solution.py:433
  184.0 7.3 %all-to-all-start.4 = ((bf16[4,48,1152]{2,1,0:T(8,128)(2,1)}), bf16[4,48,1152]{2,1,0:T(8,128)(2,1)S(1)}, u32[]{:S(2)}, u32[]{:S(2)}) async-start(bf16[4,48,1152]{2,1,0:T(8,128)(2,1)} %broadcast_in_dim.22), calls=%async_computation.4 | async-start | bytes 884736 | tf_op jit(solution)/shard_map/all_to_all | solution.py:433
  191.3 2.5 %mapgrad.1 = bf16[64,256]{1,0:T(8,128)(2,1)} custom-call(bf16[192,256]{1,0:T(8,128)(2,1)S(1)} %get-tuple-element.72.low_ref, f32[64,256]{1,0:T(8,128)S(1)} %get-tuple-element.73.own_ref, bf16[2,64,576]{2,1,0:T(8,128)(2,1)S(1)} %get-tuple-element.39.refs_1_.w_ref, s32[48,256]{1,0:T(8,128)S(1)} %get-tuple-element.42.pos_ref), custom_call_target="tpu_custom_call" | custom-call | tf_op jit(solution)/shard_map/mapgrad/pallas_call | solution.py:417
  193.7 6.1 %all-to-all-done.4.sum_ref = bf16[4,48,1152]{2,1,0:T(8,128)(2,1)S(1)} async-done(((bf16[4,48,1152]{2,1,0:T(8,128)(2,1)}), bf16[4,48,1152]{2,1,0:T(8,128)(2,1)S(1)}, u32[]{:S(2)}, u32[]{:S(2)}) %all-to-all-start.4) | async-done | bytes 442400 | tf_op jit(solution)/shard_map/all_to_all | solution.py:433
  199.9 1.5 final.1
  (41 shorter events, 23.5 us)
Async XLA Ops:
  2.1 9.9 %collective-permute-start = (bf16[112,256]{1,0:T(8,128)(2,1)}, bf16[112,256]{1,0:T(8,128)(2,1)S(1)}, u32[]{:S(2)}, u32[]{:S(2)}) collective-permute-start(bf16[112,256]{1,0:T(8,128)(2,1)} %pack.1.own_ref), channel_id=1, source_target_pairs={{0,1},{1,0},{2,3},{3,2},{4,5},{5,4},{6,7},{7,6},{8,9},{9,8},{10,11... | collective-permute-start | bytes 172040 | tf_op jit(solution)/shard_map/ppermute | solution.py:24
  12.0 0.8 copy-start.1
  12.8 14.3 %copy-start.2 = (bf16[9,32,256]{2,1,0:T(8,128)(2,1)S(1)}, bf16[9,32,256]{2,1,0:T(8,128)(2,1)}, u32[]{:S(2)}) copy-start(bf16[9,32,256]{2,1,0:T(8,128)(2,1)} %param.12) | copy-start | bytes 442372
  12.8 7.2 %collective-permute-start.1 = (bf16[224,256]{1,0:T(8,128)(2,1)S(1)}, bf16[224,256]{1,0:T(8,128)(2,1)S(1)}, u32[]{:S(2)}, u32[]{:S(2)}) collective-permute-start(bf16[224,256]{1,0:T(8,128)(2,1)S(1)} %pair.1.x_ref), channel_id=1, source_target_pairs={{0,2},{2,4},{4,6},{6,8},{8,10},{10,12},{12,14},{14,16},{16,18},{18... | collective-permute-start | bytes 344072 | tf_op jit(solution)/shard_map/ppermute | solution.py:30
  14.2 1.2 copy-start
  15.8 32.2 %copy-start.3 = (bf16[256,64]{0,1:T(8,128)(2,1)S(1)}, bf16[256,64]{0,1:T(8,128)(2,1)}, u32[]{:S(2)}) copy-start(bf16[256,64]{0,1:T(8,128)(2,1)} %param.11) | copy-start | bytes 98308
  20.0 3.2 %collective-permute-start.2 = (bf16[224,256]{1,0:T(8,128)(2,1)S(1)}, bf16[224,256]{1,0:T(8,128)(2,1)S(1)}, u32[]{:S(2)}, u32[]{:S(2)}) collective-permute-start(bf16[224,256]{1,0:T(8,128)(2,1)S(1)} %relay.5.got_ref), channel_id=1, source_target_pairs={{0,1},{1,0},{2,3},{3,2},{4,5},{5,4},{6,7},{7,6},{8,9},{9,8},{10,11... | collective-permute-start | bytes 344072 | tf_op jit(solution)/shard_map/ppermute | solution.py:24
  25.8 6.5 %collective-permute-start.3 = (bf16[128,256]{1,0:T(8,128)(2,1)S(1)}, bf16[128,256]{1,0:T(8,128)(2,1)S(1)}, u32[]{:S(2)}, u32[]{:S(2)}) collective-permute-start(bf16[128,256]{1,0:T(8,128)(2,1)S(1)} %get-tuple-element.40.x_ref), channel_id=1, source_target_pairs={{0,2},{2,4},{4,6},{6,8},{8,10},{10,12},{12,14},{14,16},{16,18},{18... | collective-permute-start | bytes 196616 | tf_op jit(solution)/shard_map/ppermute | solution.py:30
  32.3 3.1 %collective-permute-start.4 = (bf16[128,256]{1,0:T(8,128)(2,1)S(1)}, bf16[128,256]{1,0:T(8,128)(2,1)S(1)}, u32[]{:S(2)}, u32[]{:S(2)}) collective-permute-start(bf16[128,256]{1,0:T(8,128)(2,1)S(1)} %relay.6.got_ref), channel_id=1, source_target_pairs={{0,1},{1,0},{2,3},{3,2},{4,5},{5,4},{6,7},{7,6},{8,9},{9,8},{10,11... | collective-permute-start | bytes 196616 | tf_op jit(solution)/shard_map/ppermute | solution.py:24
  38.0 6.5 %collective-permute-start.5 = (bf16[128,256]{1,0:T(8,128)(2,1)S(1)}, bf16[128,256]{1,0:T(8,128)(2,1)S(1)}, u32[]{:S(2)}, u32[]{:S(2)}) collective-permute-start(bf16[128,256]{1,0:T(8,128)(2,1)S(1)} %get-tuple-element.46.x_ref), channel_id=1, source_target_pairs={{0,2},{2,4},{4,6},{6,8},{8,10},{10,12},{12,14},{14,16},{16,18},{18... | collective-permute-start | bytes 196616 | tf_op jit(solution)/shard_map/ppermute | solution.py:30
  44.5 3.4 %collective-permute-start.6 = (bf16[128,256]{1,0:T(8,128)(2,1)S(1)}, bf16[128,256]{1,0:T(8,128)(2,1)S(1)}, u32[]{:S(2)}, u32[]{:S(2)}) collective-permute-start(bf16[128,256]{1,0:T(8,128)(2,1)S(1)} %collective-permute-done.5.got_ref), channel_id=1, source_target_pairs={{0,1},{1,0},{2,3},{3,2},{4,5},{5,4},{6,7},{7,6},{8,9},{9,8},{10,11... | collective-permute-start | bytes 196616 | tf_op jit(solution)/shard_map/ppermute | solution.py:24
  69.4 5.3 %collective-permute-start.7 = (bf16[128,256]{1,0:T(8,128)(2,1)S(1)}, bf16[128,256]{1,0:T(8,128)(2,1)S(1)}, u32[]{:S(2)}, u32[]{:S(2)}) collective-permute-start(bf16[128,256]{1,0:T(8,128)(2,1)S(1)} %head.1.own_ref), channel_id=1, source_target_pairs={{0,1},{1,0},{2,3},{3,2},{4,5},{5,4},{6,7},{7,6},{8,9},{9,8},{10,11... | collective-permute-start | bytes 196616 | tf_op jit(solution)/shard_map/ppermute | solution.py:24
  74.7 8.2 %collective-permute-start.8 = (bf16[192,256]{1,0:T(8,128)(2,1)S(1)}, bf16[192,256]{1,0:T(8,128)(2,1)S(1)}, u32[]{:S(2)}, u32[]{:S(2)}) collective-permute-start(bf16[192,256]{1,0:T(8,128)(2,1)S(1)} %get-tuple-element.50.refs_0_.x_ref), channel_id=1, source_target_pairs={{0,2},{2,4},{4,6},{6,8},{8,10},{10,12},{12,14},{14,16},{16,18},{18... | collective-permute-start | bytes 294920 | tf_op jit(solution)/shard_map/ppermute | solution.py:30
  82.9 4.6 %collective-permute-start.9 = (bf16[192,256]{1,0:T(8,128)(2,1)S(1)}, bf16[192,256]{1,0:T(8,128)(2,1)S(1)}, u32[]{:S(2)}, u32[]{:S(2)}) collective-permute-start(bf16[192,256]{1,0:T(8,128)(2,1)S(1)} %relay.7.got_ref), channel_id=1, source_target_pairs={{0,1},{1,0},{2,3},{3,2},{4,5},{5,4},{6,7},{7,6},{8,9},{9,8},{10,11... | collective-permute-start | bytes 294920 | tf_op jit(solution)/shard_map/ppermute | solution.py:24
  92.2 7.6 %collective-permute-start.10 = (bf16[192,256]{1,0:T(8,128)(2,1)S(1)}, bf16[192,256]{1,0:T(8,128)(2,1)S(1)}, u32[]{:S(2)}, u32[]{:S(2)}) collective-permute-start(bf16[192,256]{1,0:T(8,128)(2,1)S(1)} %get-tuple-element.56.refs_0_.x_ref), channel_id=1, source_target_pairs={{0,2},{2,4},{4,6},{6,8},{8,10},{10,12},{12,14},{14,16},{16,18},{18... | collective-permute-start | bytes 294920 | tf_op jit(solution)/shard_map/ppermute | solution.py:30
  99.8 4.6 %collective-permute-start.11 = (bf16[192,256]{1,0:T(8,128)(2,1)S(1)}, bf16[192,256]{1,0:T(8,128)(2,1)S(1)}, u32[]{:S(2)}, u32[]{:S(2)}) collective-permute-start(bf16[192,256]{1,0:T(8,128)(2,1)S(1)} %relay.8.got_ref), channel_id=1, source_target_pairs={{0,1},{1,0},{2,3},{3,2},{4,5},{5,4},{6,7},{7,6},{8,9},{9,8},{10,11... | collective-permute-start | bytes 294920 | tf_op jit(solution)/shard_map/ppermute | solution.py:24
  109.1 7.6 %collective-permute-start.12 = (bf16[192,256]{1,0:T(8,128)(2,1)S(1)}, bf16[192,256]{1,0:T(8,128)(2,1)S(1)}, u32[]{:S(2)}, u32[]{:S(2)}) collective-permute-start(bf16[192,256]{1,0:T(8,128)(2,1)S(1)} %get-tuple-element.63.refs_0_.x_ref), channel_id=1, source_target_pairs={{0,2},{2,4},{4,6},{6,8},{8,10},{10,12},{12,14},{14,16},{16,18},{18... | collective-permute-start | bytes 294920 | tf_op jit(solution)/shard_map/ppermute | solution.py:30
  116.8 4.6 %collective-permute-start.13 = (bf16[192,256]{1,0:T(8,128)(2,1)S(1)}, bf16[192,256]{1,0:T(8,128)(2,1)S(1)}, u32[]{:S(2)}, u32[]{:S(2)}) collective-permute-start(bf16[192,256]{1,0:T(8,128)(2,1)S(1)} %relay.9.got_ref), channel_id=1, source_target_pairs={{0,1},{1,0},{2,3},{3,2},{4,5},{5,4},{6,7},{7,6},{8,9},{9,8},{10,11... | collective-permute-start | bytes 294920 | tf_op jit(solution)/shard_map/ppermute | solution.py:24
  123.3 8.8 %collective-permute-start.14 = (bf16[48,1152]{1,0:T(8,128)(2,1)S(1)}, bf16[48,1152]{1,0:T(8,128)(2,1)S(1)}, u32[]{:S(2)}, u32[]{:S(2)}) collective-permute-start(bf16[48,1152]{1,0:T(8,128)(2,1)S(1)} %get-tuple-element.75), channel_id=1, source_target_pairs={{0,2},{2,0},{1,3},{3,1},{4,6},{6,4},{5,7},{7,5},{8,10},{10,8},{9,1... | collective-permute-start | bytes 331784 | tf_op jit(solution)/shard_map/ppermute | solution.py:446
  184.0 15.9 %all-to-all-start.4 = ((bf16[4,48,1152]{2,1,0:T(8,128)(2,1)}), bf16[4,48,1152]{2,1,0:T(8,128)(2,1)S(1)}, u32[]{:S(2)}, u32[]{:S(2)}) async-start(bf16[4,48,1152]{2,1,0:T(8,128)(2,1)} %broadcast_in_dim.22), calls=%async_computation.4 | async-start | bytes 884736 | tf_op jit(solution)/shard_map/all_to_all | solution.py:433

commit v6 on v5

--- a/solution.py
+++ b/solution.py
@@ -9,7 +9,6 @@
 from jax.sharding import Mesh, PartitionSpec as P
 
 SKY = ("z", "yh", "core")
-QUAD = ("yh", "core")
 C = 64
 R = 256
 TAPS = 9
@@ -42,8 +41,8 @@
 
 
 def ordered(got, other):
-    even = lax.axis_index("core") == 0
-    return jnp.where(even, got, other), jnp.where(even, other, got)
+    got, other = got[...], other[...]
+    return own_of(got, other), own_of(other, got)
 
 
 def own_of(first, second):
@@ -129,11 +128,18 @@
     return hidden
 
 
-def pair_kernel(own_ref, other_ref, out_ref):
+def pair_kernel(own_ref, other_ref, out_ref, sent_ref):
     size = own_ref.shape[0]
+    each = size - 16 - C
     own, other = own_ref[...], other_ref[...]
-    out_ref[:size, :] = own_of(own, other)
-    out_ref[size:, :] = own_of(other, own)
+    first, second = own_of(own, other), own_of(other, own)
+    out_ref[:size, :] = first
+    out_ref[size:, :] = second
+    sent_ref[:C, :] = first[:C]
+    sent_ref[C : 2 * C, :] = second[:C]
+    sent_ref[2 * C : 2 * C + 16, :] = first[C + each :]
+    sent_ref[2 * C + 16 : 2 * C + 32, :] = second[C + each :]
+    sent_ref[2 * C + 32 :, :] = own_of(second, first)[C : C + each]
 
 
 def first_kernel(
@@ -141,12 +147,19 @@
     h_ref, picked_ref, slopes_ref, last_ref, pos_ref, kept_ref, near_pos_ref, near_cot_ref, scratch,
 ):
     size = x_ref.shape[0] // 2
-    below, above = ordered(got_ref[...], other_ref[...])
-    packs = [below[:size], below[size:], x_ref[:size, :], x_ref[size:, :], above[:size], above[size:]]
+    below, above = ordered(got_ref, other_ref)
+    each = size - 16 - C
+    pair = [x_ref[:size, :], x_ref[size:, :]]
+    metas = [
+        below[2 * C : 2 * C + 16], below[2 * C + 16 : 2 * C + 32], pair[0][C + each :],
+        pair[1][C + each :], above[2 * C : 2 * C + 16], above[2 * C + 16 : 2 * C + 32],
+    ]
+    cots = [below[2 * C + 32 :], pair[0][C : C + each], pair[1][C : C + each], above[2 * C + 32 :]]
+    blocks = [below[:C], below[C : 2 * C], pair[0][:C], pair[1][:C], above[:C], above[C : 2 * C]]
     column = lax.broadcasted_iota(jnp.int32, (16, R), 1)
     pos, kept = [], []
-    for b, pack in enumerate(packs):
-        offset = pack[size - 16 :].astype(F32)
+    for b, meta in enumerate(metas):
+        offset = meta.astype(F32)
         at = jnp.where(offset > 400.0, 768, offset.astype(jnp.int32) + column + R)
         pos_ref[16 * b : 16 * (b + 1), :] = at
         keep = offset[TAPS : TAPS + 1]
@@ -154,13 +167,9 @@
         pos.append(at)
         kept.append(keep)
     kept_ref[6:8, :] = jnp.zeros((2, R), F32)
-    each = size - 16 - C
     for i in range(3):
         near_pos_ref[16 * i : 16 * (i + 1), :] = own_of(pos[i + 1], pos[i + 2])
-        near_cot_ref[each * i : each * (i + 1), :] = own_of(
-            packs[i + 1][C : C + each], packs[i + 2][C : C + each]
-        )
-    blocks = [pack[:C] for pack in packs]
+        near_cot_ref[each * i : each * (i + 1), :] = own_of(cots[i], cots[i + 1])
     hidden = two_layers(blocks, pos, kept, w_ref, picked_ref, slopes_ref, last_ref, scratch)
     for i in range(2):
         h_ref[i * C : (i + 1) * C, :] = hidden[i]
@@ -173,7 +182,7 @@
 
 
 def read_blocks(x_ref, got_ref, other_ref):
-    below, above = ordered(got_ref[...], other_ref[...])
+    below, above = ordered(got_ref, other_ref)
     return [below[:C], below[C:], x_ref[:C, :], x_ref[C:, :], above[:C], above[C:]]
 
 
@@ -332,7 +341,7 @@
     x_ref, got_ref, other_ref, masked_ref, own_ref, w_ref, pos_ref, kept_ref, slopes_ref
 ):
     pos, kept = read_tables(pos_ref, kept_ref)
-    below, above = ordered(got_ref[...], other_ref[...])
+    below, above = ordered(got_ref, other_ref)
     acts = {0: below[:C], 1: below[C : 2 * C], 4: above[:C], 5: above[C : 2 * C]}
     masked = [
         below[2 * C :].astype(F32), masked_ref[0], masked_ref[1], above[2 * C :].astype(F32)
@@ -386,19 +395,32 @@
     send_ref[...] = jnp.where(low_half, second, first)
 
 
-def map_kernel(low_ref, own_ref, w_ref, pos_ref, map_ref):
+def map_kernel(low_ref, own_ref, w_ref, pos_ref, map_ref, token_ref):
     own = own_ref[...]
     for i, part in ((0, 2), (1, 1), (2, 0)):
         act = low_ref[i * C : (i + 1) * C, :]
         own = own + spread(act, pos_ref[16 * i : 16 * (i + 1), :], w_ref[0], (part,))[part]
     map_ref[...] = own.astype(BF16)
-
-
-def final_kernel(scale, sum_ref, out_ref):
+    token_ref[...] = own[:8, :128]
+
+
+def add_kernel(keep_ref, got_ref, _, out_ref):
+    out_ref[...] = (keep_ref[...].astype(F32) + got_ref[...].astype(F32)).astype(BF16)
+
+
+def rows_kernel(own_ref, got_ref, out_ref):
+    rows = own_ref.shape[0]
+    low_half = lax.axis_index("yh") == 0
+    own, got = own_ref[...], got_ref[...]
+    out_ref[:rows, :] = jnp.where(low_half, own, got)
+    out_ref[rows:, :] = jnp.where(low_half, got, own)
+
+
+def final_kernel(scale, own_ref, other_ref, out_ref):
     wide = TAPS * C
     half_rows = C // 2
-    for core in range(2):
-        rows = jnp.concatenate([sum_ref[core], sum_ref[2 + core]], axis=0).astype(F32) * scale
+    for core, sums in enumerate(ordered(own_ref, other_ref)):
+        rows = sums.astype(F32) * scale
         for slot, pair in enumerate(((4, 3), (2, 1), (0, 5))):
             for half, layer in enumerate(pair):
                 for k in range(TAPS):
@@ -441,10 +463,17 @@
     return jnp.broadcast_to(value[None], (count,) + value.shape)
 
 
-def sum_over_sky(keep, send, quads, length):
+def swap_halves(value):
+    return lax.ppermute(value, "yh", [(0, 1), (1, 0)])
+
+
+def sum_over_sky(keep, send, length, after):
     rows, lanes = keep.shape
-    got = lax.ppermute(send, "yh", [(0, 1), (1, 0)])
-    chunk = (keep.astype(F32) + got.astype(F32)).astype(BF16)
+    out = [sds(keep.shape, BF16)]
+    any_space = pl.BlockSpec(memory_space=pl.ANY)
+    chunk = call(
+        add_kernel, "add", [v(keep), v(swap_halves(send)), (any_space, after)], out
+    )[0]
     tiles = (rows // 8) * (lanes // 128)
     each = -(-tiles // length)
     chunk = chunk.reshape(rows // 8, 8, lanes // 128, 128).transpose(0, 2, 1, 3)
@@ -452,7 +481,10 @@
     chunk = add_up(exchange(chunk.reshape(length, each, 8, 128), "z"))
     chunk = exchange(copies(chunk, length), "z").reshape(each * length, 8, 128)[:tiles]
     chunk = chunk.reshape(rows // 8, lanes // 128, 8, 128).transpose(0, 2, 1, 3)
-    return exchange(copies(chunk.reshape(rows, lanes), quads), QUAD)
+    chunk = chunk.reshape(rows, lanes)
+    return call(
+        rows_kernel, "rows", [v(chunk), v(swap_halves(chunk))], [sds((2 * rows, lanes), BF16)]
+    )[0]
 
 
 def per_device(sky_maps, footprint, neighbours, enc_weight, join_weight, dec_weight, cotangent):
@@ -477,13 +509,14 @@
         [sds((size, R), BF16)],
         [pltpu.VMEM((TAPS, R), jnp.int32), pltpu.VMEM((1, R), jnp.int32), dma((4,))], None,
     )[0]
-    pack = call(
-        pair_kernel, "pair", [v(pack), v(swap_cores(pack))], [sds((2 * size, R), BF16)]
-    )[0]
+    pack, sent = call(
+        pair_kernel, "pair", [v(pack), v(swap_cores(pack))],
+        [sds((2 * size, R), BF16), sds((2 * C + 32 + each, R), BF16)],
+    )
     pair = sds((2, C, R), F32)
     layer_outs = [sds((2 * C, R), BF16), sds((2, 2, wide, R), BF16), sds((4, C, R), F32), pair]
     scratch = [pltpu.VMEM((2, wide, R), BF16)]
-    got, other = widen(pack, [weights[0]])
+    got, other = widen(sent, [weights[0]])
     hidden, picked, slopes, last, pos, kept, near_pos, near_cot = call(
         first_kernel, "layers01", [v(pack), v(got), v(other), v(weights[0])],
         layer_outs
@@ -543,12 +576,14 @@
                 last_back_kernel, "lastback", ins + [v(picked)] + [v(g) for g in grads],
                 [sds((3 * C, R), BF16), sds((C, R), F32), half, half],
             )
-    map_grads = call(
-        map_kernel, "mapgrad", [v(low), v(own), v(weights[0]), v(near_pos)], [sds((C, R), BF16)]
-    )[0]
-    total = sum_over_sky(keep, send, lax.axis_size(QUAD), lax.axis_size("z"))
+    map_grads, token = call(
+        map_kernel, "mapgrad", [v(low), v(own), v(weights[0]), v(near_pos)],
+        [sds((C, R), BF16), sds((8, 128), F32)],
+    )
+    total = sum_over_sky(keep, send, lax.axis_size("z"), token)
     summed = call(
-        functools.partial(final_kernel, 1.0 / math.sqrt(R * peers)), "final", [v(total)],
+        functools.partial(final_kernel, 1.0 / math.sqrt(R * peers)), "final",
+        [v(total), v(swap_cores(total))],
         [sds((depth, TAPS, C, C), F32)],
     )[0]
     return map_grads[None], summed[None]

time: 202 us -> 200 us (0.990)
  waiting for transfers between devices: 45 us -> 42.1 us
    all_to_all x1 -> x0, starting transfers between devices: 7.26 us -> none  [exchange(): return lax.all_to_all(value, axes, 0, 0, tiled=True)]
    ppermute x8 -> x9, starting transfers between devices: 30.8 us -> 37.7 us  [swap_cores(): return lax.ppermute(value, 'core', [(0, 1), (1, 0)])]
    all_to_all x1 -> x0, waiting for transfers between devices: 6.13 us -> none  [exchange(): return lax.all_to_all(value, axes, 0, 0, tiled=True)]
    ppermute x1 -> x2, waiting for transfers between devices: 3.13 us -> 5.52 us  [swap_halves(): return lax.ppermute(value, 'yh', [(0, 1), (1, 0)])]
    ppermute x1 -> x2, starting transfers between devices: 5.62 us -> 7.75 us  [swap_halves(): return lax.ppermute(value, 'yh', [(0, 1), (1, 0)])]
    ppermute x8 -> x9, waiting for transfers between devices: 7.94 us -> 8.99 us  [swap_cores(): return lax.ppermute(value, 'core', [(0, 1), (1, 0)])]
    pallas_call x23 -> x25, Pallas kernels: 31.5 us -> 31.6 us  [call(): pl.pallas_call(body, name=name, in_specs=specs, out_specs=[pl.BlockSpec(m...]
  transfers between devices with their start and end apart: 16 -> 17, of which waited for: 16 -> 17; matrix products, arithmetic and copies ran while one was open for 0% -> 0% of each run, Pallas kernels for 5% -> 5%
where the time goes in v6:
time: 200 us; the launch traced here: 199 us
  blocking collectives  69.5 us (35%)
  starting transfers between devices  53.2 us (27%)
  waiting for transfers between devices  42.1 us (21%)
  Pallas kernels  31.6 us (16%)
  local copies, waits for them, and re-layouts  2.03 us (1%)
    all_to_all x4, blocking collectives, exchange(): return lax.all_to_all(value, axes, 0, 0, tiled=True)  69.5 us
    ppermute x9, starting transfers between devices, swap_cores(): return lax.ppermute(value, 'core', [(0, 1), (1, 0)])  37.7 us
    pallas_call x25, Pallas kernels, call(): pl.pallas_call(body, name=name, in_specs=specs, out_specs=[pl.BlockSpec(m...  31.6 us
    ppermute x6, waiting for transfers between devices, widen(): got = lax.ppermute(value, SKY, pairs)  27.6 us
    ppermute x9, waiting for transfers between devices, swap_cores(): return lax.ppermute(value, 'core', [(0, 1), (1, 0)])  8.99 us
    ppermute x6, starting transfers between devices, widen(): got = lax.ppermute(value, SKY, pairs)  7.75 us
    ppermute x2, starting transfers between devices, swap_halves(): return lax.ppermute(value, 'yh', [(0, 1), (1, 0)])  7.75 us
    ppermute x2, waiting for transfers between devices, swap_halves(): return lax.ppermute(value, 'yh', [(0, 1), (1, 0)])  5.52 us
  transfers between devices with their start and end apart: 17, of which 17 were waited for; matrix products, arithmetic and copies ran while one was open for 0% of the time, Pallas kernels for 5%

profile of v6, /device:TPU:1, one launch (start us, length us, event | category | flops | bytes accessed | tf_op | source)
XLA Modules:
  0.0 199.4 jit_solution(9586848715196919629)
XLA Ops:
  2.1 8.8 %collective-permute-start = (bf16[112,256]{1,0:T(8,128)(2,1)}, bf16[112,256]{1,0:T(8,128)(2,1)S(1)}, u32[]{:S(2)}, u32[]{:S(2)}) collective-permute-start(bf16[112,256]{1,0:T(8,128)(2,1)} %pack.1.own_ref), channel_id=1, source_target_pairs={{0,1},{1,0},{2,3},{3,2},{4,5},{5,4},{6,7},{7,6},{8,9},{9,8},{10,11... | collective-permute-start | bytes 172040 | tf_op jit(solution)/shard_map/ppermute | solution.py:23
  15.7 4.0 %collective-permute-done.1.refs_0_ = bf16[192,256]{1,0:T(8,128)(2,1)S(1)} collective-permute-done((bf16[192,256]{1,0:T(8,128)(2,1)S(1)}, bf16[192,256]{1,0:T(8,128)(2,1)S(1)}, u32[]{:S(2)}, u32[]{:S(2)}) %collective-permute-start.1) | collective-permute-done | bytes 98336 | tf_op jit(solution)/shard_map/ppermute | solution.py:29
  19.7 1.9 collective-permute-start.2
  22.9 2.6 %layers01.1 = (bf16[128,256]{1,0:T(8,128)(2,1)S(1)}, bf16[2,2,576,256]{3,2,1,0:T(8,128)(2,1)S(1)}, f32[4,64,256]{2,1,0:T(8,128)S(1)}, f32[2,64,256]{2,1,0:T(8,12...) custom-call(bf16[224,256]{1,0:T(8,128)(2,1)S(1)} %get-tuple-element., ...), custom_call_target="tpu_custom_call" | custom-call | tf_op jit(solution)/shard_map/layers01/pallas_call | solution.py:439
  28.1 3.9 %collective-permute-done.3.refs_0_ = bf16[128,256]{1,0:T(8,128)(2,1)S(1)} collective-permute-done((bf16[128,256]{1,0:T(8,128)(2,1)S(1)}, bf16[128,256]{1,0:T(8,128)(2,1)S(1)}, u32[]{:S(2)}, u32[]{:S(2)}) %collective-permute-start.3) | collective-permute-done | bytes 65568 | tf_op jit(solution)/shard_map/ppermute | solution.py:29
  32.0 1.9 collective-permute-start.4
  35.1 2.6 %layers.1 = (bf16[128,256]{1,0:T(8,128)(2,1)S(1)}, bf16[2,2,576,256]{3,2,1,0:T(8,128)(2,1)S(1)}, f32[4,64,256]{2,1,0:T(8,128)S(1)}, f32[2,64,256]{2,1,0:T(8,128)S(1)}) custom-call(bf16[128,256]{1,0:T(8,128)(2,1)S(1)} %get-tuple-element.46.x_ref, bf16[128,256]{1,0:T(8,128)(2,1)S(1)} %relay.6.got_ref, bf16[128,256]{1,0:T(8,128)(2,1)S(1)} %collective-permute-done.4.other_ref, ...), custom_call_target="tpu_custom_call" | custom-call | tf_op jit(solution)/shard_map/layers/pallas_call | solution.py:439
  39.0 5.2 %collective-permute-done.5.got_ref = bf16[128,256]{1,0:T(8,128)(2,1)S(1)} collective-permute-done((bf16[128,256]{1,0:T(8,128)(2,1)S(1)}, bf16[128,256]{1,0:T(8,128)(2,1)S(1)}, u32[]{:S(2)}, u32[]{:S(2)}) %collective-permute-start.5) | collective-permute-done | bytes 65568 | tf_op jit(solution)/shard_map/ppermute | solution.py:29
  44.2 2.5 %collective-permute-start.6 = (bf16[128,256]{1,0:T(8,128)(2,1)S(1)}, bf16[128,256]{1,0:T(8,128)(2,1)S(1)}, u32[]{:S(2)}, u32[]{:S(2)}) collective-permute-start(bf16[128,256]{1,0:T(8,128)(2,1)S(1)} %collective-permute-done.5.got_ref), channel_id=1, source_target_pairs={{0,1},{1,0},{2,3},{3,2},{4,5},{5,4},{6,7},{7,6},{8,9},{9,8},{10,11... | collective-permute-start | bytes 196616 | tf_op jit(solution)/shard_map/ppermute | solution.py:23
  47.6 2.7 %lastlayers.1 = (bf16[8,64,256]{2,1,0:T(8,128)(2,1)S(1)}, bf16[2,2,576,256]{3,2,1,0:T(8,128)(2,1)S(1)}, f32[4,64,256]{2,1,0:T(8,128)S(1)}, f32[2,64,256]{2,1,0:T(8,128)S(1)}) custom-call(bf16[128,256]{1,0:T(8,128)(2,1)S(1)} %get-tuple-element.52.x_ref, bf16[128,256]{1,0:T(8,128)(2,1)S(1)} %collective-permute-done.5.got_ref, ...), custom_call_target="tpu_custom_call" | custom-call | tf_op jit(solution)/shard_map/lastlayers/pallas_call | solution.py:439
  50.4 10.4 %all_to_all.20.parts_ref = bf16[8,64,256]{2,1,0:T(8,128)(2,1)S(1)} all-to-all(bf16[8,64,256]{2,1,0:T(8,128)(2,1)S(1)} %get-tuple-element.54), channel_id=1, replica_groups=mesh['branch'=8,'z'=16,'yh'=2,'core'=2] {'branch'}, dimensions={0} | all-to-all | bytes 524288 | tf_op jit(solution)/shard_map/all_to_all | solution.py:455
  60.9 7.8 %all_to_all.21.unit_ref = bf16[8,32,256]{2,1,0:T(8,128)(2,1)S(1)} all-to-all(bf16[8,32,256]{2,1,0:T(8,128)(2,1)S(1)} %slope.1), channel_id=1, replica_groups=mesh['branch'=8,'z'=16,'yh'=2,'core'=2] {'branch'}, dimensions={0} | all-to-all | bytes 262144 | tf_op jit(solution)/shard_map/all_to_all | solution.py:455
  68.9 4.4 %collective-permute-start.7 = (bf16[128,256]{1,0:T(8,128)(2,1)S(1)}, bf16[128,256]{1,0:T(8,128)(2,1)S(1)}, u32[]{:S(2)}, u32[]{:S(2)}) collective-permute-start(bf16[128,256]{1,0:T(8,128)(2,1)S(1)} %head.1.own_ref), channel_id=1, source_target_pairs={{0,1},{1,0},{2,3},{3,2},{4,5},{5,4},{6,7},{7,6},{8,9},{9,8},{10,11... | collective-permute-start | bytes 196616 | tf_op jit(solution)/shard_map/ppermute | solution.py:23
  76.9 5.5 %collective-permute-done.8.refs_0_ = bf16[192,256]{1,0:T(8,128)(2,1)S(1)} collective-permute-done((bf16[192,256]{1,0:T(8,128)(2,1)S(1)}, bf16[192,256]{1,0:T(8,128)(2,1)S(1)}, u32[]{:S(2)}, u32[]{:S(2)}) %collective-permute-start.8) | collective-permute-done | bytes 98336 | tf_op jit(solution)/shard_map/ppermute | solution.py:29
  82.4 3.9 %collective-permute-start.9 = (bf16[192,256]{1,0:T(8,128)(2,1)S(1)}, bf16[192,256]{1,0:T(8,128)(2,1)S(1)}, u32[]{:S(2)}, u32[]{:S(2)}) collective-permute-start(bf16[192,256]{1,0:T(8,128)(2,1)S(1)} %relay.7.got_ref), channel_id=1, source_target_pairs={{0,1},{1,0},{2,3},{3,2},{4,5},{5,4},{6,7},{7,6},{8,9},{9,8},{10,11... | collective-permute-start | bytes 294920 | tf_op jit(solution)/shard_map/ppermute | solution.py:23
  87.0 4.7 %back.2 = (bf16[192,256]{1,0:T(8,128)(2,1)S(1)}, f32[2,64,256]{2,1,0:T(8,128)S(1)}, bf16[128,256]{1,0:T(8,128)(2,1)S(1)}) custom-call(bf16[192,256]{1,0:T(8,128)(2,1)S(1)} %get-tuple-element.56.refs_0_.x_ref, bf16[192,256]{1,0:T(8,128)(2,1)S(1)} %relay.7.got_ref, bf16[192,256]{1,0:T(8,128)(2,1)S(1)} %collective-permute-done.9.other_ref, ...), custom_call_target="tpu_custom_call" | custom-call | tf_op jit(solution)/shard_map/back/pallas_call | solution.py:439
  93.0 1.8 beside.4
  94.8 4.5 %collective-permute-done.10.refs_0_ = bf16[192,256]{1,0:T(8,128)(2,1)S(1)} collective-permute-done((bf16[192,256]{1,0:T(8,128)(2,1)S(1)}, bf16[192,256]{1,0:T(8,128)(2,1)S(1)}, u32[]{:S(2)}, u32[]{:S(2)}) %collective-permute-start.10) | collective-permute-done | bytes 98336 | tf_op jit(solution)/shard_map/ppermute | solution.py:29
  99.3 3.7 %collective-permute-start.11 = (bf16[192,256]{1,0:T(8,128)(2,1)S(1)}, bf16[192,256]{1,0:T(8,128)(2,1)S(1)}, u32[]{:S(2)}, u32[]{:S(2)}) collective-permute-start(bf16[192,256]{1,0:T(8,128)(2,1)S(1)} %relay.8.got_ref), channel_id=1, source_target_pairs={{0,1},{1,0},{2,3},{3,2},{4,5},{5,4},{6,7},{7,6},{8,9},{9,8},{10,11... | collective-permute-start | bytes 294920 | tf_op jit(solution)/shard_map/ppermute | solution.py:23
  104.0 4.7 %back.3 = (bf16[192,256]{1,0:T(8,128)(2,1)S(1)}, f32[2,64,256]{2,1,0:T(8,128)S(1)}, bf16[128,256]{1,0:T(8,128)(2,1)S(1)}) custom-call(bf16[192,256]{1,0:T(8,128)(2,1)S(1)} %get-tuple-element.62.refs_0_.x_ref, bf16[192,256]{1,0:T(8,128)(2,1)S(1)} %relay.8.got_ref, bf16[192,256]{1,0:T(8,128)(2,1)S(1)} %collective-permute-done.11.other_ref, ...), custom_call_target="tpu_custom_call" | custom-call | tf_op jit(solution)/shard_map/back/pallas_call | solution.py:439
  109.9 1.8 beside.5
  111.8 4.5 %collective-permute-done.12.refs_0_ = bf16[192,256]{1,0:T(8,128)(2,1)S(1)} collective-permute-done((bf16[192,256]{1,0:T(8,128)(2,1)S(1)}, bf16[192,256]{1,0:T(8,128)(2,1)S(1)}, u32[]{:S(2)}, u32[]{:S(2)}) %collective-permute-start.12) | collective-permute-done | bytes 98336 | tf_op jit(solution)/shard_map/ppermute | solution.py:29
  116.3 3.7 %collective-permute-start.13 = (bf16[192,256]{1,0:T(8,128)(2,1)S(1)}, bf16[192,256]{1,0:T(8,128)(2,1)S(1)}, u32[]{:S(2)}, u32[]{:S(2)}) collective-permute-start(bf16[192,256]{1,0:T(8,128)(2,1)S(1)} %relay.9.got_ref), channel_id=1, source_target_pairs={{0,1},{1,0},{2,3},{3,2},{4,5},{5,4},{6,7},{7,6},{8,9},{9,8},{10,11... | collective-permute-start | bytes 294920 | tf_op jit(solution)/shard_map/ppermute | solution.py:23
  120.9 1.8 lastback.1
  122.8 5.6 %collective-permute-start.14 = (bf16[48,1152]{1,0:T(8,128)(2,1)S(1)}, bf16[48,1152]{1,0:T(8,128)(2,1)S(1)}, u32[]{:S(2)}, u32[]{:S(2)}) collective-permute-start(bf16[48,1152]{1,0:T(8,128)(2,1)S(1)} %get-tuple-element.82), channel_id=1, source_target_pairs={{0,2},{2,0},{1,3},{3,1},{4,6},{6,4},{5,7},{7,5},{8,10},{10,8},{9,1... | collective-permute-start | bytes 331784 | tf_op jit(solution)/shard_map/ppermute | solution.py:467
  128.4 2.5 %mapgrad.1 = (bf16[64,256]{1,0:T(8,128)(2,1)}, f32[8,128]{1,0:T(8,128)S(1)}) custom-call(bf16[192,256]{1,0:T(8,128)(2,1)S(1)} %get-tuple-element.78.low_ref, f32[64,256]{1,0:T(8,128)S(1)} %get-tuple-element.79.own_ref, bf16[2,64,576]{2,1,0:T(8,128)(2,1)S(1)} %get-tuple-element.45.refs_1_.w_ref, s32[48,256]{1,0:T(8,128)S(1)} %get-tuple-element.48.pos_ref), custom_call_target="tpu_custom_call" | custom-call | tf_op jit(solution)/shard_map/mapgrad/pallas_call | solution.py:439
  131.6 33.8 %all_to_all.22 = bf16[16,4,8,128]{3,2,1,0:T(8,128)(2,1)S(1)} all-to-all(bf16[16,4,8,128]{3,2,1,0:T(8,128)(2,1)S(1)} %bitcast.26), channel_id=1, replica_groups=mesh['branch'=8,'z'=16,'yh'=2,'core'=2] {'z'}, dimensions={0} | all-to-all | bytes 262144 | tf_op jit(solution)/shard_map/all_to_all | solution.py:455
  165.4 17.5 %all_to_all.23 = bf16[16,4,8,128]{3,2,1,0:T(8,128)(2,1)S(1)} all-to-all(bf16[16,4,8,128]{3,2,1,0:T(8,128)(2,1)S(1)} %broadcast_in_dim.13), channel_id=1, replica_groups=mesh['branch'=8,'z'=16,'yh'=2,'core'=2] {'z'}, dimensions={0} | all-to-all | bytes 262144 | tf_op jit(solution)/shard_map/all_to_all | solution.py:455
  182.9 2.1 %collective-permute-start.15 = (bf16[48,1152]{1,0:T(8,128)(2,1)S(1)}, bf16[48,1152]{1,0:T(8,128)(2,1)S(1)}, u32[]{:S(2)}, u32[]{:S(2)}) collective-permute-start(bf16[48,1152]{1,0:T(8,128)(2,1)S(1)} %bitcast.19), channel_id=1, source_target_pairs={{0,2},{2,0},{1,3},{3,1},{4,6},{6,4},{5,7},{7,5},{8,10},{10,8},{9,1... | collective-permute-start | bytes 331784 | tf_op jit(solution)/shard_map/ppermute | solution.py:467
  185.0 4.9 %collective-permute-done.15.got_ref = bf16[48,1152]{1,0:T(8,128)(2,1)S(1)} collective-permute-done((bf16[48,1152]{1,0:T(8,128)(2,1)S(1)}, bf16[48,1152]{1,0:T(8,128)(2,1)S(1)}, u32[]{:S(2)}, u32[]{:S(2)}) %collective-permute-start.15) | collective-permute-done | bytes 110624 | tf_op jit(solution)/shard_map/ppermute | solution.py:467
  189.9 6.9 %collective-permute-start.16 = (bf16[96,1152]{1,0:T(8,128)(2,1)S(1)}, bf16[96,1152]{1,0:T(8,128)(2,1)S(1)}, u32[]{:S(2)}, u32[]{:S(2)}) collective-permute-start(bf16[96,1152]{1,0:T(8,128)(2,1)S(1)} %rows.1.own_ref), channel_id=1, source_target_pairs={{0,1},{1,0},{2,3},{3,2},{4,5},{5,4},{6,7},{7,6},{8,9},{9,8},{10,11... | collective-permute-start | bytes 663560 | tf_op jit(solution)/shard_map/ppermute | solution.py:23
  197.9 1.5 final.1
  (43 shorter events, 24.3 us)
Async XLA Ops:
  2.1 9.9 %collective-permute-start = (bf16[112,256]{1,0:T(8,128)(2,1)}, bf16[112,256]{1,0:T(8,128)(2,1)S(1)}, u32[]{:S(2)}, u32[]{:S(2)}) collective-permute-start(bf16[112,256]{1,0:T(8,128)(2,1)} %pack.1.own_ref), channel_id=1, source_target_pairs={{0,1},{1,0},{2,3},{3,2},{4,5},{5,4},{6,7},{7,6},{8,9},{9,8},{10,11... | collective-permute-start | bytes 172040 | tf_op jit(solution)/shard_map/ppermute | solution.py:23
  12.0 0.8 copy-start.1
  12.8 6.9 %collective-permute-start.1 = (bf16[192,256]{1,0:T(8,128)(2,1)S(1)}, bf16[192,256]{1,0:T(8,128)(2,1)S(1)}, u32[]{:S(2)}, u32[]{:S(2)}) collective-permute-start(bf16[192,256]{1,0:T(8,128)(2,1)S(1)} %get-tuple-element.44), channel_id=1, source_target_pairs={{0,2},{2,4},{4,6},{6,8},{8,10},{10,12},{12,14},{14,16},{16,18},{18... | collective-permute-start | bytes 294920 | tf_op jit(solution)/shard_map/ppermute | solution.py:29
  14.1 1.2 copy-start
  15.3 11.5 %copy-start.2 = (bf16[9,32,256]{2,1,0:T(8,128)(2,1)S(1)}, bf16[9,32,256]{2,1,0:T(8,128)(2,1)}, u32[]{:S(2)}) copy-start(bf16[9,32,256]{2,1,0:T(8,128)(2,1)} %param.12) | copy-start | bytes 442372
  15.7 32.0 %copy-start.3 = (bf16[256,64]{0,1:T(8,128)(2,1)S(1)}, bf16[256,64]{0,1:T(8,128)(2,1)}, u32[]{:S(2)}) copy-start(bf16[256,64]{0,1:T(8,128)(2,1)} %param.11) | copy-start | bytes 98308
  19.7 3.2 %collective-permute-start.2 = (bf16[192,256]{1,0:T(8,128)(2,1)S(1)}, bf16[192,256]{1,0:T(8,128)(2,1)S(1)}, u32[]{:S(2)}, u32[]{:S(2)}) collective-permute-start(bf16[192,256]{1,0:T(8,128)(2,1)S(1)} %relay.5.got_ref), channel_id=1, source_target_pairs={{0,1},{1,0},{2,3},{3,2},{4,5},{5,4},{6,7},{7,6},{8,9},{9,8},{10,11... | collective-permute-start | bytes 294920 | tf_op jit(solution)/shard_map/ppermute | solution.py:23
  25.5 6.5 %collective-permute-start.3 = (bf16[128,256]{1,0:T(8,128)(2,1)S(1)}, bf16[128,256]{1,0:T(8,128)(2,1)S(1)}, u32[]{:S(2)}, u32[]{:S(2)}) collective-permute-start(bf16[128,256]{1,0:T(8,128)(2,1)S(1)} %get-tuple-element.46.x_ref), channel_id=1, source_target_pairs={{0,2},{2,4},{4,6},{6,8},{8,10},{10,12},{12,14},{14,16},{16,18},{18... | collective-permute-start | bytes 196616 | tf_op jit(solution)/shard_map/ppermute | solution.py:29
  32.0 3.1 %collective-permute-start.4 = (bf16[128,256]{1,0:T(8,128)(2,1)S(1)}, bf16[128,256]{1,0:T(8,128)(2,1)S(1)}, u32[]{:S(2)}, u32[]{:S(2)}) collective-permute-start(bf16[128,256]{1,0:T(8,128)(2,1)S(1)} %relay.6.got_ref), channel_id=1, source_target_pairs={{0,1},{1,0},{2,3},{3,2},{4,5},{5,4},{6,7},{7,6},{8,9},{9,8},{10,11... | collective-permute-start | bytes 196616 | tf_op jit(solution)/shard_map/ppermute | solution.py:23
  37.7 6.5 %collective-permute-start.5 = (bf16[128,256]{1,0:T(8,128)(2,1)S(1)}, bf16[128,256]{1,0:T(8,128)(2,1)S(1)}, u32[]{:S(2)}, u32[]{:S(2)}) collective-permute-start(bf16[128,256]{1,0:T(8,128)(2,1)S(1)} %get-tuple-element.52.x_ref), channel_id=1, source_target_pairs={{0,2},{2,4},{4,6},{6,8},{8,10},{10,12},{12,14},{14,16},{16,18},{18... | collective-permute-start | bytes 196616 | tf_op jit(solution)/shard_map/ppermute | solution.py:29
  44.2 3.4 %collective-permute-start.6 = (bf16[128,256]{1,0:T(8,128)(2,1)S(1)}, bf16[128,256]{1,0:T(8,128)(2,1)S(1)}, u32[]{:S(2)}, u32[]{:S(2)}) collective-permute-start(bf16[128,256]{1,0:T(8,128)(2,1)S(1)} %collective-permute-done.5.got_ref), channel_id=1, source_target_pairs={{0,1},{1,0},{2,3},{3,2},{4,5},{5,4},{6,7},{7,6},{8,9},{9,8},{10,11... | collective-permute-start | bytes 196616 | tf_op jit(solution)/shard_map/ppermute | solution.py:23
  68.9 5.3 %collective-permute-start.7 = (bf16[128,256]{1,0:T(8,128)(2,1)S(1)}, bf16[128,256]{1,0:T(8,128)(2,1)S(1)}, u32[]{:S(2)}, u32[]{:S(2)}) collective-permute-start(bf16[128,256]{1,0:T(8,128)(2,1)S(1)} %head.1.own_ref), channel_id=1, source_target_pairs={{0,1},{1,0},{2,3},{3,2},{4,5},{5,4},{6,7},{7,6},{8,9},{9,8},{10,11... | collective-permute-start | bytes 196616 | tf_op jit(solution)/shard_map/ppermute | solution.py:23
  74.2 8.2 %collective-permute-start.8 = (bf16[192,256]{1,0:T(8,128)(2,1)S(1)}, bf16[192,256]{1,0:T(8,128)(2,1)S(1)}, u32[]{:S(2)}, u32[]{:S(2)}) collective-permute-start(bf16[192,256]{1,0:T(8,128)(2,1)S(1)} %get-tuple-element.56.refs_0_.x_ref), channel_id=1, source_target_pairs={{0,2},{2,4},{4,6},{6,8},{8,10},{10,12},{12,14},{14,16},{16,18},{18... | collective-permute-start | bytes 294920 | tf_op jit(solution)/shard_map/ppermute | solution.py:29
  82.4 4.6 %collective-permute-start.9 = (bf16[192,256]{1,0:T(8,128)(2,1)S(1)}, bf16[192,256]{1,0:T(8,128)(2,1)S(1)}, u32[]{:S(2)}, u32[]{:S(2)}) collective-permute-start(bf16[192,256]{1,0:T(8,128)(2,1)S(1)} %relay.7.got_ref), channel_id=1, source_target_pairs={{0,1},{1,0},{2,3},{3,2},{4,5},{5,4},{6,7},{7,6},{8,9},{9,8},{10,11... | collective-permute-start | bytes 294920 | tf_op jit(solution)/shard_map/ppermute | solution.py:23
  91.7 7.6 %collective-permute-start.10 = (bf16[192,256]{1,0:T(8,128)(2,1)S(1)}, bf16[192,256]{1,0:T(8,128)(2,1)S(1)}, u32[]{:S(2)}, u32[]{:S(2)}) collective-permute-start(bf16[192,256]{1,0:T(8,128)(2,1)S(1)} %get-tuple-element.62.refs_0_.x_ref), channel_id=1, source_target_pairs={{0,2},{2,4},{4,6},{6,8},{8,10},{10,12},{12,14},{14,16},{16,18},{18... | collective-permute-start | bytes 294920 | tf_op jit(solution)/shard_map/ppermute | solution.py:29
  99.3 4.6 %collective-permute-start.11 = (bf16[192,256]{1,0:T(8,128)(2,1)S(1)}, bf16[192,256]{1,0:T(8,128)(2,1)S(1)}, u32[]{:S(2)}, u32[]{:S(2)}) collective-permute-start(bf16[192,256]{1,0:T(8,128)(2,1)S(1)} %relay.8.got_ref), channel_id=1, source_target_pairs={{0,1},{1,0},{2,3},{3,2},{4,5},{5,4},{6,7},{7,6},{8,9},{9,8},{10,11... | collective-permute-start | bytes 294920 | tf_op jit(solution)/shard_map/ppermute | solution.py:23
  108.6 7.6 %collective-permute-start.12 = (bf16[192,256]{1,0:T(8,128)(2,1)S(1)}, bf16[192,256]{1,0:T(8,128)(2,1)S(1)}, u32[]{:S(2)}, u32[]{:S(2)}) collective-permute-start(bf16[192,256]{1,0:T(8,128)(2,1)S(1)} %get-tuple-element.69.refs_0_.x_ref), channel_id=1, source_target_pairs={{0,2},{2,4},{4,6},{6,8},{8,10},{10,12},{12,14},{14,16},{16,18},{18... | collective-permute-start | bytes 294920 | tf_op jit(solution)/shard_map/ppermute | solution.py:29
  116.3 4.6 %collective-permute-start.13 = (bf16[192,256]{1,0:T(8,128)(2,1)S(1)}, bf16[192,256]{1,0:T(8,128)(2,1)S(1)}, u32[]{:S(2)}, u32[]{:S(2)}) collective-permute-start(bf16[192,256]{1,0:T(8,128)(2,1)S(1)} %relay.9.got_ref), channel_id=1, source_target_pairs={{0,1},{1,0},{2,3},{3,2},{4,5},{5,4},{6,7},{7,6},{8,9},{9,8},{10,11... | collective-permute-start | bytes 294920 | tf_op jit(solution)/shard_map/ppermute | solution.py:23
  122.8 8.8 %collective-permute-start.14 = (bf16[48,1152]{1,0:T(8,128)(2,1)S(1)}, bf16[48,1152]{1,0:T(8,128)(2,1)S(1)}, u32[]{:S(2)}, u32[]{:S(2)}) collective-permute-start(bf16[48,1152]{1,0:T(8,128)(2,1)S(1)} %get-tuple-element.82), channel_id=1, source_target_pairs={{0,2},{2,0},{1,3},{3,1},{4,6},{6,4},{5,7},{7,5},{8,10},{10,8},{9,1... | collective-permute-start | bytes 331784 | tf_op jit(solution)/shard_map/ppermute | solution.py:467
  182.9 7.0 %collective-permute-start.15 = (bf16[48,1152]{1,0:T(8,128)(2,1)S(1)}, bf16[48,1152]{1,0:T(8,128)(2,1)S(1)}, u32[]{:S(2)}, u32[]{:S(2)}) collective-permute-start(bf16[48,1152]{1,0:T(8,128)(2,1)S(1)} %bitcast.19), channel_id=1, source_target_pairs={{0,2},{2,0},{1,3},{3,1},{4,6},{6,4},{5,7},{7,5},{8,10},{10,8},{9,1... | collective-permute-start | bytes 331784 | tf_op jit(solution)/shard_map/ppermute | solution.py:467
  189.9 8.0 %collective-permute-start.16 = (bf16[96,1152]{1,0:T(8,128)(2,1)S(1)}, bf16[96,1152]{1,0:T(8,128)(2,1)S(1)}, u32[]{:S(2)}, u32[]{:S(2)}) collective-permute-start(bf16[96,1152]{1,0:T(8,128)(2,1)S(1)} %rows.1.own_ref), channel_id=1, source_target_pairs={{0,1},{1,0},{2,3},{3,2},{4,5},{5,4},{6,7},{7,6},{8,9},{9,8},{10,11... | collective-permute-start | bytes 663560 | tf_op jit(solution)/shard_map/ppermute | solution.py:23

commit v7 on v6

--- a/solution.py
+++ b/solution.py
@@ -68,8 +68,14 @@
     return sigmoid * (1.0 + value * (1.0 - sigmoid))
 
 
-def low_onehot(low):
-    return (lax.broadcasted_iota(jnp.int32, (R, R), 0) == low).astype(BF16)
+def low_onehot(low, dim=0):
+    return (lax.broadcasted_iota(jnp.int32, (R, R), dim) == low).astype(BF16)
+
+
+def low_table(tables):
+    low = (tables & 255).astype(F32)
+    padded = jnp.concatenate([low, jnp.zeros((128 - low.shape[0], R), F32)], axis=0)
+    return jnp.transpose(padded).astype(jnp.int32)
 
 
 def conv(blocks, pos, weight, picked_ref):
@@ -90,20 +96,19 @@
     return jnp.dot(weight, picked_ref[...], preferred_element_type=F32)
 
 
-def spread(act, pos, weight, parts):
+def spread(act, b, pos_ref, low_ref, weight, parts):
     terms = lax.dot_general(weight, act, (((0,), (0,)), ((), ())), preferred_element_type=F32)
+    pos = pos_ref[16 * b : 16 * b + 16, :]
     total = None
     for k in range(TAPS):
         if k == 4:
             continue
-        at = pos[k : k + 1]
-        block = at >> 8
+        block = pos[k : k + 1] >> 8
         term = terms[k * C : (k + 1) * C].astype(BF16)
         zero = jnp.zeros_like(term)
         sent = jnp.concatenate([jnp.where(block == part, term, zero) for part in parts], axis=0)
-        added = lax.dot_general(
-            sent, low_onehot(at & 255), (((1,), (1,)), ((), ())), preferred_element_type=F32
-        )
+        low = low_ref[:, 16 * b + k : 16 * b + k + 1]
+        added = jnp.dot(sent, low_onehot(low, 1), preferred_element_type=F32)
         total = added if total is None else total + added
     out = {part: total[i * C : (i + 1) * C] for i, part in enumerate(parts)}
     if 1 in out:
@@ -144,7 +149,8 @@
 
 def first_kernel(
     x_ref, got_ref, other_ref, w_ref,
-    h_ref, picked_ref, slopes_ref, last_ref, pos_ref, kept_ref, near_pos_ref, near_cot_ref, scratch,
+    h_ref, picked_ref, slopes_ref, last_ref, pos_ref, kept_ref, low_ref, near_pos_ref, near_low_ref,
+    cot_ref, scratch,
 ):
     size = x_ref.shape[0] // 2
     below, above = ordered(got_ref, other_ref)
@@ -167,9 +173,12 @@
         pos.append(at)
         kept.append(keep)
     kept_ref[6:8, :] = jnp.zeros((2, R), F32)
-    for i in range(3):
-        near_pos_ref[16 * i : 16 * (i + 1), :] = own_of(pos[i + 1], pos[i + 2])
-        near_cot_ref[each * i : each * (i + 1), :] = own_of(cots[i], cots[i + 1])
+    near = jnp.concatenate([own_of(pos[i + 1], pos[i + 2]) for i in range(3)], axis=0)
+    near_pos_ref[...] = near
+    near_low_ref[...] = low_table(near)
+    low_ref[...] = low_table(jnp.concatenate(pos, axis=0))
+    for i in range(4):
+        cot_ref[each * i : each * (i + 1), :] = cots[i]
     hidden = two_layers(blocks, pos, kept, w_ref, picked_ref, slopes_ref, last_ref, scratch)
     for i in range(2):
         h_ref[i * C : (i + 1) * C, :] = hidden[i]
@@ -204,14 +213,17 @@
     pos, kept = read_tables(pos_ref, kept_ref)
     blocks = read_blocks(x_ref, got_ref, other_ref)
     hidden = two_layers(blocks, pos, kept, w_ref, picked_ref, slopes_ref, last_ref, scratch)
-    partial = lax.dot_general(
-        joinw_ref[...], own_of(*hidden), (((0,), (0,)), ((), ())), preferred_element_type=F32
-    ).astype(BF16)
     count = share_ref.shape[0]
-    each = partial.shape[0] // count
-    for c in range(count):
-        share_ref[c, :each, :] = partial[c * each : (c + 1) * each]
-        share_ref[c, each:, :] = unit_ref[c * each : (c + 1) * each, :]
+    each = share_ref.shape[1] // 4
+    for i in range(2):
+        partial = lax.dot_general(
+            joinw_ref[...], hidden[i], (((0,), (0,)), ((), ())), preferred_element_type=F32
+        ).astype(BF16)
+        for c in range(count):
+            share_ref[c, i * each : (i + 1) * each, :] = partial[c * each : (c + 1) * each]
+            share_ref[c, (2 + i) * each : (3 + i) * each, :] = unit_ref[
+                i, c * each : (c + 1) * each, :
+            ]
 
 
 def pack_kernel(
@@ -240,26 +252,35 @@
             out_ref[i] = jnp.concatenate([w_ref[layer, k] for k in range(TAPS)], axis=1)
 
 
-def unit_kernel(cot_ref, pos_ref, dec_ref, unit_ref, scratch):
-    each = cot_ref.shape[0] // 3
-    sources = [cot_ref[each * i : each * (i + 1), :] for i in range(3)]
-    pos = [pos_ref[16 * i : 16 * (i + 1), :] for i in range(3)]
+def unit_kernel(cot_ref, pos_ref, low_ref, dec_ref, unit_ref, scratch):
+    each = cot_ref.shape[0] // 4
+    cots = [cot_ref[each * i : each * (i + 1), :] for i in range(4)]
+    targets = [(0,), (0, 1), (0, 1), (1,)]
     for k in range(TAPS):
-        if k == 4:
-            scratch[k * each : (k + 1) * each, :] = sources[1]
-            continue
-        total = None
-        for i in range(3):
-            at = pos[i][k : k + 1]
-            sent = jnp.where((at >> 8) == 2 - i, sources[i], jnp.zeros_like(sources[i]))
-            added = lax.dot_general(
-                sent, low_onehot(at & 255), (((1,), (1,)), ((), ())), preferred_element_type=F32
+        total = [None, None]
+        for i in range(4):
+            b = i + 1
+            if k == 4:
+                if b in (2, 3):
+                    scratch[b - 2, k * each : (k + 1) * each, :] = cots[i]
+                continue
+            block = pos_ref[16 * b + k : 16 * b + k + 1, :] >> 8
+            zero = jnp.zeros_like(cots[i])
+            sent = jnp.concatenate(
+                [jnp.where(block == t + 3 - b, cots[i], zero) for t in targets[i]], axis=0
             )
-            total = added if total is None else total + added
-        scratch[k * each : (k + 1) * each, :] = total.astype(BF16)
-    unit_ref[...] = lax.dot_general(
-        dec_ref[...], scratch[...], (((0,), (0,)), ((), ())), preferred_element_type=F32
-    ).astype(BF16)
+            low = low_ref[:, 16 * b + k : 16 * b + k + 1]
+            added = jnp.dot(sent, low_onehot(low, 1), preferred_element_type=F32)
+            for j, t in enumerate(targets[i]):
+                part = added[j * each : (j + 1) * each]
+                total[t] = part if total[t] is None else total[t] + part
+        if k != 4:
+            for t in range(2):
+                scratch[t, k * each : (k + 1) * each, :] = total[t].astype(BF16)
+    for t in range(2):
+        unit_ref[t] = lax.dot_general(
+            dec_ref[...], scratch[t], (((0,), (0,)), ((), ())), preferred_element_type=F32
+        ).astype(BF16)
 
 
 def slope_kernel(parts_ref, out_ref):
@@ -274,14 +295,6 @@
         out_ref[i] = grad
 
 
-def head_kernel(unit_ref, joinw_ref, kept_ref, last_ref, pack_ref):
-    unit_grad = jnp.concatenate([unit_ref[d] for d in range(unit_ref.shape[0])], axis=0)
-    gradient = jnp.dot(joinw_ref[...], unit_grad, preferred_element_type=F32)
-    masked = own_of(kept_ref[2:3, :], kept_ref[3:4, :]) * gradient
-    pack_ref[:C, :] = (masked * own_of(last_ref[0], last_ref[1])).astype(BF16)
-    pack_ref[C:, :] = masked.astype(BF16)
-
-
 def store_pack(pack_ref, masked_ref, acts, masked):
     for i in range(2):
         pack_ref[i * C : (i + 1) * C, :] = acts[i]
@@ -289,13 +302,17 @@
     pack_ref[2 * C :, :] = own_of(masked[1], masked[0]).astype(BF16)
 
 
-def top_kernel(own_ref, other_ref, pack_ref, masked_ref):
-    own, other = own_ref[...], other_ref[...]
-    first, second = own_of(own, other), own_of(other, own)
-    store_pack(
-        pack_ref, masked_ref, [first[:C], second[:C]],
-        [first[C:].astype(F32), second[C:].astype(F32)],
-    )
+def head_kernel(unit_ref, joinw_ref, kept_ref, last_ref, pack_ref, masked_ref):
+    each = unit_ref.shape[1] // 2
+    acts, masked = [], []
+    for i in range(2):
+        unit_grad = jnp.concatenate(
+            [unit_ref[d, i * each : (i + 1) * each, :] for d in range(unit_ref.shape[0])], axis=0
+        )
+        gradient = jnp.dot(joinw_ref[...], unit_grad, preferred_element_type=F32)
+        masked.append(kept_ref[2 + i : 3 + i, :] * gradient)
+        acts.append((masked[i] * last_ref[i]).astype(BF16))
+    store_pack(pack_ref, masked_ref, acts, masked)
 
 
 def weight_grad(acts, picked):
@@ -319,16 +336,16 @@
 
 def beside_kernel(has_low, *refs):
     if has_low:
-        x_ref, w_ref, pos_ref, picked_ref, low_ref, low_picked_ref, own_ref, grad_ref = refs
+        x_ref, w_ref, pos_ref, low_ref, picked_ref, lower_ref, lower_picked_ref, own_ref, grad_ref = refs
         grad_ref[...] = jnp.concatenate(
-            [weight_grad(pair_of(low_ref), both(low_picked_ref, 0)),
+            [weight_grad(pair_of(lower_ref), both(lower_picked_ref, 0)),
              weight_grad(pair_of(x_ref), both(picked_ref, 1))], axis=1,
         )
     else:
-        x_ref, w_ref, pos_ref, picked_ref, own_ref, grad_ref = refs
+        x_ref, w_ref, pos_ref, low_ref, picked_ref, own_ref, grad_ref = refs
         grad_ref[...] = weight_grad(pair_of(x_ref), both(picked_ref, 1))
     first, second = [
-        spread(act, pos_ref[16 * b : 16 * b + 16, :], w_ref[1], (0, 1, 2))
+        spread(act, b, pos_ref, low_ref, w_ref[1], (0, 1, 2))
         for b, act in zip((2, 3), pair_of(x_ref))
     ]
     own_ref[0] = first[0]
@@ -338,9 +355,8 @@
 
 
 def upper_layer(
-    x_ref, got_ref, other_ref, masked_ref, own_ref, w_ref, pos_ref, kept_ref, slopes_ref
+    x_ref, got_ref, other_ref, masked_ref, own_ref, w_ref, pos_ref, low_ref, kept_ref, slopes_ref
 ):
-    pos, kept = read_tables(pos_ref, kept_ref)
     below, above = ordered(got_ref, other_ref)
     acts = {0: below[:C], 1: below[C : 2 * C], 4: above[:C], 5: above[C : 2 * C]}
     masked = [
@@ -348,42 +364,43 @@
     ]
     gradient = [masked[i] + own_ref[i] for i in range(4)]
     for b, parts in ((0, (2,)), (1, (1, 2)), (4, (0, 1)), (5, (0,))):
-        for part, value in spread(acts[b], pos[b], w_ref[1], parts).items():
+        for part, value in spread(acts[b], b, pos_ref, low_ref, w_ref[1], parts).items():
             gradient[b + part - 2] = gradient[b + part - 2] + value
-    lower = [kept[i + 1] * gradient[i] for i in range(4)]
+    lower = [kept_ref[i + 1 : i + 2, :] * gradient[i] for i in range(4)]
     low_acts = [(lower[i] * slopes_ref[i]).astype(BF16) for i in range(4)]
     return lower, low_acts
 
 
 def back_kernel(
-    x_ref, got_ref, other_ref, masked_ref, own_ref, w_ref, pos_ref, kept_ref, slopes_ref, next_ref,
-    pack_ref, out_ref, low_ref,
+    x_ref, got_ref, other_ref, masked_ref, own_ref, w_ref, pos_ref, low_ref, kept_ref, slopes_ref,
+    next_ref, pack_ref, out_ref, lower_ref,
 ):
     lower, low_acts = upper_layer(
-        x_ref, got_ref, other_ref, masked_ref, own_ref, w_ref, pos_ref, kept_ref, slopes_ref
-    )
-    pos, kept = read_tables(pos_ref, kept_ref)
+        x_ref, got_ref, other_ref, masked_ref, own_ref, w_ref, pos_ref, low_ref, kept_ref,
+        slopes_ref,
+    )
     result = [lower[1], lower[2]]
     for b, parts in ((1, (2,)), (2, (1, 2)), (3, (0, 1)), (4, (0,))):
-        for part, value in spread(low_acts[b - 1], pos[b], w_ref[0], parts).items():
+        for part, value in spread(low_acts[b - 1], b, pos_ref, low_ref, w_ref[0], parts).items():
             result[b + part - 3] = result[b + part - 3] + value
-    masked = [kept[2 + i] * result[i] for i in range(2)]
+    masked = [kept_ref[2 + i : 3 + i, :] * result[i] for i in range(2)]
     acts = [(masked[i] * next_ref[i]).astype(BF16) for i in range(2)]
     store_pack(pack_ref, out_ref, acts, masked)
     for i in range(2):
-        low_ref[i * C : (i + 1) * C, :] = low_acts[1 + i]
+        lower_ref[i * C : (i + 1) * C, :] = low_acts[1 + i]
 
 
 def last_back_kernel(
-    x_ref, got_ref, other_ref, masked_ref, own_ref, w_ref, pos_ref, kept_ref, slopes_ref,
-    picked_ref, grad5_ref, grad43_ref, grad21_ref, low_ref, out_ref, keep_ref, send_ref,
+    x_ref, got_ref, other_ref, masked_ref, own_ref, w_ref, pos_ref, low_ref, kept_ref, slopes_ref,
+    picked_ref, grad5_ref, grad43_ref, grad21_ref, lower_ref, out_ref, keep_ref, send_ref,
 ):
     lower, low_acts = upper_layer(
-        x_ref, got_ref, other_ref, masked_ref, own_ref, w_ref, pos_ref, kept_ref, slopes_ref
+        x_ref, got_ref, other_ref, masked_ref, own_ref, w_ref, pos_ref, low_ref, kept_ref,
+        slopes_ref,
     )
     out_ref[...] = own_of(lower[1], lower[2])
     for i in range(3):
-        low_ref[i * C : (i + 1) * C, :] = own_of(low_acts[i], low_acts[i + 1])
+        lower_ref[i * C : (i + 1) * C, :] = own_of(low_acts[i], low_acts[i + 1])
     last = jnp.concatenate(
         [weight_grad(low_acts[1:3], both(picked_ref, 0)), grad5_ref[...]], axis=1
     )
@@ -395,11 +412,11 @@
     send_ref[...] = jnp.where(low_half, second, first)
 
 
-def map_kernel(low_ref, own_ref, w_ref, pos_ref, map_ref, token_ref):
+def map_kernel(lower_ref, own_ref, w_ref, pos_ref, low_ref, map_ref, token_ref):
     own = own_ref[...]
     for i, part in ((0, 2), (1, 1), (2, 0)):
-        act = low_ref[i * C : (i + 1) * C, :]
-        own = own + spread(act, pos_ref[16 * i : 16 * (i + 1), :], w_ref[0], (part,))[part]
+        act = lower_ref[i * C : (i + 1) * C, :]
+        own = own + spread(act, i, pos_ref, low_ref, w_ref[0], (part,))[part]
     map_ref[...] = own.astype(BF16)
     token_ref[...] = own[:8, :128]
 
@@ -517,17 +534,18 @@
     layer_outs = [sds((2 * C, R), BF16), sds((2, 2, wide, R), BF16), sds((4, C, R), F32), pair]
     scratch = [pltpu.VMEM((2, wide, R), BF16)]
     got, other = widen(sent, [weights[0]])
-    hidden, picked, slopes, last, pos, kept, near_pos, near_cot = call(
+    low_lanes = sds((R, 128), jnp.int32)
+    hidden, picked, slopes, last, pos, kept, low, near_pos, near_low, cots = call(
         first_kernel, "layers01", [v(pack), v(got), v(other), v(weights[0])],
         layer_outs
-        + [sds((96, R), jnp.int32), sds((8, R), F32), sds((48, R), jnp.int32),
-           sds((3 * each, R), BF16)],
+        + [sds((96, R), jnp.int32), sds((8, R), F32), low_lanes, sds((48, R), jnp.int32),
+           low_lanes, sds((4 * each, R), BF16)],
         scratch,
     )
     saved = [(picked, slopes, last)]
     unit = call(
-        unit_kernel, "unit", [v(near_cot), v(near_pos), v(dec)],
-        [sds((full, R), BF16)], [pltpu.VMEM((TAPS * each, R), BF16)],
+        unit_kernel, "unit", [v(cots), v(pos), v(low), v(dec)],
+        [sds((2, full, R), BF16)], [pltpu.VMEM((2, TAPS * each, R), BF16)],
     )[0]
     for group in range(1, depth // 2):
         got, other = widen(hidden, [unit] if group == 1 else ())
@@ -537,47 +555,46 @@
         else:
             share, picked, slopes, last = call(
                 last_layers_kernel, "lastlayers", ins + [v(joinw), v(unit)],
-                [sds((branches, 2 * each, R), BF16)] + layer_outs[1:], scratch,
+                [sds((branches, 4 * each, R), BF16)] + layer_outs[1:], scratch,
             )
         saved.append((picked, slopes, last))
     parts = exchange(share, "branch")
-    mine = call(slope_kernel, "slope", [v(parts)], [sds((branches, each, R), BF16)])[0]
-    top = call(
+    mine = call(slope_kernel, "slope", [v(parts)], [sds((branches, 2 * each, R), BF16)])[0]
+    pack_outs = [sds((3 * C, R), BF16), pair]
+    pack, masked = call(
         head_kernel, "head",
-        [v(exchange(mine, "branch")), v(joinw), v(kept), v(saved[-1][2])], [sds((2 * C, R), BF16)],
-    )[0]
-    pack_outs = [sds((3 * C, R), BF16), pair]
-    pack, masked = call(top_kernel, "top", [v(top), v(swap_cores(top))], pack_outs)
+        [v(exchange(mine, "branch")), v(joinw), v(kept), v(saved[-1][2])], pack_outs,
+    )
     grads = []
-    low = None
+    lower = None
     for group in reversed(range(depth // 2)):
         picked, slopes, _ = saved[group]
-        beside = [v(pack), v(weights[group]), v(pos), v(picked)]
-        if low is not None:
-            beside = beside + [v(low), v(saved[group + 1][0])]
+        beside = [v(pack), v(weights[group]), v(pos), v(low), v(picked)]
+        if lower is not None:
+            beside = beside + [v(lower), v(saved[group + 1][0])]
         own, grad = call(
-            functools.partial(beside_kernel, low is not None), "beside", beside,
-            [sds((4, C, R), F32), sds((C // 2, wide if low is None else 2 * wide), BF16)],
+            functools.partial(beside_kernel, lower is not None), "beside", beside,
+            [sds((4, C, R), F32), sds((C // 2, wide if lower is None else 2 * wide), BF16)],
         )
         grads.append(grad)
         got, other = widen(pack, [own])
         ins = [
-            v(pack), v(got), v(other), v(masked), v(own), v(weights[group]), v(pos), v(kept),
-            v(slopes),
+            v(pack), v(got), v(other), v(masked), v(own), v(weights[group]), v(pos), v(low),
+            v(kept), v(slopes),
         ]
         if group:
-            pack, masked, low = call(
+            pack, masked, lower = call(
                 back_kernel, "back", ins + [v(saved[group - 1][2])],
                 pack_outs + [sds((2 * C, R), BF16)],
             )
         else:
             half = sds((3 * C // 4, 2 * wide), BF16)
-            low, own, keep, send = call(
+            lower, own, keep, send = call(
                 last_back_kernel, "lastback", ins + [v(picked)] + [v(g) for g in grads],
                 [sds((3 * C, R), BF16), sds((C, R), F32), half, half],
             )
     map_grads, token = call(
-        map_kernel, "mapgrad", [v(low), v(own), v(weights[0]), v(near_pos)],
+        map_kernel, "mapgrad", [v(lower), v(own), v(weights[0]), v(near_pos), v(near_low)],
         [sds((C, R), BF16), sds((8, 128), F32)],
     )
     total = sum_over_sky(keep, send, lax.axis_size("z"), token)

time: 200 us -> 197 us (0.985)
  blocking collectives: 69.5 us -> 74.4 us
  Pallas kernels: 31.6 us -> 27.3 us
  starting transfers between devices: 53.2 us -> 49.6 us
    all_to_all x4, blocking collectives: 69.5 us -> 74.4 us  [exchange(): return lax.all_to_all(value, axes, 0, 0, tiled=True)]
    pallas_call x25 -> x24, Pallas kernels: 31.6 us -> 27.3 us  [call(): pl.pallas_call(body, name=name, in_specs=specs, out_specs=[pl.BlockSpec(m...]
    ppermute x9 -> x8, starting transfers between devices: 37.7 us -> 34.1 us  [swap_cores(): return lax.ppermute(value, 'core', [(0, 1), (1, 0)])]
    ppermute x9 -> x8, waiting for transfers between devices: 8.99 us -> 8.11 us  [swap_cores(): return lax.ppermute(value, 'core', [(0, 1), (1, 0)])]
  transfers between devices with their start and end apart: 17 -> 16, of which waited for: 17 -> 16; matrix products, arithmetic and copies ran while one was open for 0% -> 0% of each run, Pallas kernels for 5% -> 4%
where the time goes in v7:
time: 197 us; the launch traced here: 196 us
  blocking collectives  74.4 us (38%)
  starting transfers between devices  49.6 us (25%)
  waiting for transfers between devices  41.9 us (21%)
  Pallas kernels  27.3 us (14%)
  local copies, waits for them, and re-layouts  2.03 us (1%)
    all_to_all x4, blocking collectives, exchange(): return lax.all_to_all(value, axes, 0, 0, tiled=True)  74.4 us
    ppermute x8, starting transfers between devices, swap_cores(): return lax.ppermute(value, 'core', [(0, 1), (1, 0)])  34.1 us
    ppermute x6, waiting for transfers between devices, widen(): got = lax.ppermute(value, SKY, pairs)  27.6 us
    pallas_call x24, Pallas kernels, call(): pl.pallas_call(body, name=name, in_specs=specs, out_specs=[pl.BlockSpec(m...  27.3 us
    ppermute x8, waiting for transfers between devices, swap_cores(): return lax.ppermute(value, 'core', [(0, 1), (1, 0)])  8.11 us
    ppermute x6, starting transfers between devices, widen(): got = lax.ppermute(value, SKY, pairs)  7.75 us
    ppermute x2, starting transfers between devices, swap_halves(): return lax.ppermute(value, 'yh', [(0, 1), (1, 0)])  7.75 us
    ppermute x2, waiting for transfers between devices, swap_halves(): return lax.ppermute(value, 'yh', [(0, 1), (1, 0)])  6.17 us
  transfers between devices with their start and end apart: 16, of which 16 were waited for; matrix products, arithmetic and copies ran while one was open for 0% of the time, Pallas kernels for 4%

profile of v7, /device:TPU:1, one launch (start us, length us, event | category | flops | bytes accessed | tf_op | source)
XLA Modules:
  0.0 196.2 jit_solution(638771874552590348)
XLA Ops:
  2.1 8.8 %collective-permute-start = (bf16[112,256]{1,0:T(8,128)(2,1)}, bf16[112,256]{1,0:T(8,128)(2,1)S(1)}, u32[]{:S(2)}, u32[]{:S(2)}) collective-permute-start(bf16[112,256]{1,0:T(8,128)(2,1)} %pack.1.own_ref), channel_id=1, source_target_pairs={{0,1},{1,0},{2,3},{3,2},{4,5},{5,4},{6,7},{7,6},{8,9},{9,8},{10,11... | collective-permute-start | bytes 172040 | tf_op jit(solution)/shard_map/ppermute | solution.py:23
  15.7 4.0 %collective-permute-done.1.refs_0_ = bf16[192,256]{1,0:T(8,128)(2,1)S(1)} collective-permute-done((bf16[192,256]{1,0:T(8,128)(2,1)S(1)}, bf16[192,256]{1,0:T(8,128)(2,1)S(1)}, u32[]{:S(2)}, u32[]{:S(2)}) %collective-permute-start.1) | collective-permute-done | bytes 98336 | tf_op jit(solution)/shard_map/ppermute | solution.py:29
  19.7 1.9 collective-permute-start.2
  22.9 2.6 %layers01.1 = (bf16[128,256]{1,0:T(8,128)(2,1)S(1)}, bf16[2,2,576,256]{3,2,1,0:T(8,128)(2,1)S(1)}, f32[4,64,256]{2,1,0:T(8,128)S(1)}, f32[2,64,256]{2,1,0:T(8,12...) custom-call(bf16[224,256]{1,0:T(8,128)(2,1)S(1)} %get-tuple-element., ...), custom_call_target="tpu_custom_call" | custom-call | tf_op jit(solution)/shard_map/layers01/pallas_call | solution.py:456
  26.8 1.7 unit.1.refs_1_.unit_ref
  28.5 3.5 %collective-permute-done.3.refs_0_ = bf16[128,256]{1,0:T(8,128)(2,1)S(1)} collective-permute-done((bf16[128,256]{1,0:T(8,128)(2,1)S(1)}, bf16[128,256]{1,0:T(8,128)(2,1)S(1)}, u32[]{:S(2)}, u32[]{:S(2)}) %collective-permute-start.3) | collective-permute-done | bytes 65568 | tf_op jit(solution)/shard_map/ppermute | solution.py:29
  32.0 1.9 collective-permute-start.4
  35.1 2.6 %layers.1 = (bf16[128,256]{1,0:T(8,128)(2,1)S(1)}, bf16[2,2,576,256]{3,2,1,0:T(8,128)(2,1)S(1)}, f32[4,64,256]{2,1,0:T(8,128)S(1)}, f32[2,64,256]{2,1,0:T(8,128)S(1)}) custom-call(bf16[128,256]{1,0:T(8,128)(2,1)S(1)} %get-tuple-element.48.x_ref, bf16[128,256]{1,0:T(8,128)(2,1)S(1)} %relay.6.got_ref, bf16[128,256]{1,0:T(8,128)(2,1)S(1)} %collective-permute-done.4.other_ref, ...), custom_call_target="tpu_custom_call" | custom-call | tf_op jit(solution)/shard_map/layers/pallas_call | solution.py:456
  39.0 5.2 %collective-permute-done.5.got_ref = bf16[128,256]{1,0:T(8,128)(2,1)S(1)} collective-permute-done((bf16[128,256]{1,0:T(8,128)(2,1)S(1)}, bf16[128,256]{1,0:T(8,128)(2,1)S(1)}, u32[]{:S(2)}, u32[]{:S(2)}) %collective-permute-start.5) | collective-permute-done | bytes 65568 | tf_op jit(solution)/shard_map/ppermute | solution.py:29
  44.2 2.5 %collective-permute-start.6 = (bf16[128,256]{1,0:T(8,128)(2,1)S(1)}, bf16[128,256]{1,0:T(8,128)(2,1)S(1)}, u32[]{:S(2)}, u32[]{:S(2)}) collective-permute-start(bf16[128,256]{1,0:T(8,128)(2,1)S(1)} %collective-permute-done.5.got_ref), channel_id=1, source_target_pairs={{0,1},{1,0},{2,3},{3,2},{4,5},{5,4},{6,7},{7,6},{8,9},{9,8},{10,11... | collective-permute-start | bytes 196616 | tf_op jit(solution)/shard_map/ppermute | solution.py:23
  47.7 2.8 %lastlayers.1 = (bf16[8,128,256]{2,1,0:T(8,128)(2,1)S(1)}, bf16[2,2,576,256]{3,2,1,0:T(8,128)(2,1)S(1)}, f32[4,64,256]{2,1,0:T(8,128)S(1)}, f32[2,64,256]{2,1,0:T(8,128)S(1)}) custom-call(bf16[128,256]{1,0:T(8,128)(2,1)S(1)} %get-tuple-element.54.x_ref, bf16[128,256]{1,0:T(8,128)(2,1)S(1)} %collective-permute-done.5.got_ref, ...), custom_call_target="tpu_custom_call" | custom-call | tf_op jit(solution)/shard_map/lastlayers/pallas_call | solution.py:456
  50.4 13.2 %all_to_all.20.parts_ref = bf16[8,128,256]{2,1,0:T(8,128)(2,1)S(1)} all-to-all(bf16[8,128,256]{2,1,0:T(8,128)(2,1)S(1)} %get-tuple-element.56), channel_id=1, replica_groups=mesh['branch'=8,'z'=16,'yh'=2,'core'=2] {'branch'}, dimensions={0} | all-to-all | bytes 1048576 | tf_op jit(solution)/shard_map/all_to_all | solution.py:472
  63.8 8.9 %all_to_all.21.unit_ref = bf16[8,64,256]{2,1,0:T(8,128)(2,1)S(1)} all-to-all(bf16[8,64,256]{2,1,0:T(8,128)(2,1)S(1)} %slope.1), channel_id=1, replica_groups=mesh['branch'=8,'z'=16,'yh'=2,'core'=2] {'branch'}, dimensions={0} | all-to-all | bytes 524288 | tf_op jit(solution)/shard_map/all_to_all | solution.py:472
  75.4 5.6 %collective-permute-done.7.refs_0_ = bf16[192,256]{1,0:T(8,128)(2,1)S(1)} collective-permute-done((bf16[192,256]{1,0:T(8,128)(2,1)S(1)}, bf16[192,256]{1,0:T(8,128)(2,1)S(1)}, u32[]{:S(2)}, u32[]{:S(2)}) %collective-permute-start.7) | collective-permute-done | bytes 98336 | tf_op jit(solution)/shard_map/ppermute | solution.py:29
  81.0 4.7 %collective-permute-start.8 = (bf16[192,256]{1,0:T(8,128)(2,1)S(1)}, bf16[192,256]{1,0:T(8,128)(2,1)S(1)}, u32[]{:S(2)}, u32[]{:S(2)}) collective-permute-start(bf16[192,256]{1,0:T(8,128)(2,1)S(1)} %relay.7.got_ref), channel_id=1, source_target_pairs={{0,1},{1,0},{2,3},{3,2},{4,5},{5,4},{6,7},{7,6},{8,9},{9,8},{10,11... | collective-permute-start | bytes 294920 | tf_op jit(solution)/shard_map/ppermute | solution.py:23
  86.5 3.0 %back.2 = (bf16[192,256]{1,0:T(8,128)(2,1)S(1)}, f32[2,64,256]{2,1,0:T(8,128)S(1)}, bf16[128,256]{1,0:T(8,128)(2,1)S(1)}) custom-call(bf16[192,256]{1,0:T(8,128)(2,1)S(1)} %get-tuple-element.58.refs_0_.x_ref, bf16[192,256]{1,0:T(8,128)(2,1)S(1)} %relay.7.got_ref, bf16[192,256]{1,0:T(8,128)(2,1)S(1)} %collective-permute-done.8.other_ref, ...), custom_call_target="tpu_custom_call" | custom-call | tf_op jit(solution)/shard_map/back/pallas_call | solution.py:456
  90.7 1.7 beside.4
  92.4 4.6 %collective-permute-done.9.refs_0_ = bf16[192,256]{1,0:T(8,128)(2,1)S(1)} collective-permute-done((bf16[192,256]{1,0:T(8,128)(2,1)S(1)}, bf16[192,256]{1,0:T(8,128)(2,1)S(1)}, u32[]{:S(2)}, u32[]{:S(2)}) %collective-permute-start.9) | collective-permute-done | bytes 98336 | tf_op jit(solution)/shard_map/ppermute | solution.py:29
  97.0 3.7 %collective-permute-start.10 = (bf16[192,256]{1,0:T(8,128)(2,1)S(1)}, bf16[192,256]{1,0:T(8,128)(2,1)S(1)}, u32[]{:S(2)}, u32[]{:S(2)}) collective-permute-start(bf16[192,256]{1,0:T(8,128)(2,1)S(1)} %relay.8.got_ref), channel_id=1, source_target_pairs={{0,1},{1,0},{2,3},{3,2},{4,5},{5,4},{6,7},{7,6},{8,9},{9,8},{10,11... | collective-permute-start | bytes 294920 | tf_op jit(solution)/shard_map/ppermute | solution.py:23
  101.6 3.0 %back.3 = (bf16[192,256]{1,0:T(8,128)(2,1)S(1)}, f32[2,64,256]{2,1,0:T(8,128)S(1)}, bf16[128,256]{1,0:T(8,128)(2,1)S(1)}) custom-call(bf16[192,256]{1,0:T(8,128)(2,1)S(1)} %get-tuple-element.64.refs_0_.x_ref, bf16[192,256]{1,0:T(8,128)(2,1)S(1)} %relay.8.got_ref, bf16[192,256]{1,0:T(8,128)(2,1)S(1)} %collective-permute-done.10.other_ref, ...), custom_call_target="tpu_custom_call" | custom-call | tf_op jit(solution)/shard_map/back/pallas_call | solution.py:456
  105.9 1.7 beside.5
  107.6 4.7 %collective-permute-done.11.refs_0_ = bf16[192,256]{1,0:T(8,128)(2,1)S(1)} collective-permute-done((bf16[192,256]{1,0:T(8,128)(2,1)S(1)}, bf16[192,256]{1,0:T(8,128)(2,1)S(1)}, u32[]{:S(2)}, u32[]{:S(2)}) %collective-permute-start.11) | collective-permute-done | bytes 98336 | tf_op jit(solution)/shard_map/ppermute | solution.py:29
  112.2 3.7 %collective-permute-start.12 = (bf16[192,256]{1,0:T(8,128)(2,1)S(1)}, bf16[192,256]{1,0:T(8,128)(2,1)S(1)}, u32[]{:S(2)}, u32[]{:S(2)}) collective-permute-start(bf16[192,256]{1,0:T(8,128)(2,1)S(1)} %relay.9.got_ref), channel_id=1, source_target_pairs={{0,1},{1,0},{2,3},{3,2},{4,5},{5,4},{6,7},{7,6},{8,9},{9,8},{10,11... | collective-permute-start | bytes 294920 | tf_op jit(solution)/shard_map/ppermute | solution.py:23
  116.9 1.6 lastback.1
  118.5 5.6 %collective-permute-start.13 = (bf16[48,1152]{1,0:T(8,128)(2,1)S(1)}, bf16[48,1152]{1,0:T(8,128)(2,1)S(1)}, u32[]{:S(2)}, u32[]{:S(2)}) collective-permute-start(bf16[48,1152]{1,0:T(8,128)(2,1)S(1)} %get-tuple-element.86), channel_id=1, source_target_pairs={{0,2},{2,0},{1,3},{3,1},{4,6},{6,4},{5,7},{7,5},{8,10},{10,8},{9,1... | collective-permute-start | bytes 331784 | tf_op jit(solution)/shard_map/ppermute | solution.py:484
  124.1 1.8 mapgrad.1
  127.3 34.8 %all_to_all.22 = bf16[16,4,8,128]{3,2,1,0:T(8,128)(2,1)S(1)} all-to-all(bf16[16,4,8,128]{3,2,1,0:T(8,128)(2,1)S(1)} %bitcast.26), channel_id=1, replica_groups=mesh['branch'=8,'z'=16,'yh'=2,'core'=2] {'z'}, dimensions={0} | all-to-all | bytes 262144 | tf_op jit(solution)/shard_map/all_to_all | solution.py:472
  162.2 17.5 %all_to_all.23 = bf16[16,4,8,128]{3,2,1,0:T(8,128)(2,1)S(1)} all-to-all(bf16[16,4,8,128]{3,2,1,0:T(8,128)(2,1)S(1)} %broadcast_in_dim.13), channel_id=1, replica_groups=mesh['branch'=8,'z'=16,'yh'=2,'core'=2] {'z'}, dimensions={0} | all-to-all | bytes 262144 | tf_op jit(solution)/shard_map/all_to_all | solution.py:472
  179.7 2.1 %collective-permute-start.14 = (bf16[48,1152]{1,0:T(8,128)(2,1)S(1)}, bf16[48,1152]{1,0:T(8,128)(2,1)S(1)}, u32[]{:S(2)}, u32[]{:S(2)}) collective-permute-start(bf16[48,1152]{1,0:T(8,128)(2,1)S(1)} %bitcast.19), channel_id=1, source_target_pairs={{0,2},{2,0},{1,3},{3,1},{4,6},{6,4},{5,7},{7,5},{8,10},{10,8},{9,1... | collective-permute-start | bytes 331784 | tf_op jit(solution)/shard_map/ppermute | solution.py:484
  181.8 4.9 %collective-permute-done.14.got_ref = bf16[48,1152]{1,0:T(8,128)(2,1)S(1)} collective-permute-done((bf16[48,1152]{1,0:T(8,128)(2,1)S(1)}, bf16[48,1152]{1,0:T(8,128)(2,1)S(1)}, u32[]{:S(2)}, u32[]{:S(2)}) %collective-permute-start.14) | collective-permute-done | bytes 110624 | tf_op jit(solution)/shard_map/ppermute | solution.py:484
  186.7 6.9 %collective-permute-start.15 = (bf16[96,1152]{1,0:T(8,128)(2,1)S(1)}, bf16[96,1152]{1,0:T(8,128)(2,1)S(1)}, u32[]{:S(2)}, u32[]{:S(2)}) collective-permute-start(bf16[96,1152]{1,0:T(8,128)(2,1)S(1)} %rows.1.own_ref), channel_id=1, source_target_pairs={{0,1},{1,0},{2,3},{3,2},{4,5},{5,4},{6,7},{7,6},{8,9},{9,8},{10,11... | collective-permute-start | bytes 663560 | tf_op jit(solution)/shard_map/ppermute | solution.py:23
  194.7 1.5 final.1
  (40 shorter events, 22.7 us)
Async XLA Ops:
  2.1 9.9 %collective-permute-start = (bf16[112,256]{1,0:T(8,128)(2,1)}, bf16[112,256]{1,0:T(8,128)(2,1)S(1)}, u32[]{:S(2)}, u32[]{:S(2)}) collective-permute-start(bf16[112,256]{1,0:T(8,128)(2,1)} %pack.1.own_ref), channel_id=1, source_target_pairs={{0,1},{1,0},{2,3},{3,2},{4,5},{5,4},{6,7},{7,6},{8,9},{9,8},{10,11... | collective-permute-start | bytes 172040 | tf_op jit(solution)/shard_map/ppermute | solution.py:23
  12.0 0.8 copy-start.1
  12.8 6.9 %collective-permute-start.1 = (bf16[192,256]{1,0:T(8,128)(2,1)S(1)}, bf16[192,256]{1,0:T(8,128)(2,1)S(1)}, u32[]{:S(2)}, u32[]{:S(2)}) collective-permute-start(bf16[192,256]{1,0:T(8,128)(2,1)S(1)} %get-tuple-element.46), channel_id=1, source_target_pairs={{0,2},{2,4},{4,6},{6,8},{8,10},{10,12},{12,14},{14,16},{16,18},{18... | collective-permute-start | bytes 294920 | tf_op jit(solution)/shard_map/ppermute | solution.py:29
  14.1 1.2 copy-start
  15.3 11.5 %copy-start.2 = (bf16[9,32,256]{2,1,0:T(8,128)(2,1)S(1)}, bf16[9,32,256]{2,1,0:T(8,128)(2,1)}, u32[]{:S(2)}) copy-start(bf16[9,32,256]{2,1,0:T(8,128)(2,1)} %param.12) | copy-start | bytes 442372
  19.7 28.0 %copy-start.3 = (bf16[256,64]{0,1:T(8,128)(2,1)S(1)}, bf16[256,64]{0,1:T(8,128)(2,1)}, u32[]{:S(2)}) copy-start(bf16[256,64]{0,1:T(8,128)(2,1)} %param.11) | copy-start | bytes 98308
  19.7 3.2 %collective-permute-start.2 = (bf16[192,256]{1,0:T(8,128)(2,1)S(1)}, bf16[192,256]{1,0:T(8,128)(2,1)S(1)}, u32[]{:S(2)}, u32[]{:S(2)}) collective-permute-start(bf16[192,256]{1,0:T(8,128)(2,1)S(1)} %relay.5.got_ref), channel_id=1, source_target_pairs={{0,1},{1,0},{2,3},{3,2},{4,5},{5,4},{6,7},{7,6},{8,9},{9,8},{10,11... | collective-permute-start | bytes 294920 | tf_op jit(solution)/shard_map/ppermute | solution.py:23
  25.5 6.5 %collective-permute-start.3 = (bf16[128,256]{1,0:T(8,128)(2,1)S(1)}, bf16[128,256]{1,0:T(8,128)(2,1)S(1)}, u32[]{:S(2)}, u32[]{:S(2)}) collective-permute-start(bf16[128,256]{1,0:T(8,128)(2,1)S(1)} %get-tuple-element.48.x_ref), channel_id=1, source_target_pairs={{0,2},{2,4},{4,6},{6,8},{8,10},{10,12},{12,14},{14,16},{16,18},{18... | collective-permute-start | bytes 196616 | tf_op jit(solution)/shard_map/ppermute | solution.py:29
  32.0 3.1 %collective-permute-start.4 = (bf16[128,256]{1,0:T(8,128)(2,1)S(1)}, bf16[128,256]{1,0:T(8,128)(2,1)S(1)}, u32[]{:S(2)}, u32[]{:S(2)}) collective-permute-start(bf16[128,256]{1,0:T(8,128)(2,1)S(1)} %relay.6.got_ref), channel_id=1, source_target_pairs={{0,1},{1,0},{2,3},{3,2},{4,5},{5,4},{6,7},{7,6},{8,9},{9,8},{10,11... | collective-permute-start | bytes 196616 | tf_op jit(solution)/shard_map/ppermute | solution.py:23
  37.7 6.5 %collective-permute-start.5 = (bf16[128,256]{1,0:T(8,128)(2,1)S(1)}, bf16[128,256]{1,0:T(8,128)(2,1)S(1)}, u32[]{:S(2)}, u32[]{:S(2)}) collective-permute-start(bf16[128,256]{1,0:T(8,128)(2,1)S(1)} %get-tuple-element.54.x_ref), channel_id=1, source_target_pairs={{0,2},{2,4},{4,6},{6,8},{8,10},{10,12},{12,14},{14,16},{16,18},{18... | collective-permute-start | bytes 196616 | tf_op jit(solution)/shard_map/ppermute | solution.py:29
  44.2 3.4 %collective-permute-start.6 = (bf16[128,256]{1,0:T(8,128)(2,1)S(1)}, bf16[128,256]{1,0:T(8,128)(2,1)S(1)}, u32[]{:S(2)}, u32[]{:S(2)}) collective-permute-start(bf16[128,256]{1,0:T(8,128)(2,1)S(1)} %collective-permute-done.5.got_ref), channel_id=1, source_target_pairs={{0,1},{1,0},{2,3},{3,2},{4,5},{5,4},{6,7},{7,6},{8,9},{9,8},{10,11... | collective-permute-start | bytes 196616 | tf_op jit(solution)/shard_map/ppermute | solution.py:23
  72.8 8.2 %collective-permute-start.7 = (bf16[192,256]{1,0:T(8,128)(2,1)S(1)}, bf16[192,256]{1,0:T(8,128)(2,1)S(1)}, u32[]{:S(2)}, u32[]{:S(2)}) collective-permute-start(bf16[192,256]{1,0:T(8,128)(2,1)S(1)} %get-tuple-element.58.refs_0_.x_ref), channel_id=1, source_target_pairs={{0,2},{2,4},{4,6},{6,8},{8,10},{10,12},{12,14},{14,16},{16,18},{18... | collective-permute-start | bytes 294920 | tf_op jit(solution)/shard_map/ppermute | solution.py:29
  81.0 5.4 %collective-permute-start.8 = (bf16[192,256]{1,0:T(8,128)(2,1)S(1)}, bf16[192,256]{1,0:T(8,128)(2,1)S(1)}, u32[]{:S(2)}, u32[]{:S(2)}) collective-permute-start(bf16[192,256]{1,0:T(8,128)(2,1)S(1)} %relay.7.got_ref), channel_id=1, source_target_pairs={{0,1},{1,0},{2,3},{3,2},{4,5},{5,4},{6,7},{7,6},{8,9},{9,8},{10,11... | collective-permute-start | bytes 294920 | tf_op jit(solution)/shard_map/ppermute | solution.py:23
  89.4 7.5 %collective-permute-start.9 = (bf16[192,256]{1,0:T(8,128)(2,1)S(1)}, bf16[192,256]{1,0:T(8,128)(2,1)S(1)}, u32[]{:S(2)}, u32[]{:S(2)}) collective-permute-start(bf16[192,256]{1,0:T(8,128)(2,1)S(1)} %get-tuple-element.64.refs_0_.x_ref), channel_id=1, source_target_pairs={{0,2},{2,4},{4,6},{6,8},{8,10},{10,12},{12,14},{14,16},{16,18},{18... | collective-permute-start | bytes 294920 | tf_op jit(solution)/shard_map/ppermute | solution.py:29
  97.0 4.6 %collective-permute-start.10 = (bf16[192,256]{1,0:T(8,128)(2,1)S(1)}, bf16[192,256]{1,0:T(8,128)(2,1)S(1)}, u32[]{:S(2)}, u32[]{:S(2)}) collective-permute-start(bf16[192,256]{1,0:T(8,128)(2,1)S(1)} %relay.8.got_ref), channel_id=1, source_target_pairs={{0,1},{1,0},{2,3},{3,2},{4,5},{5,4},{6,7},{7,6},{8,9},{9,8},{10,11... | collective-permute-start | bytes 294920 | tf_op jit(solution)/shard_map/ppermute | solution.py:23
  104.6 7.6 %collective-permute-start.11 = (bf16[192,256]{1,0:T(8,128)(2,1)S(1)}, bf16[192,256]{1,0:T(8,128)(2,1)S(1)}, u32[]{:S(2)}, u32[]{:S(2)}) collective-permute-start(bf16[192,256]{1,0:T(8,128)(2,1)S(1)} %get-tuple-element.71.refs_0_.x_ref), channel_id=1, source_target_pairs={{0,2},{2,4},{4,6},{6,8},{8,10},{10,12},{12,14},{14,16},{16,18},{18... | collective-permute-start | bytes 294920 | tf_op jit(solution)/shard_map/ppermute | solution.py:29
  112.2 4.6 %collective-permute-start.12 = (bf16[192,256]{1,0:T(8,128)(2,1)S(1)}, bf16[192,256]{1,0:T(8,128)(2,1)S(1)}, u32[]{:S(2)}, u32[]{:S(2)}) collective-permute-start(bf16[192,256]{1,0:T(8,128)(2,1)S(1)} %relay.9.got_ref), channel_id=1, source_target_pairs={{0,1},{1,0},{2,3},{3,2},{4,5},{5,4},{6,7},{7,6},{8,9},{9,8},{10,11... | collective-permute-start | bytes 294920 | tf_op jit(solution)/shard_map/ppermute | solution.py:23
  118.5 8.8 %collective-permute-start.13 = (bf16[48,1152]{1,0:T(8,128)(2,1)S(1)}, bf16[48,1152]{1,0:T(8,128)(2,1)S(1)}, u32[]{:S(2)}, u32[]{:S(2)}) collective-permute-start(bf16[48,1152]{1,0:T(8,128)(2,1)S(1)} %get-tuple-element.86), channel_id=1, source_target_pairs={{0,2},{2,0},{1,3},{3,1},{4,6},{6,4},{5,7},{7,5},{8,10},{10,8},{9,1... | collective-permute-start | bytes 331784 | tf_op jit(solution)/shard_map/ppermute | solution.py:484
  179.7 7.0 %collective-permute-start.14 = (bf16[48,1152]{1,0:T(8,128)(2,1)S(1)}, bf16[48,1152]{1,0:T(8,128)(2,1)S(1)}, u32[]{:S(2)}, u32[]{:S(2)}) collective-permute-start(bf16[48,1152]{1,0:T(8,128)(2,1)S(1)} %bitcast.19), channel_id=1, source_target_pairs={{0,2},{2,0},{1,3},{3,1},{4,6},{6,4},{5,7},{7,5},{8,10},{10,8},{9,1... | collective-permute-start | bytes 331784 | tf_op jit(solution)/shard_map/ppermute | solution.py:484
  186.7 8.0 %collective-permute-start.15 = (bf16[96,1152]{1,0:T(8,128)(2,1)S(1)}, bf16[96,1152]{1,0:T(8,128)(2,1)S(1)}, u32[]{:S(2)}, u32[]{:S(2)}) collective-permute-start(bf16[96,1152]{1,0:T(8,128)(2,1)S(1)} %rows.1.own_ref), channel_id=1, source_target_pairs={{0,1},{1,0},{2,3},{3,2},{4,5},{5,4},{6,7},{7,6},{8,9},{9,8},{10,11... | collective-permute-start | bytes 663560 | tf_op jit(solution)/shard_map/ppermute | solution.py:23

commit v8 on v7

--- a/solution.py
+++ b/solution.py
@@ -177,8 +177,8 @@
     near_pos_ref[...] = near
     near_low_ref[...] = low_table(near)
     low_ref[...] = low_table(jnp.concatenate(pos, axis=0))
-    for i in range(4):
-        cot_ref[each * i : each * (i + 1), :] = cots[i]
+    for i in range(3):
+        cot_ref[each * i : each * (i + 1), :] = own_of(cots[i], cots[i + 1])
     hidden = two_layers(blocks, pos, kept, w_ref, picked_ref, slopes_ref, last_ref, scratch)
     for i in range(2):
         h_ref[i * C : (i + 1) * C, :] = hidden[i]
@@ -213,17 +213,14 @@
     pos, kept = read_tables(pos_ref, kept_ref)
     blocks = read_blocks(x_ref, got_ref, other_ref)
     hidden = two_layers(blocks, pos, kept, w_ref, picked_ref, slopes_ref, last_ref, scratch)
+    partial = lax.dot_general(
+        joinw_ref[...], own_of(*hidden), (((0,), (0,)), ((), ())), preferred_element_type=F32
+    ).astype(BF16)
     count = share_ref.shape[0]
-    each = share_ref.shape[1] // 4
-    for i in range(2):
-        partial = lax.dot_general(
-            joinw_ref[...], hidden[i], (((0,), (0,)), ((), ())), preferred_element_type=F32
-        ).astype(BF16)
-        for c in range(count):
-            share_ref[c, i * each : (i + 1) * each, :] = partial[c * each : (c + 1) * each]
-            share_ref[c, (2 + i) * each : (3 + i) * each, :] = unit_ref[
-                i, c * each : (c + 1) * each, :
-            ]
+    each = partial.shape[0] // count
+    for c in range(count):
+        share_ref[c, :each, :] = partial[c * each : (c + 1) * each]
+        share_ref[c, each:, :] = unit_ref[c * each : (c + 1) * each, :]
 
 
 def pack_kernel(
@@ -253,34 +250,23 @@
 
 
 def unit_kernel(cot_ref, pos_ref, low_ref, dec_ref, unit_ref, scratch):
-    each = cot_ref.shape[0] // 4
-    cots = [cot_ref[each * i : each * (i + 1), :] for i in range(4)]
-    targets = [(0,), (0, 1), (0, 1), (1,)]
+    each = cot_ref.shape[0] // 3
+    cots = [cot_ref[each * i : each * (i + 1), :] for i in range(3)]
     for k in range(TAPS):
-        total = [None, None]
-        for i in range(4):
-            b = i + 1
-            if k == 4:
-                if b in (2, 3):
-                    scratch[b - 2, k * each : (k + 1) * each, :] = cots[i]
-                continue
-            block = pos_ref[16 * b + k : 16 * b + k + 1, :] >> 8
-            zero = jnp.zeros_like(cots[i])
-            sent = jnp.concatenate(
-                [jnp.where(block == t + 3 - b, cots[i], zero) for t in targets[i]], axis=0
-            )
-            low = low_ref[:, 16 * b + k : 16 * b + k + 1]
+        if k == 4:
+            scratch[k * each : (k + 1) * each, :] = cots[1]
+            continue
+        total = None
+        for i in range(3):
+            block = pos_ref[16 * i + k : 16 * i + k + 1, :] >> 8
+            sent = jnp.where(block == 2 - i, cots[i], jnp.zeros_like(cots[i]))
+            low = low_ref[:, 16 * i + k : 16 * i + k + 1]
             added = jnp.dot(sent, low_onehot(low, 1), preferred_element_type=F32)
-            for j, t in enumerate(targets[i]):
-                part = added[j * each : (j + 1) * each]
-                total[t] = part if total[t] is None else total[t] + part
-        if k != 4:
-            for t in range(2):
-                scratch[t, k * each : (k + 1) * each, :] = total[t].astype(BF16)
-    for t in range(2):
-        unit_ref[t] = lax.dot_general(
-            dec_ref[...], scratch[t], (((0,), (0,)), ((), ())), preferred_element_type=F32
-        ).astype(BF16)
+            total = added if total is None else total + added
+        scratch[k * each : (k + 1) * each, :] = total.astype(BF16)
+    unit_ref[...] = lax.dot_general(
+        dec_ref[...], scratch[...], (((0,), (0,)), ((), ())), preferred_element_type=F32
+    ).astype(BF16)
 
 
 def slope_kernel(parts_ref, out_ref):
@@ -290,9 +276,15 @@
     each = total.shape[0] // 2
     joined = total[:each]
     slope = slope_of(joined, jax.nn.sigmoid(joined)).astype(BF16).astype(F32)
-    grad = (total[each:] * slope).astype(BF16)
+    out_ref[...] = (total[each:] * slope).astype(BF16)
+
+
+def copies_kernel(own_ref, other_ref, out_ref):
+    each = own_ref.shape[0]
+    first, second = ordered(own_ref, other_ref)
     for i in range(out_ref.shape[0]):
-        out_ref[i] = grad
+        out_ref[i, :each, :] = first
+        out_ref[i, each:, :] = second
 
 
 def store_pack(pack_ref, masked_ref, acts, masked):
@@ -539,13 +531,13 @@
         first_kernel, "layers01", [v(pack), v(got), v(other), v(weights[0])],
         layer_outs
         + [sds((96, R), jnp.int32), sds((8, R), F32), low_lanes, sds((48, R), jnp.int32),
-           low_lanes, sds((4 * each, R), BF16)],
+           low_lanes, sds((3 * each, R), BF16)],
         scratch,
     )
     saved = [(picked, slopes, last)]
     unit = call(
-        unit_kernel, "unit", [v(cots), v(pos), v(low), v(dec)],
-        [sds((2, full, R), BF16)], [pltpu.VMEM((2, TAPS * each, R), BF16)],
+        unit_kernel, "unit", [v(cots), v(near_pos), v(near_low), v(dec)],
+        [sds((full, R), BF16)], [pltpu.VMEM((TAPS * each, R), BF16)],
     )[0]
     for group in range(1, depth // 2):
         got, other = widen(hidden, [unit] if group == 1 else ())
@@ -555,11 +547,15 @@
         else:
             share, picked, slopes, last = call(
                 last_layers_kernel, "lastlayers", ins + [v(joinw), v(unit)],
-                [sds((branches, 4 * each, R), BF16)] + layer_outs[1:], scratch,
+                [sds((branches, 2 * each, R), BF16)] + layer_outs[1:], scratch,
             )
         saved.append((picked, slopes, last))
     parts = exchange(share, "branch")
-    mine = call(slope_kernel, "slope", [v(parts)], [sds((branches, 2 * each, R), BF16)])[0]
+    mine = call(slope_kernel, "slope", [v(parts)], [sds((each, R), BF16)])[0]
+    mine = call(
+        copies_kernel, "copies", [v(mine), v(swap_cores(mine))],
+        [sds((branches, 2 * each, R), BF16)],
+    )[0]
     pack_outs = [sds((3 * C, R), BF16), pair]
     pack, masked = call(
         head_kernel, "head",

time: 197 us -> 198 us (level)
  blocking collectives: 74.4 us -> 71.9 us
  starting transfers between devices: 49.6 us -> 52 us
    all_to_all x4, blocking collectives: 74.4 us -> 71.9 us  [exchange(): return lax.all_to_all(value, axes, 0, 0, tiled=True)]
    ppermute x8 -> x9, starting transfers between devices: 34.1 us -> 36.5 us  [swap_cores(): return lax.ppermute(value, 'core', [(0, 1), (1, 0)])]
    ppermute x8 -> x9, waiting for transfers between devices: 8.11 us -> 8.93 us  [swap_cores(): return lax.ppermute(value, 'core', [(0, 1), (1, 0)])]
    pallas_call x24 -> x25, Pallas kernels: 27.3 us -> 26.9 us  [call(): pl.pallas_call(body, name=name, in_specs=specs, out_specs=[pl.BlockSpec(m...]
  transfers between devices with their start and end apart: 16 -> 17, of which waited for: 16 -> 17; matrix products, arithmetic and copies ran while one was open for 0% -> 0% of each run, Pallas kernels for 4% -> 4%
where the time goes in v8:
time: 198 us; the launch traced here: 197 us
  blocking collectives  71.9 us (36%)
  starting transfers between devices  52 us (26%)
  waiting for transfers between devices  43.1 us (22%)
  Pallas kernels  26.9 us (14%)
  local copies, waits for them, and re-layouts  2.03 us (1%)
    all_to_all x4, blocking collectives, exchange(): return lax.all_to_all(value, axes, 0, 0, tiled=True)  71.9 us
    ppermute x9, starting transfers between devices, swap_cores(): return lax.ppermute(value, 'core', [(0, 1), (1, 0)])  36.5 us
    ppermute x6, waiting for transfers between devices, widen(): got = lax.ppermute(value, SKY, pairs)  28 us
    pallas_call x25, Pallas kernels, call(): pl.pallas_call(body, name=name, in_specs=specs, out_specs=[pl.BlockSpec(m...  26.9 us
    ppermute x9, waiting for transfers between devices, swap_cores(): return lax.ppermute(value, 'core', [(0, 1), (1, 0)])  8.93 us
    ppermute x6, starting transfers between devices, widen(): got = lax.ppermute(value, SKY, pairs)  7.75 us
    ppermute x2, starting transfers between devices, swap_halves(): return lax.ppermute(value, 'yh', [(0, 1), (1, 0)])  7.74 us
    ppermute x2, waiting for transfers between devices, swap_halves(): return lax.ppermute(value, 'yh', [(0, 1), (1, 0)])  6.17 us
  transfers between devices with their start and end apart: 17, of which 17 were waited for; matrix products, arithmetic and copies ran while one was open for 0% of the time, Pallas kernels for 4%

profile of v8, /device:TPU:1, one launch (start us, length us, event | category | flops | bytes accessed | tf_op | source)
XLA Modules:
  0.0 196.9 jit_solution(4717014241296036098)
XLA Ops:
  2.1 8.8 %collective-permute-start = (bf16[112,256]{1,0:T(8,128)(2,1)}, bf16[112,256]{1,0:T(8,128)(2,1)S(1)}, u32[]{:S(2)}, u32[]{:S(2)}) collective-permute-start(bf16[112,256]{1,0:T(8,128)(2,1)} %pack.1.own_ref), channel_id=1, source_target_pairs={{0,1},{1,0},{2,3},{3,2},{4,5},{5,4},{6,7},{7,6},{8,9},{9,8},{10,11... | collective-permute-start | bytes 172040 | tf_op jit(solution)/shard_map/ppermute | solution.py:23
  15.7 4.0 %collective-permute-done.1.refs_0_ = bf16[192,256]{1,0:T(8,128)(2,1)S(1)} collective-permute-done((bf16[192,256]{1,0:T(8,128)(2,1)S(1)}, bf16[192,256]{1,0:T(8,128)(2,1)S(1)}, u32[]{:S(2)}, u32[]{:S(2)}) %collective-permute-start.1) | collective-permute-done | bytes 98336 | tf_op jit(solution)/shard_map/ppermute | solution.py:29
  19.7 1.9 collective-permute-start.2
  22.9 2.6 %layers01.1 = (bf16[128,256]{1,0:T(8,128)(2,1)S(1)}, bf16[2,2,576,256]{3,2,1,0:T(8,128)(2,1)S(1)}, f32[4,64,256]{2,1,0:T(8,128)S(1)}, f32[2,64,256]{2,1,0:T(8,12...) custom-call(bf16[224,256]{1,0:T(8,128)(2,1)S(1)} %get-tuple-element., ...), custom_call_target="tpu_custom_call" | custom-call | tf_op jit(solution)/shard_map/layers01/pallas_call | solution.py:448
  28.1 3.8 %collective-permute-done.3.refs_0_ = bf16[128,256]{1,0:T(8,128)(2,1)S(1)} collective-permute-done((bf16[128,256]{1,0:T(8,128)(2,1)S(1)}, bf16[128,256]{1,0:T(8,128)(2,1)S(1)}, u32[]{:S(2)}, u32[]{:S(2)}) %collective-permute-start.3) | collective-permute-done | bytes 65568 | tf_op jit(solution)/shard_map/ppermute | solution.py:29
  32.0 1.9 collective-permute-start.4
  35.1 2.6 %layers.1 = (bf16[128,256]{1,0:T(8,128)(2,1)S(1)}, bf16[2,2,576,256]{3,2,1,0:T(8,128)(2,1)S(1)}, f32[4,64,256]{2,1,0:T(8,128)S(1)}, f32[2,64,256]{2,1,0:T(8,128)S(1)}) custom-call(bf16[128,256]{1,0:T(8,128)(2,1)S(1)} %get-tuple-element.48.x_ref, bf16[128,256]{1,0:T(8,128)(2,1)S(1)} %relay.6.got_ref, bf16[128,256]{1,0:T(8,128)(2,1)S(1)} %collective-permute-done.4.other_ref, ...), custom_call_target="tpu_custom_call" | custom-call | tf_op jit(solution)/shard_map/layers/pallas_call | solution.py:448
  39.0 5.2 %collective-permute-done.5.got_ref = bf16[128,256]{1,0:T(8,128)(2,1)S(1)} collective-permute-done((bf16[128,256]{1,0:T(8,128)(2,1)S(1)}, bf16[128,256]{1,0:T(8,128)(2,1)S(1)}, u32[]{:S(2)}, u32[]{:S(2)}) %collective-permute-start.5) | collective-permute-done | bytes 65568 | tf_op jit(solution)/shard_map/ppermute | solution.py:29
  44.2 2.5 %collective-permute-start.6 = (bf16[128,256]{1,0:T(8,128)(2,1)S(1)}, bf16[128,256]{1,0:T(8,128)(2,1)S(1)}, u32[]{:S(2)}, u32[]{:S(2)}) collective-permute-start(bf16[128,256]{1,0:T(8,128)(2,1)S(1)} %collective-permute-done.5.got_ref), channel_id=1, source_target_pairs={{0,1},{1,0},{2,3},{3,2},{4,5},{5,4},{6,7},{7,6},{8,9},{9,8},{10,11... | collective-permute-start | bytes 196616 | tf_op jit(solution)/shard_map/ppermute | solution.py:23
  47.6 2.7 %lastlayers.1 = (bf16[8,64,256]{2,1,0:T(8,128)(2,1)S(1)}, bf16[2,2,576,256]{3,2,1,0:T(8,128)(2,1)S(1)}, f32[4,64,256]{2,1,0:T(8,128)S(1)}, f32[2,64,256]{2,1,0:T(8,128)S(1)}) custom-call(bf16[128,256]{1,0:T(8,128)(2,1)S(1)} %get-tuple-element.55.x_ref, bf16[128,256]{1,0:T(8,128)(2,1)S(1)} %collective-permute-done.5.got_ref, ...), custom_call_target="tpu_custom_call" | custom-call | tf_op jit(solution)/shard_map/lastlayers/pallas_call | solution.py:448
  50.4 10.4 %all_to_all.20.parts_ref = bf16[8,64,256]{2,1,0:T(8,128)(2,1)S(1)} all-to-all(bf16[8,64,256]{2,1,0:T(8,128)(2,1)S(1)} %get-tuple-element.57), channel_id=1, replica_groups=mesh['branch'=8,'z'=16,'yh'=2,'core'=2] {'branch'}, dimensions={0} | all-to-all | bytes 524288 | tf_op jit(solution)/shard_map/all_to_all | solution.py:464
  60.9 3.1 %collective-permute-start.7 = (bf16[32,256]{1,0:T(8,128)(2,1)S(1)}, bf16[32,256]{1,0:T(8,128)(2,1)S(1)}, u32[]{:S(2)}, u32[]{:S(2)}) collective-permute-start(bf16[32,256]{1,0:T(8,128)(2,1)S(1)} %slope.1.own_ref), channel_id=1, source_target_pairs={{0,1},{1,0},{2,3},{3,2},{4,5},{5,4},{6,7},{7,6},{8,9},{9,8},{10,11... | collective-permute-start | bytes 49160 | tf_op jit(solution)/shard_map/ppermute | solution.py:23
  64.8 9.8 %all_to_all.21.unit_ref = bf16[8,64,256]{2,1,0:T(8,128)(2,1)S(1)} all-to-all(bf16[8,64,256]{2,1,0:T(8,128)(2,1)S(1)} %copies.1), channel_id=1, replica_groups=mesh['branch'=8,'z'=16,'yh'=2,'core'=2] {'branch'}, dimensions={0} | all-to-all | bytes 524288 | tf_op jit(solution)/shard_map/all_to_all | solution.py:464
  77.4 5.6 %collective-permute-done.8.refs_0_ = bf16[192,256]{1,0:T(8,128)(2,1)S(1)} collective-permute-done((bf16[192,256]{1,0:T(8,128)(2,1)S(1)}, bf16[192,256]{1,0:T(8,128)(2,1)S(1)}, u32[]{:S(2)}, u32[]{:S(2)}) %collective-permute-start.8) | collective-permute-done | bytes 98336 | tf_op jit(solution)/shard_map/ppermute | solution.py:29
  83.0 4.0 %collective-permute-start.9 = (bf16[192,256]{1,0:T(8,128)(2,1)S(1)}, bf16[192,256]{1,0:T(8,128)(2,1)S(1)}, u32[]{:S(2)}, u32[]{:S(2)}) collective-permute-start(bf16[192,256]{1,0:T(8,128)(2,1)S(1)} %relay.7.got_ref), channel_id=1, source_target_pairs={{0,1},{1,0},{2,3},{3,2},{4,5},{5,4},{6,7},{7,6},{8,9},{9,8},{10,11... | collective-permute-start | bytes 294920 | tf_op jit(solution)/shard_map/ppermute | solution.py:23
  87.8 3.0 %back.2 = (bf16[192,256]{1,0:T(8,128)(2,1)S(1)}, f32[2,64,256]{2,1,0:T(8,128)S(1)}, bf16[128,256]{1,0:T(8,128)(2,1)S(1)}) custom-call(bf16[192,256]{1,0:T(8,128)(2,1)S(1)} %get-tuple-element.59.refs_0_.x_ref, bf16[192,256]{1,0:T(8,128)(2,1)S(1)} %relay.7.got_ref, bf16[192,256]{1,0:T(8,128)(2,1)S(1)} %collective-permute-done.9.other_ref, ...), custom_call_target="tpu_custom_call" | custom-call | tf_op jit(solution)/shard_map/back/pallas_call | solution.py:448
  92.0 1.7 beside.4
  93.7 4.7 %collective-permute-done.10.refs_0_ = bf16[192,256]{1,0:T(8,128)(2,1)S(1)} collective-permute-done((bf16[192,256]{1,0:T(8,128)(2,1)S(1)}, bf16[192,256]{1,0:T(8,128)(2,1)S(1)}, u32[]{:S(2)}, u32[]{:S(2)}) %collective-permute-start.10) | collective-permute-done | bytes 98336 | tf_op jit(solution)/shard_map/ppermute | solution.py:29
  98.4 3.7 %collective-permute-start.11 = (bf16[192,256]{1,0:T(8,128)(2,1)S(1)}, bf16[192,256]{1,0:T(8,128)(2,1)S(1)}, u32[]{:S(2)}, u32[]{:S(2)}) collective-permute-start(bf16[192,256]{1,0:T(8,128)(2,1)S(1)} %relay.8.got_ref), channel_id=1, source_target_pairs={{0,1},{1,0},{2,3},{3,2},{4,5},{5,4},{6,7},{7,6},{8,9},{9,8},{10,11... | collective-permute-start | bytes 294920 | tf_op jit(solution)/shard_map/ppermute | solution.py:23
  103.0 3.0 %back.3 = (bf16[192,256]{1,0:T(8,128)(2,1)S(1)}, f32[2,64,256]{2,1,0:T(8,128)S(1)}, bf16[128,256]{1,0:T(8,128)(2,1)S(1)}) custom-call(bf16[192,256]{1,0:T(8,128)(2,1)S(1)} %get-tuple-element.66.refs_0_.x_ref, bf16[192,256]{1,0:T(8,128)(2,1)S(1)} %relay.8.got_ref, bf16[192,256]{1,0:T(8,128)(2,1)S(1)} %collective-permute-done.11.other_ref, ...), custom_call_target="tpu_custom_call" | custom-call | tf_op jit(solution)/shard_map/back/pallas_call | solution.py:448
  107.3 1.7 beside.5
  109.0 4.7 %collective-permute-done.12.refs_0_ = bf16[192,256]{1,0:T(8,128)(2,1)S(1)} collective-permute-done((bf16[192,256]{1,0:T(8,128)(2,1)S(1)}, bf16[192,256]{1,0:T(8,128)(2,1)S(1)}, u32[]{:S(2)}, u32[]{:S(2)}) %collective-permute-start.12) | collective-permute-done | bytes 98336 | tf_op jit(solution)/shard_map/ppermute | solution.py:29
  113.6 3.7 %collective-permute-start.13 = (bf16[192,256]{1,0:T(8,128)(2,1)S(1)}, bf16[192,256]{1,0:T(8,128)(2,1)S(1)}, u32[]{:S(2)}, u32[]{:S(2)}) collective-permute-start(bf16[192,256]{1,0:T(8,128)(2,1)S(1)} %relay.9.got_ref), channel_id=1, source_target_pairs={{0,1},{1,0},{2,3},{3,2},{4,5},{5,4},{6,7},{7,6},{8,9},{9,8},{10,11... | collective-permute-start | bytes 294920 | tf_op jit(solution)/shard_map/ppermute | solution.py:23
  118.3 1.6 lastback.1
  119.9 5.6 %collective-permute-start.14 = (bf16[48,1152]{1,0:T(8,128)(2,1)S(1)}, bf16[48,1152]{1,0:T(8,128)(2,1)S(1)}, u32[]{:S(2)}, u32[]{:S(2)}) collective-permute-start(bf16[48,1152]{1,0:T(8,128)(2,1)S(1)} %get-tuple-element.86), channel_id=1, source_target_pairs={{0,2},{2,0},{1,3},{3,1},{4,6},{6,4},{5,7},{7,5},{8,10},{10,8},{9,1... | collective-permute-start | bytes 331784 | tf_op jit(solution)/shard_map/ppermute | solution.py:476
  125.5 1.8 mapgrad.1
  128.7 34.1 %all_to_all.22 = bf16[16,4,8,128]{3,2,1,0:T(8,128)(2,1)S(1)} all-to-all(bf16[16,4,8,128]{3,2,1,0:T(8,128)(2,1)S(1)} %bitcast.26), channel_id=1, replica_groups=mesh['branch'=8,'z'=16,'yh'=2,'core'=2] {'z'}, dimensions={0} | all-to-all | bytes 262144 | tf_op jit(solution)/shard_map/all_to_all | solution.py:464
  162.9 17.5 %all_to_all.23 = bf16[16,4,8,128]{3,2,1,0:T(8,128)(2,1)S(1)} all-to-all(bf16[16,4,8,128]{3,2,1,0:T(8,128)(2,1)S(1)} %broadcast_in_dim.13), channel_id=1, replica_groups=mesh['branch'=8,'z'=16,'yh'=2,'core'=2] {'z'}, dimensions={0} | all-to-all | bytes 262144 | tf_op jit(solution)/shard_map/all_to_all | solution.py:464
  180.4 2.1 %collective-permute-start.15 = (bf16[48,1152]{1,0:T(8,128)(2,1)S(1)}, bf16[48,1152]{1,0:T(8,128)(2,1)S(1)}, u32[]{:S(2)}, u32[]{:S(2)}) collective-permute-start(bf16[48,1152]{1,0:T(8,128)(2,1)S(1)} %bitcast.19), channel_id=1, source_target_pairs={{0,2},{2,0},{1,3},{3,1},{4,6},{6,4},{5,7},{7,5},{8,10},{10,8},{9,1... | collective-permute-start | bytes 331784 | tf_op jit(solution)/shard_map/ppermute | solution.py:476
  182.5 4.9 %collective-permute-done.15.got_ref = bf16[48,1152]{1,0:T(8,128)(2,1)S(1)} collective-permute-done((bf16[48,1152]{1,0:T(8,128)(2,1)S(1)}, bf16[48,1152]{1,0:T(8,128)(2,1)S(1)}, u32[]{:S(2)}, u32[]{:S(2)}) %collective-permute-start.15) | collective-permute-done | bytes 110624 | tf_op jit(solution)/shard_map/ppermute | solution.py:476
  187.4 6.9 %collective-permute-start.16 = (bf16[96,1152]{1,0:T(8,128)(2,1)S(1)}, bf16[96,1152]{1,0:T(8,128)(2,1)S(1)}, u32[]{:S(2)}, u32[]{:S(2)}) collective-permute-start(bf16[96,1152]{1,0:T(8,128)(2,1)S(1)} %rows.1.own_ref), channel_id=1, source_target_pairs={{0,1},{1,0},{2,3},{3,2},{4,5},{5,4},{6,7},{7,6},{8,9},{9,8},{10,11... | collective-permute-start | bytes 663560 | tf_op jit(solution)/shard_map/ppermute | solution.py:23
  195.4 1.5 final.1
  (43 shorter events, 24.9 us)
Async XLA Ops:
  2.1 9.9 %collective-permute-start = (bf16[112,256]{1,0:T(8,128)(2,1)}, bf16[112,256]{1,0:T(8,128)(2,1)S(1)}, u32[]{:S(2)}, u32[]{:S(2)}) collective-permute-start(bf16[112,256]{1,0:T(8,128)(2,1)} %pack.1.own_ref), channel_id=1, source_target_pairs={{0,1},{1,0},{2,3},{3,2},{4,5},{5,4},{6,7},{7,6},{8,9},{9,8},{10,11... | collective-permute-start | bytes 172040 | tf_op jit(solution)/shard_map/ppermute | solution.py:23
  12.0 0.8 copy-start.1
  12.8 6.9 %collective-permute-start.1 = (bf16[192,256]{1,0:T(8,128)(2,1)S(1)}, bf16[192,256]{1,0:T(8,128)(2,1)S(1)}, u32[]{:S(2)}, u32[]{:S(2)}) collective-permute-start(bf16[192,256]{1,0:T(8,128)(2,1)S(1)} %get-tuple-element.46), channel_id=1, source_target_pairs={{0,2},{2,4},{4,6},{6,8},{8,10},{10,12},{12,14},{14,16},{16,18},{18... | collective-permute-start | bytes 294920 | tf_op jit(solution)/shard_map/ppermute | solution.py:29
  14.1 1.2 copy-start
  15.3 11.5 %copy-start.2 = (bf16[9,32,256]{2,1,0:T(8,128)(2,1)S(1)}, bf16[9,32,256]{2,1,0:T(8,128)(2,1)}, u32[]{:S(2)}) copy-start(bf16[9,32,256]{2,1,0:T(8,128)(2,1)} %param.12) | copy-start | bytes 442372
  15.7 32.0 %copy-start.3 = (bf16[256,64]{0,1:T(8,128)(2,1)S(1)}, bf16[256,64]{0,1:T(8,128)(2,1)}, u32[]{:S(2)}) copy-start(bf16[256,64]{0,1:T(8,128)(2,1)} %param.11) | copy-start | bytes 98308
  19.7 3.2 %collective-permute-start.2 = (bf16[192,256]{1,0:T(8,128)(2,1)S(1)}, bf16[192,256]{1,0:T(8,128)(2,1)S(1)}, u32[]{:S(2)}, u32[]{:S(2)}) collective-permute-start(bf16[192,256]{1,0:T(8,128)(2,1)S(1)} %relay.5.got_ref), channel_id=1, source_target_pairs={{0,1},{1,0},{2,3},{3,2},{4,5},{5,4},{6,7},{7,6},{8,9},{9,8},{10,11... | collective-permute-start | bytes 294920 | tf_op jit(solution)/shard_map/ppermute | solution.py:23
  25.5 6.5 %collective-permute-start.3 = (bf16[128,256]{1,0:T(8,128)(2,1)S(1)}, bf16[128,256]{1,0:T(8,128)(2,1)S(1)}, u32[]{:S(2)}, u32[]{:S(2)}) collective-permute-start(bf16[128,256]{1,0:T(8,128)(2,1)S(1)} %get-tuple-element.48.x_ref), channel_id=1, source_target_pairs={{0,2},{2,4},{4,6},{6,8},{8,10},{10,12},{12,14},{14,16},{16,18},{18... | collective-permute-start | bytes 196616 | tf_op jit(solution)/shard_map/ppermute | solution.py:29
  32.0 3.1 %collective-permute-start.4 = (bf16[128,256]{1,0:T(8,128)(2,1)S(1)}, bf16[128,256]{1,0:T(8,128)(2,1)S(1)}, u32[]{:S(2)}, u32[]{:S(2)}) collective-permute-start(bf16[128,256]{1,0:T(8,128)(2,1)S(1)} %relay.6.got_ref), channel_id=1, source_target_pairs={{0,1},{1,0},{2,3},{3,2},{4,5},{5,4},{6,7},{7,6},{8,9},{9,8},{10,11... | collective-permute-start | bytes 196616 | tf_op jit(solution)/shard_map/ppermute | solution.py:23
  37.7 6.5 %collective-permute-start.5 = (bf16[128,256]{1,0:T(8,128)(2,1)S(1)}, bf16[128,256]{1,0:T(8,128)(2,1)S(1)}, u32[]{:S(2)}, u32[]{:S(2)}) collective-permute-start(bf16[128,256]{1,0:T(8,128)(2,1)S(1)} %get-tuple-element.55.x_ref), channel_id=1, source_target_pairs={{0,2},{2,4},{4,6},{6,8},{8,10},{10,12},{12,14},{14,16},{16,18},{18... | collective-permute-start | bytes 196616 | tf_op jit(solution)/shard_map/ppermute | solution.py:29
  44.2 3.4 %collective-permute-start.6 = (bf16[128,256]{1,0:T(8,128)(2,1)S(1)}, bf16[128,256]{1,0:T(8,128)(2,1)S(1)}, u32[]{:S(2)}, u32[]{:S(2)}) collective-permute-start(bf16[128,256]{1,0:T(8,128)(2,1)S(1)} %collective-permute-done.5.got_ref), channel_id=1, source_target_pairs={{0,1},{1,0},{2,3},{3,2},{4,5},{5,4},{6,7},{7,6},{8,9},{9,8},{10,11... | collective-permute-start | bytes 196616 | tf_op jit(solution)/shard_map/ppermute | solution.py:23
  60.9 3.9 %collective-permute-start.7 = (bf16[32,256]{1,0:T(8,128)(2,1)S(1)}, bf16[32,256]{1,0:T(8,128)(2,1)S(1)}, u32[]{:S(2)}, u32[]{:S(2)}) collective-permute-start(bf16[32,256]{1,0:T(8,128)(2,1)S(1)} %slope.1.own_ref), channel_id=1, source_target_pairs={{0,1},{1,0},{2,3},{3,2},{4,5},{5,4},{6,7},{7,6},{8,9},{9,8},{10,11... | collective-permute-start | bytes 49160 | tf_op jit(solution)/shard_map/ppermute | solution.py:23
  74.8 8.2 %collective-permute-start.8 = (bf16[192,256]{1,0:T(8,128)(2,1)S(1)}, bf16[192,256]{1,0:T(8,128)(2,1)S(1)}, u32[]{:S(2)}, u32[]{:S(2)}) collective-permute-start(bf16[192,256]{1,0:T(8,128)(2,1)S(1)} %get-tuple-element.59.refs_0_.x_ref), channel_id=1, source_target_pairs={{0,2},{2,4},{4,6},{6,8},{8,10},{10,12},{12,14},{14,16},{16,18},{18... | collective-permute-start | bytes 294920 | tf_op jit(solution)/shard_map/ppermute | solution.py:29
  83.0 4.7 %collective-permute-start.9 = (bf16[192,256]{1,0:T(8,128)(2,1)S(1)}, bf16[192,256]{1,0:T(8,128)(2,1)S(1)}, u32[]{:S(2)}, u32[]{:S(2)}) collective-permute-start(bf16[192,256]{1,0:T(8,128)(2,1)S(1)} %relay.7.got_ref), channel_id=1, source_target_pairs={{0,1},{1,0},{2,3},{3,2},{4,5},{5,4},{6,7},{7,6},{8,9},{9,8},{10,11... | collective-permute-start | bytes 294920 | tf_op jit(solution)/shard_map/ppermute | solution.py:23
  90.7 7.6 %collective-permute-start.10 = (bf16[192,256]{1,0:T(8,128)(2,1)S(1)}, bf16[192,256]{1,0:T(8,128)(2,1)S(1)}, u32[]{:S(2)}, u32[]{:S(2)}) collective-permute-start(bf16[192,256]{1,0:T(8,128)(2,1)S(1)} %get-tuple-element.66.refs_0_.x_ref), channel_id=1, source_target_pairs={{0,2},{2,4},{4,6},{6,8},{8,10},{10,12},{12,14},{14,16},{16,18},{18... | collective-permute-start | bytes 294920 | tf_op jit(solution)/shard_map/ppermute | solution.py:29
  98.4 4.6 %collective-permute-start.11 = (bf16[192,256]{1,0:T(8,128)(2,1)S(1)}, bf16[192,256]{1,0:T(8,128)(2,1)S(1)}, u32[]{:S(2)}, u32[]{:S(2)}) collective-permute-start(bf16[192,256]{1,0:T(8,128)(2,1)S(1)} %relay.8.got_ref), channel_id=1, source_target_pairs={{0,1},{1,0},{2,3},{3,2},{4,5},{5,4},{6,7},{7,6},{8,9},{9,8},{10,11... | collective-permute-start | bytes 294920 | tf_op jit(solution)/shard_map/ppermute | solution.py:23
  106.0 7.6 %collective-permute-start.12 = (bf16[192,256]{1,0:T(8,128)(2,1)S(1)}, bf16[192,256]{1,0:T(8,128)(2,1)S(1)}, u32[]{:S(2)}, u32[]{:S(2)}) collective-permute-start(bf16[192,256]{1,0:T(8,128)(2,1)S(1)} %get-tuple-element.73.refs_0_.x_ref), channel_id=1, source_target_pairs={{0,2},{2,4},{4,6},{6,8},{8,10},{10,12},{12,14},{14,16},{16,18},{18... | collective-permute-start | bytes 294920 | tf_op jit(solution)/shard_map/ppermute | solution.py:29
  113.6 4.6 %collective-permute-start.13 = (bf16[192,256]{1,0:T(8,128)(2,1)S(1)}, bf16[192,256]{1,0:T(8,128)(2,1)S(1)}, u32[]{:S(2)}, u32[]{:S(2)}) collective-permute-start(bf16[192,256]{1,0:T(8,128)(2,1)S(1)} %relay.9.got_ref), channel_id=1, source_target_pairs={{0,1},{1,0},{2,3},{3,2},{4,5},{5,4},{6,7},{7,6},{8,9},{9,8},{10,11... | collective-permute-start | bytes 294920 | tf_op jit(solution)/shard_map/ppermute | solution.py:23
  119.9 8.8 %collective-permute-start.14 = (bf16[48,1152]{1,0:T(8,128)(2,1)S(1)}, bf16[48,1152]{1,0:T(8,128)(2,1)S(1)}, u32[]{:S(2)}, u32[]{:S(2)}) collective-permute-start(bf16[48,1152]{1,0:T(8,128)(2,1)S(1)} %get-tuple-element.86), channel_id=1, source_target_pairs={{0,2},{2,0},{1,3},{3,1},{4,6},{6,4},{5,7},{7,5},{8,10},{10,8},{9,1... | collective-permute-start | bytes 331784 | tf_op jit(solution)/shard_map/ppermute | solution.py:476
  180.4 7.0 %collective-permute-start.15 = (bf16[48,1152]{1,0:T(8,128)(2,1)S(1)}, bf16[48,1152]{1,0:T(8,128)(2,1)S(1)}, u32[]{:S(2)}, u32[]{:S(2)}) collective-permute-start(bf16[48,1152]{1,0:T(8,128)(2,1)S(1)} %bitcast.19), channel_id=1, source_target_pairs={{0,2},{2,0},{1,3},{3,1},{4,6},{6,4},{5,7},{7,5},{8,10},{10,8},{9,1... | collective-permute-start | bytes 331784 | tf_op jit(solution)/shard_map/ppermute | solution.py:476
  187.4 8.0 %collective-permute-start.16 = (bf16[96,1152]{1,0:T(8,128)(2,1)S(1)}, bf16[96,1152]{1,0:T(8,128)(2,1)S(1)}, u32[]{:S(2)}, u32[]{:S(2)}) collective-permute-start(bf16[96,1152]{1,0:T(8,128)(2,1)S(1)} %rows.1.own_ref), channel_id=1, source_target_pairs={{0,1},{1,0},{2,3},{3,2},{4,5},{5,4},{6,7},{7,6},{8,9},{9,8},{10,11... | collective-permute-start | bytes 663560 | tf_op jit(solution)/shard_map/ppermute | solution.py:23

commit v9 on v7

--- a/solution.py
+++ b/solution.py
@@ -527,7 +527,8 @@
         [pltpu.VMEM((TAPS, R), jnp.int32), pltpu.VMEM((1, R), jnp.int32), dma((4,))], None,
     )[0]
     pack, sent = call(
-        pair_kernel, "pair", [v(pack), v(swap_cores(pack))],
+        pair_kernel, "pair",
+        [v(call(relay_kernel, "held", [v(pack)], [sds(pack.shape, BF16)])[0]), v(swap_cores(pack))],
         [sds((2 * size, R), BF16), sds((2 * C + 32 + each, R), BF16)],
     )
     pair = sds((2, C, R), F32)

time: 197 us -> 196 us (level)
    pallas_call x24 -> x25, Pallas kernels: 27.3 us -> 27.3 us  [call(): pl.pallas_call(body, name=name, in_specs=specs, out_specs=[pl.BlockSpec(m...]
where the time goes in v9:
time: 196 us; the launch traced here: 195 us
  blocking collectives  74.4 us (38%)
  starting transfers between devices  49.6 us (25%)
  waiting for transfers between devices  41 us (21%)
  Pallas kernels  27.3 us (14%)
  local copies, waits for them, and re-layouts  2.03 us (1%)
    all_to_all x4, blocking collectives, exchange(): return lax.all_to_all(value, axes, 0, 0, tiled=True)  74.4 us
    ppermute x8, starting transfers between devices, swap_cores(): return lax.ppermute(value, 'core', [(0, 1), (1, 0)])  34.1 us
    ppermute x6, waiting for transfers between devices, widen(): got = lax.ppermute(value, SKY, pairs)  27.6 us
    pallas_call x25, Pallas kernels, call(): pl.pallas_call(body, name=name, in_specs=specs, out_specs=[pl.BlockSpec(m...  27.3 us
    ppermute x6, starting transfers between devices, widen(): got = lax.ppermute(value, SKY, pairs)  7.75 us
    ppermute x2, starting transfers between devices, swap_halves(): return lax.ppermute(value, 'yh', [(0, 1), (1, 0)])  7.75 us
    ppermute x8, waiting for transfers between devices, swap_cores(): return lax.ppermute(value, 'core', [(0, 1), (1, 0)])  7.28 us
    ppermute x2, waiting for transfers between devices, swap_halves(): return lax.ppermute(value, 'yh', [(0, 1), (1, 0)])  6.17 us
  transfers between devices with their start and end apart: 16, of which 16 were waited for; matrix products, arithmetic and copies ran while one was open for 0% of the time, Pallas kernels for 4%

profile of v9, /device:TPU:1, one launch (start us, length us, event | category | flops | bytes accessed | tf_op | source)
XLA Modules:
  0.0 195.4 jit_solution(1442369405442889780)
XLA Ops:
  2.1 8.8 %collective-permute-start = (bf16[112,256]{1,0:T(8,128)(2,1)}, bf16[112,256]{1,0:T(8,128)(2,1)S(1)}, u32[]{:S(2)}, u32[]{:S(2)}) collective-permute-start(bf16[112,256]{1,0:T(8,128)(2,1)} %pack.1.refs_0_), channel_id=1, source_target_pairs={{0,1},{1,0},{2,3},{3,2},{4,5},{5,4},{6,7},{7,6},{8,9},{9,8},{10,11... | collective-permute-start | bytes 172040 | tf_op jit(solution)/shard_map/ppermute | solution.py:23
  14.8 4.0 %collective-permute-done.1.refs_0_ = bf16[192,256]{1,0:T(8,128)(2,1)S(1)} collective-permute-done((bf16[192,256]{1,0:T(8,128)(2,1)S(1)}, bf16[192,256]{1,0:T(8,128)(2,1)S(1)}, u32[]{:S(2)}, u32[]{:S(2)}) %collective-permute-start.1) | collective-permute-done | bytes 98336 | tf_op jit(solution)/shard_map/ppermute | solution.py:29
  18.9 1.9 collective-permute-start.2
  22.1 2.6 %layers01.1 = (bf16[128,256]{1,0:T(8,128)(2,1)S(1)}, bf16[2,2,576,256]{3,2,1,0:T(8,128)(2,1)S(1)}, f32[4,64,256]{2,1,0:T(8,128)S(1)}, f32[2,64,256]{2,1,0:T(8,12...) custom-call(bf16[224,256]{1,0:T(8,128)(2,1)S(1)} %get-tuple-element., ...), custom_call_target="tpu_custom_call" | custom-call | tf_op jit(solution)/shard_map/layers01/pallas_call | solution.py:456
  26.0 1.7 unit.1.refs_1_.unit_ref
  27.6 3.5 %collective-permute-done.3.refs_0_ = bf16[128,256]{1,0:T(8,128)(2,1)S(1)} collective-permute-done((bf16[128,256]{1,0:T(8,128)(2,1)S(1)}, bf16[128,256]{1,0:T(8,128)(2,1)S(1)}, u32[]{:S(2)}, u32[]{:S(2)}) %collective-permute-start.3) | collective-permute-done | bytes 65568 | tf_op jit(solution)/shard_map/ppermute | solution.py:29
  31.2 1.9 collective-permute-start.4
  34.3 2.6 %layers.1 = (bf16[128,256]{1,0:T(8,128)(2,1)S(1)}, bf16[2,2,576,256]{3,2,1,0:T(8,128)(2,1)S(1)}, f32[4,64,256]{2,1,0:T(8,128)S(1)}, f32[2,64,256]{2,1,0:T(8,128)S(1)}) custom-call(bf16[128,256]{1,0:T(8,128)(2,1)S(1)} %get-tuple-element.48.x_ref, bf16[128,256]{1,0:T(8,128)(2,1)S(1)} %relay.6.got_ref, bf16[128,256]{1,0:T(8,128)(2,1)S(1)} %collective-permute-done.4.other_ref, ...), custom_call_target="tpu_custom_call" | custom-call | tf_op jit(solution)/shard_map/layers/pallas_call | solution.py:456
  38.2 5.2 %collective-permute-done.5.got_ref = bf16[128,256]{1,0:T(8,128)(2,1)S(1)} collective-permute-done((bf16[128,256]{1,0:T(8,128)(2,1)S(1)}, bf16[128,256]{1,0:T(8,128)(2,1)S(1)}, u32[]{:S(2)}, u32[]{:S(2)}) %collective-permute-start.5) | collective-permute-done | bytes 65568 | tf_op jit(solution)/shard_map/ppermute | solution.py:29
  43.4 2.5 %collective-permute-start.6 = (bf16[128,256]{1,0:T(8,128)(2,1)S(1)}, bf16[128,256]{1,0:T(8,128)(2,1)S(1)}, u32[]{:S(2)}, u32[]{:S(2)}) collective-permute-start(bf16[128,256]{1,0:T(8,128)(2,1)S(1)} %collective-permute-done.5.got_ref), channel_id=1, source_target_pairs={{0,1},{1,0},{2,3},{3,2},{4,5},{5,4},{6,7},{7,6},{8,9},{9,8},{10,11... | collective-permute-start | bytes 196616 | tf_op jit(solution)/shard_map/ppermute | solution.py:23
  46.8 2.8 %lastlayers.1 = (bf16[8,128,256]{2,1,0:T(8,128)(2,1)S(1)}, bf16[2,2,576,256]{3,2,1,0:T(8,128)(2,1)S(1)}, f32[4,64,256]{2,1,0:T(8,128)S(1)}, f32[2,64,256]{2,1,0:T(8,128)S(1)}) custom-call(bf16[128,256]{1,0:T(8,128)(2,1)S(1)} %get-tuple-element.54.x_ref, bf16[128,256]{1,0:T(8,128)(2,1)S(1)} %collective-permute-done.5.got_ref, ...), custom_call_target="tpu_custom_call" | custom-call | tf_op jit(solution)/shard_map/lastlayers/pallas_call | solution.py:456
  49.6 13.3 %all_to_all.20.parts_ref = bf16[8,128,256]{2,1,0:T(8,128)(2,1)S(1)} all-to-all(bf16[8,128,256]{2,1,0:T(8,128)(2,1)S(1)} %get-tuple-element.56), channel_id=1, replica_groups=mesh['branch'=8,'z'=16,'yh'=2,'core'=2] {'branch'}, dimensions={0} | all-to-all | bytes 1048576 | tf_op jit(solution)/shard_map/all_to_all | solution.py:472
  62.9 8.9 %all_to_all.21.unit_ref = bf16[8,64,256]{2,1,0:T(8,128)(2,1)S(1)} all-to-all(bf16[8,64,256]{2,1,0:T(8,128)(2,1)S(1)} %slope.1), channel_id=1, replica_groups=mesh['branch'=8,'z'=16,'yh'=2,'core'=2] {'branch'}, dimensions={0} | all-to-all | bytes 524288 | tf_op jit(solution)/shard_map/all_to_all | solution.py:472
  74.6 5.6 %collective-permute-done.7.refs_0_ = bf16[192,256]{1,0:T(8,128)(2,1)S(1)} collective-permute-done((bf16[192,256]{1,0:T(8,128)(2,1)S(1)}, bf16[192,256]{1,0:T(8,128)(2,1)S(1)}, u32[]{:S(2)}, u32[]{:S(2)}) %collective-permute-start.7) | collective-permute-done | bytes 98336 | tf_op jit(solution)/shard_map/ppermute | solution.py:29
  80.2 4.7 %collective-permute-start.8 = (bf16[192,256]{1,0:T(8,128)(2,1)S(1)}, bf16[192,256]{1,0:T(8,128)(2,1)S(1)}, u32[]{:S(2)}, u32[]{:S(2)}) collective-permute-start(bf16[192,256]{1,0:T(8,128)(2,1)S(1)} %relay.7.got_ref), channel_id=1, source_target_pairs={{0,1},{1,0},{2,3},{3,2},{4,5},{5,4},{6,7},{7,6},{8,9},{9,8},{10,11... | collective-permute-start | bytes 294920 | tf_op jit(solution)/shard_map/ppermute | solution.py:23
  85.6 3.0 %back.2 = (bf16[192,256]{1,0:T(8,128)(2,1)S(1)}, f32[2,64,256]{2,1,0:T(8,128)S(1)}, bf16[128,256]{1,0:T(8,128)(2,1)S(1)}) custom-call(bf16[192,256]{1,0:T(8,128)(2,1)S(1)} %get-tuple-element.58.refs_0_.x_ref, bf16[192,256]{1,0:T(8,128)(2,1)S(1)} %relay.7.got_ref, bf16[192,256]{1,0:T(8,128)(2,1)S(1)} %collective-permute-done.8.other_ref, ...), custom_call_target="tpu_custom_call" | custom-call | tf_op jit(solution)/shard_map/back/pallas_call | solution.py:456
  89.9 1.7 beside.4
  91.6 4.6 %collective-permute-done.9.refs_0_ = bf16[192,256]{1,0:T(8,128)(2,1)S(1)} collective-permute-done((bf16[192,256]{1,0:T(8,128)(2,1)S(1)}, bf16[192,256]{1,0:T(8,128)(2,1)S(1)}, u32[]{:S(2)}, u32[]{:S(2)}) %collective-permute-start.9) | collective-permute-done | bytes 98336 | tf_op jit(solution)/shard_map/ppermute | solution.py:29
  96.2 3.7 %collective-permute-start.10 = (bf16[192,256]{1,0:T(8,128)(2,1)S(1)}, bf16[192,256]{1,0:T(8,128)(2,1)S(1)}, u32[]{:S(2)}, u32[]{:S(2)}) collective-permute-start(bf16[192,256]{1,0:T(8,128)(2,1)S(1)} %relay.8.got_ref), channel_id=1, source_target_pairs={{0,1},{1,0},{2,3},{3,2},{4,5},{5,4},{6,7},{7,6},{8,9},{9,8},{10,11... | collective-permute-start | bytes 294920 | tf_op jit(solution)/shard_map/ppermute | solution.py:23
  100.8 3.0 %back.3 = (bf16[192,256]{1,0:T(8,128)(2,1)S(1)}, f32[2,64,256]{2,1,0:T(8,128)S(1)}, bf16[128,256]{1,0:T(8,128)(2,1)S(1)}) custom-call(bf16[192,256]{1,0:T(8,128)(2,1)S(1)} %get-tuple-element.64.refs_0_.x_ref, bf16[192,256]{1,0:T(8,128)(2,1)S(1)} %relay.8.got_ref, bf16[192,256]{1,0:T(8,128)(2,1)S(1)} %collective-permute-done.10.other_ref, ...), custom_call_target="tpu_custom_call" | custom-call | tf_op jit(solution)/shard_map/back/pallas_call | solution.py:456
  105.1 1.7 beside.5
  106.7 4.7 %collective-permute-done.11.refs_0_ = bf16[192,256]{1,0:T(8,128)(2,1)S(1)} collective-permute-done((bf16[192,256]{1,0:T(8,128)(2,1)S(1)}, bf16[192,256]{1,0:T(8,128)(2,1)S(1)}, u32[]{:S(2)}, u32[]{:S(2)}) %collective-permute-start.11) | collective-permute-done | bytes 98336 | tf_op jit(solution)/shard_map/ppermute | solution.py:29
  111.4 3.7 %collective-permute-start.12 = (bf16[192,256]{1,0:T(8,128)(2,1)S(1)}, bf16[192,256]{1,0:T(8,128)(2,1)S(1)}, u32[]{:S(2)}, u32[]{:S(2)}) collective-permute-start(bf16[192,256]{1,0:T(8,128)(2,1)S(1)} %relay.9.got_ref), channel_id=1, source_target_pairs={{0,1},{1,0},{2,3},{3,2},{4,5},{5,4},{6,7},{7,6},{8,9},{9,8},{10,11... | collective-permute-start | bytes 294920 | tf_op jit(solution)/shard_map/ppermute | solution.py:23
  116.1 1.6 lastback.1
  117.7 5.6 %collective-permute-start.13 = (bf16[48,1152]{1,0:T(8,128)(2,1)S(1)}, bf16[48,1152]{1,0:T(8,128)(2,1)S(1)}, u32[]{:S(2)}, u32[]{:S(2)}) collective-permute-start(bf16[48,1152]{1,0:T(8,128)(2,1)S(1)} %get-tuple-element.86), channel_id=1, source_target_pairs={{0,2},{2,0},{1,3},{3,1},{4,6},{6,4},{5,7},{7,5},{8,10},{10,8},{9,1... | collective-permute-start | bytes 331784 | tf_op jit(solution)/shard_map/ppermute | solution.py:484
  123.3 1.8 mapgrad.1
  126.5 34.8 %all_to_all.22 = bf16[16,4,8,128]{3,2,1,0:T(8,128)(2,1)S(1)} all-to-all(bf16[16,4,8,128]{3,2,1,0:T(8,128)(2,1)S(1)} %bitcast.26), channel_id=1, replica_groups=mesh['branch'=8,'z'=16,'yh'=2,'core'=2] {'z'}, dimensions={0} | all-to-all | bytes 262144 | tf_op jit(solution)/shard_map/all_to_all | solution.py:472
  161.4 17.5 %all_to_all.23 = bf16[16,4,8,128]{3,2,1,0:T(8,128)(2,1)S(1)} all-to-all(bf16[16,4,8,128]{3,2,1,0:T(8,128)(2,1)S(1)} %broadcast_in_dim.13), channel_id=1, replica_groups=mesh['branch'=8,'z'=16,'yh'=2,'core'=2] {'z'}, dimensions={0} | all-to-all | bytes 262144 | tf_op jit(solution)/shard_map/all_to_all | solution.py:472
  178.9 2.1 %collective-permute-start.14 = (bf16[48,1152]{1,0:T(8,128)(2,1)S(1)}, bf16[48,1152]{1,0:T(8,128)(2,1)S(1)}, u32[]{:S(2)}, u32[]{:S(2)}) collective-permute-start(bf16[48,1152]{1,0:T(8,128)(2,1)S(1)} %bitcast.19), channel_id=1, source_target_pairs={{0,2},{2,0},{1,3},{3,1},{4,6},{6,4},{5,7},{7,5},{8,10},{10,8},{9,1... | collective-permute-start | bytes 331784 | tf_op jit(solution)/shard_map/ppermute | solution.py:484
  181.0 4.9 %collective-permute-done.14.got_ref = bf16[48,1152]{1,0:T(8,128)(2,1)S(1)} collective-permute-done((bf16[48,1152]{1,0:T(8,128)(2,1)S(1)}, bf16[48,1152]{1,0:T(8,128)(2,1)S(1)}, u32[]{:S(2)}, u32[]{:S(2)}) %collective-permute-start.14) | collective-permute-done | bytes 110624 | tf_op jit(solution)/shard_map/ppermute | solution.py:484
  185.9 6.9 %collective-permute-start.15 = (bf16[96,1152]{1,0:T(8,128)(2,1)S(1)}, bf16[96,1152]{1,0:T(8,128)(2,1)S(1)}, u32[]{:S(2)}, u32[]{:S(2)}) collective-permute-start(bf16[96,1152]{1,0:T(8,128)(2,1)S(1)} %rows.1.own_ref), channel_id=1, source_target_pairs={{0,1},{1,0},{2,3},{3,2},{4,5},{5,4},{6,7},{7,6},{8,9},{9,8},{10,11... | collective-permute-start | bytes 663560 | tf_op jit(solution)/shard_map/ppermute | solution.py:23
  193.9 1.5 final.1
  (41 shorter events, 21.9 us)
Async XLA Ops:
  2.1 9.9 %collective-permute-start = (bf16[112,256]{1,0:T(8,128)(2,1)}, bf16[112,256]{1,0:T(8,128)(2,1)S(1)}, u32[]{:S(2)}, u32[]{:S(2)}) collective-permute-start(bf16[112,256]{1,0:T(8,128)(2,1)} %pack.1.refs_0_), channel_id=1, source_target_pairs={{0,1},{1,0},{2,3},{3,2},{4,5},{5,4},{6,7},{7,6},{8,9},{9,8},{10,11... | collective-permute-start | bytes 172040 | tf_op jit(solution)/shard_map/ppermute | solution.py:23
  10.9 0.8 copy-start.1
  11.7 14.2 %copy-start.2 = (bf16[9,32,256]{2,1,0:T(8,128)(2,1)S(1)}, bf16[9,32,256]{2,1,0:T(8,128)(2,1)}, u32[]{:S(2)}) copy-start(bf16[9,32,256]{2,1,0:T(8,128)(2,1)} %param.12) | copy-start | bytes 442372
  12.0 6.9 %collective-permute-start.1 = (bf16[192,256]{1,0:T(8,128)(2,1)S(1)}, bf16[192,256]{1,0:T(8,128)(2,1)S(1)}, u32[]{:S(2)}, u32[]{:S(2)}) collective-permute-start(bf16[192,256]{1,0:T(8,128)(2,1)S(1)} %get-tuple-element.46), channel_id=1, source_target_pairs={{0,2},{2,4},{4,6},{6,8},{8,10},{10,12},{12,14},{14,16},{16,18},{18... | collective-permute-start | bytes 294920 | tf_op jit(solution)/shard_map/ppermute | solution.py:29
  13.3 1.2 copy-start
  18.9 28.0 %copy-start.3 = (bf16[256,64]{0,1:T(8,128)(2,1)S(1)}, bf16[256,64]{0,1:T(8,128)(2,1)}, u32[]{:S(2)}) copy-start(bf16[256,64]{0,1:T(8,128)(2,1)} %param.11) | copy-start | bytes 98308
  18.9 3.2 %collective-permute-start.2 = (bf16[192,256]{1,0:T(8,128)(2,1)S(1)}, bf16[192,256]{1,0:T(8,128)(2,1)S(1)}, u32[]{:S(2)}, u32[]{:S(2)}) collective-permute-start(bf16[192,256]{1,0:T(8,128)(2,1)S(1)} %relay.5.got_ref), channel_id=1, source_target_pairs={{0,1},{1,0},{2,3},{3,2},{4,5},{5,4},{6,7},{7,6},{8,9},{9,8},{10,11... | collective-permute-start | bytes 294920 | tf_op jit(solution)/shard_map/ppermute | solution.py:23
  24.7 6.5 %collective-permute-start.3 = (bf16[128,256]{1,0:T(8,128)(2,1)S(1)}, bf16[128,256]{1,0:T(8,128)(2,1)S(1)}, u32[]{:S(2)}, u32[]{:S(2)}) collective-permute-start(bf16[128,256]{1,0:T(8,128)(2,1)S(1)} %get-tuple-element.48.x_ref), channel_id=1, source_target_pairs={{0,2},{2,4},{4,6},{6,8},{8,10},{10,12},{12,14},{14,16},{16,18},{18... | collective-permute-start | bytes 196616 | tf_op jit(solution)/shard_map/ppermute | solution.py:29
  31.2 3.1 %collective-permute-start.4 = (bf16[128,256]{1,0:T(8,128)(2,1)S(1)}, bf16[128,256]{1,0:T(8,128)(2,1)S(1)}, u32[]{:S(2)}, u32[]{:S(2)}) collective-permute-start(bf16[128,256]{1,0:T(8,128)(2,1)S(1)} %relay.6.got_ref), channel_id=1, source_target_pairs={{0,1},{1,0},{2,3},{3,2},{4,5},{5,4},{6,7},{7,6},{8,9},{9,8},{10,11... | collective-permute-start | bytes 196616 | tf_op jit(solution)/shard_map/ppermute | solution.py:23
  36.9 6.5 %collective-permute-start.5 = (bf16[128,256]{1,0:T(8,128)(2,1)S(1)}, bf16[128,256]{1,0:T(8,128)(2,1)S(1)}, u32[]{:S(2)}, u32[]{:S(2)}) collective-permute-start(bf16[128,256]{1,0:T(8,128)(2,1)S(1)} %get-tuple-element.54.x_ref), channel_id=1, source_target_pairs={{0,2},{2,4},{4,6},{6,8},{8,10},{10,12},{12,14},{14,16},{16,18},{18... | collective-permute-start | bytes 196616 | tf_op jit(solution)/shard_map/ppermute | solution.py:29
  43.4 3.4 %collective-permute-start.6 = (bf16[128,256]{1,0:T(8,128)(2,1)S(1)}, bf16[128,256]{1,0:T(8,128)(2,1)S(1)}, u32[]{:S(2)}, u32[]{:S(2)}) collective-permute-start(bf16[128,256]{1,0:T(8,128)(2,1)S(1)} %collective-permute-done.5.got_ref), channel_id=1, source_target_pairs={{0,1},{1,0},{2,3},{3,2},{4,5},{5,4},{6,7},{7,6},{8,9},{9,8},{10,11... | collective-permute-start | bytes 196616 | tf_op jit(solution)/shard_map/ppermute | solution.py:23
  72.0 8.2 %collective-permute-start.7 = (bf16[192,256]{1,0:T(8,128)(2,1)S(1)}, bf16[192,256]{1,0:T(8,128)(2,1)S(1)}, u32[]{:S(2)}, u32[]{:S(2)}) collective-permute-start(bf16[192,256]{1,0:T(8,128)(2,1)S(1)} %get-tuple-element.58.refs_0_.x_ref), channel_id=1, source_target_pairs={{0,2},{2,4},{4,6},{6,8},{8,10},{10,12},{12,14},{14,16},{16,18},{18... | collective-permute-start | bytes 294920 | tf_op jit(solution)/shard_map/ppermute | solution.py:29
  80.2 5.4 %collective-permute-start.8 = (bf16[192,256]{1,0:T(8,128)(2,1)S(1)}, bf16[192,256]{1,0:T(8,128)(2,1)S(1)}, u32[]{:S(2)}, u32[]{:S(2)}) collective-permute-start(bf16[192,256]{1,0:T(8,128)(2,1)S(1)} %relay.7.got_ref), channel_id=1, source_target_pairs={{0,1},{1,0},{2,3},{3,2},{4,5},{5,4},{6,7},{7,6},{8,9},{9,8},{10,11... | collective-permute-start | bytes 294920 | tf_op jit(solution)/shard_map/ppermute | solution.py:23
  88.6 7.5 %collective-permute-start.9 = (bf16[192,256]{1,0:T(8,128)(2,1)S(1)}, bf16[192,256]{1,0:T(8,128)(2,1)S(1)}, u32[]{:S(2)}, u32[]{:S(2)}) collective-permute-start(bf16[192,256]{1,0:T(8,128)(2,1)S(1)} %get-tuple-element.64.refs_0_.x_ref), channel_id=1, source_target_pairs={{0,2},{2,4},{4,6},{6,8},{8,10},{10,12},{12,14},{14,16},{16,18},{18... | collective-permute-start | bytes 294920 | tf_op jit(solution)/shard_map/ppermute | solution.py:29
  96.2 4.6 %collective-permute-start.10 = (bf16[192,256]{1,0:T(8,128)(2,1)S(1)}, bf16[192,256]{1,0:T(8,128)(2,1)S(1)}, u32[]{:S(2)}, u32[]{:S(2)}) collective-permute-start(bf16[192,256]{1,0:T(8,128)(2,1)S(1)} %relay.8.got_ref), channel_id=1, source_target_pairs={{0,1},{1,0},{2,3},{3,2},{4,5},{5,4},{6,7},{7,6},{8,9},{9,8},{10,11... | collective-permute-start | bytes 294920 | tf_op jit(solution)/shard_map/ppermute | solution.py:23
  103.8 7.6 %collective-permute-start.11 = (bf16[192,256]{1,0:T(8,128)(2,1)S(1)}, bf16[192,256]{1,0:T(8,128)(2,1)S(1)}, u32[]{:S(2)}, u32[]{:S(2)}) collective-permute-start(bf16[192,256]{1,0:T(8,128)(2,1)S(1)} %get-tuple-element.71.refs_0_.x_ref), channel_id=1, source_target_pairs={{0,2},{2,4},{4,6},{6,8},{8,10},{10,12},{12,14},{14,16},{16,18},{18... | collective-permute-start | bytes 294920 | tf_op jit(solution)/shard_map/ppermute | solution.py:29
  111.4 4.6 %collective-permute-start.12 = (bf16[192,256]{1,0:T(8,128)(2,1)S(1)}, bf16[192,256]{1,0:T(8,128)(2,1)S(1)}, u32[]{:S(2)}, u32[]{:S(2)}) collective-permute-start(bf16[192,256]{1,0:T(8,128)(2,1)S(1)} %relay.9.got_ref), channel_id=1, source_target_pairs={{0,1},{1,0},{2,3},{3,2},{4,5},{5,4},{6,7},{7,6},{8,9},{9,8},{10,11... | collective-permute-start | bytes 294920 | tf_op jit(solution)/shard_map/ppermute | solution.py:23
  117.7 8.8 %collective-permute-start.13 = (bf16[48,1152]{1,0:T(8,128)(2,1)S(1)}, bf16[48,1152]{1,0:T(8,128)(2,1)S(1)}, u32[]{:S(2)}, u32[]{:S(2)}) collective-permute-start(bf16[48,1152]{1,0:T(8,128)(2,1)S(1)} %get-tuple-element.86), channel_id=1, source_target_pairs={{0,2},{2,0},{1,3},{3,1},{4,6},{6,4},{5,7},{7,5},{8,10},{10,8},{9,1... | collective-permute-start | bytes 331784 | tf_op jit(solution)/shard_map/ppermute | solution.py:484
  178.9 7.0 %collective-permute-start.14 = (bf16[48,1152]{1,0:T(8,128)(2,1)S(1)}, bf16[48,1152]{1,0:T(8,128)(2,1)S(1)}, u32[]{:S(2)}, u32[]{:S(2)}) collective-permute-start(bf16[48,1152]{1,0:T(8,128)(2,1)S(1)} %bitcast.19), channel_id=1, source_target_pairs={{0,2},{2,0},{1,3},{3,1},{4,6},{6,4},{5,7},{7,5},{8,10},{10,8},{9,1... | collective-permute-start | bytes 331784 | tf_op jit(solution)/shard_map/ppermute | solution.py:484
  185.9 8.0 %collective-permute-start.15 = (bf16[96,1152]{1,0:T(8,128)(2,1)S(1)}, bf16[96,1152]{1,0:T(8,128)(2,1)S(1)}, u32[]{:S(2)}, u32[]{:S(2)}) collective-permute-start(bf16[96,1152]{1,0:T(8,128)(2,1)S(1)} %rows.1.own_ref), channel_id=1, source_target_pairs={{0,1},{1,0},{2,3},{3,2},{4,5},{5,4},{6,7},{7,6},{8,9},{9,8},{10,11... | collective-permute-start | bytes 663560 | tf_op jit(solution)/shard_map/ppermute | solution.py:23

commit v10 on v9

--- a/solution.py
+++ b/solution.py
@@ -421,11 +421,11 @@
     token_ref[...] = own[:8, :128]
 
 
-def add_kernel(keep_ref, got_ref, _, out_ref):
+def add_kernel(keep_ref, got_ref, out_ref):
     out_ref[...] = (keep_ref[...].astype(F32) + got_ref[...].astype(F32)).astype(BF16)
 
 
-def rows_kernel(own_ref, got_ref, out_ref):
+def rows_kernel(own_ref, got_ref, _, out_ref):
     rows = own_ref.shape[0]
     low_half = lax.axis_index("yh") == 0
     own, got = own_ref[...], got_ref[...]
@@ -489,7 +489,7 @@
     out = [sds(keep.shape, BF16)]
     any_space = pl.BlockSpec(memory_space=pl.ANY)
     chunk = call(
-        add_kernel, "add", [v(keep), v(swap_halves(send)), (any_space, after)], out
+        add_kernel, "add", [v(keep), v(swap_halves(send))], out
     )[0]
     tiles = (rows // 8) * (lanes // 128)
     each = -(-tiles // length)
@@ -500,7 +500,7 @@
     chunk = chunk.reshape(rows // 8, lanes // 128, 8, 128).transpose(0, 2, 1, 3)
     chunk = chunk.reshape(rows, lanes)
     return call(
-        rows_kernel, "rows", [v(chunk), v(swap_halves(chunk))], [sds((2 * rows, lanes), BF16)]
+        rows_kernel, "rows", [v(chunk), v(swap_halves(chunk)), (any_space, after)], [sds((2 * rows, lanes), BF16)]
     )[0]
 
 

time: 196 us -> 196 us (level)
  no operation moved by 1% of the time
where the time goes in v10:
time: 196 us; the launch traced here: 195 us
  blocking collectives  74.5 us (38%)
  starting transfers between devices  49.6 us (25%)
  waiting for transfers between devices  41.1 us (21%)
  Pallas kernels  27.3 us (14%)
  local copies, waits for them, and re-layouts  2.03 us (1%)
    all_to_all x4, blocking collectives, exchange(): return lax.all_to_all(value, axes, 0, 0, tiled=True)  74.5 us
    ppermute x8, starting transfers between devices, swap_cores(): return lax.ppermute(value, 'core', [(0, 1), (1, 0)])  34.1 us
    ppermute x6, waiting for transfers between devices, widen(): got = lax.ppermute(value, SKY, pairs)  27.6 us
    pallas_call x25, Pallas kernels, call(): pl.pallas_call(body, name=name, in_specs=specs, out_specs=[pl.BlockSpec(m...  27.3 us
    ppermute x6, starting transfers between devices, widen(): got = lax.ppermute(value, SKY, pairs)  7.75 us
    ppermute x2, starting transfers between devices, swap_halves(): return lax.ppermute(value, 'yh', [(0, 1), (1, 0)])  7.73 us
    ppermute x8, waiting for transfers between devices, swap_cores(): return lax.ppermute(value, 'core', [(0, 1), (1, 0)])  7.28 us
    ppermute x2, waiting for transfers between devices, swap_halves(): return lax.ppermute(value, 'yh', [(0, 1), (1, 0)])  6.19 us
  transfers between devices with their start and end apart: 16, of which 16 were waited for; matrix products, arithmetic and copies ran while one was open for 0% of the time, Pallas kernels for 4%

profile of v10, /device:TPU:1, one launch (start us, length us, event | category | flops | bytes accessed | tf_op | source)
XLA Modules:
  0.0 195.4 jit_solution(15786923927638813189)
XLA Ops:
  2.1 8.8 %collective-permute-start = (bf16[112,256]{1,0:T(8,128)(2,1)}, bf16[112,256]{1,0:T(8,128)(2,1)S(1)}, u32[]{:S(2)}, u32[]{:S(2)}) collective-permute-start(bf16[112,256]{1,0:T(8,128)(2,1)} %pack.1.refs_0_), channel_id=1, source_target_pairs={{0,1},{1,0},{2,3},{3,2},{4,5},{5,4},{6,7},{7,6},{8,9},{9,8},{10,11... | collective-permute-start | bytes 172040 | tf_op jit(solution)/shard_map/ppermute | solution.py:23
  14.8 4.0 %collective-permute-done.1.refs_0_ = bf16[192,256]{1,0:T(8,128)(2,1)S(1)} collective-permute-done((bf16[192,256]{1,0:T(8,128)(2,1)S(1)}, bf16[192,256]{1,0:T(8,128)(2,1)S(1)}, u32[]{:S(2)}, u32[]{:S(2)}) %collective-permute-start.1) | collective-permute-done | bytes 98336 | tf_op jit(solution)/shard_map/ppermute | solution.py:29
  18.9 1.9 collective-permute-start.2
  22.1 2.6 %layers01.1 = (bf16[128,256]{1,0:T(8,128)(2,1)S(1)}, bf16[2,2,576,256]{3,2,1,0:T(8,128)(2,1)S(1)}, f32[4,64,256]{2,1,0:T(8,128)S(1)}, f32[2,64,256]{2,1,0:T(8,12...) custom-call(bf16[224,256]{1,0:T(8,128)(2,1)S(1)} %get-tuple-element., ...), custom_call_target="tpu_custom_call" | custom-call | tf_op jit(solution)/shard_map/layers01/pallas_call | solution.py:456
  26.0 1.7 unit.1.refs_1_.unit_ref
  27.6 3.5 %collective-permute-done.3.refs_0_ = bf16[128,256]{1,0:T(8,128)(2,1)S(1)} collective-permute-done((bf16[128,256]{1,0:T(8,128)(2,1)S(1)}, bf16[128,256]{1,0:T(8,128)(2,1)S(1)}, u32[]{:S(2)}, u32[]{:S(2)}) %collective-permute-start.3) | collective-permute-done | bytes 65568 | tf_op jit(solution)/shard_map/ppermute | solution.py:29
  31.2 1.9 collective-permute-start.4
  34.3 2.6 %layers.1 = (bf16[128,256]{1,0:T(8,128)(2,1)S(1)}, bf16[2,2,576,256]{3,2,1,0:T(8,128)(2,1)S(1)}, f32[4,64,256]{2,1,0:T(8,128)S(1)}, f32[2,64,256]{2,1,0:T(8,128)S(1)}) custom-call(bf16[128,256]{1,0:T(8,128)(2,1)S(1)} %get-tuple-element.48.x_ref, bf16[128,256]{1,0:T(8,128)(2,1)S(1)} %relay.6.got_ref, bf16[128,256]{1,0:T(8,128)(2,1)S(1)} %collective-permute-done.4.other_ref, ...), custom_call_target="tpu_custom_call" | custom-call | tf_op jit(solution)/shard_map/layers/pallas_call | solution.py:456
  38.2 5.2 %collective-permute-done.5.got_ref = bf16[128,256]{1,0:T(8,128)(2,1)S(1)} collective-permute-done((bf16[128,256]{1,0:T(8,128)(2,1)S(1)}, bf16[128,256]{1,0:T(8,128)(2,1)S(1)}, u32[]{:S(2)}, u32[]{:S(2)}) %collective-permute-start.5) | collective-permute-done | bytes 65568 | tf_op jit(solution)/shard_map/ppermute | solution.py:29
  43.4 2.5 %collective-permute-start.6 = (bf16[128,256]{1,0:T(8,128)(2,1)S(1)}, bf16[128,256]{1,0:T(8,128)(2,1)S(1)}, u32[]{:S(2)}, u32[]{:S(2)}) collective-permute-start(bf16[128,256]{1,0:T(8,128)(2,1)S(1)} %collective-permute-done.5.got_ref), channel_id=1, source_target_pairs={{0,1},{1,0},{2,3},{3,2},{4,5},{5,4},{6,7},{7,6},{8,9},{9,8},{10,11... | collective-permute-start | bytes 196616 | tf_op jit(solution)/shard_map/ppermute | solution.py:23
  46.8 2.8 %lastlayers.1 = (bf16[8,128,256]{2,1,0:T(8,128)(2,1)S(1)}, bf16[2,2,576,256]{3,2,1,0:T(8,128)(2,1)S(1)}, f32[4,64,256]{2,1,0:T(8,128)S(1)}, f32[2,64,256]{2,1,0:T(8,128)S(1)}) custom-call(bf16[128,256]{1,0:T(8,128)(2,1)S(1)} %get-tuple-element.54.x_ref, bf16[128,256]{1,0:T(8,128)(2,1)S(1)} %collective-permute-done.5.got_ref, ...), custom_call_target="tpu_custom_call" | custom-call | tf_op jit(solution)/shard_map/lastlayers/pallas_call | solution.py:456
  49.6 13.3 %all_to_all.20.parts_ref = bf16[8,128,256]{2,1,0:T(8,128)(2,1)S(1)} all-to-all(bf16[8,128,256]{2,1,0:T(8,128)(2,1)S(1)} %get-tuple-element.56), channel_id=1, replica_groups=mesh['branch'=8,'z'=16,'yh'=2,'core'=2] {'branch'}, dimensions={0} | all-to-all | bytes 1048576 | tf_op jit(solution)/shard_map/all_to_all | solution.py:472
  62.9 8.9 %all_to_all.21.unit_ref = bf16[8,64,256]{2,1,0:T(8,128)(2,1)S(1)} all-to-all(bf16[8,64,256]{2,1,0:T(8,128)(2,1)S(1)} %slope.1), channel_id=1, replica_groups=mesh['branch'=8,'z'=16,'yh'=2,'core'=2] {'branch'}, dimensions={0} | all-to-all | bytes 524288 | tf_op jit(solution)/shard_map/all_to_all | solution.py:472
  74.6 5.6 %collective-permute-done.7.refs_0_ = bf16[192,256]{1,0:T(8,128)(2,1)S(1)} collective-permute-done((bf16[192,256]{1,0:T(8,128)(2,1)S(1)}, bf16[192,256]{1,0:T(8,128)(2,1)S(1)}, u32[]{:S(2)}, u32[]{:S(2)}) %collective-permute-start.7) | collective-permute-done | bytes 98336 | tf_op jit(solution)/shard_map/ppermute | solution.py:29
  80.2 4.7 %collective-permute-start.8 = (bf16[192,256]{1,0:T(8,128)(2,1)S(1)}, bf16[192,256]{1,0:T(8,128)(2,1)S(1)}, u32[]{:S(2)}, u32[]{:S(2)}) collective-permute-start(bf16[192,256]{1,0:T(8,128)(2,1)S(1)} %relay.7.got_ref), channel_id=1, source_target_pairs={{0,1},{1,0},{2,3},{3,2},{4,5},{5,4},{6,7},{7,6},{8,9},{9,8},{10,11... | collective-permute-start | bytes 294920 | tf_op jit(solution)/shard_map/ppermute | solution.py:23
  85.6 3.0 %back.2 = (bf16[192,256]{1,0:T(8,128)(2,1)S(1)}, f32[2,64,256]{2,1,0:T(8,128)S(1)}, bf16[128,256]{1,0:T(8,128)(2,1)S(1)}) custom-call(bf16[192,256]{1,0:T(8,128)(2,1)S(1)} %get-tuple-element.58.refs_0_.x_ref, bf16[192,256]{1,0:T(8,128)(2,1)S(1)} %relay.7.got_ref, bf16[192,256]{1,0:T(8,128)(2,1)S(1)} %collective-permute-done.8.other_ref, ...), custom_call_target="tpu_custom_call" | custom-call | tf_op jit(solution)/shard_map/back/pallas_call | solution.py:456
  89.9 1.7 beside.4
  91.6 4.6 %collective-permute-done.9.refs_0_ = bf16[192,256]{1,0:T(8,128)(2,1)S(1)} collective-permute-done((bf16[192,256]{1,0:T(8,128)(2,1)S(1)}, bf16[192,256]{1,0:T(8,128)(2,1)S(1)}, u32[]{:S(2)}, u32[]{:S(2)}) %collective-permute-start.9) | collective-permute-done | bytes 98336 | tf_op jit(solution)/shard_map/ppermute | solution.py:29
  96.2 3.7 %collective-permute-start.10 = (bf16[192,256]{1,0:T(8,128)(2,1)S(1)}, bf16[192,256]{1,0:T(8,128)(2,1)S(1)}, u32[]{:S(2)}, u32[]{:S(2)}) collective-permute-start(bf16[192,256]{1,0:T(8,128)(2,1)S(1)} %relay.8.got_ref), channel_id=1, source_target_pairs={{0,1},{1,0},{2,3},{3,2},{4,5},{5,4},{6,7},{7,6},{8,9},{9,8},{10,11... | collective-permute-start | bytes 294920 | tf_op jit(solution)/shard_map/ppermute | solution.py:23
  100.8 3.0 %back.3 = (bf16[192,256]{1,0:T(8,128)(2,1)S(1)}, f32[2,64,256]{2,1,0:T(8,128)S(1)}, bf16[128,256]{1,0:T(8,128)(2,1)S(1)}) custom-call(bf16[192,256]{1,0:T(8,128)(2,1)S(1)} %get-tuple-element.64.refs_0_.x_ref, bf16[192,256]{1,0:T(8,128)(2,1)S(1)} %relay.8.got_ref, bf16[192,256]{1,0:T(8,128)(2,1)S(1)} %collective-permute-done.10.other_ref, ...), custom_call_target="tpu_custom_call" | custom-call | tf_op jit(solution)/shard_map/back/pallas_call | solution.py:456
  105.1 1.7 beside.5
  106.7 4.7 %collective-permute-done.11.refs_0_ = bf16[192,256]{1,0:T(8,128)(2,1)S(1)} collective-permute-done((bf16[192,256]{1,0:T(8,128)(2,1)S(1)}, bf16[192,256]{1,0:T(8,128)(2,1)S(1)}, u32[]{:S(2)}, u32[]{:S(2)}) %collective-permute-start.11) | collective-permute-done | bytes 98336 | tf_op jit(solution)/shard_map/ppermute | solution.py:29
  111.4 3.7 %collective-permute-start.12 = (bf16[192,256]{1,0:T(8,128)(2,1)S(1)}, bf16[192,256]{1,0:T(8,128)(2,1)S(1)}, u32[]{:S(2)}, u32[]{:S(2)}) collective-permute-start(bf16[192,256]{1,0:T(8,128)(2,1)S(1)} %relay.9.got_ref), channel_id=1, source_target_pairs={{0,1},{1,0},{2,3},{3,2},{4,5},{5,4},{6,7},{7,6},{8,9},{9,8},{10,11... | collective-permute-start | bytes 294920 | tf_op jit(solution)/shard_map/ppermute | solution.py:23
  116.1 1.6 lastback.1
  117.7 5.6 %collective-permute-start.13 = (bf16[48,1152]{1,0:T(8,128)(2,1)S(1)}, bf16[48,1152]{1,0:T(8,128)(2,1)S(1)}, u32[]{:S(2)}, u32[]{:S(2)}) collective-permute-start(bf16[48,1152]{1,0:T(8,128)(2,1)S(1)} %get-tuple-element.86), channel_id=1, source_target_pairs={{0,2},{2,0},{1,3},{3,1},{4,6},{6,4},{5,7},{7,5},{8,10},{10,8},{9,1... | collective-permute-start | bytes 331784 | tf_op jit(solution)/shard_map/ppermute | solution.py:484
  123.3 3.1 %collective-permute-done.13.got_ref = bf16[48,1152]{1,0:T(8,128)(2,1)S(1)} collective-permute-done((bf16[48,1152]{1,0:T(8,128)(2,1)S(1)}, bf16[48,1152]{1,0:T(8,128)(2,1)S(1)}, u32[]{:S(2)}, u32[]{:S(2)}) %collective-permute-start.13) | collective-permute-done | bytes 110624 | tf_op jit(solution)/shard_map/ppermute | solution.py:484
  126.5 34.8 %all_to_all.22 = bf16[16,4,8,128]{3,2,1,0:T(8,128)(2,1)S(1)} all-to-all(bf16[16,4,8,128]{3,2,1,0:T(8,128)(2,1)S(1)} %bitcast.26), channel_id=1, replica_groups=mesh['branch'=8,'z'=16,'yh'=2,'core'=2] {'z'}, dimensions={0} | all-to-all | bytes 262144 | tf_op jit(solution)/shard_map/all_to_all | solution.py:472
  161.4 17.5 %all_to_all.23 = bf16[16,4,8,128]{3,2,1,0:T(8,128)(2,1)S(1)} all-to-all(bf16[16,4,8,128]{3,2,1,0:T(8,128)(2,1)S(1)} %broadcast_in_dim.13), channel_id=1, replica_groups=mesh['branch'=8,'z'=16,'yh'=2,'core'=2] {'z'}, dimensions={0} | all-to-all | bytes 262144 | tf_op jit(solution)/shard_map/all_to_all | solution.py:472
  178.9 2.1 %collective-permute-start.14 = (bf16[48,1152]{1,0:T(8,128)(2,1)S(1)}, bf16[48,1152]{1,0:T(8,128)(2,1)S(1)}, u32[]{:S(2)}, u32[]{:S(2)}) collective-permute-start(bf16[48,1152]{1,0:T(8,128)(2,1)S(1)} %bitcast.19), channel_id=1, source_target_pairs={{0,2},{2,0},{1,3},{3,1},{4,6},{6,4},{5,7},{7,5},{8,10},{10,8},{9,1... | collective-permute-start | bytes 331784 | tf_op jit(solution)/shard_map/ppermute | solution.py:484
  181.0 1.8 mapgrad.1
  182.8 3.1 %collective-permute-done.14.got_ref = bf16[48,1152]{1,0:T(8,128)(2,1)S(1)} collective-permute-done((bf16[48,1152]{1,0:T(8,128)(2,1)S(1)}, bf16[48,1152]{1,0:T(8,128)(2,1)S(1)}, u32[]{:S(2)}, u32[]{:S(2)}) %collective-permute-start.14) | collective-permute-done | bytes 110624 | tf_op jit(solution)/shard_map/ppermute | solution.py:484
  185.9 6.9 %collective-permute-start.15 = (bf16[96,1152]{1,0:T(8,128)(2,1)S(1)}, bf16[96,1152]{1,0:T(8,128)(2,1)S(1)}, u32[]{:S(2)}, u32[]{:S(2)}) collective-permute-start(bf16[96,1152]{1,0:T(8,128)(2,1)S(1)} %rows.1.own_ref), channel_id=1, source_target_pairs={{0,1},{1,0},{2,3},{3,2},{4,5},{5,4},{6,7},{7,6},{8,9},{9,8},{10,11... | collective-permute-start | bytes 663560 | tf_op jit(solution)/shard_map/ppermute | solution.py:23
  (41 shorter events, 22.1 us)
Async XLA Ops:
  2.1 9.9 %collective-permute-start = (bf16[112,256]{1,0:T(8,128)(2,1)}, bf16[112,256]{1,0:T(8,128)(2,1)S(1)}, u32[]{:S(2)}, u32[]{:S(2)}) collective-permute-start(bf16[112,256]{1,0:T(8,128)(2,1)} %pack.1.refs_0_), channel_id=1, source_target_pairs={{0,1},{1,0},{2,3},{3,2},{4,5},{5,4},{6,7},{7,6},{8,9},{9,8},{10,11... | collective-permute-start | bytes 172040 | tf_op jit(solution)/shard_map/ppermute | solution.py:23
  10.9 0.8 copy-start.1
  11.7 14.2 %copy-start.2 = (bf16[9,32,256]{2,1,0:T(8,128)(2,1)S(1)}, bf16[9,32,256]{2,1,0:T(8,128)(2,1)}, u32[]{:S(2)}) copy-start(bf16[9,32,256]{2,1,0:T(8,128)(2,1)} %param.12) | copy-start | bytes 442372
  12.0 6.9 %collective-permute-start.1 = (bf16[192,256]{1,0:T(8,128)(2,1)S(1)}, bf16[192,256]{1,0:T(8,128)(2,1)S(1)}, u32[]{:S(2)}, u32[]{:S(2)}) collective-permute-start(bf16[192,256]{1,0:T(8,128)(2,1)S(1)} %get-tuple-element.46), channel_id=1, source_target_pairs={{0,2},{2,4},{4,6},{6,8},{8,10},{10,12},{12,14},{14,16},{16,18},{18... | collective-permute-start | bytes 294920 | tf_op jit(solution)/shard_map/ppermute | solution.py:29
  13.3 1.2 copy-start
  18.9 28.0 %copy-start.3 = (bf16[256,64]{0,1:T(8,128)(2,1)S(1)}, bf16[256,64]{0,1:T(8,128)(2,1)}, u32[]{:S(2)}) copy-start(bf16[256,64]{0,1:T(8,128)(2,1)} %param.11) | copy-start | bytes 98308
  18.9 3.2 %collective-permute-start.2 = (bf16[192,256]{1,0:T(8,128)(2,1)S(1)}, bf16[192,256]{1,0:T(8,128)(2,1)S(1)}, u32[]{:S(2)}, u32[]{:S(2)}) collective-permute-start(bf16[192,256]{1,0:T(8,128)(2,1)S(1)} %relay.5.got_ref), channel_id=1, source_target_pairs={{0,1},{1,0},{2,3},{3,2},{4,5},{5,4},{6,7},{7,6},{8,9},{9,8},{10,11... | collective-permute-start | bytes 294920 | tf_op jit(solution)/shard_map/ppermute | solution.py:23
  24.7 6.5 %collective-permute-start.3 = (bf16[128,256]{1,0:T(8,128)(2,1)S(1)}, bf16[128,256]{1,0:T(8,128)(2,1)S(1)}, u32[]{:S(2)}, u32[]{:S(2)}) collective-permute-start(bf16[128,256]{1,0:T(8,128)(2,1)S(1)} %get-tuple-element.48.x_ref), channel_id=1, source_target_pairs={{0,2},{2,4},{4,6},{6,8},{8,10},{10,12},{12,14},{14,16},{16,18},{18... | collective-permute-start | bytes 196616 | tf_op jit(solution)/shard_map/ppermute | solution.py:29
  31.2 3.1 %collective-permute-start.4 = (bf16[128,256]{1,0:T(8,128)(2,1)S(1)}, bf16[128,256]{1,0:T(8,128)(2,1)S(1)}, u32[]{:S(2)}, u32[]{:S(2)}) collective-permute-start(bf16[128,256]{1,0:T(8,128)(2,1)S(1)} %relay.6.got_ref), channel_id=1, source_target_pairs={{0,1},{1,0},{2,3},{3,2},{4,5},{5,4},{6,7},{7,6},{8,9},{9,8},{10,11... | collective-permute-start | bytes 196616 | tf_op jit(solution)/shard_map/ppermute | solution.py:23
  36.9 6.5 %collective-permute-start.5 = (bf16[128,256]{1,0:T(8,128)(2,1)S(1)}, bf16[128,256]{1,0:T(8,128)(2,1)S(1)}, u32[]{:S(2)}, u32[]{:S(2)}) collective-permute-start(bf16[128,256]{1,0:T(8,128)(2,1)S(1)} %get-tuple-element.54.x_ref), channel_id=1, source_target_pairs={{0,2},{2,4},{4,6},{6,8},{8,10},{10,12},{12,14},{14,16},{16,18},{18... | collective-permute-start | bytes 196616 | tf_op jit(solution)/shard_map/ppermute | solution.py:29
  43.4 3.4 %collective-permute-start.6 = (bf16[128,256]{1,0:T(8,128)(2,1)S(1)}, bf16[128,256]{1,0:T(8,128)(2,1)S(1)}, u32[]{:S(2)}, u32[]{:S(2)}) collective-permute-start(bf16[128,256]{1,0:T(8,128)(2,1)S(1)} %collective-permute-done.5.got_ref), channel_id=1, source_target_pairs={{0,1},{1,0},{2,3},{3,2},{4,5},{5,4},{6,7},{7,6},{8,9},{9,8},{10,11... | collective-permute-start | bytes 196616 | tf_op jit(solution)/shard_map/ppermute | solution.py:23
  72.0 8.2 %collective-permute-start.7 = (bf16[192,256]{1,0:T(8,128)(2,1)S(1)}, bf16[192,256]{1,0:T(8,128)(2,1)S(1)}, u32[]{:S(2)}, u32[]{:S(2)}) collective-permute-start(bf16[192,256]{1,0:T(8,128)(2,1)S(1)} %get-tuple-element.58.refs_0_.x_ref), channel_id=1, source_target_pairs={{0,2},{2,4},{4,6},{6,8},{8,10},{10,12},{12,14},{14,16},{16,18},{18... | collective-permute-start | bytes 294920 | tf_op jit(solution)/shard_map/ppermute | solution.py:29
  80.2 5.4 %collective-permute-start.8 = (bf16[192,256]{1,0:T(8,128)(2,1)S(1)}, bf16[192,256]{1,0:T(8,128)(2,1)S(1)}, u32[]{:S(2)}, u32[]{:S(2)}) collective-permute-start(bf16[192,256]{1,0:T(8,128)(2,1)S(1)} %relay.7.got_ref), channel_id=1, source_target_pairs={{0,1},{1,0},{2,3},{3,2},{4,5},{5,4},{6,7},{7,6},{8,9},{9,8},{10,11... | collective-permute-start | bytes 294920 | tf_op jit(solution)/shard_map/ppermute | solution.py:23
  88.6 7.5 %collective-permute-start.9 = (bf16[192,256]{1,0:T(8,128)(2,1)S(1)}, bf16[192,256]{1,0:T(8,128)(2,1)S(1)}, u32[]{:S(2)}, u32[]{:S(2)}) collective-permute-start(bf16[192,256]{1,0:T(8,128)(2,1)S(1)} %get-tuple-element.64.refs_0_.x_ref), channel_id=1, source_target_pairs={{0,2},{2,4},{4,6},{6,8},{8,10},{10,12},{12,14},{14,16},{16,18},{18... | collective-permute-start | bytes 294920 | tf_op jit(solution)/shard_map/ppermute | solution.py:29
  96.2 4.6 %collective-permute-start.10 = (bf16[192,256]{1,0:T(8,128)(2,1)S(1)}, bf16[192,256]{1,0:T(8,128)(2,1)S(1)}, u32[]{:S(2)}, u32[]{:S(2)}) collective-permute-start(bf16[192,256]{1,0:T(8,128)(2,1)S(1)} %relay.8.got_ref), channel_id=1, source_target_pairs={{0,1},{1,0},{2,3},{3,2},{4,5},{5,4},{6,7},{7,6},{8,9},{9,8},{10,11... | collective-permute-start | bytes 294920 | tf_op jit(solution)/shard_map/ppermute | solution.py:23
  103.8 7.6 %collective-permute-start.11 = (bf16[192,256]{1,0:T(8,128)(2,1)S(1)}, bf16[192,256]{1,0:T(8,128)(2,1)S(1)}, u32[]{:S(2)}, u32[]{:S(2)}) collective-permute-start(bf16[192,256]{1,0:T(8,128)(2,1)S(1)} %get-tuple-element.71.refs_0_.x_ref), channel_id=1, source_target_pairs={{0,2},{2,4},{4,6},{6,8},{8,10},{10,12},{12,14},{14,16},{16,18},{18... | collective-permute-start | bytes 294920 | tf_op jit(solution)/shard_map/ppermute | solution.py:29
  111.4 4.6 %collective-permute-start.12 = (bf16[192,256]{1,0:T(8,128)(2,1)S(1)}, bf16[192,256]{1,0:T(8,128)(2,1)S(1)}, u32[]{:S(2)}, u32[]{:S(2)}) collective-permute-start(bf16[192,256]{1,0:T(8,128)(2,1)S(1)} %relay.9.got_ref), channel_id=1, source_target_pairs={{0,1},{1,0},{2,3},{3,2},{4,5},{5,4},{6,7},{7,6},{8,9},{9,8},{10,11... | collective-permute-start | bytes 294920 | tf_op jit(solution)/shard_map/ppermute | solution.py:23
  117.7 8.8 %collective-permute-start.13 = (bf16[48,1152]{1,0:T(8,128)(2,1)S(1)}, bf16[48,1152]{1,0:T(8,128)(2,1)S(1)}, u32[]{:S(2)}, u32[]{:S(2)}) collective-permute-start(bf16[48,1152]{1,0:T(8,128)(2,1)S(1)} %get-tuple-element.86), channel_id=1, source_target_pairs={{0,2},{2,0},{1,3},{3,1},{4,6},{6,4},{5,7},{7,5},{8,10},{10,8},{9,1... | collective-permute-start | bytes 331784 | tf_op jit(solution)/shard_map/ppermute | solution.py:484
  178.9 7.0 %collective-permute-start.14 = (bf16[48,1152]{1,0:T(8,128)(2,1)S(1)}, bf16[48,1152]{1,0:T(8,128)(2,1)S(1)}, u32[]{:S(2)}, u32[]{:S(2)}) collective-permute-start(bf16[48,1152]{1,0:T(8,128)(2,1)S(1)} %bitcast.19), channel_id=1, source_target_pairs={{0,2},{2,0},{1,3},{3,1},{4,6},{6,4},{5,7},{7,5},{8,10},{10,8},{9,1... | collective-permute-start | bytes 331784 | tf_op jit(solution)/shard_map/ppermute | solution.py:484
  185.9 8.0 %collective-permute-start.15 = (bf16[96,1152]{1,0:T(8,128)(2,1)S(1)}, bf16[96,1152]{1,0:T(8,128)(2,1)S(1)}, u32[]{:S(2)}, u32[]{:S(2)}) collective-permute-start(bf16[96,1152]{1,0:T(8,128)(2,1)S(1)} %rows.1.own_ref), channel_id=1, source_target_pairs={{0,1},{1,0},{2,3},{3,2},{4,5},{5,4},{6,7},{7,6},{8,9},{9,8},{10,11... | collective-permute-start | bytes 663560 | tf_op jit(solution)/shard_map/ppermute | solution.py:23
